TPU v7x, 32 devices: a whole 2x2x4 slice. The times are simulated.
32 devices in a mesh: outer: 4 (over y, x), inner: 8 (over z, core).
Axes of the slice: x: 2, y: 2, z: 4, core: 2. Of those that a mesh axis runs over, the one named last changes fastest.
Arguments:
- inputs: bfloat16 [8192, 8192], P(('outer', 'inner')), may hold values from -6 to 6
- step_size: float32 [8192, 128], P(('outer', 'inner')), may hold values from 0 to 1
- log_decay: float32 [8192, 128], P(('outer', 'inner')), may hold values from -1.25 to 0
- b_matrix: bfloat16 [8192, 1024], P(('outer', 'inner')), may hold values from -1 to 1
- c_matrix: bfloat16 [8192, 1024], P(('outer', 'inner')), may hold values from -1 to 1
- skip_gain: float32 [128], replicated, may hold values from 0.5 to 1.5
Outputs:
- mixed: bfloat16 [8192, 8192], P(('outer', 'inner'))
All inputs are finite; a program needn't handle non-finite values.
Results may differ from a plain program's by a relative error of at most 0.006.
Values may be sent and summed in bfloat16 or wider, within the bound.
No kernel may reach another device: no remote copies, remote signals or barrier semaphores. Data moves between devices by JAX's collectives and lax.ppermute only.
A program may use at most 128 MiB of HBM per device.

v0:
```python
import jax
import jax.numpy as jnp
from jax import lax
from jax.sharding import PartitionSpec as P

GROUPS = 8
BLOCK_LENGTH = 256


MIXED_PREC = lax.Precision.HIGH


def passed_along(block, axis, distance):
    devices = range(lax.axis_size(axis))
    route = [(i - distance, i) for i in devices if i - distance in devices]
    return lax.ppermute(block, axis, route)


def group_pass(scaled, decay_log, b_rows, c_rows):
    seq_rows, head_count, head_width = scaled.shape
    state_width = b_rows.shape[1]
    block_rows = min(BLOCK_LENGTH, seq_rows)
    per_turn = min(8, seq_rows // block_rows)
    turn_count = seq_rows // (block_rows * per_turn)
    lower_mask = jnp.tril(jnp.ones((block_rows, block_rows), dtype=bool))

    def advance(carried_pair, pieces):
        carried, offset = carried_pair
        scaled_part, log_part, b_part, c_part = pieces
        running = jnp.cumsum(log_part, axis=1)
        scores = jnp.einsum("ktn,ksn->kts", c_part, b_part, preferred_element_type=jnp.float32)
        spread = running[:, :, None, :] - running[:, None, :, :]
        weights = scores[..., None] * jnp.exp(
            jnp.where(lower_mask[None, :, :, None], spread, -jnp.inf)
        )
        as_float = scaled_part.astype(jnp.float32)
        within = jnp.einsum("ktsh,kshp->kthp", weights, as_float, precision=MIXED_PREC)
        span_total = running[:, -1, :]
        to_end = jnp.exp(span_total[:, None, :] - running)
        local_states = jnp.einsum(
            "kshp,ksn->khpn",
            as_float * to_end[..., None],
            b_part.astype(jnp.float32),
            precision=MIXED_PREC,
        )
        entering = []
        for member in range(per_turn):
            entering.append(carried)
            carried = jnp.exp(span_total[member])[:, None, None] * carried + local_states[member]
        entering = jnp.stack(entering)
        from_carry = (
            jnp.einsum("ktn,khpn->kthp", c_part.astype(jnp.float32), entering, precision=MIXED_PREC)
            * jnp.exp(running)[..., None]
        )
        before = jnp.cumsum(span_total, axis=0) - span_total + offset[None, :]
        return (
            (carried, offset + jnp.sum(span_total, axis=0)),
            (within + from_carry, running + before[:, None, :]),
        )

    start_pair = (
        jnp.zeros((head_count, head_width, state_width), jnp.float32),
        jnp.zeros((head_count,), jnp.float32),
    )
    pieces = (
        scaled.reshape(turn_count, per_turn, block_rows, head_count, head_width),
        decay_log.reshape(turn_count, per_turn, block_rows, head_count),
        b_rows.reshape(turn_count, per_turn, block_rows, state_width),
        c_rows.reshape(turn_count, per_turn, block_rows, state_width),
    )
    (end_state, block_log), (outputs, running_all) = lax.scan(advance, start_pair, pieces)
    return (
        outputs.reshape(seq_rows, head_count, head_width),
        end_state,
        block_log,
        running_all.reshape(seq_rows, head_count),
    )


def carry_chain(block_log, end_state):
    incoming = jnp.zeros_like(end_state)
    for handoff_turn in range(lax.axis_size("outer") - 1):
        incoming = passed_along(
            jnp.exp(block_log)[:, None, None] * incoming + end_state, "outer", 1
        )
    return incoming


def local(inputs, step_size, log_decay, b_matrix, c_matrix, skip_gain):
    tokens = inputs.shape[0]
    head_count = step_size.shape[1]
    head_width = inputs.shape[1] // head_count
    state_width = b_matrix.shape[1] // GROUPS
    inner_count = lax.axis_size("inner")
    heads_dev = head_count // inner_count
    copies = inner_count // GROUPS
    b_copy = jnp.repeat(b_matrix.reshape(tokens, GROUPS, state_width), copies, axis=1).reshape(
        tokens, inner_count * state_width
    )
    c_copy = jnp.repeat(c_matrix.reshape(tokens, GROUPS, state_width), copies, axis=1).reshape(
        tokens, inner_count * state_width
    )
    head_inputs, b_rows, c_rows = (
        lax.all_to_all(inputs, "inner", split_axis=1, concat_axis=0, tiled=True),
        lax.all_to_all(b_copy, "inner", split_axis=1, concat_axis=0, tiled=True),
        lax.all_to_all(c_copy, "inner", split_axis=1, concat_axis=0, tiled=True),
    )
    step_rates, decay_log = (
        lax.all_to_all(step_size, "inner", split_axis=1, concat_axis=0, tiled=True),
        lax.all_to_all(log_decay, "inner", split_axis=1, concat_axis=0, tiled=True),
    )
    seq_rows = head_inputs.shape[0]
    head_inputs = head_inputs.reshape(seq_rows, heads_dev, head_width)
    scaled = (head_inputs.astype(jnp.float32) * step_rates[:, :, None]).astype(jnp.bfloat16)
    outputs, end_state, block_log, running_all = group_pass(scaled, decay_log, b_rows, c_rows)
    incoming = carry_chain(block_log, end_state)
    carried_term = (
        jnp.einsum("tn,hpn->thp", c_rows.astype(jnp.float32), incoming, precision=MIXED_PREC)
        * jnp.exp(running_all)[:, :, None]
    )
    skip_local = lax.dynamic_slice_in_dim(skip_gain, lax.axis_index("inner") * heads_dev, heads_dev)
    mixed_out = outputs + carried_term + skip_local[None, :, None] * head_inputs.astype(jnp.float32)
    mixed_out = mixed_out.astype(jnp.bfloat16).reshape(seq_rows, heads_dev * head_width)
    return lax.all_to_all(mixed_out, "inner", split_axis=0, concat_axis=1, tiled=True)


def solution(mesh):
    placed = (
        P(("outer", "inner"), None),
        P(("outer", "inner"), None),
        P(("outer", "inner"), None),
        P(("outer", "inner"), None),
        P(("outer", "inner"), None),
        P(),
    )
    return jax.shard_map(
        local, mesh=mesh, in_specs=placed, out_specs=P(("outer", "inner"), None), check_vma=False
    )
```

profile of v0, /device:TPU:0, one launch (start us, length us, event | category | flops | bytes accessed | tf_op | source)
XLA Modules:
  0.0 358.2 jit_solution(7346321738298869880)
XLA Ops:
  1.6 6.4 %all-to-all-start.4 = ((f32[256,8,16]{0,2,1:T(8,128)}), f32[256,8,16]{0,2,1:T(8,128)S(1)}, u32[]{:S(2)}, u32[]{:S(2)}) async-start(f32[256,8,16]{0,2,1:T(8,128)} %bitcast.9), calls=%async_computation.4 | async-start | bytes 262144 | tf_op jit(solution)/shard_map/all_to_all | solution.py:110
  10.2 4.5 %all-to-all-done.4 = f32[256,8,16]{0,2,1:T(8,128)S(1)} async-done(((f32[256,8,16]{0,2,1:T(8,128)}), f32[256,8,16]{0,2,1:T(8,128)S(1)}, u32[]{:S(2)}, u32[]{:S(2)}) %all-to-all-start.4) | async-done | bytes 131104 | tf_op jit(solution)/shard_map/all_to_all | solution.py:110
  14.7 3.5 all-to-all-start.3
  20.5 13.0 %all-to-all-done.3 = bf16[256,8,128]{2,0,1:T(8,128)(2,1)S(1)} async-done(((bf16[256,8,128]{2,0,1:T(8,128)(2,1)}), bf16[256,8,128]{2,0,1:T(8,128)(2,1)S(1)}, u32[]{:S(2)}, u32[]{:S(2)}) %all-to-all-start.3) | async-done | bytes 524320 | tf_op jit(solution)/shard_map/all_to_all | solution.py:105
  33.5 3.5 all-to-all-start.2
  37.0 6.4 %copy.45 = bf16[256,8192]{0,1:T(8,128)(2,1)} copy(bf16[256,8192]{1,0:T(8,128)(2,1)} %param.6) | data formatting | bytes 8388608 | tf_op args[0]
  43.4 8.9 %all-to-all-done.2 = bf16[256,8,128]{2,0,1:T(8,128)(2,1)S(1)} async-done(((bf16[256,8,128]{2,0,1:T(8,128)(2,1)}), bf16[256,8,128]{2,0,1:T(8,128)(2,1)S(1)}, u32[]{:S(2)}, u32[]{:S(2)}) %all-to-all-start.2) | async-done | bytes 524320 | tf_op jit(solution)/shard_map/all_to_all | solution.py:106
  52.3 4.7 %all-to-all-start = ((bf16[256,8,1024]{0,2,1:T(8,128)(2,1)}), bf16[256,8,1024]{0,2,1:T(8,128)(2,1)}, u32[]{:S(2)}, u32[]{:S(2)}) async-start(bf16[256,8,1024]{0,2,1:T(8,128)(2,1)} %bitcast.156), calls=%async_computation | async-start | bytes 8388608 | tf_op jit(solution)/shard_map/all_to_all | solution.py:104
  59.8 4.6 %reduce-window.6 = f32[8,16,2,128]{3,1,2,0:T(8,128)S(1)} reduce-window(f32[8,16,2,128]{3,1,2,0:T(8,128)S(1)} %copy_bitcast_fusion, f32[]{:T(128)} %constant.19.clone.1), window={size=1x1x1x128 pad=0_0x0_0x0_0x127_0}, to_apply=%region_0.1 | reduce-window | flops 4161536 | bytes 262148 | tf_op jit(solution)/shard_map/reduce-window
  67.9 83.0 %all-to-all-done = bf16[256,8,1024]{0,2,1:T(8,128)(2,1)} async-done(((bf16[256,8,1024]{0,2,1:T(8,128)(2,1)}), bf16[256,8,1024]{0,2,1:T(8,128)(2,1)}, u32[]{:S(2)}, u32[]{:S(2)}) %all-to-all-start) | async-done | bytes 4194336 | tf_op jit(solution)/shard_map/all_to_all | solution.py:104
  154.3 9.6 %convert_bitcast_fusion = (f32[8,256,1024]{1,2,0:T(8,128)}, f32[256,8,1024]{0,2,1:T(8,128)}) fusion(bf16[256,8,1024]{0,2,1:T(8,128)(2,1)} %all-to-all-done), kind=kLoop, calls=%fused_computation.22 | loop fusion | flops 2097152 | bytes 20971520 | tf_op jit(solution)/shard_map/convert_element_type | solution.py:114
  164.0 6.1 %fusion.15 = f32[8,16,64,128]{3,2,1,0:T(8,128)S(1)} fusion(f32[8,256,16]{1,2,0:T(8,128)} %get-tuple-element.56, f32[8,256,16,64]{1,3,2,0:T(8,128)} %bitcast.153, f32[8,256,16]{1,2,0:T(8,128)S(1)} %bitcast.163, bf16[256,8,128]{2,0,1:T(8,128)(2,1)S(1)} %all-to-all-done.3), kind=kOutput, calls=%fused_computation.17 | convolution fusion | flops 1619001344 | bytes 13369344 | tf_op jit(solution)/shard_map/while/body/eval_jaxpr/kshp,ksn->khpn/dot_general | solution.py:40
  170.5 3.7 %collective-permute-start = (f32[16,64,128]{2,1,0:T(8,128)S(1)}, f32[16,64,128]{2,1,0:T(8,128)S(1)}, u32[]{:S(2)}, u32[]{:S(2)}) collective-permute-start(f32[16,64,128]{2,1,0:T(8,128)S(1)} %get-tuple-element.45), channel_id=1, source_target_pairs={{0,8},{8,16},{16,24},{1,9},{9,17},{17,25},{2,10},{10,18},{18,26},{... | collective-permute-start | bytes 1572872 | tf_op jit(solution)/shard_map/ppermute | solution.py:16
  174.7 17.2 %fusion = f32[8,16,64,256]{3,2,1,0:T(8,128)} fusion(f32[8,256,16]{1,2,0:T(8,128)S(1)} %bitcast_bitcast_fusion, f32[8,256,256]{2,1,0:T(8,128)S(1)} %fusion.29, pred[256,256]{1,0:T(8,128)(4,1)S(1)} %copy-done.5, f32[8,256,16,64]{1,3,2,0:T(8,128)S(1)} %bitcast.154, f32[8,256,16]{1,2,0:T(8,128)S(1)} %bitcast.164), kind=kOutput, calls=%fused_computation | convolution fusion | flops 3250585600 | bytes 19202048 | tf_op jit(solution)/shard_map/while/body/eval_jaxpr/ktsh,kshp->kthp/dot_general | solution.py:37
  192.6 3.4 collective-permute-start.1
  198.3 9.1 %collective-permute-done.1 = f32[16,64,128]{2,1,0:T(8,128)S(1)} collective-permute-done((f32[16,64,128]{2,1,0:T(8,128)S(1)}, f32[16,64,128]{2,1,0:T(8,128)S(1)}, u32[]{:S(2)}, u32[]{:S(2)}) %collective-permute-start.1) | collective-permute-done | bytes 524320 | tf_op jit(solution)/shard_map/ppermute | solution.py:16
  207.6 4.9 %collective-permute-start.2 = (f32[16,64,128]{2,1,0:T(8,128)S(1)}, f32[16,64,128]{2,1,0:T(8,128)S(1)}, u32[]{:S(2)}, u32[]{:S(2)}) collective-permute-start(f32[16,64,128]{2,1,0:T(8,128)S(1)} %multiply_add_fusion), channel_id=1, source_target_pairs={{0,8},{8,16},{16,24},{1,9},{9,17},{17,25},{2,10},{10,18},{18,26},{... | collective-permute-start | bytes 1572872 | tf_op jit(solution)/shard_map/ppermute | solution.py:16
  212.4 7.8 %fusion.14 = f32[8,16,8,8,256]{4,3,2,1,0:T(8,128)S(1)} fusion(f32[8,16,64,256]{3,2,1,0:T(8,128)} %fusion, f32[8,256,16]{1,2,0:T(8,128)S(1)} %copy-done.3, f32[8,16,64,128]{3,2,1,0:T(8,128)} %copy-done.2, bf16[256,8,128]{2,0,1:T(8,128)(2,1)S(1)} %all-to-all-done.2), kind=kOutput, calls=%fused_computation.16 | convolution fusion | flops 1614807040 | bytes 21626880 | tf_op jit(solution)/shard_map/while/body/eval_jaxpr/ktn,khpn->kthp/dot_general | solution.py:52
  220.3 4.3 %copy.65 = f32[8,16,8,8,256]{4,3,0,2,1:T(8,128)} copy(f32[8,16,8,8,256]{4,3,2,1,0:T(8,128)S(1)} %fusion.14) | data formatting | bytes 16777216 | tf_op jit(solution)/shard_map/reshape | solution.py:73
  224.5 8.1 %copy.58 = f32[8,256,1024]{1,0,2:T(8,128)} copy(f32[8,256,1024]{1,2,0:T(8,128)S(1)} %bitcast.152) | data formatting | bytes 16777216 | tf_op jit(solution)/shard_map/convert_element_type | solution.py:114
  232.6 9.3 %reshape.159 = f32[2048,16,64]{0,2,1:T(8,128)} reshape(f32[8,256,1024]{1,0,2:T(8,128)} %copy.58) | data formatting | bytes 16777216 | tf_op jit(solution)/shard_map/convert_element_type | solution.py:114
  241.9 9.0 %fusion.12 = bf16[2048,16,64]{0,2,1:T(8,128)(2,1)S(1)} fusion(f32[2048,16,64]{0,2,1:T(8,128)} %bitcast.150, f32[2048,16,64]{0,2,1:T(8,128)} %reshape.159, f32[16,64,128]{2,1,0:T(8,128)S(1)} %collective-permute-done.2, bf16[2048,128,1]{1,0,2:T(8,128)(2,1)S(1)} %bitcast.159, f32[16]{0:T(128)S(1)} %copy-done.11, f32[2048,16]{0,1:T(8,128)S(1)} %bitcast.162), kind=kOutput, calls=%fused_computation.13 | convolution fusion | flops 1621098496 | bytes 22151232 | tf_op jit(solution)/shard_map/tn,hpn->thp/dot_general | solution.py:118
  253.3 98.6 %all_to_all.90 = bf16[8,256,1024]{1,2,0:T(8,128)(2,1)} all-to-all(bf16[8,256,1024]{1,2,0:T(8,128)(2,1)S(1)} %copy.59), channel_id=1, replica_groups=mesh['outer'=4,'inner'=8] {'inner'}, dimensions={0} | all-to-all | bytes 8388608 | tf_op jit(solution)/shard_map/all_to_all | solution.py:124
  351.9 6.3 %copy.60 = bf16[256,8192]{1,0:T(8,128)(2,1)} copy(bf16[256,8192]{0,1:T(8,128)(2,1)} %bitcast.158) | data formatting | bytes 8388608 | tf_op jit(solution)/shard_map/all_to_all | solution.py:124
  (72 shorter events, 22.2 us)
Async XLA Ops:
  1.6 13.1 %all-to-all-start.4 = ((f32[256,8,16]{0,2,1:T(8,128)}), f32[256,8,16]{0,2,1:T(8,128)S(1)}, u32[]{:S(2)}, u32[]{:S(2)}) async-start(f32[256,8,16]{0,2,1:T(8,128)} %bitcast.9), calls=%async_computation.4 | async-start | bytes 262144 | tf_op jit(solution)/shard_map/all_to_all | solution.py:110
  14.7 18.8 %all-to-all-start.3 = ((bf16[256,8,128]{2,0,1:T(8,128)(2,1)}), bf16[256,8,128]{2,0,1:T(8,128)(2,1)S(1)}, u32[]{:S(2)}, u32[]{:S(2)}) async-start(bf16[256,8,128]{2,0,1:T(8,128)(2,1)} %copy.50), calls=%async_computation.3 | async-start | bytes 1048576 | tf_op jit(solution)/shard_map/all_to_all | solution.py:105
  33.5 18.8 %all-to-all-start.2 = ((bf16[256,8,128]{2,0,1:T(8,128)(2,1)}), bf16[256,8,128]{2,0,1:T(8,128)(2,1)S(1)}, u32[]{:S(2)}, u32[]{:S(2)}) async-start(bf16[256,8,128]{2,0,1:T(8,128)(2,1)} %copy.48), calls=%async_computation.2 | async-start | bytes 1048576 | tf_op jit(solution)/shard_map/all_to_all | solution.py:106
  52.3 4.7 %copy-start.4 = (f32[256,128]{1,0:T(8,128)S(1)}, f32[256,128]{1,0:T(8,128)}, u32[]{:S(2)}) copy-start(f32[256,128]{1,0:T(8,128)} %param.7) | copy-start | bytes 393220
  52.3 5.5 %copy-start.13 = (f32[128]{0:T(128)S(1)}, f32[128]{0:T(128)}, u32[]{:S(2)}) copy-start(f32[128]{0:T(128)} %param.11) | copy-start | bytes 1540
  52.3 98.7 %all-to-all-start = ((bf16[256,8,1024]{0,2,1:T(8,128)(2,1)}), bf16[256,8,1024]{0,2,1:T(8,128)(2,1)}, u32[]{:S(2)}, u32[]{:S(2)}) async-start(bf16[256,8,1024]{0,2,1:T(8,128)(2,1)} %bitcast.156), calls=%async_computation | async-start | bytes 8388608 | tf_op jit(solution)/shard_map/all_to_all | solution.py:104
  150.9 13.0 %all-to-all-start.1 = ((f32[256,8,16]{0,2,1:T(8,128)}), f32[256,8,16]{0,2,1:T(8,128)S(1)}, u32[]{:S(2)}, u32[]{:S(2)}) async-start(f32[256,8,16]{0,2,1:T(8,128)} %bitcast.165), calls=%async_computation.1 | async-start | bytes 262144 | tf_op jit(solution)/shard_map/all_to_all | solution.py:109
  163.9 6.2 %copy-start.6 = (f32[16]{0:T(128)S(1)}, f32[16]{0:T(128)}, u32[]{:S(2)}) copy-start(f32[16]{0:T(128)} %get-tuple-element.27) | copy-start | bytes 196
  163.9 6.2 %copy-start.7 = (f32[16]{0:T(128)S(1)}, f32[16]{0:T(128)}, u32[]{:S(2)}) copy-start(f32[16]{0:T(128)} %get-tuple-element.29) | copy-start | bytes 196
  163.9 6.2 %copy-start.8 = (f32[16]{0:T(128)S(1)}, f32[16]{0:T(128)}, u32[]{:S(2)}) copy-start(f32[16]{0:T(128)} %get-tuple-element.42) | copy-start | bytes 196
  163.9 6.2 %copy-start.10 = (f32[16]{0:T(128)S(1)}, f32[16]{0:T(128)}, u32[]{:S(2)}) copy-start(f32[16]{0:T(128)} %get-tuple-element.25) | copy-start | bytes 196
  163.9 6.2 %copy-start.12 = (f32[16]{0:T(128)S(1)}, f32[16]{0:T(128)}, u32[]{:S(2)}) copy-start(f32[16]{0:T(128)} %get-tuple-element.59) | copy-start | bytes 196
  163.9 10.3 %copy-start.1 = (f32[8,16,64,128]{3,2,1,0:T(8,128)S(1)}, f32[8,16,64,128]{3,2,1,0:T(8,128)}, u32[]{:S(2)}) copy-start(f32[8,16,64,128]{3,2,1,0:T(8,128)} %broadcast_dynamic-update-slice_fusion) | copy-start | bytes 12582916
  170.1 4.6 %copy-start = (f32[256,8,1024]{0,2,1:T(8,128)S(1)}, f32[256,8,1024]{0,2,1:T(8,128)}, u32[]{:S(2)}) copy-start(f32[256,8,1024]{0,2,1:T(8,128)} %get-tuple-element.54) | copy-start | bytes 25165828
  170.1 4.6 %copy-start.5 = (pred[256,256]{1,0:T(8,128)(4,1)S(1)}, pred[256,256]{1,0:T(8,128)(4,1)}, u32[]{:S(2)}) copy-start(pred[256,256]{1,0:T(8,128)(4,1)} %iota_compare_fusion) | copy-start | bytes 196612
  170.5 21.7 %collective-permute-start = (f32[16,64,128]{2,1,0:T(8,128)S(1)}, f32[16,64,128]{2,1,0:T(8,128)S(1)}, u32[]{:S(2)}, u32[]{:S(2)}) collective-permute-start(f32[16,64,128]{2,1,0:T(8,128)S(1)} %get-tuple-element.45), channel_id=1, source_target_pairs={{0,8},{8,16},{16,24},{1,9},{9,17},{17,25},{2,10},{10,18},{18,26},{... | collective-permute-start | bytes 1572872 | tf_op jit(solution)/shard_map/ppermute | solution.py:16
  191.8 0.6 copy-start.9
  192.1 20.4 %copy-start.3 = (f32[8,256,16]{1,2,0:T(8,128)S(1)}, f32[8,256,16]{1,2,0:T(8,128)}, u32[]{:S(2)}) copy-start(f32[8,256,16]{1,2,0:T(8,128)} %get-tuple-element.57) | copy-start | bytes 393220
  192.6 14.8 %collective-permute-start.1 = (f32[16,64,128]{2,1,0:T(8,128)S(1)}, f32[16,64,128]{2,1,0:T(8,128)S(1)}, u32[]{:S(2)}, u32[]{:S(2)}) collective-permute-start(f32[16,64,128]{2,1,0:T(8,128)S(1)} %multiply_add_fusion.1), channel_id=1, source_target_pairs={{0,8},{8,16},{16,24},{1,9},{9,17},{17,25},{2,10},{10,18},{18,26},{... | collective-permute-start | bytes 1572872 | tf_op jit(solution)/shard_map/ppermute | solution.py:16
  196.3 2.0 copy-start.2
  207.4 17.1 %slice-start = ((s8[8388608]{0:T(1024)(128)(4,1)}), s8[4194304]{0:T(1024)(128)(4,1)S(1)}, s32[]{:S(2)}) async-start(s8[8388608]{0:T(1024)(128)(4,1)} %bitcast.151), calls=%async_computation.6 | async-start | bytes 8388608
  207.6 34.3 %collective-permute-start.2 = (f32[16,64,128]{2,1,0:T(8,128)S(1)}, f32[16,64,128]{2,1,0:T(8,128)S(1)}, u32[]{:S(2)}, u32[]{:S(2)}) collective-permute-start(f32[16,64,128]{2,1,0:T(8,128)S(1)} %multiply_add_fusion), channel_id=1, source_target_pairs={{0,8},{8,16},{16,24},{1,9},{9,17},{17,25},{2,10},{10,18},{18,26},{... | collective-permute-start | bytes 1572872 | tf_op jit(solution)/shard_map/ppermute | solution.py:16
  212.4 12.1 %slice-start.1 = ((s8[8388608]{0:T(1024)(128)(4,1)}), s8[4194304]{0:T(1024)(128)(4,1)S(1)}, s32[]{:S(2)}) async-start(s8[8388608]{0:T(1024)(128)(4,1)} %bitcast.151), calls=%async_computation.7 | async-start | bytes 8388608
  232.6 9.3 %copy-start.11 = (f32[16]{0:T(128)S(1)}, f32[16]{0:T(128)}, u32[]{:S(2)}) copy-start(f32[16]{0:T(128)} %dynamic_slice.14) | copy-start | bytes 196
where the time goes:
time: 359 us; the launch traced here: 358 us
  waiting for transfers between devices  119 us (33%)
  blocking collectives  98.6 us (27%)
  local copies, waits for them, and re-layouts  47.6 us (13%)
  matrix products  40.5 us (11%)
  starting transfers between devices  33.4 us (9%)
  other arithmetic  19.2 us (5%)
    all_to_all x1, blocking collectives, local(): lax.all_to_all(mixed_out, 'inner', split_axis=0, concat_axis=1, tiled=True)  98.6 us
    all_to_all x1, waiting for transfers between devices, local(): lax.all_to_all(inputs, 'inner', split_axis=1, concat_axis=0, tiled=True)  83 us
    convert_element_type x2, local copies, waits for them, and re-layouts, local(): head_inputs.astype(jnp.float32) * step_rates[:, :, None]  17.4 us
    dot_general x1, matrix products, advance(): jnp.einsum('ktsh,kshp->kthp', weights, as_float, precision=MIXED_PREC)  17.2 us
    unnamed x39, local copies, waits for them, and re-layouts  15.9 us
    all_to_all x1, waiting for transfers between devices, local(): lax.all_to_all(b_copy, 'inner', split_axis=1, concat_axis=0, tiled=True)  13 us
    ppermute x3, starting transfers between devices, passed_along(): return lax.ppermute(block, axis, route)  12 us
    convert_element_type x1, other arithmetic, local(): head_inputs.astype(jnp.float32) * step_rates[:, :, None]  9.6 us
  transfers between devices with their start and end apart: 8, of which 5 were waited for; matrix products, arithmetic and copies ran while one was open for 22% of the time, Pallas kernels for 0%

commit v1 on v0

v1 whole, which is shorter than its diff:
```python
import functools
import math

import jax
import jax.numpy as jnp
from jax import lax
from jax.experimental import pallas as pl
from jax.experimental.pallas import tpu as pltpu
from jax.sharding import Mesh, PartitionSpec as P

GROUPS = 8
CORES = 2
LANES = 128
ROW_TILE = 8
HALF_ROWS = 128
ROW_BLOCK = 32
LOG2E = 1.0 / math.log(2.0)

F32 = jnp.float32
BF16 = jnp.bfloat16


def dot(a, b, contract=(1, 0), precision=None):
    dims = (((contract[0],), (contract[1],)), ((), ()))
    return lax.dot_general(a, b, dims, precision=precision, preferred_element_type=F32)


def spreader(heads, lanes, width):
    shape = (2 * lanes, heads * width)
    row = lax.broadcasted_iota(jnp.int32, shape, 0)
    col = lax.broadcasted_iota(jnp.int32, shape, 1)
    row = jnp.where(row >= lanes, row - lanes, row)
    return jnp.where(row == col // width, 1.0, 0.0).astype(BF16)


def high_low(values):
    high = values.astype(BF16)
    low = (values - high.astype(F32)).astype(BF16)
    return high, low


def spread(values, matrix):
    return dot(jnp.concatenate(high_low(values), axis=1), matrix)


def group_first(values, group, per_group):
    lanes = values.shape[1]
    return pltpu.roll(values, lax.rem(lanes - group * per_group, lanes), 1)


def params():
    return pltpu.CompilerParams(dimension_semantics=("arbitrary",))


def state_rows(x, b, factor, total, matrix):
    scaled = (x.astype(F32) * spread(factor, matrix)).astype(BF16)
    return dot(b, scaled, (0, 0)), spread(total, matrix)


def send_state_kernel(half, x, b, step, log, out, run_out, run_t_out, factor_out, total_out, matrix, *, dims):
    per_half, per_group, width = dims
    turn = pl.program_id(0)

    @pl.when(turn == 0)
    def _():
        rows = log.shape[0]
        upto = lax.broadcasted_iota(jnp.int32, (rows, rows), 1) <= lax.broadcasted_iota(jnp.int32, (rows, rows), 0)
        running = dot(upto.astype(F32), log[...], precision=lax.Precision.HIGHEST) * LOG2E
        last = running[rows - 1 :, :]
        run_out[...] = running
        run_t_out[...] = running.T
        factor_out[...] = step[...] * jnp.exp2(last - running)
        total_out[...] = jnp.broadcast_to(jnp.exp2(last), total_out.shape)
        matrix[...] = spreader(per_group, log.shape[1], width)

    group = half[0] * per_half + turn
    factor = group_first(factor_out[...], group, per_group)
    total = group_first(total_out[...], group, per_group)
    state, decay = state_rows(x[...], b[...], factor, total, matrix[...])
    states = state.shape[0]
    out[:states, :] = state.astype(BF16)
    high, low = high_low(decay)
    total_high, total_low = high_low(total_out[...])
    heads = total_high.shape[1]
    row = lax.broadcasted_iota(jnp.int32, decay.shape, 0)
    out[states:, :] = jnp.where(row == 0, high.astype(F32), low.astype(F32)).astype(BF16)
    tail = out[states:, :heads].astype(F32)
    packed = jnp.where(row[:, :heads] == 2, total_high.astype(F32), total_low.astype(F32))
    out[states:, :heads] = jnp.where(row[:, :heads] < 2, tail, packed).astype(BF16)


def own_state_kernel(half, x, b, factor_in, total_in, out, matrix, *, dims):
    per_half, per_group, width = dims
    turn = pl.program_id(0)

    @pl.when(turn == 0)
    def _():
        matrix[...] = spreader(per_group, factor_in.shape[1], width)

    group = half[0] * per_half + turn
    factor = group_first(factor_in[...], group, per_group)
    total = group_first(total_in[...], group, per_group)
    state, decay = state_rows(x[...], b[...], factor, total, matrix[...])
    states = state.shape[0]
    out[:states, :] = state
    out[states:, :] = decay


def both_decays(own_tail, got_tail):
    own_decay = own_tail[:1, :]
    got_decay = got_tail[:1, :].astype(F32) + got_tail[1:2, :].astype(F32)
    return own_decay, got_decay


def chip_total_kernel(core, own, own_tail, got, got_tail, total, out):
    first = core[0] == 0
    cols = own.shape[1]
    own_decay, got_decay = both_decays(own_tail[...], got_tail[...])
    on_own = jnp.where(first, got_decay, jnp.ones_like(got_decay))
    on_got = jnp.where(first, jnp.ones_like(own_decay), own_decay)
    out[:, :cols] = (on_own * own[...] + on_got * got[...].astype(F32)).astype(BF16)
    lanes = total.shape[1]
    half = lanes // CORES
    other_total = got_tail[2:3, :lanes].astype(F32) + got_tail[3:4, :lanes].astype(F32)
    both = total[...] * other_total
    both = jnp.where(first, both, pltpu.roll(both, half, 1))
    high, low = high_low(both)
    lane = lax.broadcasted_iota(jnp.int32, both.shape, 1)
    packed = jnp.where(lane < half, high.astype(F32), pltpu.roll(low.astype(F32), half, 1))
    out[:, cols:] = jnp.concatenate([packed] * (out.shape[0] // packed.shape[0]), axis=0).astype(BF16)


def prefix_kernel(sent, decays, out, *, width):
    chips, rows, lanes = sent.shape
    heads_here = lanes // width
    block = pl.program_id(0)
    half = decays.shape[2] // 2
    packed = decays[...]
    first_rows = jnp.concatenate([packed[k, :1, :].astype(F32) for k in range(chips)], axis=0)
    values = first_rows + pltpu.roll(first_rows, half, 1)
    values = pltpu.roll(values, lax.rem(2 * half - block * heads_here, 2 * half), 1)
    decay = spread(values, spreader(heads_here, 2 * half, width))
    state = jnp.zeros((rows, lanes), F32)
    for k in range(chips):
        out[k] = state.astype(BF16)
        state = decay[k : k + 1, :] * state + sent[k].astype(F32)


def incoming_kernel(core, own, own_tail, got, got_tail, entering, mine, send):
    first = core[0] == 0
    own_decay, got_decay = both_decays(own_tail[...], got_tail[...])
    state = entering[...].astype(F32)
    decay = jnp.where(first, own_decay, got_decay)
    later = decay * state + jnp.where(first, own[...], got[...].astype(F32))
    mine[...] = jnp.where(first, state, later).astype(BF16)
    send[...] = jnp.where(first, later, state).astype(BF16)


def within_kernel(x_ref, b_ref, c_ref, step_ref, run_ref, run_t_ref, skip_ref, out, matrix, *, dims):
    per_group, width = dims
    group = pl.program_id(0)
    rows = x_ref.shape[0]

    @pl.when(group == 0)
    def _():
        matrix[...] = spreader(per_group, step_ref.shape[1], width)

    spreading = matrix[...]
    step = group_first(step_ref[...], group, per_group)
    run = group_first(run_ref[...], group, per_group)
    skip = group_first(jnp.broadcast_to(skip_ref[...], (ROW_TILE, skip_ref.shape[1])), group, per_group)
    run_t = run_t_ref[pl.ds(pl.multiple_of(group * per_group, per_group), per_group), :]
    x = x_ref[...].astype(F32)
    scaled = (x * spread(step, spreading)).astype(BF16)
    skipped = spread(skip, spreading)[:1, :] * x
    pair = LANES // width
    lane = lax.broadcasted_iota(jnp.int32, (HALF_ROWS, LANES), 1) // width
    lower = lax.broadcasted_iota(jnp.int32, (HALF_ROWS, HALF_ROWS), 1) <= lax.broadcasted_iota(
        jnp.int32, (HALF_ROWS, HALF_ROWS), 0
    )
    b = b_ref[...]
    c = c_ref[...]
    for start in range(0, rows, HALF_ROWS):
        stop = start + HALF_ROWS
        scores = jnp.where(lower, dot(c[start:stop, :], b[start:stop, :], (1, 1)), 0.0)
        if start:
            edge = run[start - 1 : start, :]
            before = step[:start, :] * jnp.exp2(edge - run[:start, :])
            before = (x[:start, :] * spread(before, spreading)).astype(BF16)
            cross = dot(c[start:stop, :], b[:start, :], (1, 1)).astype(BF16)
            after = spread(jnp.exp2(run[start:stop, :] - edge), spreading)
            base = skipped[start:stop, :] + after * dot(cross, before)
        else:
            base = skipped[start:stop, :]
        for first in range(0, per_group, pair):
            cols = slice(first * width, (first + pair) * width)
            here = scaled[start:stop, cols]
            weights = []
            values = []
            for k in range(pair):
                head = first + k
                gap = run[start:stop, head : head + 1] - run_t[head : head + 1, start:stop]
                weights.append((scores * jnp.exp2(jnp.minimum(gap, 0.0))).astype(BF16))
                values.append(jnp.where(lane == k, here, jnp.zeros_like(here)))
            part = dot(jnp.concatenate(weights, axis=1), jnp.concatenate(values, axis=0))
            out[start:stop, cols] = base[:, cols] + part


def final_kernel(half, within, c, state, run_ref, *rest, dims):
    per_half, per_group, width = dims
    out, matrix = rest[-2:]
    turn = pl.program_id(0)

    @pl.when(turn == 0)
    def _():
        matrix[...] = spreader(per_group, run_ref.shape[1], width)

    group = half[0] * per_half + turn
    grown = spread(jnp.exp2(group_first(run_ref[...], group, per_group)), matrix[...])
    out[...] = (within[...] + grown * dot(c[...], state[...])).astype(BF16)


def local(inputs, step_size, log_decay, b_matrix, c_matrix, skip_gain, *, chip_axes, core_axis):
    tokens, channels = inputs.shape
    heads = step_size.shape[1]
    width = channels // heads
    states = b_matrix.shape[1] // GROUPS
    per_group = heads // GROUPS
    group_cols = per_group * width
    per_half = GROUPS // CORES
    half_cols = channels // CORES
    half_heads = heads // CORES
    chips = lax.axis_size(chip_axes)
    rows = states // chips
    tall = states + ROW_TILE

    core = lax.axis_index(core_axis).astype(jnp.int32)
    mine = core.reshape(1)
    other = (1 - core).reshape(1)

    def of_half(block_rows):
        return pl.BlockSpec((block_rows, group_cols), lambda i, half: (0, half[0] * per_half + i))

    def matrix_of_half():
        return pl.BlockSpec((tokens, states), lambda i, half: (0, half[0] * per_half + i))

    def by_turn(block_rows):
        return pl.BlockSpec((block_rows, group_cols), lambda i, half: (0, i))

    def whole(shape):
        return pl.BlockSpec(shape, lambda i, *_: (0,) * len(shape))

    spread_scratch = pltpu.VMEM((2 * heads, group_cols), BF16)
    half_dims = (per_half, per_group, width)

    send, run, run_t, factor, total = pl.pallas_call(
        functools.partial(send_state_kernel, dims=half_dims),
        grid_spec=pltpu.PrefetchScalarGridSpec(
            num_scalar_prefetch=1,
            grid=(per_half,),
            in_specs=[of_half(tokens), matrix_of_half(), whole((tokens, heads)), whole((tokens, heads))],
            out_specs=[
                by_turn(tall),
                whole((tokens, heads)),
                whole((heads, tokens)),
                whole((tokens, heads)),
                whole((ROW_TILE, heads)),
            ],
            scratch_shapes=[spread_scratch],
        ),
        out_shape=[
            jax.ShapeDtypeStruct((tall, half_cols), BF16),
            jax.ShapeDtypeStruct((tokens, heads), F32),
            jax.ShapeDtypeStruct((heads, tokens), F32),
            jax.ShapeDtypeStruct((tokens, heads), F32),
            jax.ShapeDtypeStruct((ROW_TILE, heads), F32),
        ],
        compiler_params=params(),
        name="send_state",
    )(other, inputs, b_matrix, step_size, log_decay)

    swap = [(0, 1), (1, 0)]
    got = lax.ppermute(send, core_axis, swap)

    own = pl.pallas_call(
        functools.partial(own_state_kernel, dims=half_dims),
        grid_spec=pltpu.PrefetchScalarGridSpec(
            num_scalar_prefetch=1,
            grid=(per_half,),
            in_specs=[of_half(tokens), matrix_of_half(), whole((tokens, heads)), whole((ROW_TILE, heads))],
            out_specs=by_turn(tall),
            scratch_shapes=[spread_scratch],
        ),
        out_shape=jax.ShapeDtypeStruct((tall, half_cols), F32),
        compiler_params=params(),
        name="own_state",
    )(mine, inputs, b_matrix, factor, total)

    def row_block(cols):
        return pl.BlockSpec((ROW_BLOCK, cols), lambda i, _: (i, 0))

    def tail():
        return pl.BlockSpec((ROW_TILE, half_cols), lambda i, _: (states // ROW_TILE, 0))

    state_specs = [row_block(half_cols), tail(), row_block(half_cols), tail()]
    chip_total = pl.pallas_call(
        chip_total_kernel,
        grid_spec=pltpu.PrefetchScalarGridSpec(
            num_scalar_prefetch=1,
            grid=(states // ROW_BLOCK,),
            in_specs=state_specs + [whole((ROW_TILE, heads))],
            out_specs=row_block(half_cols + heads),
        ),
        out_shape=jax.ShapeDtypeStruct((states, half_cols + heads), BF16),
        compiler_params=params(),
        name="chip_total",
    )(mine, own, own, got, got, total)

    sent = lax.all_to_all(
        chip_total.reshape(chips, rows, half_cols + heads), chip_axes, split_axis=0, concat_axis=0, tiled=True
    )

    within = pl.pallas_call(
        functools.partial(within_kernel, dims=(per_group, width)),
        grid=(GROUPS,),
        in_specs=[
            pl.BlockSpec((tokens, group_cols), lambda i: (0, i)),
            pl.BlockSpec((tokens, states), lambda i: (0, i)),
            pl.BlockSpec((tokens, states), lambda i: (0, i)),
            whole((tokens, heads)),
            whole((tokens, heads)),
            whole((heads, tokens)),
            whole((1, heads)),
        ],
        out_specs=pl.BlockSpec((tokens, group_cols), lambda i: (0, i)),
        out_shape=jax.ShapeDtypeStruct((tokens, channels), F32),
        scratch_shapes=[spread_scratch],
        compiler_params=params(),
        name="within",
    )(inputs, b_matrix, c_matrix, step_size, run, run_t, skip_gain.reshape(1, heads))

    entering = pl.pallas_call(
        functools.partial(prefix_kernel, width=width),
        grid=(per_half,),
        in_specs=[
            pl.BlockSpec((chips, rows, group_cols), lambda i: (0, 0, i)),
            pl.BlockSpec((chips, rows, heads), lambda i: (0, 0, half_cols // heads)),
        ],
        out_specs=pl.BlockSpec((chips, rows, group_cols), lambda i: (0, 0, i)),
        out_shape=jax.ShapeDtypeStruct((chips, rows, half_cols), BF16),
        compiler_params=params(),
        name="prefix",
    )(sent, sent)
    entering = lax.all_to_all(entering, chip_axes, split_axis=0, concat_axis=0, tiled=True)
    entering = entering.reshape(states, half_cols)

    own_entering, send_entering = pl.pallas_call(
        incoming_kernel,
        grid_spec=pltpu.PrefetchScalarGridSpec(
            num_scalar_prefetch=1,
            grid=(states // ROW_BLOCK,),
            in_specs=state_specs + [row_block(half_cols)],
            out_specs=[row_block(half_cols)] * 2,
        ),
        out_shape=[jax.ShapeDtypeStruct((states, half_cols), BF16)] * 2,
        compiler_params=params(),
        name="incoming",
    )(mine, own, own, got, got, entering)
    got_entering = lax.ppermute(send_entering, core_axis, swap)

    def finish(half, state, *result):
        return pl.pallas_call(
            functools.partial(final_kernel, dims=half_dims),
            grid_spec=pltpu.PrefetchScalarGridSpec(
                num_scalar_prefetch=1,
                grid=(per_half,),
                in_specs=[of_half(tokens), matrix_of_half(), by_turn(states), whole((tokens, heads))]
                + [pl.BlockSpec(memory_space=pl.ANY)] * len(result),
                out_specs=of_half(tokens),
                scratch_shapes=[spread_scratch],
            ),
            out_shape=jax.ShapeDtypeStruct((tokens, channels), BF16),
            input_output_aliases={5: 0} if result else {},
            compiler_params=params(),
            name="finish",
        )(half, within, c_matrix, state, run, *result)

    result = finish(mine, own_entering)
    return finish(other, got_entering, result)


def solution(mesh):
    outer, inner = mesh.axis_names
    chip_mesh = Mesh(
        mesh.devices.reshape(mesh.shape[outer], mesh.shape[inner] // CORES, CORES), (outer, "chip", "core")
    )
    placed = P((outer, "chip", "core"), None)
    return jax.shard_map(
        functools.partial(local, chip_axes=(outer, "chip"), core_axis="core"),
        mesh=chip_mesh,
        in_specs=(placed,) * 5 + (P(),),
        out_specs=placed,
        check_vma=False,
    )
```

time: 359 us -> 118 us (0.33)
  waiting for transfers between devices: 119 us -> 0.01 us
  Pallas kernels: 0 us -> 46.4 us
  local copies, waits for them, and re-layouts: 47.6 us -> 2.02 us
  matrix products: 40.5 us -> 0 us
  starting transfers between devices: 33.4 us -> 0.51 us
  blocking collectives: 98.6 us -> 68 us
  other arithmetic: 19.2 us -> 0 us
    all_to_all x5 -> x0, waiting for transfers between devices: 109 us -> none  [the longest x1 83 us: local(): lax.all_to_all(inputs, 'inner', split_axis=1, concat_axis=0, tiled=True)]
    pallas_call x0 -> x8, Pallas kernels: none -> 46.4 us  [the longest x1 12.6 us: local(): pl.pallas_call(functools.partial(within_kernel, dims=(per_group, width)),...]
    dot_general x5 -> x0, matrix products: 40.5 us -> none  [the longest x1 17.2 us: advance(): jnp.einsum('ktsh,kshp->kthp', weights, as_float, precision=MIXED_PREC)]
    all_to_all x1 -> x2, blocking collectives: 98.6 us -> 68 us  [the longest x1 36.8 us: local(): lax.all_to_all(chip_total.reshape(chips, rows, half_cols + heads), chip_a...]
    all_to_all x5 -> x0, starting transfers between devices: 21.4 us -> none  [the longest x1 6.35 us: local(): lax.all_to_all(log_decay, 'inner', split_axis=1, concat_axis=0, tiled=True)]
    convert_element_type x2 -> x0, local copies, waits for them, and re-layouts: 17.4 us -> none  [local(): head_inputs.astype(jnp.float32) * step_rates[:, :, None]]
    unnamed x39 -> x4, local copies, waits for them, and re-layouts: 15.9 us -> 2.02 us
    ppermute x3 -> x2, starting transfers between devices: 12 us -> 0.51 us  [the longest x1 0.51 us: local(): got = lax.ppermute(send, core_axis, swap)]
  transfers between devices with their start and end apart: 8 -> 2, of which waited for: 5 -> 0; matrix products, arithmetic and copies ran while one was open for 22% -> 0% of each run, Pallas kernels for 0% -> 20%
where the time goes in v1:
time: 118 us; the launch traced here: 117 us
  blocking collectives  68 us (58%)
  Pallas kernels  46.4 us (39%)
  local copies, waits for them, and re-layouts  2.02 us (2%)
    all_to_all x1, blocking collectives, local(): lax.all_to_all(chip_total.reshape(chips, rows, half_cols + heads), chip_a...  36.8 us
    all_to_all x1, blocking collectives, local(): lax.all_to_all(entering, chip_axes, split_axis=0, concat_axis=0, tiled=True)  31.2 us
    pallas_call x1, Pallas kernels, local(): pl.pallas_call(functools.partial(within_kernel, dims=(per_group, width)),...  12.6 us
    pallas_call x2, Pallas kernels, finish(): pl.pallas_call(functools.partial(final_kernel, dims=half_dims), grid_spec...  10.9 us
    pallas_call x1, Pallas kernels, local(): pl.pallas_call(functools.partial(send_state_kernel, dims=half_dims), grid...  5.26 us
    pallas_call x1, Pallas kernels, local(): pl.pallas_call(functools.partial(own_state_kernel, dims=half_dims), grid_...  4.97 us
    pallas_call x1, Pallas kernels, local(): pl.pallas_call(incoming_kernel, grid_spec=pltpu.PrefetchScalarGridSpec(nu...  4.35 us
    pallas_call x1, Pallas kernels, local(): pl.pallas_call(chip_total_kernel, grid_spec=pltpu.PrefetchScalarGridSpec(...  4.27 us
  transfers between devices with their start and end apart: 2, of which 0 were waited for; matrix products, arithmetic and copies ran while one was open for 0% of the time, Pallas kernels for 20%

profile of v1, /device:TPU:0, one launch (start us, length us, event | category | flops | bytes accessed | tf_op | source)
XLA Modules:
  0.0 116.9 jit_solution(8260609461751042167)
XLA Ops:
  0.0 5.3 %send_state.1 = (bf16[136,4096]{1,0:T(8,128)(2,1)}, f32[256,128]{1,0:T(8,128)}, f32[128,256]{1,0:T(8,128)}, f32[256,128]{1,0:T(8,128)}, f32[8,128]{1,0:T(8,128)}) custom-call(s32[1]{0:T(128)} %bitcast.half, bf16[256,8192]{1,0:T(8,128)(2,1)} %x.3, bf16[256,1024]{1,0:T(8,128)(2,1)} %b.3, f32[256,128]{1,0:T(8,128)} %step_ref.1, f32[256,128]{1,0:T(8,128)} %log.1), custom_call_target="tpu_custom_call" | custom-call | tf_op jit(solution)/shard_map/send_state/pallas_call | solution.py:256
  5.3 0.5 collective-permute-start
  5.8 5.0 %own_state.1.own.own_tail = f32[136,4096]{1,0:T(8,128)} custom-call(s32[1]{0:T(128)} %bitcast.2.half.core, bf16[256,8192]{1,0:T(8,128)(2,1)} %x.3, bf16[256,1024]{1,0:T(8,128)(2,1)} %b.3, f32[256,128]{1,0:T(8,128)} %get-tuple-element.14.factor_in, f32[8,128]{1,0:T(8,128)} %get-tuple-element.15.total_in.total), custom_call_target="tpu_custom_call" | custom-call | tf_op jit(solution)/shard_map/own_state/pallas_call | solution.py:285
  10.7 0.0 collective-permute-done.got.got_tail
  10.8 0.0 copy-start
  10.8 1.0 copy-done
  11.7 4.3 %chip_total.1 = bf16[128,4224]{1,0:T(8,128)(2,1)} custom-call(s32[1]{0:T(128)} %bitcast.2.half.core, f32[136,4096]{1,0:T(8,128)} %own_state.1.own.own_tail, f32[136,4096]{1,0:T(8,128)} %own_state.1.own.own_tail, bf16[136,4096]{1,0:T(8,128)(2,1)} %copy-done, bf16[136,4096]{1,0:T(8,128)(2,1)} %copy-done, f32[8,128]{1,0:T(8,128)} %get-tuple-element.15.total_in.total), custom_call_target="tpu_custom_call" | custom-call | tf_op jit(solution)/shard_map/chip_total/pallas_call | solution.py:306
  16.0 36.8 %all_to_all.10.sent.decays = bf16[16,8,4224]{2,1,0:T(8,128)(2,1)} all-to-all(bf16[16,8,4224]{2,1,0:T(8,128)(2,1)} %bitcast.5), channel_id=1, replica_groups=mesh['outer'=4,'chip'=4,'core'=2] {'outer','chip'}, dimensions={0} | all-to-all | bytes 2162688 | tf_op jit(solution)/shard_map/all_to_all | solution.py:319
  52.8 4.1 %prefix.1 = bf16[16,8,4096]{2,1,0:T(8,128)(2,1)} custom-call(bf16[16,8,4224]{2,1,0:T(8,128)(2,1)} %all_to_all.10.sent.decays, bf16[16,8,4224]{2,1,0:T(8,128)(2,1)} %all_to_all.10.sent.decays), custom_call_target="tpu_custom_call" | custom-call | tf_op jit(solution)/shard_map/prefix/pallas_call | solution.py:342
  56.8 31.2 %all_to_all.11 = bf16[16,8,4096]{2,1,0:T(8,128)(2,1)} all-to-all(bf16[16,8,4096]{2,1,0:T(8,128)(2,1)} %prefix.1), channel_id=1, replica_groups=mesh['outer'=4,'chip'=4,'core'=2] {'outer','chip'}, dimensions={0} | all-to-all | bytes 2097152 | tf_op jit(solution)/shard_map/all_to_all | solution.py:354
  88.1 4.4 %incoming.1 = (bf16[128,4096]{1,0:T(8,128)(2,1)}, bf16[128,4096]{1,0:T(8,128)(2,1)}) custom-call(s32[1]{0:T(128)} %bitcast.2.half.core, f32[136,4096]{1,0:T(8,128)} %own_state.1.own.own_tail, f32[136,4096]{1,0:T(8,128)} %own_state.1.own.own_tail, bf16[136,4096]{1,0:T(8,128)(2,1)} %copy-done, bf16[136,4096]{1,0:T(8,128)(2,1)} %copy-done, ...), custom_call_target="tpu_custom_call" | custom-call | tf_op jit(solution)/shard_map/incoming/pallas_call | solution.py:357
  92.4 0.0 collective-permute-start.1
  92.4 12.6 %within.1 = f32[256,8192]{1,0:T(8,128)} custom-call(bf16[256,8192]{1,0:T(8,128)(2,1)} %x.3, bf16[256,1024]{1,0:T(8,128)(2,1)} %b.3, bf16[256,1024]{1,0:T(8,128)(2,1)} %c.3, f32[256,128]{1,0:T(8,128)} %step_ref.1, f32[256,128]{1,0:T(8,128)} %get-tuple-element.12.run_ref, f32[128,256]{1,0:T(8,128)} %get-tuple-element.13.run_t_ref, f32[1,128]{1,0:T(1,128)} %bitcast.7), custom_call_target="tpu_custom_call" | custom-call | tf_op jit(solution)/shard_map/within/pallas_call | solution.py:323
  105.0 5.4 %finish.2.rest_0_ = bf16[256,8192]{1,0:T(8,128)(2,1)} custom-call(s32[1]{0:T(128)} %bitcast.2.half.core, f32[256,8192]{1,0:T(8,128)} %within.1, bf16[256,1024]{1,0:T(8,128)(2,1)} %c.3, bf16[128,4096]{1,0:T(8,128)(2,1)} %get-tuple-element.18.state, f32[256,128]{1,0:T(8,128)} %get-tuple-element.12.run_ref), custom_call_target="tpu_custom_call" | custom-call | tf_op jit(solution)/shard_map/finish/pallas_call | solution.py:372
  110.5 0.0 collective-permute-done.1.state
  110.5 0.0 copy-start.1
  110.5 1.0 copy-done.1
  111.5 5.4 %finish.3 = bf16[256,8192]{1,0:T(8,128)(2,1)} custom-call(s32[1]{0:T(128)} %bitcast.half, f32[256,8192]{1,0:T(8,128)} %within.1, bf16[256,1024]{1,0:T(8,128)(2,1)} %c.3, bf16[128,4096]{1,0:T(8,128)(2,1)} %copy-done.1, f32[256,128]{1,0:T(8,128)} %get-tuple-element.12.run_ref, bf16[256,8192]{1,0:T(8,128)(2,1)} %finish.2.rest_0_), custom_call_target="tpu_custom_call", output_to_operand_aliasing={{}: (5, {})} | custom-call | tf_op jit(solution)/shard_map/finish/pallas_call | solution.py:372
Async XLA Ops:
  5.3 5.5 %collective-permute-start = (bf16[136,4096]{1,0:T(8,128)(2,1)}, bf16[136,4096]{1,0:T(8,128)(2,1)S(1)}, u32[]{:S(2)}, u32[]{:S(2)}) collective-permute-start(bf16[136,4096]{1,0:T(8,128)(2,1)} %get-tuple-element.16), channel_id=1, source_target_pairs={{0,1},{1,0},{2,3},{3,2},{4,5},{5,4},{6,7},{7,6},{8,9},{9,8},{10,11... | collective-permute-start | bytes 3342344 | tf_op jit(solution)/shard_map/ppermute | solution.py:283
  10.8 1.0 copy-start
  92.4 18.0 %collective-permute-start.1 = (bf16[128,4096]{1,0:T(8,128)(2,1)}, bf16[128,4096]{1,0:T(8,128)(2,1)S(1)}, u32[]{:S(2)}, u32[]{:S(2)}) collective-permute-start(bf16[128,4096]{1,0:T(8,128)(2,1)} %get-tuple-element.17), channel_id=1, source_target_pairs={{0,1},{1,0},{2,3},{3,2},{4,5},{5,4},{6,7},{7,6},{8,9},{9,8},{10,11... | collective-permute-start | bytes 3145736 | tf_op jit(solution)/shard_map/ppermute | solution.py:369
  110.5 1.0 copy-start.1

commit v2 on v1

v2 whole, which is shorter than its diff:
```python
import functools
import math

import jax
import jax.numpy as jnp
from jax import lax
from jax.experimental import pallas as pl
from jax.experimental.pallas import tpu as pltpu
from jax.sharding import Mesh, PartitionSpec as P

GROUPS = 8
CORES = 2
LANES = 128
ROW_TILE = 8
HALF_ROWS = 128
ROW_BLOCK = 16
VMEM_LIMIT = 24 * 1024 * 1024
LOG2E = 1.0 / math.log(2.0)

F32 = jnp.float32
BF16 = jnp.bfloat16


def dot(a, b, contract=(1, 0), precision=None):
    dims = (((contract[0],), (contract[1],)), ((), ()))
    return lax.dot_general(a, b, dims, precision=precision, preferred_element_type=F32)


def spreader(heads, width):
    shape = (2 * heads, heads * width)
    row = lax.broadcasted_iota(jnp.int32, shape, 0)
    col = lax.broadcasted_iota(jnp.int32, shape, 1)
    row = jnp.where(row >= heads, row - heads, row)
    return jnp.where(row == col // width, 1.0, 0.0).astype(BF16)


def high_low(values):
    high = values.astype(BF16).astype(F32)
    return high, values - high


def spread(values, matrix):
    heads = matrix.shape[0] // 2
    high, low = high_low(values)
    lane = lax.broadcasted_iota(jnp.int32, values.shape, 1)
    packed = jnp.where(lane < heads, high, pltpu.roll(low, heads, 1))
    return dot(packed.astype(BF16)[:, : 2 * heads], matrix)


def group_first(values, group, per_group):
    lanes = values.shape[1]
    return pltpu.roll(values, lax.rem(lanes - group * per_group, lanes), 1)


def params():
    return pltpu.CompilerParams(dimension_semantics=("arbitrary",), vmem_limit_bytes=VMEM_LIMIT)


def running_sums(step, log, run_out, run_t_out, factor_out, total_out):
    rows = log.shape[0]
    upto = lax.broadcasted_iota(jnp.int32, (rows, rows), 1) <= lax.broadcasted_iota(jnp.int32, (rows, rows), 0)
    running = dot(upto.astype(F32), log[...], precision=lax.Precision.HIGHEST) * LOG2E
    last = running[rows - 1 :, :]
    run_out[...] = running
    run_t_out[...] = running.T
    factor_out[...] = step[...] * jnp.exp2(last - running)
    total_out[...] = jnp.broadcast_to(last, total_out.shape)


def state_block(group, per_group, x, b, factor_ref, total_ref, matrix, out):
    factor = group_first(factor_ref[...], group, per_group)
    log_total = total_ref[...]
    decay = spread(jnp.exp2(group_first(log_total, group, per_group)), matrix)
    scaled = (x.astype(F32) * spread(factor, matrix)).astype(BF16)
    state = dot(b, scaled, (0, 0))
    out[: state.shape[0], :] = state.astype(BF16)
    row = lax.broadcasted_iota(jnp.int32, decay.shape, 0)
    heads = log_total.shape[1]
    high, low = high_low(decay)
    tail = jnp.where(row == 0, high, low)
    high, low = high_low(log_total)
    low_high, low_low = high_low(low)
    logs = jnp.where(row[:, :heads] == 2, high, jnp.where(row[:, :heads] == 3, low_high, low_low))
    logs = jnp.where(row[:, :heads] < 2, tail[:, :heads], logs)
    out[state.shape[0] :, :] = jnp.concatenate([logs, tail[:, heads:]], axis=1).astype(BF16)


def send_state_kernel(half, x, b, step, log, out, run_out, run_t_out, factor_out, total_out, matrix, *, dims):
    per_half, per_group, width = dims
    turn = pl.program_id(0)

    @pl.when(turn == 0)
    def _():
        running_sums(step, log, run_out, run_t_out, factor_out, total_out)
        matrix[...] = spreader(per_group, width)

    group = half[0] * per_half + turn
    state_block(group, per_group, x[...], b[...], factor_out, total_out, matrix[...], out)


def own_state_kernel(half, x, b, factor, total, out, matrix, *, dims):
    per_half, per_group, width = dims
    turn = pl.program_id(0)

    @pl.when(turn == 0)
    def _():
        matrix[...] = spreader(per_group, width)

    group = half[0] * per_half + turn
    state_block(group, per_group, x[...], b[...], factor, total, matrix[...], out)


def other_log(got, states, heads):
    return (
        got[states + 2 : states + 3, :heads].astype(F32)
        + got[states + 3 : states + 4, :heads].astype(F32)
        + got[states + 4 : states + 5, :heads].astype(F32)
    )


def chip_total_kernel(core, own, got, total, out, base_out):
    first = core[0] == 0
    cols = own.shape[1]
    states = out.shape[0]
    heads = total.shape[1]
    half = heads // CORES
    own_tail = own[states : states + 2, :].astype(F32)
    got_tail = got[states : states + 2, :].astype(F32)
    decay = jnp.where(first, got_tail, own_tail)
    decay = decay[:1, :] + decay[1:, :]
    one = jnp.ones_like(decay)
    on_own = jnp.where(first, decay, one)
    on_got = jnp.where(first, one, decay)
    for row in range(0, states, ROW_BLOCK):
        rows = slice(row, row + ROW_BLOCK)
        out[rows, :cols] = (on_own * own[rows, :].astype(F32) + on_got * got[rows, :].astype(F32)).astype(BF16)
    partner = jnp.broadcast_to(other_log(got, states, heads), total.shape)
    base_out[...] = jnp.where(first, jnp.zeros_like(partner), partner)
    both = jnp.exp2(total[...] + partner)
    both = jnp.where(first, both, pltpu.roll(both, half, 1))
    high, low = high_low(both)
    lane = lax.broadcasted_iota(jnp.int32, both.shape, 1)
    packed = jnp.where(lane < half, high, pltpu.roll(low, half, 1))
    out[:, cols:] = jnp.concatenate([packed] * (states // packed.shape[0]), axis=0).astype(BF16)


def prefix_kernel(sent, ready, out, *, width, group_cols):
    del ready
    chips, rows, cols = out.shape
    heads_here = group_cols // width
    half = (sent.shape[2] - cols) // 2
    first_rows = jnp.concatenate([sent[k, :1, cols:].astype(F32) for k in range(chips)], axis=0)
    values = first_rows + pltpu.roll(first_rows, half, 1)
    matrix = spreader(heads_here, width)
    for start in range(0, cols, group_cols):
        here = slice(start, start + group_cols)
        shift = (2 * half - start // width) % (2 * half)
        decay = spread(pltpu.roll(values, shift, 1) if shift else values, matrix)
        state = jnp.zeros((rows, group_cols), F32)
        for k in range(chips):
            out[k, :, here] = state.astype(BF16)
            state = decay[k : k + 1, :] * state + sent[k, :, here].astype(F32)


def within_kernel(
    core, x_ref, b_ref, c_ref, step_ref, run_ref, run_t_ref, skip_ref, low_ref, high_ref, out, ready, matrix, *, dims
):
    per_half, per_group, width = dims
    group = pl.program_id(0)
    rows = x_ref.shape[0]

    @pl.when(group == 0)
    def _():
        matrix[...] = spreader(per_group, width)
        ready[...] = jnp.zeros_like(ready)

    spreading = matrix[...]
    step = group_first(step_ref[...], group, per_group)
    run = group_first(run_ref[...], group, per_group)
    skip = group_first(jnp.broadcast_to(skip_ref[...], (ROW_TILE, skip_ref.shape[1])), group, per_group)
    run_t = run_t_ref[pl.ds(pl.multiple_of(group * per_group, per_group), per_group), :]
    x = x_ref[...].astype(F32)
    scaled = (x * spread(step, spreading)).astype(BF16)
    skipped = spread(skip, spreading)[:1, :] * x
    upper = high_ref[...] * core[0].astype(BF16)
    before_state = jnp.where(group < per_half, low_ref[...], upper)
    skipped = skipped + spread(jnp.exp2(run), spreading) * dot(c_ref[...], before_state)
    pair = LANES // width
    lane = lax.broadcasted_iota(jnp.int32, (HALF_ROWS, LANES), 1) // width
    lower = lax.broadcasted_iota(jnp.int32, (HALF_ROWS, HALF_ROWS), 1) <= lax.broadcasted_iota(
        jnp.int32, (HALF_ROWS, HALF_ROWS), 0
    )
    b = b_ref[...]
    c = c_ref[...]
    for start in range(0, rows, HALF_ROWS):
        stop = start + HALF_ROWS
        scores = jnp.where(lower, dot(c[start:stop, :], b[start:stop, :], (1, 1)), 0.0)
        if start:
            edge = run[start - 1 : start, :]
            before = step[:start, :] * jnp.exp2(edge - run[:start, :])
            before = (x[:start, :] * spread(before, spreading)).astype(BF16)
            cross = dot(c[start:stop, :], b[:start, :], (1, 1)).astype(BF16)
            after = spread(jnp.exp2(run[start:stop, :] - edge), spreading)
            base = skipped[start:stop, :] + after * dot(cross, before)
        else:
            base = skipped[start:stop, :]
        for first in range(0, per_group, pair):
            cols = slice(first * width, (first + pair) * width)
            here = scaled[start:stop, cols]
            weights = []
            values = []
            for k in range(pair):
                head = first + k
                gap = run[start:stop, head : head + 1] - run_t[head : head + 1, start:stop]
                weights.append((scores * jnp.exp2(jnp.minimum(gap, 0.0))).astype(BF16))
                values.append(jnp.where(lane == k, here, jnp.zeros_like(here)))
            part = dot(jnp.concatenate(weights, axis=1), jnp.concatenate(values, axis=0))
            out[start:stop, cols] = base[:, cols] + part


def final_kernel(half, within, c, state, run_ref, base_ref, *rest, dims):
    per_half, per_group, width = dims
    out, matrix = rest[-2:]
    turn = pl.program_id(0)

    @pl.when(turn == 0)
    def _():
        matrix[...] = spreader(per_group, width)

    group = half[0] * per_half + turn
    grown = jnp.exp2(group_first(run_ref[...] + base_ref[:1, :], group, per_group))
    out[...] = (within[...] + spread(grown, matrix[...]) * dot(c[...], state[...])).astype(BF16)


def local(inputs, step_size, log_decay, b_matrix, c_matrix, skip_gain, *, chip_axes, core_axis):
    tokens, channels = inputs.shape
    heads = step_size.shape[1]
    width = channels // heads
    states = b_matrix.shape[1] // GROUPS
    per_group = heads // GROUPS
    group_cols = per_group * width
    per_half = GROUPS // CORES
    half_cols = channels // CORES
    half_heads = heads // CORES
    chips = lax.axis_size(chip_axes)
    rows = states // chips
    tall = states + ROW_TILE

    core = lax.axis_index(core_axis).astype(jnp.int32)
    mine = core.reshape(1)
    other = (1 - core).reshape(1)

    def of_half(block_rows):
        return pl.BlockSpec((block_rows, group_cols), lambda i, half: (0, half[0] * per_half + i))

    def matrix_of_half():
        return pl.BlockSpec((tokens, states), lambda i, half: (0, half[0] * per_half + i))

    def by_turn(block_rows):
        return pl.BlockSpec((block_rows, group_cols), lambda i, half: (0, i))

    def whole(shape):
        return pl.BlockSpec(shape, lambda i, *_: (0,) * len(shape))

    spread_scratch = pltpu.VMEM((2 * per_group, group_cols), BF16)
    half_dims = (per_half, per_group, width)

    send, run, run_t, factor, total = pl.pallas_call(
        functools.partial(send_state_kernel, dims=half_dims),
        grid_spec=pltpu.PrefetchScalarGridSpec(
            num_scalar_prefetch=1,
            grid=(per_half,),
            in_specs=[of_half(tokens), matrix_of_half(), whole((tokens, heads)), whole((tokens, heads))],
            out_specs=[
                by_turn(tall),
                whole((tokens, heads)),
                whole((heads, tokens)),
                whole((tokens, heads)),
                whole((ROW_TILE, heads)),
            ],
            scratch_shapes=[spread_scratch],
        ),
        out_shape=[
            jax.ShapeDtypeStruct((tall, half_cols), BF16),
            jax.ShapeDtypeStruct((tokens, heads), F32),
            jax.ShapeDtypeStruct((heads, tokens), F32),
            jax.ShapeDtypeStruct((tokens, heads), F32),
            jax.ShapeDtypeStruct((ROW_TILE, heads), F32),
        ],
        compiler_params=params(),
        name="send_state",
    )(other, inputs, b_matrix, step_size, log_decay)

    swap = [(0, 1), (1, 0)]
    got = lax.ppermute(send, core_axis, swap)

    own = pl.pallas_call(
        functools.partial(own_state_kernel, dims=half_dims),
        grid_spec=pltpu.PrefetchScalarGridSpec(
            num_scalar_prefetch=1,
            grid=(per_half,),
            in_specs=[of_half(tokens), matrix_of_half(), whole((tokens, heads)), whole((ROW_TILE, heads))],
            out_specs=by_turn(tall),
            scratch_shapes=[spread_scratch],
        ),
        out_shape=jax.ShapeDtypeStruct((tall, half_cols), BF16),
        compiler_params=params(),
        name="own_state",
    )(mine, inputs, b_matrix, factor, total)

    smem = pl.BlockSpec(memory_space=pltpu.SMEM)
    vmem = pl.BlockSpec(memory_space=pltpu.VMEM)
    anywhere = pl.BlockSpec(memory_space=pl.ANY)
    chip_total, base = pl.pallas_call(
        chip_total_kernel,
        in_specs=[smem, vmem, vmem, vmem],
        out_specs=[vmem, vmem],
        out_shape=[
            jax.ShapeDtypeStruct((states, half_cols + heads), BF16),
            jax.ShapeDtypeStruct((ROW_TILE, heads), F32),
        ],
        compiler_params=pltpu.CompilerParams(vmem_limit_bytes=VMEM_LIMIT),
        name="chip_total",
    )(mine, own, got, total)

    sent = lax.all_to_all(
        chip_total.reshape(chips, rows, half_cols + heads), chip_axes, split_axis=0, concat_axis=0, tiled=True
    )
    late = lax.ppermute(own, core_axis, swap[:1])

    def by_group(block_rows, cols):
        return pl.BlockSpec((block_rows, cols), lambda i, *_: (0, i))

    within, ready = pl.pallas_call(
        functools.partial(within_kernel, dims=half_dims),
        grid_spec=pltpu.PrefetchScalarGridSpec(
            num_scalar_prefetch=1,
            grid=(GROUPS,),
            in_specs=[
                by_group(tokens, group_cols),
                by_group(tokens, states),
                by_group(tokens, states),
                whole((tokens, heads)),
                whole((tokens, heads)),
                whole((heads, tokens)),
                whole((1, heads)),
                pl.BlockSpec((states, group_cols), lambda i, _: (0, jnp.minimum(i, per_half - 1))),
                pl.BlockSpec((states, group_cols), lambda i, _: (0, jnp.maximum(i - per_half, 0))),
            ],
            out_specs=[by_group(tokens, group_cols), whole((ROW_TILE, LANES))],
            scratch_shapes=[spread_scratch],
        ),
        out_shape=[jax.ShapeDtypeStruct((tokens, channels), F32), jax.ShapeDtypeStruct((ROW_TILE, LANES), F32)],
        compiler_params=params(),
        name="within",
    )(mine, inputs, b_matrix, c_matrix, step_size, run, run_t, skip_gain.reshape(1, heads), late, got)

    entering = pl.pallas_call(
        functools.partial(prefix_kernel, width=width, group_cols=group_cols),
        in_specs=[vmem, anywhere],
        out_specs=vmem,
        out_shape=jax.ShapeDtypeStruct((chips, rows, half_cols), BF16),
        compiler_params=pltpu.CompilerParams(vmem_limit_bytes=VMEM_LIMIT),
        name="prefix",
    )(sent, ready)
    entering = lax.all_to_all(entering, chip_axes, split_axis=0, concat_axis=0, tiled=True)
    entering = entering.reshape(states, half_cols)
    got_entering = lax.ppermute(entering, core_axis, swap)

    def finish(half, state, *result):
        return pl.pallas_call(
            functools.partial(final_kernel, dims=half_dims),
            grid_spec=pltpu.PrefetchScalarGridSpec(
                num_scalar_prefetch=1,
                grid=(per_half,),
                in_specs=[
                    of_half(tokens),
                    matrix_of_half(),
                    by_turn(states),
                    whole((tokens, heads)),
                    whole((ROW_TILE, heads)),
                ]
                + [anywhere] * len(result),
                out_specs=of_half(tokens),
                scratch_shapes=[spread_scratch],
            ),
            out_shape=jax.ShapeDtypeStruct((tokens, channels), BF16),
            input_output_aliases={6: 0} if result else {},
            compiler_params=params(),
            name="finish",
        )(half, within, c_matrix, state, run, base, *result)

    result = finish(mine, entering)
    return finish(other, got_entering, result)


def solution(mesh):
    outer, inner = mesh.axis_names
    chip_mesh = Mesh(
        mesh.devices.reshape(mesh.shape[outer], mesh.shape[inner] // CORES, CORES), (outer, "chip", "core")
    )
    placed = P((outer, "chip", "core"), None)
    return jax.shard_map(
        functools.partial(local, chip_axes=(outer, "chip"), core_axis="core"),
        mesh=chip_mesh,
        in_specs=(placed,) * 5 + (P(),),
        out_specs=placed,
        check_vma=False,
    )
```

time: 118 us -> 94.4 us (0.80)
  blocking collectives: 68 us -> 30.3 us
  Pallas kernels: 46.4 us -> 30 us
  local copies, waits for them, and re-layouts: 2.02 us -> 15.8 us
  starting transfers between devices: 0.51 us -> 10.8 us
  waiting for transfers between devices: 0.01 us -> 7 us
    all_to_all x1 -> x0, blocking collectives: 36.8 us -> none  [local(): lax.all_to_all(chip_total.reshape(chips, rows, half_cols + heads), chip_a...]
    unnamed x4 -> x30, local copies, waits for them, and re-layouts: 2.02 us -> 15.8 us
    pallas_call x4 -> x3, Pallas kernels: 25.3 us -> 15.8 us  [the longest x1 13.3 us: local(): pl.pallas_call(functools.partial(within_kernel, dims=half_dims), grid_spe...]
    all_to_all x0 -> x1, starting transfers between devices: none -> 8.08 us  [local(): lax.all_to_all(chip_total.reshape(chips, rows, half_cols + heads), chip_a...]
    all_to_all x0 -> x1, waiting for transfers between devices: none -> 4.7 us  [local(): lax.all_to_all(chip_total.reshape(chips, rows, half_cols + heads), chip_a...]
    pallas_call x2, Pallas kernels: 10.9 us -> 7.72 us  [finish(): pl.pallas_call(functools.partial(final_kernel, dims=half_dims), grid_spec...]
    ppermute x1 -> x2, waiting for transfers between devices: 0.01 us -> 2.29 us  [the longest x1 2.29 us: local(): late = lax.ppermute(own, core_axis, swap[:1])]
    ppermute x1 -> x2, starting transfers between devices: 0.01 us -> 2.16 us  [the longest x1 2.15 us: local(): late = lax.ppermute(own, core_axis, swap[:1])]
  transfers between devices with their start and end apart: 2 -> 4, of which waited for: 0 -> 2; matrix products, arithmetic and copies ran while one was open for 0% -> 0% of each run, Pallas kernels for 20% -> 22%
where the time goes in v2:
time: 94.4 us; the launch traced here: 93.9 us
  blocking collectives  30.3 us (32%)
  Pallas kernels  30 us (32%)
  local copies, waits for them, and re-layouts  15.8 us (17%)
  starting transfers between devices  10.8 us (11%)
  waiting for transfers between devices  7 us (7%)
    all_to_all x1, blocking collectives, local(): lax.all_to_all(entering, chip_axes, split_axis=0, concat_axis=0, tiled=True)  30.3 us
    unnamed x30, local copies, waits for them, and re-layouts  15.8 us
    pallas_call x1, Pallas kernels, local(): pl.pallas_call(functools.partial(within_kernel, dims=half_dims), grid_spe...  13.3 us
    all_to_all x1, starting transfers between devices, local(): lax.all_to_all(chip_total.reshape(chips, rows, half_cols + heads), chip_a...  8.08 us
    pallas_call x2, Pallas kernels, finish(): pl.pallas_call(functools.partial(final_kernel, dims=half_dims), grid_spec...  7.72 us
    all_to_all x1, waiting for transfers between devices, local(): lax.all_to_all(chip_total.reshape(chips, rows, half_cols + heads), chip_a...  4.7 us
    pallas_call x1, Pallas kernels, local(): pl.pallas_call(functools.partial(send_state_kernel, dims=half_dims), grid...  3.45 us
    pallas_call x1, Pallas kernels, local(): pl.pallas_call(functools.partial(own_state_kernel, dims=half_dims), grid_...  3.03 us
  transfers between devices with their start and end apart: 4, of which 2 were waited for; matrix products, arithmetic and copies ran while one was open for 0% of the time, Pallas kernels for 22%

profile of v2, /device:TPU:0, one launch (start us, length us, event | category | flops | bytes accessed | tf_op | source)
XLA Modules:
  0.0 93.9 jit_solution(2646551110032924699)
XLA Ops:
  0.0 2.2 %copy-done = bf16[256,8192]{1,0:T(8,128)(2,1)S(1)} copy-done((bf16[256,8192]{1,0:T(8,128)(2,1)S(1)}, bf16[256,8192]{1,0:T(8,128)(2,1)}, u32[]{:S(2)}) %copy-start) | copy-done | bytes 4194328
  2.2 1.0 %copy-done.6 = bf16[256,1024]{1,0:T(8,128)(2,1)S(1)} copy-done((bf16[256,1024]{1,0:T(8,128)(2,1)S(1)}, bf16[256,1024]{1,0:T(8,128)(2,1)}, u32[]{:S(2)}) %copy-start.6) | copy-done | bytes 524312
  3.2 0.9 copy-done.9
  4.1 0.9 copy-done.13
  5.0 3.5 %send_state.1 = (bf16[136,4096]{1,0:T(8,128)(2,1)S(1)}, f32[256,128]{1,0:T(8,128)S(1)}, f32[128,256]{1,0:T(8,128)S(1)}, f32[256,128]{1,0:T(8,128)S(1)}, f32[8,128]{1,0:T(8,128)S(1)}) custom-call(s32[1]{0:T(128)} %bitcast.half, bf16[256,8192]{1,0:T(8,128)(2,1)S(1)} %copy-done, bf16[256,1024]{1,0:T(8,128)(2,1)S(1)} %copy-done.6, f32[256,128]{1,0:T(8,128)S(1)} %copy-done.9, ...), custom_call_target="tpu_custom_call" | custom-call | tf_op jit(solution)/shard_map/send_state/pallas_call | solution.py:268
  8.5 0.6 collective-permute-start.1
  9.1 3.0 %own_state.1.own = bf16[136,4096]{1,0:T(8,128)(2,1)S(1)} custom-call(s32[1]{0:T(128)} %bitcast.1.half.core, bf16[256,8192]{1,0:T(8,128)(2,1)S(1)} %copy-done.1, bf16[256,1024]{1,0:T(8,128)(2,1)S(1)} %copy-done.7, f32[256,128]{1,0:T(8,128)S(1)} %get-tuple-element.16.factor, f32[8,128]{1,0:T(8,128)S(1)} %get-tuple-element.17.total), custom_call_target="tpu_custom_call" | custom-call | tf_op jit(solution)/shard_map/own_state/pallas_call | solution.py:297
  12.1 0.0 collective-permute-done.1.high_ref.got
  12.1 0.6 chip_total.1
  12.8 0.0 copy-start.8
  12.8 1.0 %copy-done.8 = bf16[128,4224]{1,0:T(8,128)(2,1)} copy-done((bf16[128,4224]{1,0:T(8,128)(2,1)}, bf16[128,4224]{1,0:T(8,128)(2,1)S(1)}, u32[]{:S(2)}) %copy-start.8) | copy-done | bytes 1081368
  13.8 8.1 %all-to-all-start = ((bf16[16,8,4224]{2,1,0:T(8,128)(2,1)}), bf16[16,8,4224]{2,1,0:T(8,128)(2,1)}, u32[]{:S(2)}, u32[]{:S(2)}) async-start(bf16[16,8,4224]{2,1,0:T(8,128)(2,1)} %bitcast.7), calls=%async_computation | async-start | bytes 2162688 | tf_op jit(solution)/shard_map/all_to_all | solution.py:326
  21.9 2.2 %collective-permute-start = (bf16[136,4096]{1,0:T(8,128)(2,1)S(1)}, bf16[136,4096]{1,0:T(8,128)(2,1)S(1)}, u32[]{:S(2)}, u32[]{:S(2)}) collective-permute-start(bf16[136,4096]{1,0:T(8,128)(2,1)S(1)} %own_state.1.own), channel_id=1, source_target_pairs={{0,1},{2,3},{4,5},{6,7},{8,9},{10,11},{12,13},{14,15},{16,17},{18,... | collective-permute-start | bytes 3342344 | tf_op jit(solution)/shard_map/ppermute | solution.py:329
  24.0 2.3 %collective-permute-done.low_ref = bf16[136,4096]{1,0:T(8,128)(2,1)S(1)} collective-permute-done((bf16[136,4096]{1,0:T(8,128)(2,1)S(1)}, bf16[136,4096]{1,0:T(8,128)(2,1)S(1)}, u32[]{:S(2)}, u32[]{:S(2)}) %collective-permute-start) | collective-permute-done | bytes 1114144 | tf_op jit(solution)/shard_map/ppermute | solution.py:329
  26.3 2.2 %copy-done.2 = bf16[256,8192]{1,0:T(8,128)(2,1)S(1)} copy-done((bf16[256,8192]{1,0:T(8,128)(2,1)S(1)}, bf16[256,8192]{1,0:T(8,128)(2,1)}, u32[]{:S(2)}) %copy-start.2) | copy-done | bytes 4194328
  28.5 0.9 copy-done.12
  29.4 13.3 %within.1 = (f32[256,8192]{1,0:T(8,128)S(1)}, f32[8,128]{1,0:T(8,128)S(1)}) custom-call(s32[1]{0:T(128)} %bitcast.1.half.core, bf16[256,8192]{1,0:T(8,128)(2,1)S(1)} %copy-done.2, bf16[256,1024]{1,0:T(8,128)(2,1)S(1)} %copy-done.7, bf16[256,1024]{1,0:T(8,128)(2,1)S(1)} %copy-done.5, f32[256,128]{1,0:T(8,128)S(1)} %copy-done.10, ...), custom_call_target="tpu_custom_call" | custom-call | tf_op jit(solution)/shard_map/within/pallas_call | solution.py:334
  42.8 3.2 %copy-done.3 = f32[256,8192]{1,0:T(8,128)} copy-done((f32[256,8192]{1,0:T(8,128)}, f32[256,8192]{1,0:T(8,128)S(1)}, u32[]{:S(2)}) %copy-start.3) | copy-done | bytes 8388632
  46.0 4.7 %all-to-all-done.sent = bf16[16,8,4224]{2,1,0:T(8,128)(2,1)} async-done(((bf16[16,8,4224]{2,1,0:T(8,128)(2,1)}), bf16[16,8,4224]{2,1,0:T(8,128)(2,1)}, u32[]{:S(2)}, u32[]{:S(2)}) %all-to-all-start) | async-done | bytes 1081376 | tf_op jit(solution)/shard_map/all_to_all | solution.py:326
  50.7 1.8 %prefix.1 = bf16[16,8,4096]{2,1,0:T(8,128)(2,1)S(1)} custom-call(bf16[16,8,4224]{2,1,0:T(8,128)(2,1)} %all-to-all-done.sent, f32[8,128]{1,0:T(8,128)S(1)} %get-tuple-element.21.ready), custom_call_target="tpu_custom_call" | custom-call | tf_op jit(solution)/shard_map/prefix/pallas_call | solution.py:358
  52.5 30.3 %all_to_all.10 = bf16[16,8,4096]{2,1,0:T(8,128)(2,1)S(1)} all-to-all(bf16[16,8,4096]{2,1,0:T(8,128)(2,1)S(1)} %prefix.1), channel_id=1, replica_groups=mesh['outer'=4,'chip'=4,'core'=2] {'outer','chip'}, dimensions={0} | all-to-all | bytes 2097152 | tf_op jit(solution)/shard_map/all_to_all | solution.py:366
  82.8 3.4 %copy-done.4 = f32[256,8192]{1,0:T(8,128)S(1)} copy-done((f32[256,8192]{1,0:T(8,128)S(1)}, f32[256,8192]{1,0:T(8,128)}, u32[]{:S(2)}) %copy-start.4) | copy-done | bytes 8388632
  86.2 3.9 %finish.2.rest_0_ = bf16[256,8192]{1,0:T(8,128)(2,1)} custom-call(s32[1]{0:T(128)} %bitcast.1.half.core, f32[256,8192]{1,0:T(8,128)S(1)} %copy-done.4, bf16[256,1024]{1,0:T(8,128)(2,1)S(1)} %copy-done.5, bf16[128,4096]{1,0:T(8,128)(2,1)S(1)} %bitcast.6, f32[256,128]{1,0:T(8,128)S(1)} %get-tuple-element.14.run_ref, f32[8,128]{1,0:T(8,128)S(1)} %get-tuple-element.22.base_ref), custom_call_target="tpu_custom_call" | custom-call | tf_op jit(solution)/shard_map/finish/pallas_call | solution.py:371
  90.0 3.9 %finish.3 = bf16[256,8192]{1,0:T(8,128)(2,1)} custom-call(s32[1]{0:T(128)} %bitcast.half, f32[256,8192]{1,0:T(8,128)S(1)} %copy-done.4, bf16[256,1024]{1,0:T(8,128)(2,1)S(1)} %copy-done.5, bf16[128,4096]{1,0:T(8,128)(2,1)S(1)} %collective-permute-done.2.state, f32[256,128]{1,0:T(8,128)S(1)} %get-tuple-element.14.run_ref, ...), custom_call_target="tpu_custom_call", output_to_operand_aliasing={{}: (6, {})} | custom-call | tf_op jit(solution)/shard_map/finish/pallas_call | solution.py:371
  (22 shorter events, 0.0 us)
Async XLA Ops:
  0.0 2.2 %copy-start = (bf16[256,8192]{1,0:T(8,128)(2,1)S(1)}, bf16[256,8192]{1,0:T(8,128)(2,1)}, u32[]{:S(2)}) copy-start(bf16[256,8192]{1,0:T(8,128)(2,1)} %x_ref.1) | copy-start | bytes 12582916
  2.2 1.0 %copy-start.6 = (bf16[256,1024]{1,0:T(8,128)(2,1)S(1)}, bf16[256,1024]{1,0:T(8,128)(2,1)}, u32[]{:S(2)}) copy-start(bf16[256,1024]{1,0:T(8,128)(2,1)} %b_ref.1) | copy-start | bytes 1572868
  3.2 0.9 copy-start.9
  4.1 0.9 copy-start.13
  5.0 4.0 %copy-start.1 = (bf16[256,8192]{1,0:T(8,128)(2,1)S(1)}, bf16[256,8192]{1,0:T(8,128)(2,1)}, u32[]{:S(2)}) copy-start(bf16[256,8192]{1,0:T(8,128)(2,1)} %x_ref.1) | copy-start | bytes 12582916
  5.0 4.0 %copy-start.7 = (bf16[256,1024]{1,0:T(8,128)(2,1)S(1)}, bf16[256,1024]{1,0:T(8,128)(2,1)}, u32[]{:S(2)}) copy-start(bf16[256,1024]{1,0:T(8,128)(2,1)} %b_ref.1) | copy-start | bytes 1572868
  8.5 3.6 %copy-start.11 = (f32[128,256]{1,0:T(8,128)}, f32[128,256]{1,0:T(8,128)S(1)}, u32[]{:S(2)}) copy-start(f32[128,256]{1,0:T(8,128)S(1)} %get-tuple-element.15.run_t_ref) | copy-start | bytes 393220
  8.5 3.6 %collective-permute-start.1 = (bf16[136,4096]{1,0:T(8,128)(2,1)S(1)}, bf16[136,4096]{1,0:T(8,128)(2,1)S(1)}, u32[]{:S(2)}, u32[]{:S(2)}) collective-permute-start(bf16[136,4096]{1,0:T(8,128)(2,1)S(1)} %get-tuple-element.18), channel_id=1, source_target_pairs={{0,1},{1,0},{2,3},{3,2},{4,5},{5,4},{6,7},{7,6},{8,9},{9,8},{10,11... | collective-permute-start | bytes 3342344 | tf_op jit(solution)/shard_map/ppermute | solution.py:295
  12.8 1.0 %copy-start.8 = (bf16[128,4224]{1,0:T(8,128)(2,1)}, bf16[128,4224]{1,0:T(8,128)(2,1)S(1)}, u32[]{:S(2)}) copy-start(bf16[128,4224]{1,0:T(8,128)(2,1)S(1)} %get-tuple-element.20) | copy-start | bytes 3244036
  13.8 12.5 %copy-start.5 = (bf16[256,1024]{1,0:T(8,128)(2,1)S(1)}, bf16[256,1024]{1,0:T(8,128)(2,1)}, u32[]{:S(2)}) copy-start(bf16[256,1024]{1,0:T(8,128)(2,1)} %c.3) | copy-start | bytes 1572868
  13.8 12.5 %copy-start.10 = (f32[256,128]{1,0:T(8,128)S(1)}, f32[256,128]{1,0:T(8,128)}, u32[]{:S(2)}) copy-start(f32[256,128]{1,0:T(8,128)} %step_ref.1) | copy-start | bytes 393220
  13.8 12.5 %copy-start.14 = (f32[128]{0:T(128)S(1)}, f32[128]{0:T(128)}, u32[]{:S(2)}) copy-start(f32[128]{0:T(128)} %param.11) | copy-start | bytes 1540
  13.8 36.9 %all-to-all-start = ((bf16[16,8,4224]{2,1,0:T(8,128)(2,1)}), bf16[16,8,4224]{2,1,0:T(8,128)(2,1)}, u32[]{:S(2)}, u32[]{:S(2)}) async-start(bf16[16,8,4224]{2,1,0:T(8,128)(2,1)} %bitcast.7), calls=%async_computation | async-start | bytes 2162688 | tf_op jit(solution)/shard_map/all_to_all | solution.py:326
  21.9 4.5 %collective-permute-start = (bf16[136,4096]{1,0:T(8,128)(2,1)S(1)}, bf16[136,4096]{1,0:T(8,128)(2,1)S(1)}, u32[]{:S(2)}, u32[]{:S(2)}) collective-permute-start(bf16[136,4096]{1,0:T(8,128)(2,1)S(1)} %own_state.1.own), channel_id=1, source_target_pairs={{0,1},{2,3},{4,5},{6,7},{8,9},{10,11},{12,13},{14,15},{16,17},{18,... | collective-permute-start | bytes 3342344 | tf_op jit(solution)/shard_map/ppermute | solution.py:329
  26.3 2.2 %copy-start.2 = (bf16[256,8192]{1,0:T(8,128)(2,1)S(1)}, bf16[256,8192]{1,0:T(8,128)(2,1)}, u32[]{:S(2)}) copy-start(bf16[256,8192]{1,0:T(8,128)(2,1)} %x_ref.1) | copy-start | bytes 12582916
  28.5 0.9 copy-start.12
  42.8 3.3 %copy-start.3 = (f32[256,8192]{1,0:T(8,128)}, f32[256,8192]{1,0:T(8,128)S(1)}, u32[]{:S(2)}) copy-start(f32[256,8192]{1,0:T(8,128)S(1)} %get-tuple-element.19.within) | copy-start | bytes 25165828
  82.8 7.2 %collective-permute-start.2 = (bf16[128,4096]{1,0:T(8,128)(2,1)S(1)}, bf16[128,4096]{1,0:T(8,128)(2,1)S(1)}, u32[]{:S(2)}, u32[]{:S(2)}) collective-permute-start(bf16[128,4096]{1,0:T(8,128)(2,1)S(1)} %bitcast.5), channel_id=1, source_target_pairs={{0,1},{1,0},{2,3},{3,2},{4,5},{5,4},{6,7},{7,6},{8,9},{9,8},{10,11... | collective-permute-start | bytes 3145736 | tf_op jit(solution)/shard_map/ppermute | solution.py:368
  82.8 3.4 %copy-start.4 = (f32[256,8192]{1,0:T(8,128)S(1)}, f32[256,8192]{1,0:T(8,128)}, u32[]{:S(2)}) copy-start(f32[256,8192]{1,0:T(8,128)} %copy-done.3) | copy-start | bytes 25165828

commit v3 on v2

v3 whole, which is shorter than its diff:
```python
import functools
import math

import jax
import jax.numpy as jnp
from jax import lax
from jax.experimental import pallas as pl
from jax.experimental.pallas import tpu as pltpu
from jax.sharding import Mesh, PartitionSpec as P


GROUPS = 8
CORES = 2
LANES = 128
ROW_TILE = 8
HALF_ROWS = 128
ROW_BLOCK = 16
VMEM_LIMIT = 24 * 1024 * 1024
LOG2E = 1.0 / math.log(2.0)

F32 = jnp.float32
BF16 = jnp.bfloat16


def dot(a, b, contract=(1, 0)):
    dims = (((contract[0],), (contract[1],)), ((), ()))
    return lax.dot_general(a, b, dims, preferred_element_type=F32)


def high_low(values):
    high = values.astype(BF16).astype(F32)
    return high, values - high


def head_lanes(values, first_head, width):
    lane = lax.broadcasted_iota(jnp.int32, (values.shape[0], LANES), 1)
    return jnp.take_along_axis(values, first_head + lane // width, axis=1)


def spread(values, first_head, heads, width):
    pair = LANES // width
    return jnp.concatenate([head_lanes(values, first_head + k, width) for k in range(0, heads, pair)], axis=1)


def params():
    return pltpu.CompilerParams(dimension_semantics=("arbitrary",), vmem_limit_bytes=VMEM_LIMIT)


def plain_params():
    return pltpu.CompilerParams(vmem_limit_bytes=VMEM_LIMIT)


def state_copies(half, x, b, x_here, b_here, sems, dims):
    per_half, group_cols, states = dims
    copies = []
    for k in range(per_half):
        group = half * per_half + k
        copies.append(
            pltpu.make_async_copy(
                x.at[:, pl.ds(pl.multiple_of(group * group_cols, group_cols), group_cols)],
                x_here.at[:, pl.ds(k * group_cols, group_cols)],
                sems.at[2 * k],
            )
        )
        copies.append(
            pltpu.make_async_copy(
                b.at[:, pl.ds(pl.multiple_of(group * states, states), states)],
                b_here.at[:, pl.ds(k * states, states)],
                sems.at[2 * k + 1],
            )
        )
    return copies


def half_states(half, x_here, b_here, copies, factor, log_total, out, dims):
    per_half, group_cols, states = dims
    heads = factor.shape[1]
    half_heads = heads // CORES
    per_group = half_heads // per_half
    width = group_cols // per_group
    first = half * half_heads
    row = lax.broadcasted_iota(jnp.int32, (ROW_TILE, LANES), 0)
    high, low = high_low(log_total)
    middle, low = high_low(low)
    logs = jnp.where(row == 2, high, jnp.where(row == 3, middle, low))
    total = jnp.exp2(log_total)
    for k in range(per_half):
        copies[2 * k].wait()
        copies[2 * k + 1].wait()
        b = b_here[:, k * states : (k + 1) * states]
        scaled = []
        for j in range(0, group_cols, LANES):
            start = k * group_cols + j
            part = head_lanes(factor, first + start // width, width)
            scaled.append((x_here[:, start : start + LANES].astype(F32) * part).astype(BF16))
            high, low = high_low(head_lanes(total, first + start // width, width))
            tail = jnp.where(row == 0, high, low)
            if start == 0:
                tail = jnp.where(row < 2, tail, logs)
            out[states:, start : start + LANES] = tail.astype(BF16)
        cols = slice(k * group_cols, (k + 1) * group_cols)
        out[:states, cols] = dot(b, jnp.concatenate(scaled, axis=1), (0, 0)).astype(BF16)


def send_state_kernel(
    half, x, b, step, log, out, run_out, run_t_out, factor_out, total_out, x_here, b_here, step_here, log_here, sems, *, dims
):
    first = pltpu.make_async_copy(log, log_here, sems.at[2 * dims[0]])
    second = pltpu.make_async_copy(step, step_here, sems.at[2 * dims[0] + 1])
    first.start()
    second.start()
    copies = state_copies(half[0], x, b, x_here, b_here, sems, dims)
    for copy in copies:
        copy.start()
    rows, heads = log_here.shape
    upto = lax.broadcasted_iota(jnp.int32, (rows, rows), 1) <= lax.broadcasted_iota(jnp.int32, (rows, rows), 0)
    first.wait()
    high, rest = high_low(log_here[...])
    middle, low = high_low(rest)
    parts = jnp.concatenate([high, middle, low], axis=1).astype(BF16)
    sums = dot(jnp.where(upto, 1.0, 0.0).astype(BF16), parts)
    running = (sums[:, :heads] + sums[:, heads : 2 * heads] + sums[:, 2 * heads :]) * LOG2E
    last = running[rows - 1 :, :]
    run_out[...] = running
    run_t_out[...] = running.T
    second.wait()
    factor = step_here[...] * jnp.exp2(last - running)
    total = jnp.broadcast_to(last, total_out.shape)
    factor_out[...] = factor
    total_out[...] = total
    half_states(half[0], x_here, b_here, copies, factor, total, out, dims)


def own_state_kernel(half, x, b, factor, total, out, x_here, b_here, sems, *, dims):
    copies = state_copies(half[0], x, b, x_here, b_here, sems, dims)
    for copy in copies:
        copy.start()
    half_states(half[0], x_here, b_here, copies, factor[...], total[...], out, dims)


def chip_total_kernel(core, own, got, total, out, base_out):
    first = core[0] == 0
    cols = own.shape[1]
    states = out.shape[0]
    heads = total.shape[1]
    half = heads // CORES
    own_tail = own[states : states + 2, :].astype(F32)
    got_tail = got[states : states + 2, :].astype(F32)
    decay = jnp.where(first, got_tail, own_tail)
    decay = decay[:1, :] + decay[1:, :]
    one = jnp.ones_like(decay)
    on_own = jnp.where(first, decay, one)
    on_got = jnp.where(first, one, decay)
    for row in range(0, states, ROW_BLOCK):
        rows = slice(row, row + ROW_BLOCK)
        out[rows, :cols] = (on_own * own[rows, :].astype(F32) + on_got * got[rows, :].astype(F32)).astype(BF16)
    partner = got[states + 2 : states + 3, :heads].astype(F32) + got[states + 3 : states + 4, :heads].astype(F32)
    partner = partner + got[states + 4 : states + 5, :heads].astype(F32)
    partner = jnp.broadcast_to(partner, total.shape)
    base_out[...] = jnp.where(first, jnp.zeros_like(partner), partner)
    both = jnp.exp2(total[...] + partner)
    both = jnp.where(first, both, pltpu.roll(both, half, 1))
    high, low = high_low(both)
    lane = lax.broadcasted_iota(jnp.int32, both.shape, 1)
    packed = jnp.where(lane < half, high, pltpu.roll(low, half, 1))
    out[:, cols:] = jnp.concatenate([packed] * (states // packed.shape[0]), axis=0).astype(BF16)


def prefix_kernel(sent, out, ready, here, sems, *, width, blocks):
    chips, rows, cols = here.shape
    heads = ready.shape[1]
    half = heads // CORES
    step = cols // blocks
    ready[...] = jnp.zeros_like(ready)
    first_rows = jnp.concatenate([sent[k, :1, cols:].astype(F32) for k in range(chips)], axis=0)
    values = first_rows + pltpu.roll(first_rows, half, 1)
    copies = []
    for block in range(blocks):
        lanes = slice(block * step, (block + 1) * step)
        decay = spread(values, block * step // width, step // width, width)
        state = jnp.zeros((rows, step), F32)
        for k in range(chips):
            here[k, :, lanes] = state.astype(BF16)
            state = decay[k : k + 1, :] * state + sent[k, :, lanes].astype(F32)
        copies.append(
            pltpu.make_async_copy(
                here.at[:, :, pl.ds(block * step, step)], out.at[:, :, pl.ds(block * step, step)], sems.at[block]
            )
        )
        copies[-1].start()
    for copy in copies:
        copy.wait()


def within_kernel(
    core, x_ref, b_ref, c_ref, step_ref, run_ref, run_t_ref, skip_ref, low_ref, high_ref, ready, out, *, dims
):
    del ready
    per_half, per_group, width = dims
    group = pl.program_id(0)
    head = group * per_group
    rows = x_ref.shape[0]
    pair = LANES // width
    run = run_ref[...]
    own_run = pltpu.roll(run, lax.rem(run.shape[1] - head, run.shape[1]), 1)
    run_t = run_t_ref[pl.ds(pl.multiple_of(head, per_group), per_group), :]
    step = step_ref[...]
    skip = jnp.broadcast_to(skip_ref[...], (ROW_TILE, skip_ref.shape[1]))
    grown = jnp.exp2(run)
    upper = high_ref[...] * core[0].astype(BF16)
    from_before = dot(c_ref[...], jnp.where(group < per_half, low_ref[...], upper))
    lane = lax.broadcasted_iota(jnp.int32, (HALF_ROWS, LANES), 1) // width
    lower = lax.broadcasted_iota(jnp.int32, (HALF_ROWS, HALF_ROWS), 1) <= lax.broadcasted_iota(
        jnp.int32, (HALF_ROWS, HALF_ROWS), 0
    )
    b = b_ref[...]
    c = c_ref[...]
    for start in range(0, rows, HALF_ROWS):
        stop = start + HALF_ROWS
        scores = jnp.where(lower, dot(c[start:stop, :], b[start:stop, :], (1, 1)), 0.0)
        if start:
            edge = run[start - 1 : start, :]
            lead = spread(step[:start, :] * jnp.exp2(edge - run[:start, :]), head, per_group, width)
            lead = (x_ref[:start, :].astype(F32) * lead).astype(BF16)
            cross = dot(dot(c[start:stop, :], b[:start, :], (1, 1)).astype(BF16), lead)
            after = jnp.exp2(run[start:stop, :] - edge)
        for first in range(0, per_group, pair):
            cols = slice(first * width, (first + pair) * width)
            x = x_ref[start:stop, cols].astype(F32)
            here = (x * head_lanes(step[start:stop, :], head + first, width)).astype(BF16)
            weights = []
            values = []
            for k in range(pair):
                at = first + k
                gap = own_run[start:stop, at : at + 1] - run_t[at : at + 1, start:stop]
                weights.append((scores * jnp.exp2(jnp.minimum(gap, 0.0))).astype(BF16))
                values.append(jnp.where(lane == k, here, jnp.zeros_like(here)))
            part = dot(jnp.concatenate(weights, axis=1), jnp.concatenate(values, axis=0))
            part = part + head_lanes(skip, head + first, width)[:1, :] * x
            part = part + head_lanes(grown[start:stop, :], head + first, width) * from_before[start:stop, cols]
            if start:
                part = part + head_lanes(after, head + first, width) * cross[:, cols]
            out[start:stop, cols] = part.astype(BF16)


def final_kernel(half, within, c, state, run_ref, base_ref, *rest, dims):
    per_half, per_group, width = dims
    out = rest[-1]
    turn = pl.program_id(0)
    head = (half[0] * per_half + turn) * per_group
    grown = jnp.exp2(run_ref[...] + base_ref[:1, :])
    rows = c[...]
    tile = 2 * LANES
    for start in range(0, out.shape[1], tile):
        carried = dot(rows, state[:, pl.ds(pl.multiple_of(turn * out.shape[1] + start, tile), tile)])
        for j in range(0, tile, LANES):
            cols = slice(start + j, start + j + LANES)
            factor = head_lanes(grown, head + (start + j) // width, width)
            out[:, cols] = (within[:, cols].astype(F32) + factor * carried[:, j : j + LANES]).astype(BF16)


def local(inputs, step_size, log_decay, b_matrix, c_matrix, skip_gain, *, chip_axes, core_axis):
    tokens, channels = inputs.shape
    heads = step_size.shape[1]
    width = channels // heads
    states = b_matrix.shape[1] // GROUPS
    per_group = heads // GROUPS
    group_cols = per_group * width
    per_half = GROUPS // CORES
    half_cols = channels // CORES
    chips = lax.axis_size(chip_axes)
    rows = states // chips
    tall = states + ROW_TILE

    core = lax.axis_index(core_axis).astype(jnp.int32)
    mine = core.reshape(1)
    other = (1 - core).reshape(1)

    smem = pl.BlockSpec(memory_space=pltpu.SMEM)
    vmem = pl.BlockSpec(memory_space=pltpu.VMEM)
    hbm = pl.BlockSpec(memory_space=pltpu.HBM)
    anywhere = pl.BlockSpec(memory_space=pl.ANY)

    def whole(shape):
        return pl.BlockSpec(shape, lambda i, *_: (0,) * len(shape))

    def by_group(cols):
        return pl.BlockSpec((tokens, cols), lambda i, *_: (0, i))

    def of_half(cols):
        return pl.BlockSpec((tokens, cols), lambda i, half: (0, half[0] * per_half + i))

    state_dims = (per_half, group_cols, states)
    half_dims = (per_half, per_group, width)
    half_scratch = [pltpu.VMEM((tokens, half_cols), BF16), pltpu.VMEM((tokens, per_half * states), BF16)]

    inputs, step_size, log_decay, b_matrix, c_matrix = (
        pltpu.with_memory_space_constraint(array, pltpu.HBM)
        for array in (inputs, step_size, log_decay, b_matrix, c_matrix)
    )
    send, run, run_t, factor, total = pl.pallas_call(
        functools.partial(send_state_kernel, dims=state_dims),
        in_specs=[smem, hbm, hbm, hbm, hbm],
        out_specs=[vmem] * 5,
        out_shape=[
            jax.ShapeDtypeStruct((tall, half_cols), BF16),
            jax.ShapeDtypeStruct((tokens, heads), F32),
            jax.ShapeDtypeStruct((heads, tokens), F32),
            jax.ShapeDtypeStruct((tokens, heads), F32),
            jax.ShapeDtypeStruct((ROW_TILE, heads), F32),
        ],
        scratch_shapes=half_scratch
        + [pltpu.VMEM((tokens, heads), F32)] * 2
        + [pltpu.SemaphoreType.DMA((2 * per_half + 2,))],
        compiler_params=plain_params(),
        name="send_state",
    )(other, inputs, b_matrix, step_size, log_decay)

    swap = [(0, 1), (1, 0)]
    got = lax.ppermute(send, core_axis, swap)

    own = pl.pallas_call(
        functools.partial(own_state_kernel, dims=state_dims),
        in_specs=[smem, hbm, hbm, vmem, vmem],
        out_specs=vmem,
        out_shape=jax.ShapeDtypeStruct((tall, half_cols), BF16),
        scratch_shapes=half_scratch + [pltpu.SemaphoreType.DMA((2 * per_half,))],
        compiler_params=plain_params(),
        name="own_state",
    )(mine, inputs, b_matrix, factor, total)

    chip_total, base = pl.pallas_call(
        chip_total_kernel,
        in_specs=[smem, vmem, vmem, vmem],
        out_specs=[vmem, vmem],
        out_shape=[
            jax.ShapeDtypeStruct((states, half_cols + heads), BF16),
            jax.ShapeDtypeStruct((ROW_TILE, heads), F32),
        ],
        compiler_params=plain_params(),
        name="chip_total",
    )(mine, own, got, total)

    sent = lax.all_to_all(
        chip_total.reshape(chips, rows, half_cols + heads), chip_axes, split_axis=0, concat_axis=0, tiled=True
    )
    late = lax.ppermute(own, core_axis, swap[:1])

    entering, ready = pl.pallas_call(
        functools.partial(prefix_kernel, width=width, blocks=per_half),
        in_specs=[vmem],
        out_specs=[hbm, vmem],
        out_shape=[
            jax.ShapeDtypeStruct((chips, rows, half_cols), BF16),
            jax.ShapeDtypeStruct((ROW_TILE, heads), F32),
        ],
        scratch_shapes=[pltpu.VMEM((chips, rows, half_cols), BF16), pltpu.SemaphoreType.DMA((per_half,))],
        compiler_params=plain_params(),
        name="prefix",
    )(sent)
    entering = lax.all_to_all(entering, chip_axes, split_axis=0, concat_axis=0, tiled=True)

    within = pl.pallas_call(
        functools.partial(within_kernel, dims=half_dims),
        grid_spec=pltpu.PrefetchScalarGridSpec(
            num_scalar_prefetch=1,
            grid=(GROUPS,),
            in_specs=[
                by_group(group_cols),
                by_group(states),
                by_group(states),
                whole((tokens, heads)),
                whole((tokens, heads)),
                whole((heads, tokens)),
                whole((1, heads)),
                pl.BlockSpec((states, group_cols), lambda i, _: (0, jnp.minimum(i, per_half - 1))),
                pl.BlockSpec((states, group_cols), lambda i, _: (0, jnp.maximum(i - per_half, 0))),
                anywhere,
            ],
            out_specs=by_group(group_cols),
        ),
        out_shape=jax.ShapeDtypeStruct((tokens, channels), BF16),
        compiler_params=params(),
        name="within",
    )(mine, inputs, b_matrix, c_matrix, step_size, run, run_t, skip_gain.reshape(1, heads), late, got, ready)

    within = pltpu.with_memory_space_constraint(within, pltpu.HBM)
    entering = entering.reshape(states, half_cols)
    got_entering = lax.ppermute(entering, core_axis, swap)

    def finish(half, state, *result):
        return pl.pallas_call(
            functools.partial(final_kernel, dims=half_dims),
            grid_spec=pltpu.PrefetchScalarGridSpec(
                num_scalar_prefetch=1,
                grid=(per_half,),
                in_specs=[
                    of_half(group_cols),
                    of_half(states),
                    vmem,
                    vmem,
                    vmem,
                ]
                + [anywhere] * len(result),
                out_specs=of_half(group_cols),
            ),
            out_shape=jax.ShapeDtypeStruct((tokens, channels), BF16),
            input_output_aliases={6: 0} if result else {},
            compiler_params=params(),
            name="finish",
        )(half, within, c_matrix, state, run, base, *result)

    result = finish(mine, entering)
    return finish(other, got_entering, result)


def solution(mesh):
    outer, inner = mesh.axis_names
    chip_mesh = Mesh(
        mesh.devices.reshape(mesh.shape[outer], mesh.shape[inner] // CORES, CORES), (outer, "chip", "core")
    )
    placed = P((outer, "chip", "core"), None)

    def body(*args):
        return local(*args, chip_axes=(outer, "chip"), core_axis="core")

    return jax.shard_map(body, mesh=chip_mesh, in_specs=(placed,) * 5 + (P(),), out_specs=placed, check_vma=False)
```

time: 94.4 us -> 106 us (1.12)
  waiting for transfers between devices: 7 us -> 24.6 us
  local copies, waits for them, and re-layouts: 15.8 us -> 2.91 us
  blocking collectives: 30.3 us -> 36.5 us
  Pallas kernels: 30 us -> 35.2 us
  starting transfers between devices: 10.8 us -> 6.65 us
    all_to_all x1, waiting for transfers between devices: 4.7 us -> 24.6 us  [local(): lax.all_to_all(entering, chip_axes, split_axis=0, concat_axis=0, tiled=True)]
    unnamed x30 -> x6, local copies, waits for them, and re-layouts: 15.8 us -> 2.91 us
    all_to_all x1, blocking collectives: 30.3 us -> 36.5 us  [local(): lax.all_to_all(chip_total.reshape(chips, rows, half_cols + heads), chip_a...]
    all_to_all x1, starting transfers between devices: 8.08 us -> 3.79 us  [local(): lax.all_to_all(entering, chip_axes, split_axis=0, concat_axis=0, tiled=True)]
    pallas_call x1, Pallas kernels: 13.3 us -> 16.9 us  [local(): pl.pallas_call(functools.partial(within_kernel, dims=half_dims), grid_spe...]
    ppermute x1, waiting for transfers between devices: 2.29 us -> 0.01 us  [local(): late = lax.ppermute(own, core_axis, swap[:1])]
    pallas_call x2, Pallas kernels: 7.72 us -> 9.09 us  [finish(): pl.pallas_call(functools.partial(final_kernel, dims=half_dims), grid_spec...]
  transfers between devices with their start and end apart: 4 -> 4, of which waited for: 2 -> 1; matrix products, arithmetic and copies ran while one was open for 0% -> 0% of each run, Pallas kernels for 22% -> 24%
where the time goes in v3:
time: 106 us
  blocking collectives  36.5 us (34%)
  Pallas kernels  35.2 us (33%)
  waiting for transfers between devices  24.6 us (23%)
  starting transfers between devices  6.65 us (6%)
  local copies, waits for them, and re-layouts  2.91 us (3%)
    all_to_all x1, blocking collectives, local(): lax.all_to_all(chip_total.reshape(chips, rows, half_cols + heads), chip_a...  36.5 us
    all_to_all x1, waiting for transfers between devices, local(): lax.all_to_all(entering, chip_axes, split_axis=0, concat_axis=0, tiled=True)  24.6 us
    pallas_call x1, Pallas kernels, local(): pl.pallas_call(functools.partial(within_kernel, dims=half_dims), grid_spe...  16.9 us
    pallas_call x2, Pallas kernels, finish(): pl.pallas_call(functools.partial(final_kernel, dims=half_dims), grid_spec...  9.09 us
    pallas_call x1, Pallas kernels, local(): pl.pallas_call(functools.partial(send_state_kernel, dims=state_dims), in_...  3.97 us
    all_to_all x1, starting transfers between devices, local(): lax.all_to_all(entering, chip_axes, split_axis=0, concat_axis=0, tiled=True)  3.79 us
    pallas_call x1, Pallas kernels, local(): pl.pallas_call(functools.partial(own_state_kernel, dims=state_dims), in_s...  3.78 us
    unnamed x6, local copies, waits for them, and re-layouts  2.91 us
  transfers between devices with their start and end apart: 4, of which 1 were waited for; matrix products, arithmetic and copies ran while one was open for 0% of the time, Pallas kernels for 24%

profile of v3, /device:TPU:0, one launch (start us, length us, event | category | flops | bytes accessed | tf_op | source)
XLA Modules:
  0.0 105.9 jit_solution(7139652815708795301)
XLA Ops:
  0.0 4.0 %send_state.1 = (bf16[136,4096]{1,0:T(8,128)(2,1)S(1)}, f32[256,128]{1,0:T(8,128)S(1)}, f32[128,256]{1,0:T(8,128)S(1)}, f32[256,128]{1,0:T(8,128)S(1)}, f32[8,128]{1,0:T(8,128)S(1)}) custom-call(s32[1]{0:T(128)} %bitcast.half, bf16[256,8192]{1,0:T(8,128)(2,1)} %x_ref.1, bf16[256,1024]{1,0:T(8,128)(2,1)} %b_ref.1, f32[256,128]{1,0:T(8,128)} %step_ref.1, ...), custom_call_target="tpu_custom_call" | custom-call | tf_op jit(solution)/shard_map/send_state/pallas_call | solution.py:301
  4.0 0.6 collective-permute-start.1
  4.5 3.8 %own_state.1.own = bf16[136,4096]{1,0:T(8,128)(2,1)S(1)} custom-call(s32[1]{0:T(128)} %bitcast.1.half.core, bf16[256,8192]{1,0:T(8,128)(2,1)} %x_ref.1, bf16[256,1024]{1,0:T(8,128)(2,1)} %b_ref.1, f32[256,128]{1,0:T(8,128)S(1)} %get-tuple-element.16.factor, f32[8,128]{1,0:T(8,128)S(1)} %get-tuple-element.17.total), custom_call_target="tpu_custom_call" | custom-call | tf_op jit(solution)/shard_map/own_state/pallas_call | solution.py:322
  8.3 0.0 collective-permute-done.1.got.high_ref
  8.3 0.6 chip_total.1
  9.0 36.5 %all_to_all.10.sent = bf16[16,8,4224]{2,1,0:T(8,128)(2,1)S(1)} all-to-all(bf16[16,8,4224]{2,1,0:T(8,128)(2,1)S(1)} %bitcast.7), channel_id=1, replica_groups=mesh['outer'=4,'chip'=4,'core'=2] {'outer','chip'}, dimensions={0} | all-to-all | bytes 2162688 | tf_op jit(solution)/shard_map/all_to_all | solution.py:344
  45.4 0.8 prefix.1
  46.2 0.0 copy-start.1
  46.3 1.0 copy-done.1
  47.2 0.0 copy-start.2
  47.2 3.8 %all-to-all-start.1 = ((bf16[16,8,4096]{2,1,0:T(8,128)(2,1)}), bf16[16,8,4096]{2,1,0:T(8,128)(2,1)S(1)}, u32[]{:S(2)}, u32[]{:S(2)}) async-start(bf16[16,8,4096]{2,1,0:T(8,128)(2,1)} %copy-done.1), calls=%async_computation.1 | async-start | bytes 2097152 | tf_op jit(solution)/shard_map/all_to_all | solution.py:361
  51.0 2.3 %collective-permute-start = (bf16[136,4096]{1,0:T(8,128)(2,1)S(1)}, bf16[136,4096]{1,0:T(8,128)(2,1)}, u32[]{:S(2)}, u32[]{:S(2)}) collective-permute-start(bf16[136,4096]{1,0:T(8,128)(2,1)S(1)} %own_state.1.own), channel_id=1, source_target_pairs={{0,1},{2,3},{4,5},{6,7},{8,9},{10,11},{12,13},{14,15},{16,17},{18,... | collective-permute-start | bytes 3342344 | tf_op jit(solution)/shard_map/ppermute | solution.py:347
  53.3 24.6 %all-to-all-done.1 = bf16[16,8,4096]{2,1,0:T(8,128)(2,1)S(1)} async-done(((bf16[16,8,4096]{2,1,0:T(8,128)(2,1)}), bf16[16,8,4096]{2,1,0:T(8,128)(2,1)S(1)}, u32[]{:S(2)}, u32[]{:S(2)}) %all-to-all-start.1) | async-done | bytes 1048608 | tf_op jit(solution)/shard_map/all_to_all | solution.py:361
  77.9 0.0 collective-permute-start.2
  78.0 0.0 collective-permute-done.low_ref
  78.0 0.0 copy-done.2
  78.0 16.9 %within.1 = bf16[256,8192]{1,0:T(8,128)(2,1)S(1)} custom-call(s32[1]{0:T(128)} %bitcast.1.half.core, bf16[256,8192]{1,0:T(8,128)(2,1)} %x_ref.1, bf16[256,1024]{1,0:T(8,128)(2,1)} %b_ref.1, bf16[256,1024]{1,0:T(8,128)(2,1)} %c.3, f32[256,128]{1,0:T(8,128)} %step_ref.1, f32[256,128]{1,0:T(8,128)S(1)} %get-tuple-element.14.run_ref, ...), custom_call_target="tpu_custom_call" | custom-call | tf_op jit(solution)/shard_map/within/pallas_call | solution.py:363
  94.9 0.0 copy-start
  94.9 1.9 %copy-done = bf16[256,8192]{1,0:T(8,128)(2,1)} copy-done((bf16[256,8192]{1,0:T(8,128)(2,1)}, bf16[256,8192]{1,0:T(8,128)(2,1)S(1)}, u32[]{:S(2)}) %copy-start) | copy-done | bytes 4194328
  96.8 4.5 %finish.2.rest_0_ = bf16[256,8192]{1,0:T(8,128)(2,1)} custom-call(s32[1]{0:T(128)} %bitcast.1.half.core, bf16[256,8192]{1,0:T(8,128)(2,1)} %copy-done, bf16[256,1024]{1,0:T(8,128)(2,1)} %c.3, bf16[128,4096]{1,0:T(8,128)(2,1)S(1)} %bitcast.6, f32[256,128]{1,0:T(8,128)S(1)} %get-tuple-element.14.run_ref, f32[8,128]{1,0:T(8,128)S(1)} %get-tuple-element.22.base_ref), custom_call_target="tpu_custom_call" | custom-call | tf_op jit(solution)/shard_map/finish/pallas_call | solution.py:392
  101.4 0.0 collective-permute-done.2.state
  101.4 4.6 %finish.3 = bf16[256,8192]{1,0:T(8,128)(2,1)} custom-call(s32[1]{0:T(128)} %bitcast.half, bf16[256,8192]{1,0:T(8,128)(2,1)} %copy-done, bf16[256,1024]{1,0:T(8,128)(2,1)} %c.3, bf16[128,4096]{1,0:T(8,128)(2,1)S(1)} %collective-permute-done.2.state, f32[256,128]{1,0:T(8,128)S(1)} %get-tuple-element.14.run_ref, ...), custom_call_target="tpu_custom_call", output_to_operand_aliasing={{}: (6, {})} | custom-call | tf_op jit(solution)/shard_map/finish/pallas_call | solution.py:392
Async XLA Ops:
  4.0 4.4 %collective-permute-start.1 = (bf16[136,4096]{1,0:T(8,128)(2,1)S(1)}, bf16[136,4096]{1,0:T(8,128)(2,1)S(1)}, u32[]{:S(2)}, u32[]{:S(2)}) collective-permute-start(bf16[136,4096]{1,0:T(8,128)(2,1)S(1)} %get-tuple-element.18), channel_id=1, source_target_pairs={{0,1},{1,0},{2,3},{3,2},{4,5},{5,4},{6,7},{7,6},{8,9},{9,8},{10,11... | collective-permute-start | bytes 3342344 | tf_op jit(solution)/shard_map/ppermute | solution.py:320
  46.2 1.0 copy-start.1
  47.2 30.7 %copy-start.2 = (f32[128]{0:T(128)S(1)}, f32[128]{0:T(128)}, u32[]{:S(2)}) copy-start(f32[128]{0:T(128)} %param.11) | copy-start | bytes 1540
  47.2 30.7 %all-to-all-start.1 = ((bf16[16,8,4096]{2,1,0:T(8,128)(2,1)}), bf16[16,8,4096]{2,1,0:T(8,128)(2,1)S(1)}, u32[]{:S(2)}, u32[]{:S(2)}) async-start(bf16[16,8,4096]{2,1,0:T(8,128)(2,1)} %copy-done.1), calls=%async_computation.1 | async-start | bytes 2097152 | tf_op jit(solution)/shard_map/all_to_all | solution.py:361
  51.0 26.9 %collective-permute-start = (bf16[136,4096]{1,0:T(8,128)(2,1)S(1)}, bf16[136,4096]{1,0:T(8,128)(2,1)}, u32[]{:S(2)}, u32[]{:S(2)}) collective-permute-start(bf16[136,4096]{1,0:T(8,128)(2,1)S(1)} %own_state.1.own), channel_id=1, source_target_pairs={{0,1},{2,3},{4,5},{6,7},{8,9},{10,11},{12,13},{14,15},{16,17},{18,... | collective-permute-start | bytes 3342344 | tf_op jit(solution)/shard_map/ppermute | solution.py:347
  77.9 23.4 %collective-permute-start.2 = (bf16[128,4096]{1,0:T(8,128)(2,1)S(1)}, bf16[128,4096]{1,0:T(8,128)(2,1)S(1)}, u32[]{:S(2)}, u32[]{:S(2)}) collective-permute-start(bf16[128,4096]{1,0:T(8,128)(2,1)S(1)} %bitcast.5), channel_id=1, source_target_pairs={{0,1},{1,0},{2,3},{3,2},{4,5},{5,4},{6,7},{7,6},{8,9},{9,8},{10,11... | collective-permute-start | bytes 3145736 | tf_op jit(solution)/shard_map/ppermute | solution.py:389
  94.9 1.9 %copy-start = (bf16[256,8192]{1,0:T(8,128)(2,1)}, bf16[256,8192]{1,0:T(8,128)(2,1)S(1)}, u32[]{:S(2)}) copy-start(bf16[256,8192]{1,0:T(8,128)(2,1)S(1)} %within.1) | copy-start | bytes 12582916

commit v4 on v3

--- a/solution.py
+++ b/solution.py
@@ -12,6 +12,8 @@
 GROUPS = 8
 CORES = 2
 LANES = 128
+TILE = 256
+AHEAD = 2
 ROW_TILE = 8
 HALF_ROWS = 128
 ROW_BLOCK = 16
@@ -32,14 +34,40 @@
     return high, values - high
 
 
-def head_lanes(values, first_head, width):
-    lane = lax.broadcasted_iota(jnp.int32, (values.shape[0], LANES), 1)
-    return jnp.take_along_axis(values, first_head + lane // width, axis=1)
-
-
-def spread(values, first_head, heads, width):
-    pair = LANES // width
-    return jnp.concatenate([head_lanes(values, first_head + k, width) for k in range(0, heads, pair)], axis=1)
+def spreader(heads, width):
+    shape = (2 * heads, heads * width)
+    row = lax.broadcasted_iota(jnp.int32, shape, 0)
+    col = lax.broadcasted_iota(jnp.int32, shape, 1)
+    row = jnp.where(row >= heads, row - heads, row)
+    return jnp.where(row == col // width, 1.0, 0.0).astype(BF16)
+
+
+def group_first(values, head):
+    lanes = values.shape[1]
+    return pltpu.roll(values, lax.rem(lanes - head, lanes), 1)
+
+
+def packed(values, heads):
+    high, low = high_low(values)
+    lane = lax.broadcasted_iota(jnp.int32, values.shape, 1)
+    return jnp.where(lane < heads, high, pltpu.roll(low, heads, 1)).astype(BF16)[:, : 2 * heads]
+
+
+def half_spreader(matrix, width):
+    lanes, cols = matrix.shape
+    for start in range(0, cols, TILE):
+        row = lax.broadcasted_iota(jnp.int32, (lanes, TILE), 0)
+        col = start + lax.broadcasted_iota(jnp.int32, (lanes, TILE), 1)
+        row = jnp.where(row >= lanes // 2, row - lanes // 2, row)
+        matrix[:, start : start + TILE] = jnp.where(row == col // width, 1.0, 0.0).astype(BF16)
+
+
+def packed_half(values, half):
+    lanes = values.shape[1]
+    values = group_first(values, half * (lanes // 2))
+    high, low = high_low(values)
+    lane = lax.broadcasted_iota(jnp.int32, values.shape, 1)
+    return jnp.where(lane < lanes // 2, high, pltpu.roll(low, lanes // 2, 1)).astype(BF16)
 
 
 def params():
@@ -72,38 +100,63 @@
     return copies
 
 
-def half_states(half, x_here, b_here, copies, factor, log_total, out, dims):
-    per_half, group_cols, states = dims
-    heads = factor.shape[1]
-    half_heads = heads // CORES
-    per_group = half_heads // per_half
-    width = group_cols // per_group
-    first = half * half_heads
-    row = lax.broadcasted_iota(jnp.int32, (ROW_TILE, LANES), 0)
-    high, low = high_low(log_total)
-    middle, low = high_low(low)
-    logs = jnp.where(row == 2, high, jnp.where(row == 3, middle, low))
-    total = jnp.exp2(log_total)
-    for k in range(per_half):
-        copies[2 * k].wait()
-        copies[2 * k + 1].wait()
-        b = b_here[:, k * states : (k + 1) * states]
-        scaled = []
-        for j in range(0, group_cols, LANES):
-            start = k * group_cols + j
-            part = head_lanes(factor, first + start // width, width)
-            scaled.append((x_here[:, start : start + LANES].astype(F32) * part).astype(BF16))
-            high, low = high_low(head_lanes(total, first + start // width, width))
+def half_states(half, x_here, b_here, copies, factor, log_total, out, matrix, dims):
+    _, group_cols, states = dims
+    rows, heads = factor.shape
+    row = lax.broadcasted_iota(jnp.int32, (ROW_TILE, TILE), 0)
+    operand = packed_half(jnp.concatenate([factor, jnp.exp2(log_total)], axis=0), half)
+    for copy in copies:
+        copy.wait()
+    tiles = out.shape[1] // TILE
+    per_group = group_cols // TILE
+    matrices = {}
+    factors = {}
+    scaled = {}
+    for n in range(tiles + 2 * AHEAD):
+        if n < tiles:
+            factors[n] = dot(operand, matrix[:, n * TILE : (n + 1) * TILE])
+        m = n - AHEAD
+        if 0 <= m < tiles:
+            cols = slice(m * TILE, (m + 1) * TILE)
+            spread = factors.pop(m)
+            scaled[m] = (x_here[:, cols].astype(F32) * spread[:rows, :]).astype(BF16)
+            high, low = high_low(spread[rows:, :])
             tail = jnp.where(row == 0, high, low)
-            if start == 0:
-                tail = jnp.where(row < 2, tail, logs)
-            out[states:, start : start + LANES] = tail.astype(BF16)
-        cols = slice(k * group_cols, (k + 1) * group_cols)
-        out[:states, cols] = dot(b, jnp.concatenate(scaled, axis=1), (0, 0)).astype(BF16)
+            if m == 0:
+                high, low = high_low(log_total)
+                middle, low = high_low(low)
+                at = row[:, :heads]
+                logs = jnp.where(at == 2, high, jnp.where(at == 3, middle, low))
+                logs = jnp.where(at < 2, tail[:, :heads], logs)
+                tail = jnp.concatenate([logs, tail[:, heads:]], axis=1)
+            out[states:, cols] = tail.astype(BF16)
+            if m % per_group == 0:
+                k = m // per_group
+                matrices[k] = b_here[:, k * states : (k + 1) * states].T
+        m = n - 2 * AHEAD
+        if m >= 0:
+            out[:states, m * TILE : (m + 1) * TILE] = dot(matrices[m // per_group], scaled.pop(m)).astype(BF16)
 
 
 def send_state_kernel(
-    half, x, b, step, log, out, run_out, run_t_out, factor_out, total_out, x_here, b_here, step_here, log_here, sems, *, dims
+    half,
+    x,
+    b,
+    step,
+    log,
+    out,
+    run_out,
+    run_t_out,
+    factor_out,
+    total_out,
+    x_here,
+    b_here,
+    matrix,
+    step_here,
+    log_here,
+    sems,
+    *,
+    dims,
 ):
     first = pltpu.make_async_copy(log, log_here, sems.at[2 * dims[0]])
     second = pltpu.make_async_copy(step, step_here, sems.at[2 * dims[0] + 1])
@@ -113,6 +166,7 @@
     for copy in copies:
         copy.start()
     rows, heads = log_here.shape
+    half_spreader(matrix, x_here.shape[1] * CORES // heads)
     upto = lax.broadcasted_iota(jnp.int32, (rows, rows), 1) <= lax.broadcasted_iota(jnp.int32, (rows, rows), 0)
     first.wait()
     high, rest = high_low(log_here[...])
@@ -128,14 +182,15 @@
     total = jnp.broadcast_to(last, total_out.shape)
     factor_out[...] = factor
     total_out[...] = total
-    half_states(half[0], x_here, b_here, copies, factor, total, out, dims)
-
-
-def own_state_kernel(half, x, b, factor, total, out, x_here, b_here, sems, *, dims):
+    half_states(half[0], x_here, b_here, copies, factor, total, out, matrix, dims)
+
+
+def own_state_kernel(half, x, b, factor, total, out, x_here, b_here, matrix, sems, *, dims):
     copies = state_copies(half[0], x, b, x_here, b_here, sems, dims)
     for copy in copies:
         copy.start()
-    half_states(half[0], x_here, b_here, copies, factor[...], total[...], out, dims)
+    half_spreader(matrix, x_here.shape[1] * CORES // factor.shape[1])
+    half_states(half[0], x_here, b_here, copies, factor[...], total[...], out, matrix, dims)
 
 
 def chip_total_kernel(core, own, got, total, out, base_out):
@@ -174,10 +229,12 @@
     ready[...] = jnp.zeros_like(ready)
     first_rows = jnp.concatenate([sent[k, :1, cols:].astype(F32) for k in range(chips)], axis=0)
     values = first_rows + pltpu.roll(first_rows, half, 1)
+    matrix = spreader(step // width, width)
     copies = []
     for block in range(blocks):
         lanes = slice(block * step, (block + 1) * step)
-        decay = spread(values, block * step // width, step // width, width)
+        head = block * step // width
+        decay = dot(packed(pltpu.roll(values, heads - head, 1) if head else values, step // width), matrix)
         state = jnp.zeros((rows, step), F32)
         for k in range(chips):
             here[k, :, lanes] = state.astype(BF16)
@@ -193,7 +250,7 @@
 
 
 def within_kernel(
-    core, x_ref, b_ref, c_ref, step_ref, run_ref, run_t_ref, skip_ref, low_ref, high_ref, ready, out, *, dims
+    core, x_ref, b_ref, c_ref, step_ref, run_ref, run_t_ref, skip_ref, low_ref, high_ref, ready, out, matrix, *, dims
 ):
     del ready
     per_half, per_group, width = dims
@@ -201,14 +258,23 @@
     head = group * per_group
     rows = x_ref.shape[0]
     pair = LANES // width
-    run = run_ref[...]
-    own_run = pltpu.roll(run, lax.rem(run.shape[1] - head, run.shape[1]), 1)
+
+    @pl.when(group == 0)
+    def _():
+        matrix[...] = spreader(per_group, width)
+
+    def spread(values):
+        return dot(packed(values, per_group), matrix[...])
+
+    step = group_first(step_ref[...], head)
+    run = group_first(run_ref[...], head)
+    skip = group_first(jnp.broadcast_to(skip_ref[...], (ROW_TILE, skip_ref.shape[1])), head)
     run_t = run_t_ref[pl.ds(pl.multiple_of(head, per_group), per_group), :]
-    step = step_ref[...]
-    skip = jnp.broadcast_to(skip_ref[...], (ROW_TILE, skip_ref.shape[1]))
-    grown = jnp.exp2(run)
+    x = x_ref[...].astype(F32)
+    scaled = (x * spread(step)).astype(BF16)
     upper = high_ref[...] * core[0].astype(BF16)
-    from_before = dot(c_ref[...], jnp.where(group < per_half, low_ref[...], upper))
+    before = dot(c_ref[...], jnp.where(group < per_half, low_ref[...], upper))
+    outer = spread(skip)[:1, :] * x + spread(jnp.exp2(run)) * before
     lane = lax.broadcasted_iota(jnp.int32, (HALF_ROWS, LANES), 1) // width
     lower = lax.broadcasted_iota(jnp.int32, (HALF_ROWS, HALF_ROWS), 1) <= lax.broadcasted_iota(
         jnp.int32, (HALF_ROWS, HALF_ROWS), 0
@@ -218,45 +284,106 @@
     for start in range(0, rows, HALF_ROWS):
         stop = start + HALF_ROWS
         scores = jnp.where(lower, dot(c[start:stop, :], b[start:stop, :], (1, 1)), 0.0)
+        added = outer[start:stop, :]
         if start:
             edge = run[start - 1 : start, :]
-            lead = spread(step[:start, :] * jnp.exp2(edge - run[:start, :]), head, per_group, width)
-            lead = (x_ref[:start, :].astype(F32) * lead).astype(BF16)
-            cross = dot(dot(c[start:stop, :], b[:start, :], (1, 1)).astype(BF16), lead)
-            after = jnp.exp2(run[start:stop, :] - edge)
+            lead = spread(step[:start, :] * jnp.exp2(edge - run[:start, :]))
+            lead = (x[:start, :] * lead).astype(BF16)
+            cross = dot(c[start:stop, :], b[:start, :], (1, 1)).astype(BF16)
+            added = added + spread(jnp.exp2(run[start:stop, :] - edge)) * dot(cross, lead)
         for first in range(0, per_group, pair):
             cols = slice(first * width, (first + pair) * width)
-            x = x_ref[start:stop, cols].astype(F32)
-            here = (x * head_lanes(step[start:stop, :], head + first, width)).astype(BF16)
+            here = scaled[start:stop, cols]
             weights = []
             values = []
             for k in range(pair):
                 at = first + k
-                gap = own_run[start:stop, at : at + 1] - run_t[at : at + 1, start:stop]
+                gap = run[start:stop, at : at + 1] - run_t[at : at + 1, start:stop]
                 weights.append((scores * jnp.exp2(jnp.minimum(gap, 0.0))).astype(BF16))
                 values.append(jnp.where(lane == k, here, jnp.zeros_like(here)))
             part = dot(jnp.concatenate(weights, axis=1), jnp.concatenate(values, axis=0))
-            part = part + head_lanes(skip, head + first, width)[:1, :] * x
-            part = part + head_lanes(grown[start:stop, :], head + first, width) * from_before[start:stop, cols]
-            if start:
-                part = part + head_lanes(after, head + first, width) * cross[:, cols]
-            out[start:stop, cols] = part.astype(BF16)
-
-
-def final_kernel(half, within, c, state, run_ref, base_ref, *rest, dims):
-    per_half, per_group, width = dims
-    out = rest[-1]
-    turn = pl.program_id(0)
-    head = (half[0] * per_half + turn) * per_group
-    grown = jnp.exp2(run_ref[...] + base_ref[:1, :])
-    rows = c[...]
-    tile = 2 * LANES
-    for start in range(0, out.shape[1], tile):
-        carried = dot(rows, state[:, pl.ds(pl.multiple_of(turn * out.shape[1] + start, tile), tile)])
-        for j in range(0, tile, LANES):
-            cols = slice(start + j, start + j + LANES)
-            factor = head_lanes(grown, head + (start + j) // width, width)
-            out[:, cols] = (within[:, cols].astype(F32) + factor * carried[:, j : j + LANES]).astype(BF16)
+            out[start:stop, cols] = (added[:, cols] + part).astype(BF16)
+
+
+def add_carried(half, within, rows_c, state, run, base, out, result, matrix, sems, dims):
+    per_half, group_cols, _ = dims
+    operand = packed_half(jnp.exp2(run[...] + base[:1, :]), half)
+    copies = []
+    for k in range(per_half):
+        rows = rows_c(k)
+        part = within(k)
+        tiles = group_cols // TILE
+        products = {}
+        for n in range(tiles + AHEAD):
+            if n < tiles:
+                cols = slice(k * group_cols + n * TILE, k * group_cols + (n + 1) * TILE)
+                products[n] = dot(rows, state[:, cols]), dot(operand, matrix[:, cols])
+            m = n - AHEAD
+            if m >= 0:
+                cols = slice(k * group_cols + m * TILE, k * group_cols + (m + 1) * TILE)
+                carried, factor = products.pop(m)
+                result[:, cols] = (part[:, m * TILE : (m + 1) * TILE].astype(F32) + factor * carried).astype(BF16)
+        home = pl.multiple_of((half * per_half + k) * group_cols, group_cols)
+        copies.append(
+            pltpu.make_async_copy(
+                result.at[:, pl.ds(k * group_cols, group_cols)], out.at[:, pl.ds(home, group_cols)], sems.at[k]
+            )
+        )
+        copies[-1].start()
+    for copy in copies:
+        copy.wait()
+
+
+def first_final_kernel(
+    half, within, c, state, run, base, out, other_within, other_c, matrix, here, c_here, result, loads, stores, *, dims
+):
+    per_half, group_cols, states = dims
+    half_cols = per_half * group_cols
+    half_rows = per_half * states
+    mine = half[0]
+    other = 1 - mine
+    copies = []
+    for k in range(per_half):
+        home = pl.multiple_of((mine * per_half + k) * group_cols, group_cols)
+        copies.append(
+            pltpu.make_async_copy(
+                within.at[:, pl.ds(home, group_cols)], here.at[:, pl.ds(k * group_cols, group_cols)], loads.at[k]
+            )
+        )
+    home = pl.multiple_of(mine * half_rows, half_rows)
+    copies.append(pltpu.make_async_copy(c.at[:, pl.ds(home, half_rows)], c_here, loads.at[per_half]))
+    home = pl.multiple_of(other * half_rows, half_rows)
+    copies.append(pltpu.make_async_copy(c.at[:, pl.ds(home, half_rows)], other_c, loads.at[per_half + 1]))
+    home = pl.multiple_of(other * half_cols, half_cols)
+    copies.append(pltpu.make_async_copy(within.at[:, pl.ds(home, half_cols)], other_within, loads.at[per_half + 2]))
+    for copy in [copies[per_half]] + copies[:per_half] + copies[per_half + 1 :]:
+        copy.start()
+    half_spreader(matrix, out.shape[1] // run.shape[1])
+    copies[per_half].wait()
+
+    def part(k):
+        copies[k].wait()
+        return here[:, k * group_cols : (k + 1) * group_cols]
+
+    def rows_c(k):
+        return c_here[:, k * states : (k + 1) * states]
+
+    add_carried(mine, part, rows_c, state, run, base, out, result, matrix, stores, dims)
+    for copy in copies[per_half + 1 :]:
+        copy.wait()
+
+
+def second_final_kernel(half, within, c, state, run, base, matrix, filled, out, result, stores, *, dims):
+    del filled
+    _, group_cols, states = dims
+
+    def part(k):
+        return within[:, k * group_cols : (k + 1) * group_cols]
+
+    def rows_c(k):
+        return c[:, k * states : (k + 1) * states]
+
+    add_carried(half[0], part, rows_c, state, run, base, out, result, matrix, stores, dims)
 
 
 def local(inputs, step_size, log_decay, b_matrix, c_matrix, skip_gain, *, chip_axes, core_axis):
@@ -287,12 +414,13 @@
     def by_group(cols):
         return pl.BlockSpec((tokens, cols), lambda i, *_: (0, i))
 
-    def of_half(cols):
-        return pl.BlockSpec((tokens, cols), lambda i, half: (0, half[0] * per_half + i))
-
     state_dims = (per_half, group_cols, states)
     half_dims = (per_half, per_group, width)
-    half_scratch = [pltpu.VMEM((tokens, half_cols), BF16), pltpu.VMEM((tokens, per_half * states), BF16)]
+    half_scratch = [
+        pltpu.VMEM((tokens, half_cols), BF16),
+        pltpu.VMEM((tokens, per_half * states), BF16),
+        pltpu.VMEM((heads, half_cols), BF16),
+    ]
 
     inputs, step_size, log_decay, b_matrix, c_matrix = (
         pltpu.with_memory_space_constraint(array, pltpu.HBM)
@@ -351,7 +479,7 @@
         in_specs=[vmem],
         out_specs=[hbm, vmem],
         out_shape=[
-            jax.ShapeDtypeStruct((chips, rows, half_cols), BF16),
+            pltpu.HBM((chips, rows, half_cols), BF16),
             jax.ShapeDtypeStruct((ROW_TILE, heads), F32),
         ],
         scratch_shapes=[pltpu.VMEM((chips, rows, half_cols), BF16), pltpu.SemaphoreType.DMA((per_half,))],
@@ -378,8 +506,9 @@
                 anywhere,
             ],
             out_specs=by_group(group_cols),
+            scratch_shapes=[pltpu.VMEM((2 * per_group, group_cols), BF16)],
         ),
-        out_shape=jax.ShapeDtypeStruct((tokens, channels), BF16),
+        out_shape=pltpu.HBM((tokens, channels), BF16),
         compiler_params=params(),
         name="within",
     )(mine, inputs, b_matrix, c_matrix, step_size, run, run_t, skip_gain.reshape(1, heads), late, got, ready)
@@ -388,30 +517,37 @@
     entering = entering.reshape(states, half_cols)
     got_entering = lax.ppermute(entering, core_axis, swap)
 
-    def finish(half, state, *result):
-        return pl.pallas_call(
-            functools.partial(final_kernel, dims=half_dims),
-            grid_spec=pltpu.PrefetchScalarGridSpec(
-                num_scalar_prefetch=1,
-                grid=(per_half,),
-                in_specs=[
-                    of_half(group_cols),
-                    of_half(states),
-                    vmem,
-                    vmem,
-                    vmem,
-                ]
-                + [anywhere] * len(result),
-                out_specs=of_half(group_cols),
-            ),
-            out_shape=jax.ShapeDtypeStruct((tokens, channels), BF16),
-            input_output_aliases={6: 0} if result else {},
-            compiler_params=params(),
-            name="finish",
-        )(half, within, c_matrix, state, run, base, *result)
-
-    result = finish(mine, entering)
-    return finish(other, got_entering, result)
+    mixed = jax.ShapeDtypeStruct((tokens, channels), BF16)
+    result, other_within, other_c, matrix = pl.pallas_call(
+        functools.partial(first_final_kernel, dims=state_dims),
+        in_specs=[smem, hbm, hbm, vmem, vmem, vmem],
+        out_specs=[hbm, vmem, vmem, vmem],
+        out_shape=[
+            mixed,
+            jax.ShapeDtypeStruct((tokens, half_cols), BF16),
+            jax.ShapeDtypeStruct((tokens, per_half * states), BF16),
+            jax.ShapeDtypeStruct((heads, half_cols), BF16),
+        ],
+        scratch_shapes=[
+            pltpu.VMEM((tokens, half_cols), BF16),
+            pltpu.VMEM((tokens, per_half * states), BF16),
+            pltpu.VMEM((tokens, half_cols), BF16),
+            pltpu.SemaphoreType.DMA((per_half + 3,)),
+            pltpu.SemaphoreType.DMA((per_half,)),
+        ],
+        compiler_params=plain_params(),
+        name="finish_own",
+    )(mine, within, c_matrix, entering, run, base)
+    return pl.pallas_call(
+        functools.partial(second_final_kernel, dims=state_dims),
+        in_specs=[smem] + [vmem] * 6 + [hbm],
+        out_specs=hbm,
+        out_shape=mixed,
+        scratch_shapes=[pltpu.VMEM((tokens, half_cols), BF16), pltpu.SemaphoreType.DMA((per_half,))],
+        input_output_aliases={7: 0},
+        compiler_params=plain_params(),
+        name="finish_other",
+    )(other, other_within, other_c, got_entering, run, base, matrix, result)
 
 
 def solution(mesh):

time: 106 us -> 96.5 us (0.910)
  Pallas kernels: 35.2 us -> 28.4 us
  local copies, waits for them, and re-layouts: 2.91 us -> 0.01 us
    pallas_call x2, Pallas kernels: 9.09 us -> 6.13 us  [the longest x1 3.85 us: local(): pl.pallas_call(functools.partial(first_final_kernel, dims=state_dims), in...]
    unnamed x6 -> x2, local copies, waits for them, and re-layouts: 2.91 us -> 0.01 us
    pallas_call x1, Pallas kernels: 16.9 us -> 14.6 us  [local(): pl.pallas_call(functools.partial(within_kernel, dims=half_dims), grid_spe...]
  transfers between devices with their start and end apart: 4 -> 4, of which waited for: 1 -> 1; matrix products, arithmetic and copies ran while one was open for 0% -> 0% of each run, Pallas kernels for 24% -> 22%
where the time goes in v4:
time: 96.5 us; the launch traced here: 96.2 us
  blocking collectives  36.5 us (38%)
  Pallas kernels  28.4 us (29%)
  waiting for transfers between devices  24.7 us (26%)
  starting transfers between devices  6.52 us (7%)
    all_to_all x1, blocking collectives, local(): lax.all_to_all(chip_total.reshape(chips, rows, half_cols + heads), chip_a...  36.5 us
    all_to_all x1, waiting for transfers between devices, local(): lax.all_to_all(entering, chip_axes, split_axis=0, concat_axis=0, tiled=True)  24.6 us
    pallas_call x1, Pallas kernels, local(): pl.pallas_call(functools.partial(within_kernel, dims=half_dims), grid_spe...  14.6 us
    pallas_call x1, Pallas kernels, local(): pl.pallas_call(functools.partial(first_final_kernel, dims=state_dims), in...  3.85 us
    all_to_all x1, starting transfers between devices, local(): lax.all_to_all(entering, chip_axes, split_axis=0, concat_axis=0, tiled=True)  3.67 us
    pallas_call x1, Pallas kernels, local(): pl.pallas_call(functools.partial(send_state_kernel, dims=state_dims), in_...  2.94 us
    pallas_call x1, Pallas kernels, local(): pl.pallas_call(functools.partial(own_state_kernel, dims=state_dims), in_s...  2.82 us
    ppermute x1, starting transfers between devices, local(): late = lax.ppermute(own, core_axis, swap[:1])  2.29 us
  transfers between devices with their start and end apart: 4, of which 1 were waited for; matrix products, arithmetic and copies ran while one was open for 0% of the time, Pallas kernels for 22%

profile of v4, /device:TPU:0, one launch (start us, length us, event | category | flops | bytes accessed | tf_op | source)
XLA Modules:
  0.0 96.2 jit_solution(8933328192290350777)
XLA Ops:
  0.0 2.9 %send_state.1 = (bf16[136,4096]{1,0:T(8,128)(2,1)S(1)}, f32[256,128]{1,0:T(8,128)S(1)}, f32[128,256]{1,0:T(8,128)S(1)}, f32[256,128]{1,0:T(8,128)S(1)}, f32[8,128]{1,0:T(8,128)S(1)}) custom-call(s32[1]{0:T(128)} %bitcast.half, bf16[256,8192]{1,0:T(8,128)(2,1)} %x_ref.1, bf16[256,1024]{1,0:T(8,128)(2,1)} %b_ref.1, f32[256,128]{1,0:T(8,128)} %step_ref.1, ...), custom_call_target="tpu_custom_call" | custom-call | tf_op jit(solution)/shard_map/send_state/pallas_call | solution.py:429
  2.9 0.6 collective-permute-start.1
  3.5 2.8 %own_state.1.own = bf16[136,4096]{1,0:T(8,128)(2,1)S(1)} custom-call(s32[1]{0:T(128)} %bitcast.1.half.core, bf16[256,8192]{1,0:T(8,128)(2,1)} %x_ref.1, bf16[256,1024]{1,0:T(8,128)(2,1)} %b_ref.1, f32[256,128]{1,0:T(8,128)S(1)} %get-tuple-element.20.factor, f32[8,128]{1,0:T(8,128)S(1)} %get-tuple-element.21.total), custom_call_target="tpu_custom_call" | custom-call | tf_op jit(solution)/shard_map/own_state/pallas_call | solution.py:450
  6.3 0.0 collective-permute-done.1.got.high_ref
  6.3 0.7 chip_total.1
  7.0 36.5 %all_to_all.10.sent = bf16[16,8,4224]{2,1,0:T(8,128)(2,1)S(1)} all-to-all(bf16[16,8,4224]{2,1,0:T(8,128)(2,1)S(1)} %bitcast.7), channel_id=1, replica_groups=mesh['outer'=4,'chip'=4,'core'=2] {'outer','chip'}, dimensions={0} | all-to-all | bytes 2162688 | tf_op jit(solution)/shard_map/all_to_all | solution.py:472
  43.5 1.3 %prefix.1 = (bf16[16,8,4096]{2,1,0:T(8,128)(2,1)}, f32[8,128]{1,0:T(8,128)S(1)}) custom-call(bf16[16,8,4224]{2,1,0:T(8,128)(2,1)S(1)} %all_to_all.10.sent), custom_call_target="tpu_custom_call" | custom-call | tf_op jit(solution)/shard_map/prefix/pallas_call | solution.py:477
  44.8 0.0 copy-start
  44.8 3.7 %all-to-all-start.1 = ((bf16[16,8,4096]{2,1,0:T(8,128)(2,1)}), bf16[16,8,4096]{2,1,0:T(8,128)(2,1)S(1)}, u32[]{:S(2)}, u32[]{:S(2)}) async-start(bf16[16,8,4096]{2,1,0:T(8,128)(2,1)} %get-tuple-element.25), calls=%async_computation.1 | async-start | bytes 2097152 | tf_op jit(solution)/shard_map/all_to_all | solution.py:489
  48.5 2.3 %collective-permute-start = (bf16[136,4096]{1,0:T(8,128)(2,1)S(1)}, bf16[136,4096]{1,0:T(8,128)(2,1)}, u32[]{:S(2)}, u32[]{:S(2)}) collective-permute-start(bf16[136,4096]{1,0:T(8,128)(2,1)S(1)} %own_state.1.own), channel_id=1, source_target_pairs={{0,1},{2,3},{4,5},{6,7},{8,9},{10,11},{12,13},{14,15},{16,17},{18,... | collective-permute-start | bytes 3342344 | tf_op jit(solution)/shard_map/ppermute | solution.py:475
  50.8 24.6 %all-to-all-done.1 = bf16[16,8,4096]{2,1,0:T(8,128)(2,1)S(1)} async-done(((bf16[16,8,4096]{2,1,0:T(8,128)(2,1)}), bf16[16,8,4096]{2,1,0:T(8,128)(2,1)S(1)}, u32[]{:S(2)}, u32[]{:S(2)}) %all-to-all-start.1) | async-done | bytes 1048608 | tf_op jit(solution)/shard_map/all_to_all | solution.py:489
  75.4 0.0 collective-permute-start.2
  75.4 0.0 collective-permute-done.low_ref
  75.4 0.0 copy-done
  75.4 14.6 %within.1 = bf16[256,8192]{1,0:T(8,128)(2,1)} custom-call(s32[1]{0:T(128)} %bitcast.1.half.core, bf16[256,8192]{1,0:T(8,128)(2,1)} %x_ref.1, bf16[256,1024]{1,0:T(8,128)(2,1)} %b_ref.1, bf16[256,1024]{1,0:T(8,128)(2,1)} %c.1, f32[256,128]{1,0:T(8,128)} %step_ref.1, f32[256,128]{1,0:T(8,128)S(1)} %get-tuple-element.18.run_ref.run, ...), custom_call_target="tpu_custom_call" | custom-call | tf_op jit(solution)/shard_map/within/pallas_call | solution.py:491
  90.0 3.8 %finish_own.1 = (bf16[256,8192]{1,0:T(8,128)(2,1)}, bf16[256,4096]{1,0:T(8,128)(2,1)S(1)}, bf16[256,512]{1,0:T(8,128)(2,1)S(1)}, bf16[128,4096]{1,0:T(8,128)(2,1)S(1)}) custom-call(s32[1]{0:T(128)} %bitcast.1.half.core, bf16[256,8192]{1,0:T(8,128)(2,1)} %within.1, bf16[256,1024]{1,0:T(8,128)(2,1)} %c.1, bf16[128,4096]{1,0:T(8,128)(2,1)S(1)} %bitcast.6, ...), custom_call_target="tpu_custom_call" | custom-call | tf_op jit(solution)/shard_map/finish_own/pallas_call | solution.py:521
  93.9 0.0 collective-permute-done.2.state
  93.9 2.3 %finish_other.1 = bf16[256,8192]{1,0:T(8,128)(2,1)} custom-call(s32[1]{0:T(128)} %bitcast.half, bf16[256,4096]{1,0:T(8,128)(2,1)S(1)} %get-tuple-element.27.within, bf16[256,512]{1,0:T(8,128)(2,1)S(1)} %get-tuple-element.28.c, bf16[128,4096]{1,0:T(8,128)(2,1)S(1)} %collective-permute-done.2.state, ...), custom_call_target="tpu_custom_call", output_to_operand_aliasing={{}: (7, {})} | custom-call | tf_op jit(solution)/shard_map/finish_other/pallas_call | solution.py:541
Async XLA Ops:
  2.9 3.4 %collective-permute-start.1 = (bf16[136,4096]{1,0:T(8,128)(2,1)S(1)}, bf16[136,4096]{1,0:T(8,128)(2,1)S(1)}, u32[]{:S(2)}, u32[]{:S(2)}) collective-permute-start(bf16[136,4096]{1,0:T(8,128)(2,1)S(1)} %get-tuple-element.22), channel_id=1, source_target_pairs={{0,1},{1,0},{2,3},{3,2},{4,5},{5,4},{6,7},{7,6},{8,9},{9,8},{10,11... | collective-permute-start | bytes 3342344 | tf_op jit(solution)/shard_map/ppermute | solution.py:448
  44.8 30.6 %copy-start = (f32[128]{0:T(128)S(1)}, f32[128]{0:T(128)}, u32[]{:S(2)}) copy-start(f32[128]{0:T(128)} %param.11) | copy-start | bytes 1540
  44.8 30.6 %all-to-all-start.1 = ((bf16[16,8,4096]{2,1,0:T(8,128)(2,1)}), bf16[16,8,4096]{2,1,0:T(8,128)(2,1)S(1)}, u32[]{:S(2)}, u32[]{:S(2)}) async-start(bf16[16,8,4096]{2,1,0:T(8,128)(2,1)} %get-tuple-element.25), calls=%async_computation.1 | async-start | bytes 2097152 | tf_op jit(solution)/shard_map/all_to_all | solution.py:489
  48.5 26.9 %collective-permute-start = (bf16[136,4096]{1,0:T(8,128)(2,1)S(1)}, bf16[136,4096]{1,0:T(8,128)(2,1)}, u32[]{:S(2)}, u32[]{:S(2)}) collective-permute-start(bf16[136,4096]{1,0:T(8,128)(2,1)S(1)} %own_state.1.own), channel_id=1, source_target_pairs={{0,1},{2,3},{4,5},{6,7},{8,9},{10,11},{12,13},{14,15},{16,17},{18,... | collective-permute-start | bytes 3342344 | tf_op jit(solution)/shard_map/ppermute | solution.py:475
  75.4 18.4 %collective-permute-start.2 = (bf16[128,4096]{1,0:T(8,128)(2,1)S(1)}, bf16[128,4096]{1,0:T(8,128)(2,1)S(1)}, u32[]{:S(2)}, u32[]{:S(2)}) collective-permute-start(bf16[128,4096]{1,0:T(8,128)(2,1)S(1)} %bitcast.5), channel_id=1, source_target_pairs={{0,1},{1,0},{2,3},{3,2},{4,5},{5,4},{6,7},{7,6},{8,9},{9,8},{10,11... | collective-permute-start | bytes 3145736 | tf_op jit(solution)/shard_map/ppermute | solution.py:518

commit v5 on v4

--- a/solution.py
+++ b/solution.py
@@ -14,6 +14,7 @@
 LANES = 128
 TILE = 256
 AHEAD = 2
+CHUNKS = 2
 ROW_TILE = 8
 HALF_ROWS = 128
 ROW_BLOCK = 16
@@ -185,7 +186,7 @@
     half_states(half[0], x_here, b_here, copies, factor, total, out, matrix, dims)
 
 
-def own_state_kernel(half, x, b, factor, total, out, x_here, b_here, matrix, sems, *, dims):
+def own_state_kernel(half, x, b, factor, total, out, matrix, x_here, b_here, sems, *, dims):
     copies = state_copies(half[0], x, b, x_here, b_here, sems, dims)
     for copy in copies:
         copy.start()
@@ -193,40 +194,145 @@
     half_states(half[0], x_here, b_here, copies, factor[...], total[...], out, matrix, dims)
 
 
-def chip_total_kernel(core, own, got, total, out, base_out):
-    first = core[0] == 0
-    cols = own.shape[1]
-    states = out.shape[0]
-    heads = total.shape[1]
-    half = heads // CORES
-    own_tail = own[states : states + 2, :].astype(F32)
-    got_tail = got[states : states + 2, :].astype(F32)
+def mixing_rows(first, own, got, states, cols):
+    own_tail = own[states : states + 2, cols].astype(F32)
+    got_tail = got[states : states + 2, cols].astype(F32)
     decay = jnp.where(first, got_tail, own_tail)
     decay = decay[:1, :] + decay[1:, :]
     one = jnp.ones_like(decay)
-    on_own = jnp.where(first, decay, one)
-    on_got = jnp.where(first, one, decay)
-    for row in range(0, states, ROW_BLOCK):
-        rows = slice(row, row + ROW_BLOCK)
-        out[rows, :cols] = (on_own * own[rows, :].astype(F32) + on_got * got[rows, :].astype(F32)).astype(BF16)
+    return jnp.where(first, decay, one), jnp.where(first, one, decay)
+
+
+def side_by_side(values, half):
+    high, low = high_low(values)
+    lane = lax.broadcasted_iota(jnp.int32, values.shape, 1)
+    return jnp.where(lane < half, high, pltpu.roll(low, half, 1))
+
+
+def chip_decay(first, got, total, states, base_out):
+    heads = total.shape[1]
+    half = heads // CORES
     partner = got[states + 2 : states + 3, :heads].astype(F32) + got[states + 3 : states + 4, :heads].astype(F32)
     partner = partner + got[states + 4 : states + 5, :heads].astype(F32)
     partner = jnp.broadcast_to(partner, total.shape)
     base_out[...] = jnp.where(first, jnp.zeros_like(partner), partner)
     both = jnp.exp2(total[...] + partner)
     both = jnp.where(first, both, pltpu.roll(both, half, 1))
-    high, low = high_low(both)
-    lane = lax.broadcasted_iota(jnp.int32, both.shape, 1)
-    packed = jnp.where(lane < half, high, pltpu.roll(low, half, 1))
-    out[:, cols:] = jnp.concatenate([packed] * (states // packed.shape[0]), axis=0).astype(BF16)
-
-
-def prefix_kernel(sent, out, ready, here, sems, *, width, blocks):
+    return side_by_side(both, half)
+
+
+def chip_total_kernel(at, own, got, total, out, base_out):
+    first = at[0] == 0
+    cols = own.shape[1]
+    states = out.shape[0]
+    on_own, on_got = mixing_rows(first, own, got, states, slice(0, cols))
+    for row in range(0, states, ROW_BLOCK):
+        rows = slice(row, row + ROW_BLOCK)
+        out[rows, :cols] = (on_own * own[rows, :].astype(F32) + on_got * got[rows, :].astype(F32)).astype(BF16)
+    packed_decay = chip_decay(first, got, total, states, base_out)
+    out[:, cols:] = jnp.concatenate([packed_decay] * (states // ROW_TILE), axis=0).astype(BF16)
+
+
+def pieces_kernel(at, own, got, total, *outs, states, chunk):
+    base_out = outs[-1]
+    first = at[0] == 0
+    rows, cols = outs[0].shape
+    cols = cols - total.shape[1]
+    here = slice(chunk * cols, (chunk + 1) * cols)
+    on_own, on_got = mixing_rows(first, own, got, states, here)
+    packed_decay = chip_decay(first, got, total, states, base_out)
+    for k, out in enumerate(outs[:-1]):
+        start = pl.multiple_of(jnp.bitwise_xor(at[1], k) * rows, rows)
+        for row in range(0, rows, ROW_BLOCK):
+            take = pl.ds(start + row, ROW_BLOCK)
+            mixed = on_own * own[take, here].astype(F32) + on_got * got[take, here].astype(F32)
+            out[row : row + ROW_BLOCK, :cols] = mixed.astype(BF16)
+        out[:, cols:] = jnp.concatenate([packed_decay] * (rows // ROW_TILE), axis=0).astype(BF16)
+
+
+def decays_of(pieces, cols, first_head, width):
+    lanes = pieces[0].shape[1] - cols
+    sent = [piece[:ROW_TILE, cols:].astype(F32)[:1, :] for piece in pieces]
+    sent = jnp.concatenate(sent + [jnp.zeros((ROW_TILE - len(sent), lanes), F32)], axis=0)
+    values = sent + pltpu.roll(sent, lanes // CORES, 1)
+    heads = cols // width
+    here = pltpu.roll(values, lanes - first_head, 1) if first_head else values
+    return values, dot(packed(here, heads), spreader(heads, width))
+
+
+def column_kernel(at, *refs, first_head, width, count, parts):
+    pieces, outs, decay_out, total = refs[:count], refs[count : count + parts], refs[-2], refs[-1]
+    rows, cols = total.shape
+    values, decay = decays_of(pieces, cols, first_head, width)
+    decay_out[...] = decay
+    for place in range(count):
+
+        @pl.when(at[1] == place)
+        def _():
+            state = jnp.zeros((rows, cols), F32)
+            for k in range(count):
+                k = k ^ place
+                state = decay[k : k + 1, :] * state + pieces[k][:, :cols].astype(F32)
+            total[...] = state
+
+    product = values[:1, :]
+    for k in range(1, count):
+        product = product * values[k : k + 1, :]
+    product = side_by_side(jnp.broadcast_to(product, (ROW_TILE, product.shape[1])), product.shape[1] // CORES)
+    part = rows // parts
+    for k, out in enumerate(outs):
+        start = pl.multiple_of(jnp.bitwise_xor(at[2], k) * part, part)
+        out[:, :cols] = total[pl.ds(start, part), :].astype(BF16)
+        out[:, cols:] = jnp.concatenate([product] * (part // ROW_TILE), axis=0).astype(BF16)
+
+
+def outer_kernel(at, *refs, first_head, width, count):
+    pieces, outs = refs[:count], refs[count:]
+    rows, cols = outs[0].shape
+    _, decay = decays_of(pieces, cols, first_head, width)
+    for place in range(count):
+
+        @pl.when(at[2] == place)
+        def _():
+            state = jnp.zeros((rows, cols), F32)
+            for k in range(count):
+                k = k ^ place
+                outs[k][...] = state.astype(BF16)
+                state = decay[k : k + 1, :] * state + pieces[k][:, :cols].astype(F32)
+
+
+def chips_kernel(at, *refs, count, parts):
+    pieces, decay, carries = refs[:count], refs[count], refs[count + 1 : count + 1 + parts]
+    outs, carry = refs[count + 1 + parts : -1], refs[-1]
+    rows, cols = carry.shape
+    part = rows // parts
+    for k, piece in enumerate(carries):
+        start = pl.multiple_of(jnp.bitwise_xor(at[2], k) * part, part)
+        carry[pl.ds(start, part), :] = piece[...].astype(F32)
+    for place in range(count):
+
+        @pl.when(at[1] == place)
+        def _():
+            state = carry[...]
+            for k in range(count):
+                k = k ^ place
+                outs[k][...] = state.astype(BF16)
+                state = decay[k : k + 1, :] * state + pieces[k][:, :cols].astype(F32)
+
+
+def assemble_kernel(at, *refs, count):
+    out = refs[-1]
+    for n, piece in enumerate(refs[:-1]):
+        rows, cols = piece.shape
+        start = pl.multiple_of(jnp.bitwise_xor(at[1], n % count) * rows, rows)
+        out[pl.ds(start, rows), n // count * cols : (n // count + 1) * cols] = piece[...]
+
+
+def prefix_kernel(sent, out, here, sems, *, width, blocks):
     chips, rows, cols = here.shape
-    heads = ready.shape[1]
+    heads = sent.shape[2] - cols
     half = heads // CORES
     step = cols // blocks
-    ready[...] = jnp.zeros_like(ready)
     first_rows = jnp.concatenate([sent[k, :1, cols:].astype(F32) for k in range(chips)], axis=0)
     values = first_rows + pltpu.roll(first_rows, half, 1)
     matrix = spreader(step // width, width)
@@ -250,16 +356,16 @@
 
 
 def within_kernel(
-    core, x_ref, b_ref, c_ref, step_ref, run_ref, run_t_ref, skip_ref, low_ref, high_ref, ready, out, matrix, *, dims
+    at, x_ref, b_ref, c_ref, step_ref, run_ref, run_t_ref, skip_ref, before_ref, out, matrix, *, dims
 ):
-    del ready
     per_half, per_group, width = dims
-    group = pl.program_id(0)
+    turn = pl.program_id(0)
+    group = at[0] * per_half + turn
     head = group * per_group
     rows = x_ref.shape[0]
     pair = LANES // width
 
-    @pl.when(group == 0)
+    @pl.when(turn == 0)
     def _():
         matrix[...] = spreader(per_group, width)
 
@@ -272,8 +378,7 @@
     run_t = run_t_ref[pl.ds(pl.multiple_of(head, per_group), per_group), :]
     x = x_ref[...].astype(F32)
     scaled = (x * spread(step)).astype(BF16)
-    upper = high_ref[...] * core[0].astype(BF16)
-    before = dot(c_ref[...], jnp.where(group < per_half, low_ref[...], upper))
+    before = dot(c_ref[...], before_ref[...] * at[1].astype(BF16))
     outer = spread(skip)[:1, :] * x + spread(jnp.exp2(run)) * before
     lane = lax.broadcasted_iota(jnp.int32, (HALF_ROWS, LANES), 1) // width
     lower = lax.broadcasted_iota(jnp.int32, (HALF_ROWS, HALF_ROWS), 1) <= lax.broadcasted_iota(
@@ -334,59 +439,130 @@
         copy.wait()
 
 
-def first_final_kernel(
-    half, within, c, state, run, base, out, other_within, other_c, matrix, here, c_here, result, loads, stores, *, dims
-):
+def final_kernel(half, within, c, state, run, base, matrix, filled, out, result, stores, *, dims):
+    del filled
     per_half, group_cols, states = dims
-    half_cols = per_half * group_cols
-    half_rows = per_half * states
-    mine = half[0]
-    other = 1 - mine
-    copies = []
-    for k in range(per_half):
-        home = pl.multiple_of((mine * per_half + k) * group_cols, group_cols)
-        copies.append(
-            pltpu.make_async_copy(
-                within.at[:, pl.ds(home, group_cols)], here.at[:, pl.ds(k * group_cols, group_cols)], loads.at[k]
-            )
-        )
-    home = pl.multiple_of(mine * half_rows, half_rows)
-    copies.append(pltpu.make_async_copy(c.at[:, pl.ds(home, half_rows)], c_here, loads.at[per_half]))
-    home = pl.multiple_of(other * half_rows, half_rows)
-    copies.append(pltpu.make_async_copy(c.at[:, pl.ds(home, half_rows)], other_c, loads.at[per_half + 1]))
-    home = pl.multiple_of(other * half_cols, half_cols)
-    copies.append(pltpu.make_async_copy(within.at[:, pl.ds(home, half_cols)], other_within, loads.at[per_half + 2]))
-    for copy in [copies[per_half]] + copies[:per_half] + copies[per_half + 1 :]:
-        copy.start()
-    half_spreader(matrix, out.shape[1] // run.shape[1])
-    copies[per_half].wait()
-
-    def part(k):
-        copies[k].wait()
-        return here[:, k * group_cols : (k + 1) * group_cols]
-
-    def rows_c(k):
-        return c_here[:, k * states : (k + 1) * states]
-
-    add_carried(mine, part, rows_c, state, run, base, out, result, matrix, stores, dims)
-    for copy in copies[per_half + 1 :]:
-        copy.wait()
-
-
-def second_final_kernel(half, within, c, state, run, base, matrix, filled, out, result, stores, *, dims):
-    del filled
-    _, group_cols, states = dims
 
     def part(k):
         return within[:, k * group_cols : (k + 1) * group_cols]
 
     def rows_c(k):
-        return c[:, k * states : (k + 1) * states]
+        return c[:, pl.ds(pl.multiple_of((half[0] * per_half + k) * states, states), states)]
 
     add_carried(half[0], part, rows_c, state, run, base, out, result, matrix, stores, dims)
 
 
-def local(inputs, step_size, log_decay, b_matrix, c_matrix, skip_gain, *, chip_axes, core_axis):
+def first_final_kernel(half, within, c, state, run, base, matrix, out, result, stores, *, dims):
+    final_kernel(half, within, c, state, run, base, matrix, None, out, result, stores, dims=dims)
+
+
+def small_call(kernel, in_specs, out_shape, scratch=(), out_specs=None):
+    return pl.pallas_call(
+        kernel,
+        in_specs=in_specs,
+        out_specs=out_specs or [pl.BlockSpec(memory_space=pltpu.VMEM)] * len(out_shape),
+        out_shape=out_shape,
+        scratch_shapes=list(scratch),
+        compiler_params=plain_params(),
+    )
+
+
+def xor_route(size, k):
+    return [(i, i ^ k) for i in range(size)]
+
+
+def swapped(arrays, axis):
+    size = lax.axis_size(axis)
+    order = sorted(range(1, size), key=lambda k: -(k.bit_length()))
+    done = {0: arrays[0]}
+    for k in order:
+        done[k] = lax.ppermute(arrays[k], axis, xor_route(size, k))
+    return [done[k] for k in range(size)]
+
+
+def entering_by_swaps(at, own, got, total, width, states, outer_axis, chip_axis):
+    half_cols = own.shape[1]
+    heads = total.shape[1]
+    count = lax.axis_size(chip_axis)
+    parts = lax.axis_size(outer_axis)
+    rows = states // count
+    part = rows // parts
+    cols = half_cols // CHUNKS
+    smem = pl.BlockSpec(memory_space=pltpu.SMEM)
+    vmem = pl.BlockSpec(memory_space=pltpu.VMEM)
+    shape = jax.ShapeDtypeStruct
+    gathered = []
+    for chunk in range(CHUNKS):
+        *pieces, base = small_call(
+            functools.partial(pieces_kernel, states=states, chunk=chunk),
+            [smem] + [vmem] * 3,
+            [shape((rows, cols + heads), BF16)] * count + [shape((ROW_TILE, heads), F32)],
+        )(at, own, got, total)
+        gathered.append(swapped(pieces, chip_axis))
+    entering = []
+    for chunk in range(CHUNKS):
+        first_head = chunk * cols // width
+        pieces = gathered[chunk]
+        *totals, decay = small_call(
+            functools.partial(column_kernel, first_head=first_head, width=width, count=count, parts=parts),
+            [smem] + [vmem] * count,
+            [shape((part, cols + heads), BF16)] * parts + [shape((ROW_TILE, cols), F32)],
+            [pltpu.VMEM((rows, cols), F32)],
+        )(at, *pieces)
+        totals = swapped(totals, outer_axis)
+        carries = small_call(
+            functools.partial(outer_kernel, first_head=first_head, width=width, count=parts),
+            [smem] + [vmem] * parts,
+            [shape((part, cols), BF16)] * parts,
+        )(at, *totals)
+        carries = swapped(carries, outer_axis)
+        states_out = small_call(
+            functools.partial(chips_kernel, count=count, parts=parts),
+            [smem] + [vmem] * (count + 1 + parts),
+            [shape((rows, cols), BF16)] * count,
+            [pltpu.VMEM((rows, cols), F32)],
+        )(at, *pieces, decay, *carries)
+        entering += swapped(states_out, chip_axis)
+    (entering,) = small_call(
+        functools.partial(assemble_kernel, count=count),
+        [smem] + [vmem] * len(entering),
+        [shape((states, half_cols), BF16)],
+    )(at, *entering)
+    return entering, base
+
+
+def entering_by_all_to_all(at, own, got, total, width, states, outer_axis, chip_axis):
+    half_cols = own.shape[1]
+    heads = total.shape[1]
+    chips = lax.axis_size((outer_axis, chip_axis))
+    rows = states // chips
+    smem = pl.BlockSpec(memory_space=pltpu.SMEM)
+    vmem = pl.BlockSpec(memory_space=pltpu.VMEM)
+    chip_total, base = small_call(
+        chip_total_kernel,
+        [smem] + [vmem] * 3,
+        [jax.ShapeDtypeStruct((states, half_cols + heads), BF16), jax.ShapeDtypeStruct((ROW_TILE, heads), F32)],
+    )(at, own, got, total)
+    sent = lax.all_to_all(
+        chip_total.reshape(chips, rows, half_cols + heads),
+        (outer_axis, chip_axis),
+        split_axis=0,
+        concat_axis=0,
+        tiled=True,
+    )
+    blocks = GROUPS // CORES
+    (entering,) = small_call(
+        functools.partial(prefix_kernel, width=width, blocks=blocks),
+        [vmem],
+        [pltpu.HBM((chips, rows, half_cols), BF16)],
+        [pltpu.VMEM((chips, rows, half_cols), BF16), pltpu.SemaphoreType.DMA((blocks,))],
+        [pl.BlockSpec(memory_space=pltpu.HBM)],
+    )(sent)
+    entering = lax.all_to_all(entering, (outer_axis, chip_axis), split_axis=0, concat_axis=0, tiled=True)
+    return entering.reshape(states, half_cols), base
+
+
+def local(inputs, step_size, log_decay, b_matrix, c_matrix, skip_gain, *, outer_axis, chip_axis, core_axis):
     tokens, channels = inputs.shape
     heads = step_size.shape[1]
     width = channels // heads
@@ -395,36 +571,34 @@
     group_cols = per_group * width
     per_half = GROUPS // CORES
     half_cols = channels // CORES
-    chips = lax.axis_size(chip_axes)
-    rows = states // chips
+    chips = lax.axis_size((outer_axis, chip_axis))
+    by_swaps = chips & (chips - 1) == 0 and states % (chips * ROW_TILE) == 0
     tall = states + ROW_TILE
 
     core = lax.axis_index(core_axis).astype(jnp.int32)
     mine = core.reshape(1)
     other = (1 - core).reshape(1)
+    at = jnp.stack([core, lax.axis_index(chip_axis).astype(jnp.int32), lax.axis_index(outer_axis).astype(jnp.int32)])
 
     smem = pl.BlockSpec(memory_space=pltpu.SMEM)
     vmem = pl.BlockSpec(memory_space=pltpu.VMEM)
     hbm = pl.BlockSpec(memory_space=pltpu.HBM)
-    anywhere = pl.BlockSpec(memory_space=pl.ANY)
 
     def whole(shape):
         return pl.BlockSpec(shape, lambda i, *_: (0,) * len(shape))
 
     def by_group(cols):
-        return pl.BlockSpec((tokens, cols), lambda i, *_: (0, i))
+        return pl.BlockSpec((tokens, cols), lambda i, at: (0, at[0] * per_half + i))
 
     state_dims = (per_half, group_cols, states)
     half_dims = (per_half, per_group, width)
     half_scratch = [
         pltpu.VMEM((tokens, half_cols), BF16),
         pltpu.VMEM((tokens, per_half * states), BF16),
-        pltpu.VMEM((heads, half_cols), BF16),
     ]
 
-    inputs, step_size, log_decay, b_matrix, c_matrix = (
-        pltpu.with_memory_space_constraint(array, pltpu.HBM)
-        for array in (inputs, step_size, log_decay, b_matrix, c_matrix)
+    inputs, step_size, log_decay, b_matrix = (
+        pltpu.with_memory_space_constraint(array, pltpu.HBM) for array in (inputs, step_size, log_decay, b_matrix)
     )
     send, run, run_t, factor, total = pl.pallas_call(
         functools.partial(send_state_kernel, dims=state_dims),
@@ -438,6 +612,7 @@
             jax.ShapeDtypeStruct((ROW_TILE, heads), F32),
         ],
         scratch_shapes=half_scratch
+        + [pltpu.VMEM((heads, half_cols), BF16)]
         + [pltpu.VMEM((tokens, heads), F32)] * 2
         + [pltpu.SemaphoreType.DMA((2 * per_half + 2,))],
         compiler_params=plain_params(),
@@ -447,107 +622,70 @@
     swap = [(0, 1), (1, 0)]
     got = lax.ppermute(send, core_axis, swap)
 
-    own = pl.pallas_call(
+    own, matrix = small_call(
         functools.partial(own_state_kernel, dims=state_dims),
-        in_specs=[smem, hbm, hbm, vmem, vmem],
-        out_specs=vmem,
-        out_shape=jax.ShapeDtypeStruct((tall, half_cols), BF16),
-        scratch_shapes=half_scratch + [pltpu.SemaphoreType.DMA((2 * per_half,))],
-        compiler_params=plain_params(),
-        name="own_state",
+        [smem, hbm, hbm, vmem, vmem],
+        [jax.ShapeDtypeStruct((tall, half_cols), BF16), jax.ShapeDtypeStruct((heads, half_cols), BF16)],
+        half_scratch + [pltpu.SemaphoreType.DMA((2 * per_half,))],
     )(mine, inputs, b_matrix, factor, total)
 
-    chip_total, base = pl.pallas_call(
-        chip_total_kernel,
-        in_specs=[smem, vmem, vmem, vmem],
-        out_specs=[vmem, vmem],
-        out_shape=[
-            jax.ShapeDtypeStruct((states, half_cols + heads), BF16),
-            jax.ShapeDtypeStruct((ROW_TILE, heads), F32),
-        ],
-        compiler_params=plain_params(),
-        name="chip_total",
-    )(mine, own, got, total)
-
-    sent = lax.all_to_all(
-        chip_total.reshape(chips, rows, half_cols + heads), chip_axes, split_axis=0, concat_axis=0, tiled=True
-    )
+    find_entering = entering_by_swaps if by_swaps else entering_by_all_to_all
+    entering, base = find_entering(at, own, got, total, width, states, outer_axis, chip_axis)
     late = lax.ppermute(own, core_axis, swap[:1])
 
-    entering, ready = pl.pallas_call(
-        functools.partial(prefix_kernel, width=width, blocks=per_half),
-        in_specs=[vmem],
-        out_specs=[hbm, vmem],
-        out_shape=[
-            pltpu.HBM((chips, rows, half_cols), BF16),
-            jax.ShapeDtypeStruct((ROW_TILE, heads), F32),
-        ],
-        scratch_shapes=[pltpu.VMEM((chips, rows, half_cols), BF16), pltpu.SemaphoreType.DMA((per_half,))],
-        compiler_params=plain_params(),
-        name="prefix",
-    )(sent)
-    entering = lax.all_to_all(entering, chip_axes, split_axis=0, concat_axis=0, tiled=True)
-
-    within = pl.pallas_call(
-        functools.partial(within_kernel, dims=half_dims),
-        grid_spec=pltpu.PrefetchScalarGridSpec(
-            num_scalar_prefetch=1,
-            grid=(GROUPS,),
-            in_specs=[
-                by_group(group_cols),
-                by_group(states),
-                by_group(states),
-                whole((tokens, heads)),
-                whole((tokens, heads)),
-                whole((heads, tokens)),
-                whole((1, heads)),
-                pl.BlockSpec((states, group_cols), lambda i, _: (0, jnp.minimum(i, per_half - 1))),
-                pl.BlockSpec((states, group_cols), lambda i, _: (0, jnp.maximum(i - per_half, 0))),
-                anywhere,
-            ],
-            out_specs=by_group(group_cols),
-            scratch_shapes=[pltpu.VMEM((2 * per_group, group_cols), BF16)],
-        ),
-        out_shape=pltpu.HBM((tokens, channels), BF16),
-        compiler_params=params(),
-        name="within",
-    )(mine, inputs, b_matrix, c_matrix, step_size, run, run_t, skip_gain.reshape(1, heads), late, got, ready)
-
-    within = pltpu.with_memory_space_constraint(within, pltpu.HBM)
-    entering = entering.reshape(states, half_cols)
+    def within(half, before):
+        return pl.pallas_call(
+            functools.partial(within_kernel, dims=half_dims),
+            grid_spec=pltpu.PrefetchScalarGridSpec(
+                num_scalar_prefetch=1,
+                grid=(per_half,),
+                in_specs=[
+                    by_group(group_cols),
+                    by_group(states),
+                    by_group(states),
+                    whole((tokens, heads)),
+                    whole((tokens, heads)),
+                    whole((heads, tokens)),
+                    whole((1, heads)),
+                    pl.BlockSpec((states, group_cols), lambda i, at: (0, i)),
+                ],
+                out_specs=pl.BlockSpec((tokens, group_cols), lambda i, at: (0, i)),
+                scratch_shapes=[pltpu.VMEM((2 * per_group, group_cols), BF16)],
+            ),
+            out_shape=jax.ShapeDtypeStruct((tokens, half_cols), BF16),
+            compiler_params=params(),
+            name="within",
+        )(
+            jnp.concatenate([half, mine]),
+            inputs,
+            b_matrix,
+            c_matrix,
+            step_size,
+            run,
+            run_t,
+            skip_gain.reshape(1, heads),
+            before,
+        )
+
+    own_within = within(mine, got)
+    other_within = within(other, late)
+
     got_entering = lax.ppermute(entering, core_axis, swap)
-
     mixed = jax.ShapeDtypeStruct((tokens, channels), BF16)
-    result, other_within, other_c, matrix = pl.pallas_call(
-        functools.partial(first_final_kernel, dims=state_dims),
-        in_specs=[smem, hbm, hbm, vmem, vmem, vmem],
-        out_specs=[hbm, vmem, vmem, vmem],
-        out_shape=[
-            mixed,
-            jax.ShapeDtypeStruct((tokens, half_cols), BF16),
-            jax.ShapeDtypeStruct((tokens, per_half * states), BF16),
-            jax.ShapeDtypeStruct((heads, half_cols), BF16),
-        ],
-        scratch_shapes=[
-            pltpu.VMEM((tokens, half_cols), BF16),
-            pltpu.VMEM((tokens, per_half * states), BF16),
-            pltpu.VMEM((tokens, half_cols), BF16),
-            pltpu.SemaphoreType.DMA((per_half + 3,)),
-            pltpu.SemaphoreType.DMA((per_half,)),
-        ],
-        compiler_params=plain_params(),
-        name="finish_own",
-    )(mine, within, c_matrix, entering, run, base)
+    final_scratch = [pltpu.VMEM((tokens, half_cols), BF16), pltpu.SemaphoreType.DMA((per_half,))]
+    (result,) = small_call(
+        functools.partial(first_final_kernel, dims=state_dims), [smem] + [vmem] * 6, [mixed], final_scratch, [hbm]
+    )(mine, own_within, c_matrix, entering, run, base, matrix)
     return pl.pallas_call(
-        functools.partial(second_final_kernel, dims=state_dims),
+        functools.partial(final_kernel, dims=state_dims),
         in_specs=[smem] + [vmem] * 6 + [hbm],
         out_specs=hbm,
         out_shape=mixed,
-        scratch_shapes=[pltpu.VMEM((tokens, half_cols), BF16), pltpu.SemaphoreType.DMA((per_half,))],
+        scratch_shapes=final_scratch,
         input_output_aliases={7: 0},
         compiler_params=plain_params(),
         name="finish_other",
-    )(other, other_within, other_c, got_entering, run, base, matrix, result)
+    )(other, other_within, c_matrix, got_entering, run, base, matrix, result)
 
 
 def solution(mesh):
@@ -558,6 +696,6 @@
     placed = P((outer, "chip", "core"), None)
 
     def body(*args):
-        return local(*args, chip_axes=(outer, "chip"), core_axis="core")
+        return local(*args, outer_axis=outer, chip_axis="chip", core_axis="core")
 
     return jax.shard_map(body, mesh=chip_mesh, in_specs=(placed,) * 5 + (P(),), out_specs=placed, check_vma=False)

time: 96.5 us -> 96.6 us (level)
  blocking collectives: 36.5 us -> 0 us
  starting transfers between devices: 6.52 us -> 39 us
  Pallas kernels: 28.4 us -> 34.6 us
  waiting for transfers between devices: 24.7 us -> 22.3 us
    ppermute x0 -> x24, starting transfers between devices: none -> 36.8 us  [swapped(): done[k] = lax.ppermute(arrays[k], axis, xor_route(size, k))]
    all_to_all x1 -> x0, blocking collectives: 36.5 us -> none  [local(): lax.all_to_all(chip_total.reshape(chips, rows, half_cols + heads), chip_a...]
    all_to_all x1 -> x0, waiting for transfers between devices: 24.6 us -> none  [local(): lax.all_to_all(entering, chip_axes, split_axis=0, concat_axis=0, tiled=True)]
    ppermute x0 -> x24, waiting for transfers between devices: none -> 22.3 us  [swapped(): done[k] = lax.ppermute(arrays[k], axis, xor_route(size, k))]
    pallas_call x6 -> x14, Pallas kernels: 25.5 us -> 31.6 us  [the longest x2 16.1 us: within(): pl.pallas_call(functools.partial(within_kernel, dims=half_dims), grid_spe...]
    all_to_all x1 -> x0, starting transfers between devices: 3.67 us -> none  [local(): lax.all_to_all(entering, chip_axes, split_axis=0, concat_axis=0, tiled=True)]
  transfers between devices with their start and end apart: 4 -> 27, of which waited for: 1 -> 8; matrix products, arithmetic and copies ran while one was open for 0% -> 0% of each run, Pallas kernels for 22% -> 28%
where the time goes in v5:
time: 96.6 us; the launch traced here: 96.4 us
  starting transfers between devices  39 us (40%)
  Pallas kernels  34.6 us (36%)
  waiting for transfers between devices  22.3 us (23%)
    ppermute x24, starting transfers between devices, swapped(): done[k] = lax.ppermute(arrays[k], axis, xor_route(size, k))  36.8 us
    ppermute x24, waiting for transfers between devices, swapped(): done[k] = lax.ppermute(arrays[k], axis, xor_route(size, k))  22.3 us
    pallas_call x2, Pallas kernels, within(): pl.pallas_call(functools.partial(within_kernel, dims=half_dims), grid_spe...  16.1 us
    pallas_call x1, Pallas kernels, local(): pl.pallas_call(functools.partial(send_state_kernel, dims=state_dims), in_...  2.94 us
    pallas_call x1, Pallas kernels, local(): small_call(functools.partial(own_state_kernel, dims=state_dims), [smem, h...  2.88 us
    pallas_call x1, Pallas kernels, local(): small_call(functools.partial(first_final_kernel, dims=state_dims), [smem]...  2.29 us
    pallas_call x1, Pallas kernels, local(): pl.pallas_call(functools.partial(final_kernel, dims=state_dims), in_specs...  2.28 us
    pallas_call x2, Pallas kernels, entering_by_swaps(): small_call(functools.partial(column_kernel, first_head=first_head, width=...  2.17 us
  transfers between devices with their start and end apart: 27, of which 8 were waited for; matrix products, arithmetic and copies ran while one was open for 0% of the time, Pallas kernels for 28%

profile of v5, /device:TPU:0, one launch (start us, length us, event | category | flops | bytes accessed | tf_op | source)
XLA Modules:
  0.0 96.4 jit_solution(14741441374752273760)
XLA Ops:
  0.0 2.9 %send_state.1 = (bf16[136,4096]{1,0:T(8,128)(2,1)S(1)}, f32[256,128]{1,0:T(8,128)S(1)}, f32[128,256]{1,0:T(8,128)S(1)}, f32[256,128]{1,0:T(8,128)S(1)}, f32[8,128]{1,0:T(8,128)S(1)}) custom-call(s32[1]{0:T(128)} %bitcast.half, bf16[256,8192]{1,0:T(8,128)(2,1)} %x_ref.3, bf16[256,1024]{1,0:T(8,128)(2,1)} %b_ref.3, f32[256,128]{1,0:T(8,128)} %step_ref.3, ...), custom_call_target="tpu_custom_call" | custom-call | tf_op jit(solution)/shard_map/send_state/pallas_call | solution.py:603
  3.5 2.9 %shard_map.64 = (bf16[136,4096]{1,0:T(8,128)(2,1)S(1)}, bf16[128,4096]{1,0:T(8,128)(2,1)S(1)}) custom-call(s32[1]{0:T(128)} %bitcast.1.half, bf16[256,8192]{1,0:T(8,128)(2,1)} %x_ref.3, bf16[256,1024]{1,0:T(8,128)(2,1)} %b_ref.3, f32[256,128]{1,0:T(8,128)S(1)} %get-tuple-element.49.factor, f32[8,128]{1,0:T(8,128)S(1)} %get-tuple-element.50.total), custom_call_target="tpu_custom_call" | custom-call | tf_op jit(solution)/shard_map/pallas_call | solution.py:625
  7.3 2.6 %collective-permute-start.14 = (bf16[32,2176]{1,0:T(8,128)(2,1)S(1)}, bf16[32,2176]{1,0:T(8,128)(2,1)S(1)}, u32[]{:S(2)}, u32[]{:S(2)}) collective-permute-start(bf16[32,2176]{1,0:T(8,128)(2,1)S(1)} %get-tuple-element.71), channel_id=1, source_target_pairs={{0,2},{2,0},{4,6},{6,4},{1,3},{3,1},{5,7},{7,5},{8,10},{10,8},{12,... | collective-permute-start | bytes 417800 | tf_op jit(solution)/shard_map/ppermute | solution.py:479
  10.0 2.6 %collective-permute-start.15 = (bf16[32,2176]{1,0:T(8,128)(2,1)S(1)}, bf16[32,2176]{1,0:T(8,128)(2,1)S(1)}, u32[]{:S(2)}, u32[]{:S(2)}) collective-permute-start(bf16[32,2176]{1,0:T(8,128)(2,1)S(1)} %get-tuple-element.72), channel_id=1, source_target_pairs={{0,4},{2,6},{4,0},{6,2},{1,5},{3,7},{5,1},{7,3},{8,12},{10,14},{12... | collective-permute-start | bytes 417800 | tf_op jit(solution)/shard_map/ppermute | solution.py:479
  12.5 4.2 %collective-permute-done.14.refs_1_ = bf16[32,2176]{1,0:T(8,128)(2,1)S(1)} collective-permute-done((bf16[32,2176]{1,0:T(8,128)(2,1)S(1)}, bf16[32,2176]{1,0:T(8,128)(2,1)S(1)}, u32[]{:S(2)}, u32[]{:S(2)}) %collective-permute-start.14) | collective-permute-done | bytes 139296 | tf_op jit(solution)/shard_map/ppermute | solution.py:479
  16.7 6.7 %collective-permute-done.15.refs_2_ = bf16[32,2176]{1,0:T(8,128)(2,1)S(1)} collective-permute-done((bf16[32,2176]{1,0:T(8,128)(2,1)S(1)}, bf16[32,2176]{1,0:T(8,128)(2,1)S(1)}, u32[]{:S(2)}, u32[]{:S(2)}) %collective-permute-start.15) | collective-permute-done | bytes 139296 | tf_op jit(solution)/shard_map/ppermute | solution.py:479
  26.0 1.5 %collective-permute-start.18 = (bf16[8,2176]{1,0:T(8,128)(2,1)S(1)}, bf16[8,2176]{1,0:T(8,128)(2,1)S(1)}, u32[]{:S(2)}, u32[]{:S(2)}) collective-permute-start(bf16[8,2176]{1,0:T(8,128)(2,1)S(1)} %get-tuple-element.77), channel_id=1, source_target_pairs={{0,16},{8,24},{16,0},{24,8},{1,17},{9,25},{17,1},{25,9},{2,18},{10... | collective-permute-start | bytes 104456 | tf_op jit(solution)/shard_map/ppermute | solution.py:479
  29.3 2.8 %collective-permute-start.2 = (bf16[32,2176]{1,0:T(8,128)(2,1)S(1)}, bf16[32,2176]{1,0:T(8,128)(2,1)S(1)}, u32[]{:S(2)}, u32[]{:S(2)}) collective-permute-start(bf16[32,2176]{1,0:T(8,128)(2,1)S(1)} %get-tuple-element.54), channel_id=1, source_target_pairs={{0,2},{2,0},{4,6},{6,4},{1,3},{3,1},{5,7},{7,5},{8,10},{10,8},{12,... | collective-permute-start | bytes 417800 | tf_op jit(solution)/shard_map/ppermute | solution.py:479
  35.5 1.6 %collective-permute-start.20 = (bf16[8,2048]{1,0:T(8,128)(2,1)S(1)}, bf16[8,2048]{1,0:T(8,128)(2,1)S(1)}, u32[]{:S(2)}, u32[]{:S(2)}) collective-permute-start(bf16[8,2048]{1,0:T(8,128)(2,1)S(1)} %get-tuple-element.80), channel_id=1, source_target_pairs={{0,8},{8,0},{16,24},{24,16},{1,9},{9,1},{17,25},{25,17},{2,10},{10... | collective-permute-start | bytes 98312 | tf_op jit(solution)/shard_map/ppermute | solution.py:479
  39.4 2.8 %collective-permute-start.22 = (bf16[8,2048]{1,0:T(8,128)(2,1)S(1)}, bf16[8,2048]{1,0:T(8,128)(2,1)S(1)}, u32[]{:S(2)}, u32[]{:S(2)}) collective-permute-start(bf16[8,2048]{1,0:T(8,128)(2,1)S(1)} %get-tuple-element.82), channel_id=1, source_target_pairs={{0,24},{8,16},{16,8},{24,0},{1,25},{9,17},{17,9},{25,1},{2,26},{10... | collective-permute-start | bytes 98312 | tf_op jit(solution)/shard_map/ppermute | solution.py:479
  42.2 2.0 %collective-permute-done.22.refs_8_ = bf16[8,2048]{1,0:T(8,128)(2,1)S(1)} collective-permute-done((bf16[8,2048]{1,0:T(8,128)(2,1)S(1)}, bf16[8,2048]{1,0:T(8,128)(2,1)S(1)}, u32[]{:S(2)}, u32[]{:S(2)}) %collective-permute-start.22) | collective-permute-done | bytes 32800 | tf_op jit(solution)/shard_map/ppermute | solution.py:479
  48.6 1.6 %collective-permute-start.6 = (bf16[8,2176]{1,0:T(8,128)(2,1)S(1)}, bf16[8,2176]{1,0:T(8,128)(2,1)S(1)}, u32[]{:S(2)}, u32[]{:S(2)}) collective-permute-start(bf16[8,2176]{1,0:T(8,128)(2,1)S(1)} %get-tuple-element.60), channel_id=1, source_target_pairs={{0,16},{8,24},{16,0},{24,8},{1,17},{9,25},{17,1},{25,9},{2,18},{10... | collective-permute-start | bytes 104456 | tf_op jit(solution)/shard_map/ppermute | solution.py:479
  50.6 1.9 %collective-permute-start.24 = (bf16[32,2048]{1,0:T(8,128)(2,1)S(1)}, bf16[32,2048]{1,0:T(8,128)(2,1)S(1)}, u32[]{:S(2)}, u32[]{:S(2)}) collective-permute-start(bf16[32,2048]{1,0:T(8,128)(2,1)S(1)} %get-tuple-element.85), channel_id=1, source_target_pairs={{0,4},{2,6},{4,0},{6,2},{1,5},{3,7},{5,1},{7,3},{8,12},{10,14},{12... | collective-permute-start | bytes 393224 | tf_op jit(solution)/shard_map/ppermute | solution.py:479
  52.6 2.6 %collective-permute-done.7.refs_3_ = bf16[8,2176]{1,0:T(8,128)(2,1)S(1)} collective-permute-done((bf16[8,2176]{1,0:T(8,128)(2,1)S(1)}, bf16[8,2176]{1,0:T(8,128)(2,1)S(1)}, u32[]{:S(2)}, u32[]{:S(2)}) %collective-permute-start.7) | collective-permute-done | bytes 34848 | tf_op jit(solution)/shard_map/ppermute | solution.py:479
  57.0 2.6 %collective-permute-start.10 = (bf16[8,2048]{1,0:T(8,128)(2,1)S(1)}, bf16[8,2048]{1,0:T(8,128)(2,1)S(1)}, u32[]{:S(2)}, u32[]{:S(2)}) collective-permute-start(bf16[8,2048]{1,0:T(8,128)(2,1)S(1)} %get-tuple-element.65), channel_id=1, source_target_pairs={{0,24},{8,16},{16,8},{24,0},{1,25},{9,17},{17,9},{25,1},{2,26},{10... | collective-permute-start | bytes 98312 | tf_op jit(solution)/shard_map/ppermute | solution.py:479
  60.0 2.5 %collective-permute-start.25 = (bf16[32,2048]{1,0:T(8,128)(2,1)S(1)}, bf16[32,2048]{1,0:T(8,128)(2,1)S(1)}, u32[]{:S(2)}, u32[]{:S(2)}) collective-permute-start(bf16[32,2048]{1,0:T(8,128)(2,1)S(1)} %get-tuple-element.86), channel_id=1, source_target_pairs={{0,6},{2,4},{4,2},{6,0},{1,7},{3,5},{5,3},{7,1},{8,14},{10,12},{12... | collective-permute-start | bytes 393224 | tf_op jit(solution)/shard_map/ppermute | solution.py:479
  63.5 2.0 %collective-permute-start.12 = (bf16[32,2048]{1,0:T(8,128)(2,1)S(1)}, bf16[32,2048]{1,0:T(8,128)(2,1)S(1)}, u32[]{:S(2)}, u32[]{:S(2)}) collective-permute-start(bf16[32,2048]{1,0:T(8,128)(2,1)S(1)} %get-tuple-element.68), channel_id=1, source_target_pairs={{0,4},{2,6},{4,0},{6,2},{1,5},{3,7},{5,1},{7,3},{8,12},{10,14},{12... | collective-permute-start | bytes 393224 | tf_op jit(solution)/shard_map/ppermute | solution.py:479
  65.5 2.2 %collective-permute-start.13 = (bf16[32,2048]{1,0:T(8,128)(2,1)S(1)}, bf16[32,2048]{1,0:T(8,128)(2,1)S(1)}, u32[]{:S(2)}, u32[]{:S(2)}) collective-permute-start(bf16[32,2048]{1,0:T(8,128)(2,1)S(1)} %get-tuple-element.69), channel_id=1, source_target_pairs={{0,6},{2,4},{4,2},{6,0},{1,7},{3,5},{5,3},{7,1},{8,14},{10,12},{12... | collective-permute-start | bytes 393224 | tf_op jit(solution)/shard_map/ppermute | solution.py:479
  67.7 1.5 %collective-permute-start = (bf16[136,4096]{1,0:T(8,128)(2,1)S(1)}, bf16[136,4096]{1,0:T(8,128)(2,1)S(1)}, u32[]{:S(2)}, u32[]{:S(2)}) collective-permute-start(bf16[136,4096]{1,0:T(8,128)(2,1)S(1)} %get-tuple-element.51.own), channel_id=1, source_target_pairs={{0,1},{2,3},{4,5},{6,7},{8,9},{10,11},{12,13},{14,15},{16,17},{18,... | collective-permute-start | bytes 3342344 | tf_op jit(solution)/shard_map/ppermute | solution.py:634
  69.3 5.4 %collective-permute-done.12.refs_2_ = bf16[32,2048]{1,0:T(8,128)(2,1)S(1)} collective-permute-done((bf16[32,2048]{1,0:T(8,128)(2,1)S(1)}, bf16[32,2048]{1,0:T(8,128)(2,1)S(1)}, u32[]{:S(2)}, u32[]{:S(2)}) %collective-permute-start.12) | collective-permute-done | bytes 131104 | tf_op jit(solution)/shard_map/ppermute | solution.py:479
  75.5 8.1 %within.3 = bf16[256,4096]{1,0:T(8,128)(2,1)S(1)} custom-call(s32[2]{0:T(128)S(1)} %pad_add_fusion.2.at, bf16[256,8192]{1,0:T(8,128)(2,1)} %x_ref.3, bf16[256,1024]{1,0:T(8,128)(2,1)} %b_ref.3, bf16[256,1024]{1,0:T(8,128)(2,1)S(1)} %copy-done, f32[256,128]{1,0:T(8,128)} %step_ref.3, f32[256,128]{1,0:T(8,128)S(1)} %get-tuple-element.47.run_ref.run, ...), custom_call_target="tpu_custom_call" | custom-call | tf_op jit(solution)/shard_map/within/pallas_call | solution.py:637
  83.6 8.1 %within.2 = bf16[256,4096]{1,0:T(8,128)(2,1)S(1)} custom-call(s32[2]{0:T(128)S(1)} %pad_add_fusion.at, bf16[256,8192]{1,0:T(8,128)(2,1)} %x_ref.3, bf16[256,1024]{1,0:T(8,128)(2,1)} %b_ref.3, bf16[256,1024]{1,0:T(8,128)(2,1)S(1)} %copy-done, f32[256,128]{1,0:T(8,128)} %step_ref.3, f32[256,128]{1,0:T(8,128)S(1)} %get-tuple-element.47.run_ref.run, ...), custom_call_target="tpu_custom_call" | custom-call | tf_op jit(solution)/shard_map/within/pallas_call | solution.py:637
  91.6 2.3 %shard_map.74.filled = bf16[256,8192]{1,0:T(8,128)(2,1)} custom-call(s32[1]{0:T(128)} %bitcast.1.half, bf16[256,4096]{1,0:T(8,128)(2,1)S(1)} %within.3, bf16[256,1024]{1,0:T(8,128)(2,1)S(1)} %copy-done, bf16[128,4096]{1,0:T(8,128)(2,1)S(1)} %shard_map.73.state, f32[256,128]{1,0:T(8,128)S(1)} %get-tuple-element.47.run_ref.run, ...), custom_call_target="tpu_custom_call" | custom-call | tf_op jit(solution)/shard_map/pallas_call | solution.py:676
  93.9 2.3 %finish_other.1 = bf16[256,8192]{1,0:T(8,128)(2,1)} custom-call(s32[1]{0:T(128)} %bitcast.half, bf16[256,4096]{1,0:T(8,128)(2,1)S(1)} %within.2, bf16[256,1024]{1,0:T(8,128)(2,1)S(1)} %copy-done, bf16[128,4096]{1,0:T(8,128)(2,1)S(1)} %collective-permute-done.26.state, f32[256,128]{1,0:T(8,128)S(1)} %get-tuple-element.47.run_ref.run, ...), custom_call_target="tpu_custom_call", output_to_operand_aliasing={{}: (7, {})} | custom-call | tf_op jit(solution)/shard_map/finish_other/pallas_call | solution.py:679
  (52 shorter events, 20.6 us)
Async XLA Ops:
  7.3 9.4 %collective-permute-start.14 = (bf16[32,2176]{1,0:T(8,128)(2,1)S(1)}, bf16[32,2176]{1,0:T(8,128)(2,1)S(1)}, u32[]{:S(2)}, u32[]{:S(2)}) collective-permute-start(bf16[32,2176]{1,0:T(8,128)(2,1)S(1)} %get-tuple-element.71), channel_id=1, source_target_pairs={{0,2},{2,0},{4,6},{6,4},{1,3},{3,1},{5,7},{7,5},{8,10},{10,8},{12,... | collective-permute-start | bytes 417800 | tf_op jit(solution)/shard_map/ppermute | solution.py:479
  10.0 13.5 %collective-permute-start.15 = (bf16[32,2176]{1,0:T(8,128)(2,1)S(1)}, bf16[32,2176]{1,0:T(8,128)(2,1)S(1)}, u32[]{:S(2)}, u32[]{:S(2)}) collective-permute-start(bf16[32,2176]{1,0:T(8,128)(2,1)S(1)} %get-tuple-element.72), channel_id=1, source_target_pairs={{0,4},{2,6},{4,0},{6,2},{1,5},{3,7},{5,1},{7,3},{8,12},{10,14},{12... | collective-permute-start | bytes 417800 | tf_op jit(solution)/shard_map/ppermute | solution.py:479
  12.5 10.9 %collective-permute-start.16 = (bf16[32,2176]{1,0:T(8,128)(2,1)S(1)}, bf16[32,2176]{1,0:T(8,128)(2,1)S(1)}, u32[]{:S(2)}, u32[]{:S(2)}) collective-permute-start(bf16[32,2176]{1,0:T(8,128)(2,1)S(1)} %get-tuple-element.73), channel_id=1, source_target_pairs={{0,6},{2,4},{4,2},{6,0},{1,7},{3,5},{5,3},{7,1},{8,14},{10,12},{12... | collective-permute-start | bytes 417800 | tf_op jit(solution)/shard_map/ppermute | solution.py:479
  24.5 8.5 %collective-permute-start.17 = (bf16[8,2176]{1,0:T(8,128)(2,1)S(1)}, bf16[8,2176]{1,0:T(8,128)(2,1)S(1)}, u32[]{:S(2)}, u32[]{:S(2)}) collective-permute-start(bf16[8,2176]{1,0:T(8,128)(2,1)S(1)} %get-tuple-element.76), channel_id=1, source_target_pairs={{0,8},{8,0},{16,24},{24,16},{1,9},{9,1},{17,25},{25,17},{2,10},{10... | collective-permute-start | bytes 104456 | tf_op jit(solution)/shard_map/ppermute | solution.py:479
  26.0 8.5 %collective-permute-start.18 = (bf16[8,2176]{1,0:T(8,128)(2,1)S(1)}, bf16[8,2176]{1,0:T(8,128)(2,1)S(1)}, u32[]{:S(2)}, u32[]{:S(2)}) collective-permute-start(bf16[8,2176]{1,0:T(8,128)(2,1)S(1)} %get-tuple-element.77), channel_id=1, source_target_pairs={{0,16},{8,24},{16,0},{24,8},{1,17},{9,25},{17,1},{25,9},{2,18},{10... | collective-permute-start | bytes 104456 | tf_op jit(solution)/shard_map/ppermute | solution.py:479
  27.6 6.9 %collective-permute-start.19 = (bf16[8,2176]{1,0:T(8,128)(2,1)S(1)}, bf16[8,2176]{1,0:T(8,128)(2,1)S(1)}, u32[]{:S(2)}, u32[]{:S(2)}) collective-permute-start(bf16[8,2176]{1,0:T(8,128)(2,1)S(1)} %get-tuple-element.78), channel_id=1, source_target_pairs={{0,24},{8,16},{16,8},{24,0},{1,25},{9,17},{17,9},{25,1},{2,26},{10... | collective-permute-start | bytes 104456 | tf_op jit(solution)/shard_map/ppermute | solution.py:479
  29.3 16.8 %collective-permute-start.2 = (bf16[32,2176]{1,0:T(8,128)(2,1)S(1)}, bf16[32,2176]{1,0:T(8,128)(2,1)S(1)}, u32[]{:S(2)}, u32[]{:S(2)}) collective-permute-start(bf16[32,2176]{1,0:T(8,128)(2,1)S(1)} %get-tuple-element.54), channel_id=1, source_target_pairs={{0,2},{2,0},{4,6},{6,4},{1,3},{3,1},{5,7},{7,5},{8,10},{10,8},{12,... | collective-permute-start | bytes 417800 | tf_op jit(solution)/shard_map/ppermute | solution.py:479
  32.0 14.0 %collective-permute-start.3 = (bf16[32,2176]{1,0:T(8,128)(2,1)S(1)}, bf16[32,2176]{1,0:T(8,128)(2,1)S(1)}, u32[]{:S(2)}, u32[]{:S(2)}) collective-permute-start(bf16[32,2176]{1,0:T(8,128)(2,1)S(1)} %get-tuple-element.55), channel_id=1, source_target_pairs={{0,4},{2,6},{4,0},{6,2},{1,5},{3,7},{5,1},{7,3},{8,12},{10,14},{12... | collective-permute-start | bytes 417800 | tf_op jit(solution)/shard_map/ppermute | solution.py:479
  33.0 13.0 %collective-permute-start.4 = (bf16[32,2176]{1,0:T(8,128)(2,1)S(1)}, bf16[32,2176]{1,0:T(8,128)(2,1)S(1)}, u32[]{:S(2)}, u32[]{:S(2)}) collective-permute-start(bf16[32,2176]{1,0:T(8,128)(2,1)S(1)} %get-tuple-element.56), channel_id=1, source_target_pairs={{0,6},{2,4},{4,2},{6,0},{1,7},{3,5},{5,3},{7,1},{8,14},{10,12},{12... | collective-permute-start | bytes 417800 | tf_op jit(solution)/shard_map/ppermute | solution.py:479
  35.5 4.0 %collective-permute-start.20 = (bf16[8,2048]{1,0:T(8,128)(2,1)S(1)}, bf16[8,2048]{1,0:T(8,128)(2,1)S(1)}, u32[]{:S(2)}, u32[]{:S(2)}) collective-permute-start(bf16[8,2048]{1,0:T(8,128)(2,1)S(1)} %get-tuple-element.80), channel_id=1, source_target_pairs={{0,8},{8,0},{16,24},{24,16},{1,9},{9,1},{17,25},{25,17},{2,10},{10... | collective-permute-start | bytes 98312 | tf_op jit(solution)/shard_map/ppermute | solution.py:479
  37.0 5.2 %collective-permute-start.21 = (bf16[8,2048]{1,0:T(8,128)(2,1)S(1)}, bf16[8,2048]{1,0:T(8,128)(2,1)S(1)}, u32[]{:S(2)}, u32[]{:S(2)}) collective-permute-start(bf16[8,2048]{1,0:T(8,128)(2,1)S(1)} %get-tuple-element.81), channel_id=1, source_target_pairs={{0,16},{8,24},{16,0},{24,8},{1,17},{9,25},{17,1},{25,9},{2,18},{10... | collective-permute-start | bytes 98312 | tf_op jit(solution)/shard_map/ppermute | solution.py:479
  39.4 4.8 %collective-permute-start.22 = (bf16[8,2048]{1,0:T(8,128)(2,1)S(1)}, bf16[8,2048]{1,0:T(8,128)(2,1)S(1)}, u32[]{:S(2)}, u32[]{:S(2)}) collective-permute-start(bf16[8,2048]{1,0:T(8,128)(2,1)S(1)} %get-tuple-element.82), channel_id=1, source_target_pairs={{0,24},{8,16},{16,8},{24,0},{1,25},{9,17},{17,9},{25,1},{2,26},{10... | collective-permute-start | bytes 98312 | tf_op jit(solution)/shard_map/ppermute | solution.py:479
  45.0 20.6 %collective-permute-start.23 = (bf16[32,2048]{1,0:T(8,128)(2,1)S(1)}, bf16[32,2048]{1,0:T(8,128)(2,1)S(1)}, u32[]{:S(2)}, u32[]{:S(2)}) collective-permute-start(bf16[32,2048]{1,0:T(8,128)(2,1)S(1)} %get-tuple-element.84), channel_id=1, source_target_pairs={{0,2},{2,0},{4,6},{6,4},{1,3},{3,1},{5,7},{7,5},{8,10},{10,8},{12,... | collective-permute-start | bytes 393224 | tf_op jit(solution)/shard_map/ppermute | solution.py:479
  47.1 5.4 %collective-permute-start.5 = (bf16[8,2176]{1,0:T(8,128)(2,1)S(1)}, bf16[8,2176]{1,0:T(8,128)(2,1)S(1)}, u32[]{:S(2)}, u32[]{:S(2)}) collective-permute-start(bf16[8,2176]{1,0:T(8,128)(2,1)S(1)} %get-tuple-element.59), channel_id=1, source_target_pairs={{0,8},{8,0},{16,24},{24,16},{1,9},{9,1},{17,25},{25,17},{2,10},{10... | collective-permute-start | bytes 104456 | tf_op jit(solution)/shard_map/ppermute | solution.py:479
  50.2 4.9 %collective-permute-start.7 = (bf16[8,2176]{1,0:T(8,128)(2,1)S(1)}, bf16[8,2176]{1,0:T(8,128)(2,1)S(1)}, u32[]{:S(2)}, u32[]{:S(2)}) collective-permute-start(bf16[8,2176]{1,0:T(8,128)(2,1)S(1)} %get-tuple-element.61), channel_id=1, source_target_pairs={{0,24},{8,16},{16,8},{24,0},{1,25},{9,17},{17,9},{25,1},{2,26},{10... | collective-permute-start | bytes 104456 | tf_op jit(solution)/shard_map/ppermute | solution.py:479
  50.6 17.1 %collective-permute-start.24 = (bf16[32,2048]{1,0:T(8,128)(2,1)S(1)}, bf16[32,2048]{1,0:T(8,128)(2,1)S(1)}, u32[]{:S(2)}, u32[]{:S(2)}) collective-permute-start(bf16[32,2048]{1,0:T(8,128)(2,1)S(1)} %get-tuple-element.85), channel_id=1, source_target_pairs={{0,4},{2,6},{4,0},{6,2},{1,5},{3,7},{5,1},{7,3},{8,12},{10,14},{12... | collective-permute-start | bytes 393224 | tf_op jit(solution)/shard_map/ppermute | solution.py:479
  56.6 5.9 %collective-permute-start.9 = (bf16[8,2048]{1,0:T(8,128)(2,1)S(1)}, bf16[8,2048]{1,0:T(8,128)(2,1)S(1)}, u32[]{:S(2)}, u32[]{:S(2)}) collective-permute-start(bf16[8,2048]{1,0:T(8,128)(2,1)S(1)} %get-tuple-element.64), channel_id=1, source_target_pairs={{0,16},{8,24},{16,0},{24,8},{1,17},{9,25},{17,1},{25,9},{2,18},{10... | collective-permute-start | bytes 98312 | tf_op jit(solution)/shard_map/ppermute | solution.py:479
  57.0 5.6 %collective-permute-start.10 = (bf16[8,2048]{1,0:T(8,128)(2,1)S(1)}, bf16[8,2048]{1,0:T(8,128)(2,1)S(1)}, u32[]{:S(2)}, u32[]{:S(2)}) collective-permute-start(bf16[8,2048]{1,0:T(8,128)(2,1)S(1)} %get-tuple-element.65), channel_id=1, source_target_pairs={{0,24},{8,16},{16,8},{24,0},{1,25},{9,17},{17,9},{25,1},{2,26},{10... | collective-permute-start | bytes 98312 | tf_op jit(solution)/shard_map/ppermute | solution.py:479
  60.0 9.2 %collective-permute-start.25 = (bf16[32,2048]{1,0:T(8,128)(2,1)S(1)}, bf16[32,2048]{1,0:T(8,128)(2,1)S(1)}, u32[]{:S(2)}, u32[]{:S(2)}) collective-permute-start(bf16[32,2048]{1,0:T(8,128)(2,1)S(1)} %get-tuple-element.86), channel_id=1, source_target_pairs={{0,6},{2,4},{4,2},{6,0},{1,7},{3,5},{5,3},{7,1},{8,14},{10,12},{12... | collective-permute-start | bytes 393224 | tf_op jit(solution)/shard_map/ppermute | solution.py:479
  63.2 6.0 %collective-permute-start.11 = (bf16[32,2048]{1,0:T(8,128)(2,1)S(1)}, bf16[32,2048]{1,0:T(8,128)(2,1)S(1)}, u32[]{:S(2)}, u32[]{:S(2)}) collective-permute-start(bf16[32,2048]{1,0:T(8,128)(2,1)S(1)} %get-tuple-element.67), channel_id=1, source_target_pairs={{0,2},{2,0},{4,6},{6,4},{1,3},{3,1},{5,7},{7,5},{8,10},{10,8},{12,... | collective-permute-start | bytes 393224 | tf_op jit(solution)/shard_map/ppermute | solution.py:479
  63.5 11.1 %collective-permute-start.12 = (bf16[32,2048]{1,0:T(8,128)(2,1)S(1)}, bf16[32,2048]{1,0:T(8,128)(2,1)S(1)}, u32[]{:S(2)}, u32[]{:S(2)}) collective-permute-start(bf16[32,2048]{1,0:T(8,128)(2,1)S(1)} %get-tuple-element.68), channel_id=1, source_target_pairs={{0,4},{2,6},{4,0},{6,2},{1,5},{3,7},{5,1},{7,3},{8,12},{10,14},{12... | collective-permute-start | bytes 393224 | tf_op jit(solution)/shard_map/ppermute | solution.py:479
  65.5 9.1 %collective-permute-start.13 = (bf16[32,2048]{1,0:T(8,128)(2,1)S(1)}, bf16[32,2048]{1,0:T(8,128)(2,1)S(1)}, u32[]{:S(2)}, u32[]{:S(2)}) collective-permute-start(bf16[32,2048]{1,0:T(8,128)(2,1)S(1)} %get-tuple-element.69), channel_id=1, source_target_pairs={{0,6},{2,4},{4,2},{6,0},{1,7},{3,5},{5,3},{7,1},{8,14},{10,12},{12... | collective-permute-start | bytes 393224 | tf_op jit(solution)/shard_map/ppermute | solution.py:479
  67.7 15.9 %collective-permute-start = (bf16[136,4096]{1,0:T(8,128)(2,1)S(1)}, bf16[136,4096]{1,0:T(8,128)(2,1)S(1)}, u32[]{:S(2)}, u32[]{:S(2)}) collective-permute-start(bf16[136,4096]{1,0:T(8,128)(2,1)S(1)} %get-tuple-element.51.own), channel_id=1, source_target_pairs={{0,1},{2,3},{4,5},{6,7},{8,9},{10,11},{12,13},{14,15},{16,17},{18,... | collective-permute-start | bytes 3342344 | tf_op jit(solution)/shard_map/ppermute | solution.py:634
  75.2 18.7 %collective-permute-start.26 = (bf16[128,4096]{1,0:T(8,128)(2,1)S(1)}, bf16[128,4096]{1,0:T(8,128)(2,1)S(1)}, u32[]{:S(2)}, u32[]{:S(2)}) collective-permute-start(bf16[128,4096]{1,0:T(8,128)(2,1)S(1)} %shard_map.73.state), channel_id=1, source_target_pairs={{0,1},{1,0},{2,3},{3,2},{4,5},{5,4},{6,7},{7,6},{8,9},{9,8},{10,11... | collective-permute-start | bytes 3145736 | tf_op jit(solution)/shard_map/ppermute | solution.py:673
  (5 other events, 73.9 us)

commit v6 on v5

--- a/solution.py
+++ b/solution.py
@@ -260,9 +260,10 @@
     return values, dot(packed(here, heads), spreader(heads, width))
 
 
-def column_kernel(at, *refs, first_head, width, count, parts):
-    pieces, outs, decay_out, total = refs[:count], refs[count : count + parts], refs[-2], refs[-1]
-    rows, cols = total.shape
+def column_kernel(at, *refs, first_head, width, count):
+    pieces, out, decay_out = refs[:count], refs[count], refs[count + 1]
+    cols = decay_out.shape[1]
+    rows = out.shape[0]
     values, decay = decays_of(pieces, cols, first_head, width)
     decay_out[...] = decay
     for place in range(count):
@@ -273,47 +274,42 @@
             for k in range(count):
                 k = k ^ place
                 state = decay[k : k + 1, :] * state + pieces[k][:, :cols].astype(F32)
-            total[...] = state
-
+            out[:, :cols] = state.astype(BF16)
+
+    fill_decay(out, cols, values, count)
+
+
+def fill_decay(out, cols, values, count):
     product = values[:1, :]
     for k in range(1, count):
         product = product * values[k : k + 1, :]
     product = side_by_side(jnp.broadcast_to(product, (ROW_TILE, product.shape[1])), product.shape[1] // CORES)
-    part = rows // parts
-    for k, out in enumerate(outs):
-        start = pl.multiple_of(jnp.bitwise_xor(at[2], k) * part, part)
-        out[:, :cols] = total[pl.ds(start, part), :].astype(BF16)
-        out[:, cols:] = jnp.concatenate([product] * (part // ROW_TILE), axis=0).astype(BF16)
-
-
-def outer_kernel(at, *refs, first_head, width, count):
+    out[:, cols:] = jnp.concatenate([product] * (out.shape[0] // ROW_TILE), axis=0).astype(BF16)
+
+
+def pair_kernel(at, mine, theirs, out, *, first_head, width, cols):
+    odd = jnp.bitwise_and(at[2], 1) == 1
+    values, decay = decays_of((mine, theirs), cols, first_head, width)
+    one = jnp.ones_like(decay[:1, :])
+    on_mine = jnp.where(odd, one, decay[1:2, :])
+    on_theirs = jnp.where(odd, decay[:1, :], one)
+    out[:, :cols] = (on_mine * mine[:, :cols].astype(F32) + on_theirs * theirs[:, :cols].astype(F32)).astype(BF16)
+    fill_decay(out, cols, values, 2)
+
+
+def chips_kernel(at, neighbour, lower_pair, decay, *refs, first_head, width, count):
     pieces, outs = refs[:count], refs[count:]
-    rows, cols = outs[0].shape
-    _, decay = decays_of(pieces, cols, first_head, width)
-    for place in range(count):
-
-        @pl.when(at[2] == place)
-        def _():
-            state = jnp.zeros((rows, cols), F32)
-            for k in range(count):
-                k = k ^ place
-                outs[k][...] = state.astype(BF16)
-                state = decay[k : k + 1, :] * state + pieces[k][:, :cols].astype(F32)
-
-
-def chips_kernel(at, *refs, count, parts):
-    pieces, decay, carries = refs[:count], refs[count], refs[count + 1 : count + 1 + parts]
-    outs, carry = refs[count + 1 + parts : -1], refs[-1]
-    rows, cols = carry.shape
-    part = rows // parts
-    for k, piece in enumerate(carries):
-        start = pl.multiple_of(jnp.bitwise_xor(at[2], k) * part, part)
-        carry[pl.ds(start, part), :] = piece[...].astype(F32)
+    _, cols = outs[0].shape
+    odd = jnp.bitwise_and(at[2], 1) == 1
+    late = at[2] >= 2
+    _, passed = decays_of((neighbour,), cols, first_head, width)
+    on_pair = jnp.where(late, jnp.where(odd, passed[:1, :], jnp.ones_like(passed[:1, :])), 0.0)
+    carry = on_pair * lower_pair[:, :cols].astype(F32) + jnp.where(odd, neighbour[:, :cols].astype(F32), 0.0)
     for place in range(count):
 
         @pl.when(at[1] == place)
         def _():
-            state = carry[...]
+            state = carry
             for k in range(count):
                 k = k ^ place
                 outs[k][...] = state.astype(BF16)
@@ -484,9 +480,7 @@
     half_cols = own.shape[1]
     heads = total.shape[1]
     count = lax.axis_size(chip_axis)
-    parts = lax.axis_size(outer_axis)
     rows = states // count
-    part = rows // parts
     cols = half_cols // CHUNKS
     smem = pl.BlockSpec(memory_space=pltpu.SMEM)
     vmem = pl.BlockSpec(memory_space=pltpu.VMEM)
@@ -503,25 +497,23 @@
     for chunk in range(CHUNKS):
         first_head = chunk * cols // width
         pieces = gathered[chunk]
-        *totals, decay = small_call(
-            functools.partial(column_kernel, first_head=first_head, width=width, count=count, parts=parts),
+        column, decay = small_call(
+            functools.partial(column_kernel, first_head=first_head, width=width, count=count),
             [smem] + [vmem] * count,
-            [shape((part, cols + heads), BF16)] * parts + [shape((ROW_TILE, cols), F32)],
-            [pltpu.VMEM((rows, cols), F32)],
+            [shape((rows, cols + heads), BF16), shape((ROW_TILE, cols), F32)],
         )(at, *pieces)
-        totals = swapped(totals, outer_axis)
-        carries = small_call(
-            functools.partial(outer_kernel, first_head=first_head, width=width, count=parts),
-            [smem] + [vmem] * parts,
-            [shape((part, cols), BF16)] * parts,
-        )(at, *totals)
-        carries = swapped(carries, outer_axis)
+        neighbour = lax.ppermute(column, outer_axis, xor_route(4, 1))
+        (pair,) = small_call(
+            functools.partial(pair_kernel, first_head=first_head, width=width, cols=cols),
+            [smem] + [vmem] * 2,
+            [shape((rows, cols + heads), BF16)],
+        )(at, column, neighbour)
+        pair = lax.ppermute(pair, outer_axis, xor_route(4, 2))
         states_out = small_call(
-            functools.partial(chips_kernel, count=count, parts=parts),
-            [smem] + [vmem] * (count + 1 + parts),
+            functools.partial(chips_kernel, first_head=first_head, width=width, count=count),
+            [smem] + [vmem] * (count + 3),
             [shape((rows, cols), BF16)] * count,
-            [pltpu.VMEM((rows, cols), F32)],
-        )(at, *pieces, decay, *carries)
+        )(at, neighbour, pair, decay, *pieces)
         entering += swapped(states_out, chip_axis)
     (entering,) = small_call(
         functools.partial(assemble_kernel, count=count),
@@ -572,7 +564,7 @@
     per_half = GROUPS // CORES
     half_cols = channels // CORES
     chips = lax.axis_size((outer_axis, chip_axis))
-    by_swaps = chips & (chips - 1) == 0 and states % (chips * ROW_TILE) == 0
+    by_swaps = lax.axis_size(outer_axis) == 4 and chips == 16
     tall = states + ROW_TILE
 
     core = lax.axis_index(core_axis).astype(jnp.int32)

time: 96.6 us -> 92.2 us (0.954)
  starting transfers between devices: 39 us -> 30.6 us
  waiting for transfers between devices: 22.3 us -> 25.6 us
    ppermute x24 -> x12, starting transfers between devices: 36.8 us -> 22.3 us  [swapped(): done[k] = lax.ppermute(arrays[k], axis, xor_route(size, k))]
    ppermute x0 -> x4, starting transfers between devices: none -> 6.16 us  [the longest x2 3.16 us: entering_by_swaps(): pair = lax.ppermute(pair, outer_axis, xor_route(4, 2))]
    ppermute x0 -> x4, waiting for transfers between devices: none -> 2.51 us  [the longest x2 1.5 us: entering_by_swaps(): pair = lax.ppermute(pair, outer_axis, xor_route(4, 2))]
    ppermute x24 -> x12, waiting for transfers between devices: 22.3 us -> 23.1 us  [swapped(): done[k] = lax.ppermute(arrays[k], axis, xor_route(size, k))]
  transfers between devices with their start and end apart: 27 -> 19, of which waited for: 8 -> 6; matrix products, arithmetic and copies ran while one was open for 0% -> 0% of each run, Pallas kernels for 28% -> 32%
where the time goes in v6:
time: 92.2 us; the launch traced here: 91.9 us
  Pallas kernels  35.2 us (38%)
  starting transfers between devices  30.6 us (33%)
  waiting for transfers between devices  25.6 us (28%)
    ppermute x12, waiting for transfers between devices, swapped(): done[k] = lax.ppermute(arrays[k], axis, xor_route(size, k))  23.1 us
    ppermute x12, starting transfers between devices, swapped(): done[k] = lax.ppermute(arrays[k], axis, xor_route(size, k))  22.3 us
    pallas_call x2, Pallas kernels, within(): pl.pallas_call(functools.partial(within_kernel, dims=half_dims), grid_spe...  16.1 us
    ppermute x2, starting transfers between devices, entering_by_swaps(): pair = lax.ppermute(pair, outer_axis, xor_route(4, 2))  3.16 us
    ppermute x2, starting transfers between devices, entering_by_swaps(): neighbour = lax.ppermute(column, outer_axis, xor_route(4, 1))  3 us
    pallas_call x1, Pallas kernels, local(): pl.pallas_call(functools.partial(send_state_kernel, dims=state_dims), in_...  2.94 us
    pallas_call x1, Pallas kernels, local(): small_call(functools.partial(own_state_kernel, dims=state_dims), [smem, h...  2.88 us
    pallas_call x1, Pallas kernels, local(): small_call(functools.partial(first_final_kernel, dims=state_dims), [smem]...  2.29 us
  transfers between devices with their start and end apart: 19, of which 6 were waited for; matrix products, arithmetic and copies ran while one was open for 0% of the time, Pallas kernels for 32%

profile of v6, /device:TPU:0, one launch (start us, length us, event | category | flops | bytes accessed | tf_op | source)
XLA Modules:
  0.0 91.9 jit_solution(15755164095113956428)
XLA Ops:
  0.0 2.9 %send_state.1 = (bf16[136,4096]{1,0:T(8,128)(2,1)S(1)}, f32[256,128]{1,0:T(8,128)S(1)}, f32[128,256]{1,0:T(8,128)S(1)}, f32[256,128]{1,0:T(8,128)S(1)}, f32[8,128]{1,0:T(8,128)S(1)}) custom-call(s32[1]{0:T(128)} %bitcast.half, bf16[256,8192]{1,0:T(8,128)(2,1)} %x_ref.3, bf16[256,1024]{1,0:T(8,128)(2,1)} %b_ref.3, f32[256,128]{1,0:T(8,128)} %step_ref.3, ...), custom_call_target="tpu_custom_call" | custom-call | tf_op jit(solution)/shard_map/send_state/pallas_call | solution.py:595
  3.5 2.9 %shard_map.64 = (bf16[136,4096]{1,0:T(8,128)(2,1)S(1)}, bf16[128,4096]{1,0:T(8,128)(2,1)S(1)}) custom-call(s32[1]{0:T(128)} %bitcast.1.half, bf16[256,8192]{1,0:T(8,128)(2,1)} %x_ref.3, bf16[256,1024]{1,0:T(8,128)(2,1)} %b_ref.3, f32[256,128]{1,0:T(8,128)S(1)} %get-tuple-element.35.factor, f32[8,128]{1,0:T(8,128)S(1)} %get-tuple-element.36.total), custom_call_target="tpu_custom_call" | custom-call | tf_op jit(solution)/shard_map/pallas_call | solution.py:617
  7.3 2.6 %collective-permute-start.10 = (bf16[32,2176]{1,0:T(8,128)(2,1)S(1)}, bf16[32,2176]{1,0:T(8,128)(2,1)S(1)}, u32[]{:S(2)}, u32[]{:S(2)}) collective-permute-start(bf16[32,2176]{1,0:T(8,128)(2,1)S(1)} %get-tuple-element.50), channel_id=1, source_target_pairs={{0,2},{2,0},{4,6},{6,4},{1,3},{3,1},{5,7},{7,5},{8,10},{10,8},{12,... | collective-permute-start | bytes 417800 | tf_op jit(solution)/shard_map/ppermute | solution.py:475
  10.0 2.6 %collective-permute-start.11 = (bf16[32,2176]{1,0:T(8,128)(2,1)S(1)}, bf16[32,2176]{1,0:T(8,128)(2,1)S(1)}, u32[]{:S(2)}, u32[]{:S(2)}) collective-permute-start(bf16[32,2176]{1,0:T(8,128)(2,1)S(1)} %get-tuple-element.51), channel_id=1, source_target_pairs={{0,4},{2,6},{4,0},{6,2},{1,5},{3,7},{5,1},{7,3},{8,12},{10,14},{12... | collective-permute-start | bytes 417800 | tf_op jit(solution)/shard_map/ppermute | solution.py:475
  14.7 3.5 %collective-permute-start.3 = (bf16[32,2176]{1,0:T(8,128)(2,1)S(1)}, bf16[32,2176]{1,0:T(8,128)(2,1)S(1)}, u32[]{:S(2)}, u32[]{:S(2)}) collective-permute-start(bf16[32,2176]{1,0:T(8,128)(2,1)S(1)} %get-tuple-element.41), channel_id=1, source_target_pairs={{0,4},{2,6},{4,0},{6,2},{1,5},{3,7},{5,1},{7,3},{8,12},{10,14},{12... | collective-permute-start | bytes 417800 | tf_op jit(solution)/shard_map/ppermute | solution.py:475
  18.2 1.6 %collective-permute-start.4 = (bf16[32,2176]{1,0:T(8,128)(2,1)S(1)}, bf16[32,2176]{1,0:T(8,128)(2,1)S(1)}, u32[]{:S(2)}, u32[]{:S(2)}) collective-permute-start(bf16[32,2176]{1,0:T(8,128)(2,1)S(1)} %get-tuple-element.42), channel_id=1, source_target_pairs={{0,6},{2,4},{4,2},{6,0},{1,7},{3,5},{5,3},{7,1},{8,14},{10,12},{12... | collective-permute-start | bytes 417800 | tf_op jit(solution)/shard_map/ppermute | solution.py:475
  19.8 3.7 %collective-permute-done.11.refs_2_ = bf16[32,2176]{1,0:T(8,128)(2,1)S(1)} collective-permute-done((bf16[32,2176]{1,0:T(8,128)(2,1)S(1)}, bf16[32,2176]{1,0:T(8,128)(2,1)S(1)}, u32[]{:S(2)}, u32[]{:S(2)}) %collective-permute-start.11) | collective-permute-done | bytes 139296 | tf_op jit(solution)/shard_map/ppermute | solution.py:475
  24.6 1.5 %collective-permute-start.13 = (bf16[32,2176]{1,0:T(8,128)(2,1)S(1)}, bf16[32,2176]{1,0:T(8,128)(2,1)S(1)}, u32[]{:S(2)}, u32[]{:S(2)}) collective-permute-start(bf16[32,2176]{1,0:T(8,128)(2,1)S(1)} %get-tuple-element.53.mine), channel_id=1, source_target_pairs={{0,8},{8,0},{16,24},{24,16},{1,9},{9,1},{17,25},{25,17},{2,10},{10... | collective-permute-start | bytes 417800 | tf_op jit(solution)/shard_map/ppermute | solution.py:505
  26.1 9.3 %collective-permute-done.3.refs_2_ = bf16[32,2176]{1,0:T(8,128)(2,1)S(1)} collective-permute-done((bf16[32,2176]{1,0:T(8,128)(2,1)S(1)}, bf16[32,2176]{1,0:T(8,128)(2,1)S(1)}, u32[]{:S(2)}, u32[]{:S(2)}) %collective-permute-start.3) | collective-permute-done | bytes 139296 | tf_op jit(solution)/shard_map/ppermute | solution.py:475
  36.4 1.5 %collective-permute-start.5 = (bf16[32,2176]{1,0:T(8,128)(2,1)S(1)}, bf16[32,2176]{1,0:T(8,128)(2,1)S(1)}, u32[]{:S(2)}, u32[]{:S(2)}) collective-permute-start(bf16[32,2176]{1,0:T(8,128)(2,1)S(1)} %get-tuple-element.43.mine), channel_id=1, source_target_pairs={{0,8},{8,0},{16,24},{24,16},{1,9},{9,1},{17,25},{25,17},{2,10},{10... | collective-permute-start | bytes 417800 | tf_op jit(solution)/shard_map/ppermute | solution.py:505
  38.9 1.6 %collective-permute-start.14 = (bf16[32,2176]{1,0:T(8,128)(2,1)S(1)}, bf16[32,2176]{1,0:T(8,128)(2,1)S(1)}, u32[]{:S(2)}, u32[]{:S(2)}) collective-permute-start(bf16[32,2176]{1,0:T(8,128)(2,1)S(1)} %shard_map.71), channel_id=1, source_target_pairs={{0,16},{8,24},{16,0},{24,8},{1,17},{9,25},{17,1},{25,9},{2,18},{10... | collective-permute-start | bytes 417800 | tf_op jit(solution)/shard_map/ppermute | solution.py:511
  42.4 1.6 %collective-permute-start.6 = (bf16[32,2176]{1,0:T(8,128)(2,1)S(1)}, bf16[32,2176]{1,0:T(8,128)(2,1)S(1)}, u32[]{:S(2)}, u32[]{:S(2)}) collective-permute-start(bf16[32,2176]{1,0:T(8,128)(2,1)S(1)} %shard_map.67), channel_id=1, source_target_pairs={{0,16},{8,24},{16,0},{24,8},{1,17},{9,25},{17,1},{25,9},{2,18},{10... | collective-permute-start | bytes 417800 | tf_op jit(solution)/shard_map/ppermute | solution.py:511
  44.0 1.5 %collective-permute-done.14.lower_pair = bf16[32,2176]{1,0:T(8,128)(2,1)S(1)} collective-permute-done((bf16[32,2176]{1,0:T(8,128)(2,1)S(1)}, bf16[32,2176]{1,0:T(8,128)(2,1)S(1)}, u32[]{:S(2)}, u32[]{:S(2)}) %collective-permute-start.14) | collective-permute-done | bytes 139296 | tf_op jit(solution)/shard_map/ppermute | solution.py:511
  46.5 2.2 %collective-permute-start.15 = (bf16[32,2048]{1,0:T(8,128)(2,1)S(1)}, bf16[32,2048]{1,0:T(8,128)(2,1)S(1)}, u32[]{:S(2)}, u32[]{:S(2)}) collective-permute-start(bf16[32,2048]{1,0:T(8,128)(2,1)S(1)} %get-tuple-element.56), channel_id=1, source_target_pairs={{0,2},{2,0},{4,6},{6,4},{1,3},{3,1},{5,7},{7,5},{8,10},{10,8},{12,... | collective-permute-start | bytes 393224 | tf_op jit(solution)/shard_map/ppermute | solution.py:475
  49.8 1.4 %collective-permute-start.17 = (bf16[32,2048]{1,0:T(8,128)(2,1)S(1)}, bf16[32,2048]{1,0:T(8,128)(2,1)S(1)}, u32[]{:S(2)}, u32[]{:S(2)}) collective-permute-start(bf16[32,2048]{1,0:T(8,128)(2,1)S(1)} %get-tuple-element.58), channel_id=1, source_target_pairs={{0,6},{2,4},{4,2},{6,0},{1,7},{3,5},{5,3},{7,1},{8,14},{10,12},{12... | collective-permute-start | bytes 393224 | tf_op jit(solution)/shard_map/ppermute | solution.py:475
  53.3 2.0 %collective-permute-start.8 = (bf16[32,2048]{1,0:T(8,128)(2,1)S(1)}, bf16[32,2048]{1,0:T(8,128)(2,1)S(1)}, u32[]{:S(2)}, u32[]{:S(2)}) collective-permute-start(bf16[32,2048]{1,0:T(8,128)(2,1)S(1)} %get-tuple-element.47), channel_id=1, source_target_pairs={{0,4},{2,6},{4,0},{6,2},{1,5},{3,7},{5,1},{7,3},{8,12},{10,14},{12... | collective-permute-start | bytes 393224 | tf_op jit(solution)/shard_map/ppermute | solution.py:475
  55.3 3.2 %collective-permute-start.9 = (bf16[32,2048]{1,0:T(8,128)(2,1)S(1)}, bf16[32,2048]{1,0:T(8,128)(2,1)S(1)}, u32[]{:S(2)}, u32[]{:S(2)}) collective-permute-start(bf16[32,2048]{1,0:T(8,128)(2,1)S(1)} %get-tuple-element.48), channel_id=1, source_target_pairs={{0,6},{2,4},{4,2},{6,0},{1,7},{3,5},{5,3},{7,1},{8,14},{10,12},{12... | collective-permute-start | bytes 393224 | tf_op jit(solution)/shard_map/ppermute | solution.py:475
  58.5 3.1 %collective-permute-done.16.refs_6_ = bf16[32,2048]{1,0:T(8,128)(2,1)S(1)} collective-permute-done((bf16[32,2048]{1,0:T(8,128)(2,1)S(1)}, bf16[32,2048]{1,0:T(8,128)(2,1)S(1)}, u32[]{:S(2)}, u32[]{:S(2)}) %collective-permute-start.16) | collective-permute-done | bytes 131104 | tf_op jit(solution)/shard_map/ppermute | solution.py:475
  61.6 1.5 %collective-permute-start = (bf16[136,4096]{1,0:T(8,128)(2,1)S(1)}, bf16[136,4096]{1,0:T(8,128)(2,1)S(1)}, u32[]{:S(2)}, u32[]{:S(2)}) collective-permute-start(bf16[136,4096]{1,0:T(8,128)(2,1)S(1)} %get-tuple-element.37.own), channel_id=1, source_target_pairs={{0,1},{2,3},{4,5},{6,7},{8,9},{10,11},{12,13},{14,15},{16,17},{18,... | collective-permute-start | bytes 3342344 | tf_op jit(solution)/shard_map/ppermute | solution.py:626
  63.1 7.0 %collective-permute-done.8.refs_2_ = bf16[32,2048]{1,0:T(8,128)(2,1)S(1)} collective-permute-done((bf16[32,2048]{1,0:T(8,128)(2,1)S(1)}, bf16[32,2048]{1,0:T(8,128)(2,1)S(1)}, u32[]{:S(2)}, u32[]{:S(2)}) %collective-permute-start.8) | collective-permute-done | bytes 131104 | tf_op jit(solution)/shard_map/ppermute | solution.py:475
  71.0 8.1 %within.3 = bf16[256,4096]{1,0:T(8,128)(2,1)S(1)} custom-call(s32[2]{0:T(128)S(1)} %pad_add_fusion.2.at, bf16[256,8192]{1,0:T(8,128)(2,1)} %x_ref.3, bf16[256,1024]{1,0:T(8,128)(2,1)} %b_ref.3, bf16[256,1024]{1,0:T(8,128)(2,1)S(1)} %copy-done, f32[256,128]{1,0:T(8,128)} %step_ref.3, f32[256,128]{1,0:T(8,128)S(1)} %get-tuple-element.33.run_ref.run, ...), custom_call_target="tpu_custom_call" | custom-call | tf_op jit(solution)/shard_map/within/pallas_call | solution.py:629
  79.1 8.1 %within.2 = bf16[256,4096]{1,0:T(8,128)(2,1)S(1)} custom-call(s32[2]{0:T(128)S(1)} %pad_add_fusion.at, bf16[256,8192]{1,0:T(8,128)(2,1)} %x_ref.3, bf16[256,1024]{1,0:T(8,128)(2,1)} %b_ref.3, bf16[256,1024]{1,0:T(8,128)(2,1)S(1)} %copy-done, f32[256,128]{1,0:T(8,128)} %step_ref.3, f32[256,128]{1,0:T(8,128)S(1)} %get-tuple-element.33.run_ref.run, ...), custom_call_target="tpu_custom_call" | custom-call | tf_op jit(solution)/shard_map/within/pallas_call | solution.py:629
  87.2 2.3 %shard_map.74.filled = bf16[256,8192]{1,0:T(8,128)(2,1)} custom-call(s32[1]{0:T(128)} %bitcast.1.half, bf16[256,4096]{1,0:T(8,128)(2,1)S(1)} %within.3, bf16[256,1024]{1,0:T(8,128)(2,1)S(1)} %copy-done, bf16[128,4096]{1,0:T(8,128)(2,1)S(1)} %shard_map.73.state, f32[256,128]{1,0:T(8,128)S(1)} %get-tuple-element.33.run_ref.run, ...), custom_call_target="tpu_custom_call" | custom-call | tf_op jit(solution)/shard_map/pallas_call | solution.py:668
  89.5 2.3 %finish_other.1 = bf16[256,8192]{1,0:T(8,128)(2,1)} custom-call(s32[1]{0:T(128)} %bitcast.half, bf16[256,4096]{1,0:T(8,128)(2,1)S(1)} %within.2, bf16[256,1024]{1,0:T(8,128)(2,1)S(1)} %copy-done, bf16[128,4096]{1,0:T(8,128)(2,1)S(1)} %collective-permute-done.18.state, f32[256,128]{1,0:T(8,128)S(1)} %get-tuple-element.33.run_ref.run, ...), custom_call_target="tpu_custom_call", output_to_operand_aliasing={{}: (7, {})} | custom-call | tf_op jit(solution)/shard_map/finish_other/pallas_call | solution.py:671
  (36 shorter events, 13.6 us)
Async XLA Ops:
  2.9 3.5 %collective-permute-start.1 = (bf16[136,4096]{1,0:T(8,128)(2,1)S(1)}, bf16[136,4096]{1,0:T(8,128)(2,1)S(1)}, u32[]{:S(2)}, u32[]{:S(2)}) collective-permute-start(bf16[136,4096]{1,0:T(8,128)(2,1)S(1)} %get-tuple-element.38), channel_id=1, source_target_pairs={{0,1},{1,0},{2,3},{3,2},{4,5},{5,4},{6,7},{7,6},{8,9},{9,8},{10,11... | collective-permute-start | bytes 3342344 | tf_op jit(solution)/shard_map/ppermute | solution.py:615
  7.3 10.8 %collective-permute-start.10 = (bf16[32,2176]{1,0:T(8,128)(2,1)S(1)}, bf16[32,2176]{1,0:T(8,128)(2,1)S(1)}, u32[]{:S(2)}, u32[]{:S(2)}) collective-permute-start(bf16[32,2176]{1,0:T(8,128)(2,1)S(1)} %get-tuple-element.50), channel_id=1, source_target_pairs={{0,2},{2,0},{4,6},{6,4},{1,3},{3,1},{5,7},{7,5},{8,10},{10,8},{12,... | collective-permute-start | bytes 417800 | tf_op jit(solution)/shard_map/ppermute | solution.py:475
  10.0 13.5 %collective-permute-start.11 = (bf16[32,2176]{1,0:T(8,128)(2,1)S(1)}, bf16[32,2176]{1,0:T(8,128)(2,1)S(1)}, u32[]{:S(2)}, u32[]{:S(2)}) collective-permute-start(bf16[32,2176]{1,0:T(8,128)(2,1)S(1)} %get-tuple-element.51), channel_id=1, source_target_pairs={{0,4},{2,6},{4,0},{6,2},{1,5},{3,7},{5,1},{7,3},{8,12},{10,14},{12... | collective-permute-start | bytes 417800 | tf_op jit(solution)/shard_map/ppermute | solution.py:475
  12.5 10.9 %collective-permute-start.12 = (bf16[32,2176]{1,0:T(8,128)(2,1)S(1)}, bf16[32,2176]{1,0:T(8,128)(2,1)S(1)}, u32[]{:S(2)}, u32[]{:S(2)}) collective-permute-start(bf16[32,2176]{1,0:T(8,128)(2,1)S(1)} %get-tuple-element.52), channel_id=1, source_target_pairs={{0,6},{2,4},{4,2},{6,0},{1,7},{3,5},{5,3},{7,1},{8,14},{10,12},{12... | collective-permute-start | bytes 417800 | tf_op jit(solution)/shard_map/ppermute | solution.py:475
  13.8 12.3 %collective-permute-start.2 = (bf16[32,2176]{1,0:T(8,128)(2,1)S(1)}, bf16[32,2176]{1,0:T(8,128)(2,1)S(1)}, u32[]{:S(2)}, u32[]{:S(2)}) collective-permute-start(bf16[32,2176]{1,0:T(8,128)(2,1)S(1)} %get-tuple-element.40), channel_id=1, source_target_pairs={{0,2},{2,0},{4,6},{6,4},{1,3},{3,1},{5,7},{7,5},{8,10},{10,8},{12,... | collective-permute-start | bytes 417800 | tf_op jit(solution)/shard_map/ppermute | solution.py:475
  14.7 20.7 %collective-permute-start.3 = (bf16[32,2176]{1,0:T(8,128)(2,1)S(1)}, bf16[32,2176]{1,0:T(8,128)(2,1)S(1)}, u32[]{:S(2)}, u32[]{:S(2)}) collective-permute-start(bf16[32,2176]{1,0:T(8,128)(2,1)S(1)} %get-tuple-element.41), channel_id=1, source_target_pairs={{0,4},{2,6},{4,0},{6,2},{1,5},{3,7},{5,1},{7,3},{8,12},{10,14},{12... | collective-permute-start | bytes 417800 | tf_op jit(solution)/shard_map/ppermute | solution.py:475
  18.2 17.2 %collective-permute-start.4 = (bf16[32,2176]{1,0:T(8,128)(2,1)S(1)}, bf16[32,2176]{1,0:T(8,128)(2,1)S(1)}, u32[]{:S(2)}, u32[]{:S(2)}) collective-permute-start(bf16[32,2176]{1,0:T(8,128)(2,1)S(1)} %get-tuple-element.42), channel_id=1, source_target_pairs={{0,6},{2,4},{4,2},{6,0},{1,7},{3,5},{5,3},{7,1},{8,14},{10,12},{12... | collective-permute-start | bytes 417800 | tf_op jit(solution)/shard_map/ppermute | solution.py:475
  24.6 13.4 %collective-permute-start.13 = (bf16[32,2176]{1,0:T(8,128)(2,1)S(1)}, bf16[32,2176]{1,0:T(8,128)(2,1)S(1)}, u32[]{:S(2)}, u32[]{:S(2)}) collective-permute-start(bf16[32,2176]{1,0:T(8,128)(2,1)S(1)} %get-tuple-element.53.mine), channel_id=1, source_target_pairs={{0,8},{8,0},{16,24},{24,16},{1,9},{9,1},{17,25},{25,17},{2,10},{10... | collective-permute-start | bytes 417800 | tf_op jit(solution)/shard_map/ppermute | solution.py:505
  36.4 5.1 %collective-permute-start.5 = (bf16[32,2176]{1,0:T(8,128)(2,1)S(1)}, bf16[32,2176]{1,0:T(8,128)(2,1)S(1)}, u32[]{:S(2)}, u32[]{:S(2)}) collective-permute-start(bf16[32,2176]{1,0:T(8,128)(2,1)S(1)} %get-tuple-element.43.mine), channel_id=1, source_target_pairs={{0,8},{8,0},{16,24},{24,16},{1,9},{9,1},{17,25},{25,17},{2,10},{10... | collective-permute-start | bytes 417800 | tf_op jit(solution)/shard_map/ppermute | solution.py:505
  38.9 32.1 %copy-start = (bf16[256,1024]{1,0:T(8,128)(2,1)S(1)}, bf16[256,1024]{1,0:T(8,128)(2,1)}, u32[]{:S(2)}) copy-start(bf16[256,1024]{1,0:T(8,128)(2,1)} %c.3) | copy-start | bytes 1572868
  38.9 32.1 %copy-start.1 = (f32[128]{0:T(128)S(1)}, f32[128]{0:T(128)}, u32[]{:S(2)}) copy-start(f32[128]{0:T(128)} %param.11) | copy-start | bytes 1540
  38.9 6.5 %collective-permute-start.14 = (bf16[32,2176]{1,0:T(8,128)(2,1)S(1)}, bf16[32,2176]{1,0:T(8,128)(2,1)S(1)}, u32[]{:S(2)}, u32[]{:S(2)}) collective-permute-start(bf16[32,2176]{1,0:T(8,128)(2,1)S(1)} %shard_map.71), channel_id=1, source_target_pairs={{0,16},{8,24},{16,0},{24,8},{1,17},{9,25},{17,1},{25,9},{2,18},{10... | collective-permute-start | bytes 417800 | tf_op jit(solution)/shard_map/ppermute | solution.py:511
  42.4 8.8 %collective-permute-start.6 = (bf16[32,2176]{1,0:T(8,128)(2,1)S(1)}, bf16[32,2176]{1,0:T(8,128)(2,1)S(1)}, u32[]{:S(2)}, u32[]{:S(2)}) collective-permute-start(bf16[32,2176]{1,0:T(8,128)(2,1)S(1)} %shard_map.67), channel_id=1, source_target_pairs={{0,16},{8,24},{16,0},{24,8},{1,17},{9,25},{17,1},{25,9},{2,18},{10... | collective-permute-start | bytes 417800 | tf_op jit(solution)/shard_map/ppermute | solution.py:511
  46.5 8.7 %collective-permute-start.15 = (bf16[32,2048]{1,0:T(8,128)(2,1)S(1)}, bf16[32,2048]{1,0:T(8,128)(2,1)S(1)}, u32[]{:S(2)}, u32[]{:S(2)}) collective-permute-start(bf16[32,2048]{1,0:T(8,128)(2,1)S(1)} %get-tuple-element.56), channel_id=1, source_target_pairs={{0,2},{2,0},{4,6},{6,4},{1,3},{3,1},{5,7},{7,5},{8,10},{10,8},{12,... | collective-permute-start | bytes 393224 | tf_op jit(solution)/shard_map/ppermute | solution.py:475
  48.7 12.8 %collective-permute-start.16 = (bf16[32,2048]{1,0:T(8,128)(2,1)S(1)}, bf16[32,2048]{1,0:T(8,128)(2,1)S(1)}, u32[]{:S(2)}, u32[]{:S(2)}) collective-permute-start(bf16[32,2048]{1,0:T(8,128)(2,1)S(1)} %get-tuple-element.57), channel_id=1, source_target_pairs={{0,4},{2,6},{4,0},{6,2},{1,5},{3,7},{5,1},{7,3},{8,12},{10,14},{12... | collective-permute-start | bytes 393224 | tf_op jit(solution)/shard_map/ppermute | solution.py:475
  49.8 13.3 %collective-permute-start.17 = (bf16[32,2048]{1,0:T(8,128)(2,1)S(1)}, bf16[32,2048]{1,0:T(8,128)(2,1)S(1)}, u32[]{:S(2)}, u32[]{:S(2)}) collective-permute-start(bf16[32,2048]{1,0:T(8,128)(2,1)S(1)} %get-tuple-element.58), channel_id=1, source_target_pairs={{0,6},{2,4},{4,2},{6,0},{1,7},{3,5},{5,3},{7,1},{8,14},{10,12},{12... | collective-permute-start | bytes 393224 | tf_op jit(solution)/shard_map/ppermute | solution.py:475
  52.2 10.9 %collective-permute-start.7 = (bf16[32,2048]{1,0:T(8,128)(2,1)S(1)}, bf16[32,2048]{1,0:T(8,128)(2,1)S(1)}, u32[]{:S(2)}, u32[]{:S(2)}) collective-permute-start(bf16[32,2048]{1,0:T(8,128)(2,1)S(1)} %get-tuple-element.46), channel_id=1, source_target_pairs={{0,2},{2,0},{4,6},{6,4},{1,3},{3,1},{5,7},{7,5},{8,10},{10,8},{12,... | collective-permute-start | bytes 393224 | tf_op jit(solution)/shard_map/ppermute | solution.py:475
  53.3 16.9 %collective-permute-start.8 = (bf16[32,2048]{1,0:T(8,128)(2,1)S(1)}, bf16[32,2048]{1,0:T(8,128)(2,1)S(1)}, u32[]{:S(2)}, u32[]{:S(2)}) collective-permute-start(bf16[32,2048]{1,0:T(8,128)(2,1)S(1)} %get-tuple-element.47), channel_id=1, source_target_pairs={{0,4},{2,6},{4,0},{6,2},{1,5},{3,7},{5,1},{7,3},{8,12},{10,14},{12... | collective-permute-start | bytes 393224 | tf_op jit(solution)/shard_map/ppermute | solution.py:475
  55.3 14.9 %collective-permute-start.9 = (bf16[32,2048]{1,0:T(8,128)(2,1)S(1)}, bf16[32,2048]{1,0:T(8,128)(2,1)S(1)}, u32[]{:S(2)}, u32[]{:S(2)}) collective-permute-start(bf16[32,2048]{1,0:T(8,128)(2,1)S(1)} %get-tuple-element.48), channel_id=1, source_target_pairs={{0,6},{2,4},{4,2},{6,0},{1,7},{3,5},{5,3},{7,1},{8,14},{10,12},{12... | collective-permute-start | bytes 393224 | tf_op jit(solution)/shard_map/ppermute | solution.py:475
  61.6 17.5 %collective-permute-start = (bf16[136,4096]{1,0:T(8,128)(2,1)S(1)}, bf16[136,4096]{1,0:T(8,128)(2,1)S(1)}, u32[]{:S(2)}, u32[]{:S(2)}) collective-permute-start(bf16[136,4096]{1,0:T(8,128)(2,1)S(1)} %get-tuple-element.37.own), channel_id=1, source_target_pairs={{0,1},{2,3},{4,5},{6,7},{8,9},{10,11},{12,13},{14,15},{16,17},{18,... | collective-permute-start | bytes 3342344 | tf_op jit(solution)/shard_map/ppermute | solution.py:626
  70.8 18.7 %collective-permute-start.18 = (bf16[128,4096]{1,0:T(8,128)(2,1)S(1)}, bf16[128,4096]{1,0:T(8,128)(2,1)S(1)}, u32[]{:S(2)}, u32[]{:S(2)}) collective-permute-start(bf16[128,4096]{1,0:T(8,128)(2,1)S(1)} %shard_map.73.state), channel_id=1, source_target_pairs={{0,1},{1,0},{2,3},{3,2},{4,5},{5,4},{6,7},{7,6},{8,9},{9,8},{10,11... | collective-permute-start | bytes 3145736 | tf_op jit(solution)/shard_map/ppermute | solution.py:665

commit v7 on v6

--- a/solution.py
+++ b/solution.py
@@ -15,6 +15,7 @@
 TILE = 256
 AHEAD = 2
 CHUNKS = 2
+PER_CALL = 2
 ROW_TILE = 8
 HALF_ROWS = 128
 ROW_BLOCK = 16
@@ -356,7 +357,7 @@
 ):
     per_half, per_group, width = dims
     turn = pl.program_id(0)
-    group = at[0] * per_half + turn
+    group = at[0] * per_half + at[2] + turn
     head = group * per_group
     rows = x_ref.shape[0]
     pair = LANES // width
@@ -435,21 +436,19 @@
         copy.wait()
 
 
-def final_kernel(half, within, c, state, run, base, matrix, filled, out, result, stores, *, dims):
-    del filled
+def final_kernel(half, c, state, run, base, matrix, *refs, dims, parts):
+    within = refs[:parts]
+    out, result, stores = refs[-3:]
     per_half, group_cols, states = dims
+    each = per_half // parts
 
     def part(k):
-        return within[:, k * group_cols : (k + 1) * group_cols]
+        return within[k // each][:, k % each * group_cols : (k % each + 1) * group_cols]
 
     def rows_c(k):
         return c[:, pl.ds(pl.multiple_of((half[0] * per_half + k) * states, states), states)]
 
     add_carried(half[0], part, rows_c, state, run, base, out, result, matrix, stores, dims)
-
-
-def first_final_kernel(half, within, c, state, run, base, matrix, out, result, stores, *, dims):
-    final_kernel(half, within, c, state, run, base, matrix, None, out, result, stores, dims=dims)
 
 
 def small_call(kernel, in_specs, out_shape, scratch=(), out_specs=None):
@@ -469,9 +468,8 @@
 
 def swapped(arrays, axis):
     size = lax.axis_size(axis)
-    order = sorted(range(1, size), key=lambda k: -(k.bit_length()))
     done = {0: arrays[0]}
-    for k in order:
+    for k in range(1, size):
         done[k] = lax.ppermute(arrays[k], axis, xor_route(size, k))
     return [done[k] for k in range(size)]
 
@@ -580,7 +578,7 @@
         return pl.BlockSpec(shape, lambda i, *_: (0,) * len(shape))
 
     def by_group(cols):
-        return pl.BlockSpec((tokens, cols), lambda i, at: (0, at[0] * per_half + i))
+        return pl.BlockSpec((tokens, cols), lambda i, at: (0, at[0] * per_half + at[2] + i))
 
     state_dims = (per_half, group_cols, states)
     half_dims = (per_half, per_group, width)
@@ -625,12 +623,12 @@
     entering, base = find_entering(at, own, got, total, width, states, outer_axis, chip_axis)
     late = lax.ppermute(own, core_axis, swap[:1])
 
-    def within(half, before):
+    def within(half, before, first):
         return pl.pallas_call(
             functools.partial(within_kernel, dims=half_dims),
             grid_spec=pltpu.PrefetchScalarGridSpec(
                 num_scalar_prefetch=1,
-                grid=(per_half,),
+                grid=(PER_CALL,),
                 in_specs=[
                     by_group(group_cols),
                     by_group(states),
@@ -639,16 +637,16 @@
                     whole((tokens, heads)),
                     whole((heads, tokens)),
                     whole((1, heads)),
-                    pl.BlockSpec((states, group_cols), lambda i, at: (0, i)),
+                    pl.BlockSpec((states, group_cols), lambda i, at: (0, at[2] + i)),
                 ],
                 out_specs=pl.BlockSpec((tokens, group_cols), lambda i, at: (0, i)),
                 scratch_shapes=[pltpu.VMEM((2 * per_group, group_cols), BF16)],
             ),
-            out_shape=jax.ShapeDtypeStruct((tokens, half_cols), BF16),
+            out_shape=jax.ShapeDtypeStruct((tokens, PER_CALL * group_cols), BF16),
             compiler_params=params(),
             name="within",
         )(
-            jnp.concatenate([half, mine]),
+            jnp.concatenate([half, mine, jnp.full((1,), first, jnp.int32)]),
             inputs,
             b_matrix,
             c_matrix,
@@ -659,25 +657,30 @@
             before,
         )
 
-    own_within = within(mine, got)
-    other_within = within(other, late)
+    own_within = []
+    other_within = []
+    for first in range(0, per_half, PER_CALL):
+        own_within.append(within(mine, got, first))
+        other_within.append(within(other, late, first))
 
     got_entering = lax.ppermute(entering, core_axis, swap)
     mixed = jax.ShapeDtypeStruct((tokens, channels), BF16)
     final_scratch = [pltpu.VMEM((tokens, half_cols), BF16), pltpu.SemaphoreType.DMA((per_half,))]
+    parts = len(own_within)
+    final = functools.partial(final_kernel, dims=state_dims, parts=parts)
     (result,) = small_call(
-        functools.partial(first_final_kernel, dims=state_dims), [smem] + [vmem] * 6, [mixed], final_scratch, [hbm]
-    )(mine, own_within, c_matrix, entering, run, base, matrix)
+        final, [smem] + [vmem] * (5 + parts), [mixed], final_scratch, [hbm]
+    )(mine, c_matrix, entering, run, base, matrix, *own_within)
     return pl.pallas_call(
-        functools.partial(final_kernel, dims=state_dims),
-        in_specs=[smem] + [vmem] * 6 + [hbm],
+        final,
+        in_specs=[smem] + [vmem] * (5 + parts) + [hbm],
         out_specs=hbm,
         out_shape=mixed,
         scratch_shapes=final_scratch,
-        input_output_aliases={7: 0},
+        input_output_aliases={6 + parts: 0},
         compiler_params=plain_params(),
         name="finish_other",
-    )(other, other_within, c_matrix, got_entering, run, base, matrix, result)
+    )(other, c_matrix, got_entering, run, base, matrix, *other_within, result)
 
 
 def solution(mesh):

time: 92.2 us -> 95.8 us (1.039)
  Pallas kernels: 35.2 us -> 38.4 us
    pallas_call x2 -> x4, Pallas kernels: 16.1 us -> 19.4 us  [within(): pl.pallas_call(functools.partial(within_kernel, dims=half_dims), grid_spe...]
  transfers between devices with their start and end apart: 19 -> 19, of which waited for: 6 -> 6; matrix products, arithmetic and copies ran while one was open for 0% -> 0% of each run, Pallas kernels for 32% -> 33%
where the time goes in v7:
time: 95.8 us; the launch traced here: 95.5 us
  Pallas kernels  38.4 us (40%)
  starting transfers between devices  30.8 us (32%)
  waiting for transfers between devices  25.7 us (27%)
    ppermute x12, waiting for transfers between devices, swapped(): done[k] = lax.ppermute(arrays[k], axis, xor_route(size, k))  23.2 us
    ppermute x12, starting transfers between devices, swapped(): done[k] = lax.ppermute(arrays[k], axis, xor_route(size, k))  22.5 us
    pallas_call x4, Pallas kernels, within(): pl.pallas_call(functools.partial(within_kernel, dims=half_dims), grid_spe...  19.4 us
    ppermute x2, starting transfers between devices, entering_by_swaps(): pair = lax.ppermute(pair, outer_axis, xor_route(4, 2))  3.16 us
    ppermute x2, starting transfers between devices, entering_by_swaps(): neighbour = lax.ppermute(column, outer_axis, xor_route(4, 1))  3.01 us
    pallas_call x1, Pallas kernels, local(): pl.pallas_call(functools.partial(send_state_kernel, dims=state_dims), in_...  2.94 us
    pallas_call x1, Pallas kernels, local(): small_call(functools.partial(own_state_kernel, dims=state_dims), [smem, h...  2.88 us
    pallas_call x1, Pallas kernels, local(): small_call(final, [smem] + [vmem] * (5 + parts), [mixed], final_scratch,...  2.29 us
  transfers between devices with their start and end apart: 19, of which 6 were waited for; matrix products, arithmetic and copies ran while one was open for 0% of the time, Pallas kernels for 33%

profile of v7, /device:TPU:0, one launch (start us, length us, event | category | flops | bytes accessed | tf_op | source)
XLA Modules:
  0.0 95.5 jit_solution(17203416531386155411)
XLA Ops:
  0.0 2.9 %send_state.1 = (bf16[136,4096]{1,0:T(8,128)(2,1)S(1)}, f32[256,128]{1,0:T(8,128)S(1)}, f32[128,256]{1,0:T(8,128)S(1)}, f32[256,128]{1,0:T(8,128)S(1)}, f32[8,128]{1,0:T(8,128)S(1)}) custom-call(s32[1]{0:T(128)} %bitcast.half, bf16[256,8192]{1,0:T(8,128)(2,1)} %x_ref.7, bf16[256,1024]{1,0:T(8,128)(2,1)} %b_ref.7, f32[256,128]{1,0:T(8,128)} %step_ref.7, ...), custom_call_target="tpu_custom_call" | custom-call | tf_op jit(solution)/shard_map/send_state/pallas_call | solution.py:593
  3.5 2.9 %shard_map.64 = (bf16[136,4096]{1,0:T(8,128)(2,1)S(1)}, bf16[128,4096]{1,0:T(8,128)(2,1)S(1)}) custom-call(s32[1]{0:T(128)} %bitcast.1.half, bf16[256,8192]{1,0:T(8,128)(2,1)} %x_ref.7, bf16[256,1024]{1,0:T(8,128)(2,1)} %b_ref.7, f32[256,128]{1,0:T(8,128)S(1)} %get-tuple-element.33.factor, f32[8,128]{1,0:T(8,128)S(1)} %get-tuple-element.34.total), custom_call_target="tpu_custom_call" | custom-call | tf_op jit(solution)/shard_map/pallas_call | solution.py:615
  7.7 2.6 %collective-permute-start.1 = (bf16[32,2176]{1,0:T(8,128)(2,1)S(1)}, bf16[32,2176]{1,0:T(8,128)(2,1)S(1)}, u32[]{:S(2)}, u32[]{:S(2)}) collective-permute-start(bf16[32,2176]{1,0:T(8,128)(2,1)S(1)} %get-tuple-element.38), channel_id=1, source_target_pairs={{0,2},{2,0},{4,6},{6,4},{1,3},{3,1},{5,7},{7,5},{8,10},{10,8},{12,... | collective-permute-start | bytes 417800 | tf_op jit(solution)/shard_map/ppermute | solution.py:473
  10.3 2.6 %collective-permute-start.2 = (bf16[32,2176]{1,0:T(8,128)(2,1)S(1)}, bf16[32,2176]{1,0:T(8,128)(2,1)S(1)}, u32[]{:S(2)}, u32[]{:S(2)}) collective-permute-start(bf16[32,2176]{1,0:T(8,128)(2,1)S(1)} %get-tuple-element.39), channel_id=1, source_target_pairs={{0,4},{2,6},{4,0},{6,2},{1,5},{3,7},{5,1},{7,3},{8,12},{10,14},{12... | collective-permute-start | bytes 417800 | tf_op jit(solution)/shard_map/ppermute | solution.py:473
  14.7 3.5 %collective-permute-start.10 = (bf16[32,2176]{1,0:T(8,128)(2,1)S(1)}, bf16[32,2176]{1,0:T(8,128)(2,1)S(1)}, u32[]{:S(2)}, u32[]{:S(2)}) collective-permute-start(bf16[32,2176]{1,0:T(8,128)(2,1)S(1)} %get-tuple-element.49), channel_id=1, source_target_pairs={{0,4},{2,6},{4,0},{6,2},{1,5},{3,7},{5,1},{7,3},{8,12},{10,14},{12... | collective-permute-start | bytes 417800 | tf_op jit(solution)/shard_map/ppermute | solution.py:473
  18.2 2.2 %collective-permute-start.11 = (bf16[32,2176]{1,0:T(8,128)(2,1)S(1)}, bf16[32,2176]{1,0:T(8,128)(2,1)S(1)}, u32[]{:S(2)}, u32[]{:S(2)}) collective-permute-start(bf16[32,2176]{1,0:T(8,128)(2,1)S(1)} %get-tuple-element.50), channel_id=1, source_target_pairs={{0,6},{2,4},{4,2},{6,0},{1,7},{3,5},{5,3},{7,1},{8,14},{10,12},{12... | collective-permute-start | bytes 417800 | tf_op jit(solution)/shard_map/ppermute | solution.py:473
  20.4 3.4 %collective-permute-done.2.refs_2_ = bf16[32,2176]{1,0:T(8,128)(2,1)S(1)} collective-permute-done((bf16[32,2176]{1,0:T(8,128)(2,1)S(1)}, bf16[32,2176]{1,0:T(8,128)(2,1)S(1)}, u32[]{:S(2)}, u32[]{:S(2)}) %collective-permute-start.2) | collective-permute-done | bytes 139296 | tf_op jit(solution)/shard_map/ppermute | solution.py:473
  24.8 1.5 %collective-permute-start.4 = (bf16[32,2176]{1,0:T(8,128)(2,1)S(1)}, bf16[32,2176]{1,0:T(8,128)(2,1)S(1)}, u32[]{:S(2)}, u32[]{:S(2)}) collective-permute-start(bf16[32,2176]{1,0:T(8,128)(2,1)S(1)} %get-tuple-element.41.mine), channel_id=1, source_target_pairs={{0,8},{8,0},{16,24},{24,16},{1,9},{9,1},{17,25},{25,17},{2,10},{10... | collective-permute-start | bytes 417800 | tf_op jit(solution)/shard_map/ppermute | solution.py:503
  26.3 9.4 %collective-permute-done.10.refs_2_ = bf16[32,2176]{1,0:T(8,128)(2,1)S(1)} collective-permute-done((bf16[32,2176]{1,0:T(8,128)(2,1)S(1)}, bf16[32,2176]{1,0:T(8,128)(2,1)S(1)}, u32[]{:S(2)}, u32[]{:S(2)}) %collective-permute-start.10) | collective-permute-done | bytes 139296 | tf_op jit(solution)/shard_map/ppermute | solution.py:473
  36.8 1.5 %collective-permute-start.12 = (bf16[32,2176]{1,0:T(8,128)(2,1)S(1)}, bf16[32,2176]{1,0:T(8,128)(2,1)S(1)}, u32[]{:S(2)}, u32[]{:S(2)}) collective-permute-start(bf16[32,2176]{1,0:T(8,128)(2,1)S(1)} %get-tuple-element.51.mine), channel_id=1, source_target_pairs={{0,8},{8,0},{16,24},{24,16},{1,9},{9,1},{17,25},{25,17},{2,10},{10... | collective-permute-start | bytes 417800 | tf_op jit(solution)/shard_map/ppermute | solution.py:503
  39.2 1.6 %collective-permute-start.5 = (bf16[32,2176]{1,0:T(8,128)(2,1)S(1)}, bf16[32,2176]{1,0:T(8,128)(2,1)S(1)}, u32[]{:S(2)}, u32[]{:S(2)}) collective-permute-start(bf16[32,2176]{1,0:T(8,128)(2,1)S(1)} %shard_map.67), channel_id=1, source_target_pairs={{0,16},{8,24},{16,0},{24,8},{1,17},{9,25},{17,1},{25,9},{2,18},{10... | collective-permute-start | bytes 417800 | tf_op jit(solution)/shard_map/ppermute | solution.py:509
  42.8 1.6 %collective-permute-start.13 = (bf16[32,2176]{1,0:T(8,128)(2,1)S(1)}, bf16[32,2176]{1,0:T(8,128)(2,1)S(1)}, u32[]{:S(2)}, u32[]{:S(2)}) collective-permute-start(bf16[32,2176]{1,0:T(8,128)(2,1)S(1)} %shard_map.71), channel_id=1, source_target_pairs={{0,16},{8,24},{16,0},{24,8},{1,17},{9,25},{17,1},{25,9},{2,18},{10... | collective-permute-start | bytes 417800 | tf_op jit(solution)/shard_map/ppermute | solution.py:509
  46.7 2.1 %collective-permute-start.6 = (bf16[32,2048]{1,0:T(8,128)(2,1)S(1)}, bf16[32,2048]{1,0:T(8,128)(2,1)S(1)}, u32[]{:S(2)}, u32[]{:S(2)}) collective-permute-start(bf16[32,2048]{1,0:T(8,128)(2,1)S(1)} %get-tuple-element.44), channel_id=1, source_target_pairs={{0,2},{2,0},{4,6},{6,4},{1,3},{3,1},{5,7},{7,5},{8,10},{10,8},{12,... | collective-permute-start | bytes 393224 | tf_op jit(solution)/shard_map/ppermute | solution.py:473
  53.4 2.0 %collective-permute-start.15 = (bf16[32,2048]{1,0:T(8,128)(2,1)S(1)}, bf16[32,2048]{1,0:T(8,128)(2,1)S(1)}, u32[]{:S(2)}, u32[]{:S(2)}) collective-permute-start(bf16[32,2048]{1,0:T(8,128)(2,1)S(1)} %get-tuple-element.55), channel_id=1, source_target_pairs={{0,4},{2,6},{4,0},{6,2},{1,5},{3,7},{5,1},{7,3},{8,12},{10,14},{12... | collective-permute-start | bytes 393224 | tf_op jit(solution)/shard_map/ppermute | solution.py:473
  55.4 3.0 %collective-permute-start.16 = (bf16[32,2048]{1,0:T(8,128)(2,1)S(1)}, bf16[32,2048]{1,0:T(8,128)(2,1)S(1)}, u32[]{:S(2)}, u32[]{:S(2)}) collective-permute-start(bf16[32,2048]{1,0:T(8,128)(2,1)S(1)} %get-tuple-element.56), channel_id=1, source_target_pairs={{0,6},{2,4},{4,2},{6,0},{1,7},{3,5},{5,3},{7,1},{8,14},{10,12},{12... | collective-permute-start | bytes 393224 | tf_op jit(solution)/shard_map/ppermute | solution.py:473
  58.4 3.2 %collective-permute-done.7.refs_2_ = bf16[32,2048]{1,0:T(8,128)(2,1)S(1)} collective-permute-done((bf16[32,2048]{1,0:T(8,128)(2,1)S(1)}, bf16[32,2048]{1,0:T(8,128)(2,1)S(1)}, u32[]{:S(2)}, u32[]{:S(2)}) %collective-permute-start.7) | collective-permute-done | bytes 131104 | tf_op jit(solution)/shard_map/ppermute | solution.py:473
  61.6 1.5 %collective-permute-start.18 = (bf16[136,4096]{1,0:T(8,128)(2,1)S(1)}, bf16[136,4096]{1,0:T(8,128)(2,1)S(1)}, u32[]{:S(2)}, u32[]{:S(2)}) collective-permute-start(bf16[136,4096]{1,0:T(8,128)(2,1)S(1)} %get-tuple-element.35.own), channel_id=1, source_target_pairs={{0,1},{2,3},{4,5},{6,7},{8,9},{10,11},{12,13},{14,15},{16,17},{18,... | collective-permute-start | bytes 3342344 | tf_op jit(solution)/shard_map/ppermute | solution.py:624
  63.2 7.2 %collective-permute-done.15.refs_6_ = bf16[32,2048]{1,0:T(8,128)(2,1)S(1)} collective-permute-done((bf16[32,2048]{1,0:T(8,128)(2,1)S(1)}, bf16[32,2048]{1,0:T(8,128)(2,1)S(1)}, u32[]{:S(2)}, u32[]{:S(2)}) %collective-permute-start.15) | collective-permute-done | bytes 131104 | tf_op jit(solution)/shard_map/ppermute | solution.py:473
  71.3 4.8 %within.7.refs_1_ = bf16[256,2048]{1,0:T(8,128)(2,1)S(1)} custom-call(s32[3]{0:T(128)S(1)} %get-tuple-element.64.at, bf16[256,8192]{1,0:T(8,128)(2,1)} %x_ref.7, bf16[256,1024]{1,0:T(8,128)(2,1)} %b_ref.7, bf16[256,1024]{1,0:T(8,128)(2,1)S(1)} %copy-done, f32[256,128]{1,0:T(8,128)} %step_ref.7, f32[256,128]{1,0:T(8,128)S(1)} %get-tuple-element.57.run_ref.run, ...), custom_call_target="tpu_custom_call" | custom-call | tf_op jit(solution)/shard_map/within/pallas_call | solution.py:627
  76.1 4.9 %within.6.refs_0_ = bf16[256,2048]{1,0:T(8,128)(2,1)S(1)} custom-call(s32[3]{0:T(128)S(1)} %get-tuple-element.63.at, bf16[256,8192]{1,0:T(8,128)(2,1)} %x_ref.7, bf16[256,1024]{1,0:T(8,128)(2,1)} %b_ref.7, bf16[256,1024]{1,0:T(8,128)(2,1)S(1)} %copy-done, f32[256,128]{1,0:T(8,128)} %step_ref.7, f32[256,128]{1,0:T(8,128)S(1)} %get-tuple-element.57.run_ref.run, ...), custom_call_target="tpu_custom_call" | custom-call | tf_op jit(solution)/shard_map/within/pallas_call | solution.py:627
  81.0 4.8 %within.5.refs_1_ = bf16[256,2048]{1,0:T(8,128)(2,1)S(1)} custom-call(s32[3]{0:T(128)S(1)} %get-tuple-element.62.at, bf16[256,8192]{1,0:T(8,128)(2,1)} %x_ref.7, bf16[256,1024]{1,0:T(8,128)(2,1)} %b_ref.7, bf16[256,1024]{1,0:T(8,128)(2,1)S(1)} %copy-done, f32[256,128]{1,0:T(8,128)} %step_ref.7, f32[256,128]{1,0:T(8,128)S(1)} %get-tuple-element.57.run_ref.run, ...), custom_call_target="tpu_custom_call" | custom-call | tf_op jit(solution)/shard_map/within/pallas_call | solution.py:627
  85.9 4.8 %within.4.refs_0_ = bf16[256,2048]{1,0:T(8,128)(2,1)S(1)} custom-call(s32[3]{0:T(128)S(1)} %get-tuple-element.61.at, bf16[256,8192]{1,0:T(8,128)(2,1)} %x_ref.7, bf16[256,1024]{1,0:T(8,128)(2,1)} %b_ref.7, bf16[256,1024]{1,0:T(8,128)(2,1)S(1)} %copy-done, f32[256,128]{1,0:T(8,128)} %step_ref.7, f32[256,128]{1,0:T(8,128)S(1)} %get-tuple-element.57.run_ref.run, ...), custom_call_target="tpu_custom_call" | custom-call | tf_op jit(solution)/shard_map/within/pallas_call | solution.py:627
  90.7 2.3 %shard_map.74.refs_2_ = bf16[256,8192]{1,0:T(8,128)(2,1)} custom-call(s32[1]{0:T(128)} %bitcast.1.half, bf16[256,1024]{1,0:T(8,128)(2,1)S(1)} %copy-done, bf16[128,4096]{1,0:T(8,128)(2,1)S(1)} %shard_map.73.state, f32[256,128]{1,0:T(8,128)S(1)} %get-tuple-element.57.run_ref.run, f32[8,128]{1,0:T(8,128)S(1)} %get-tuple-element.58.base, ...), custom_call_target="tpu_custom_call" | custom-call | tf_op jit(solution)/shard_map/pallas_call | solution.py:671
  93.0 2.3 %finish_other.1 = bf16[256,8192]{1,0:T(8,128)(2,1)} custom-call(s32[1]{0:T(128)} %bitcast.half, bf16[256,1024]{1,0:T(8,128)(2,1)S(1)} %copy-done, bf16[128,4096]{1,0:T(8,128)(2,1)S(1)} %collective-permute-done.17.state, f32[256,128]{1,0:T(8,128)S(1)} %get-tuple-element.57.run_ref.run, ...), custom_call_target="tpu_custom_call", output_to_operand_aliasing={{}: (8, {})} | custom-call | tf_op jit(solution)/shard_map/finish_other/pallas_call | solution.py:674
  (38 shorter events, 16.5 us)
Async XLA Ops:
  2.9 3.5 %collective-permute-start = (bf16[136,4096]{1,0:T(8,128)(2,1)S(1)}, bf16[136,4096]{1,0:T(8,128)(2,1)S(1)}, u32[]{:S(2)}, u32[]{:S(2)}) collective-permute-start(bf16[136,4096]{1,0:T(8,128)(2,1)S(1)} %get-tuple-element.36), channel_id=1, source_target_pairs={{0,1},{1,0},{2,3},{3,2},{4,5},{5,4},{6,7},{7,6},{8,9},{9,8},{10,11... | collective-permute-start | bytes 3342344 | tf_op jit(solution)/shard_map/ppermute | solution.py:613
  7.7 10.5 %collective-permute-start.1 = (bf16[32,2176]{1,0:T(8,128)(2,1)S(1)}, bf16[32,2176]{1,0:T(8,128)(2,1)S(1)}, u32[]{:S(2)}, u32[]{:S(2)}) collective-permute-start(bf16[32,2176]{1,0:T(8,128)(2,1)S(1)} %get-tuple-element.38), channel_id=1, source_target_pairs={{0,2},{2,0},{4,6},{6,4},{1,3},{3,1},{5,7},{7,5},{8,10},{10,8},{12,... | collective-permute-start | bytes 417800 | tf_op jit(solution)/shard_map/ppermute | solution.py:473
  10.3 13.5 %collective-permute-start.2 = (bf16[32,2176]{1,0:T(8,128)(2,1)S(1)}, bf16[32,2176]{1,0:T(8,128)(2,1)S(1)}, u32[]{:S(2)}, u32[]{:S(2)}) collective-permute-start(bf16[32,2176]{1,0:T(8,128)(2,1)S(1)} %get-tuple-element.39), channel_id=1, source_target_pairs={{0,4},{2,6},{4,0},{6,2},{1,5},{3,7},{5,1},{7,3},{8,12},{10,14},{12... | collective-permute-start | bytes 417800 | tf_op jit(solution)/shard_map/ppermute | solution.py:473
  12.9 10.9 %collective-permute-start.3 = (bf16[32,2176]{1,0:T(8,128)(2,1)S(1)}, bf16[32,2176]{1,0:T(8,128)(2,1)S(1)}, u32[]{:S(2)}, u32[]{:S(2)}) collective-permute-start(bf16[32,2176]{1,0:T(8,128)(2,1)S(1)} %get-tuple-element.40), channel_id=1, source_target_pairs={{0,6},{2,4},{4,2},{6,0},{1,7},{3,5},{5,3},{7,1},{8,14},{10,12},{12... | collective-permute-start | bytes 417800 | tf_op jit(solution)/shard_map/ppermute | solution.py:473
  13.7 12.6 %collective-permute-start.9 = (bf16[32,2176]{1,0:T(8,128)(2,1)S(1)}, bf16[32,2176]{1,0:T(8,128)(2,1)S(1)}, u32[]{:S(2)}, u32[]{:S(2)}) collective-permute-start(bf16[32,2176]{1,0:T(8,128)(2,1)S(1)} %get-tuple-element.48), channel_id=1, source_target_pairs={{0,2},{2,0},{4,6},{6,4},{1,3},{3,1},{5,7},{7,5},{8,10},{10,8},{12,... | collective-permute-start | bytes 417800 | tf_op jit(solution)/shard_map/ppermute | solution.py:473
  14.7 21.0 %collective-permute-start.10 = (bf16[32,2176]{1,0:T(8,128)(2,1)S(1)}, bf16[32,2176]{1,0:T(8,128)(2,1)S(1)}, u32[]{:S(2)}, u32[]{:S(2)}) collective-permute-start(bf16[32,2176]{1,0:T(8,128)(2,1)S(1)} %get-tuple-element.49), channel_id=1, source_target_pairs={{0,4},{2,6},{4,0},{6,2},{1,5},{3,7},{5,1},{7,3},{8,12},{10,14},{12... | collective-permute-start | bytes 417800 | tf_op jit(solution)/shard_map/ppermute | solution.py:473
  18.2 17.6 %collective-permute-start.11 = (bf16[32,2176]{1,0:T(8,128)(2,1)S(1)}, bf16[32,2176]{1,0:T(8,128)(2,1)S(1)}, u32[]{:S(2)}, u32[]{:S(2)}) collective-permute-start(bf16[32,2176]{1,0:T(8,128)(2,1)S(1)} %get-tuple-element.50), channel_id=1, source_target_pairs={{0,6},{2,4},{4,2},{6,0},{1,7},{3,5},{5,3},{7,1},{8,14},{10,12},{12... | collective-permute-start | bytes 417800 | tf_op jit(solution)/shard_map/ppermute | solution.py:473
  24.8 13.5 %collective-permute-start.4 = (bf16[32,2176]{1,0:T(8,128)(2,1)S(1)}, bf16[32,2176]{1,0:T(8,128)(2,1)S(1)}, u32[]{:S(2)}, u32[]{:S(2)}) collective-permute-start(bf16[32,2176]{1,0:T(8,128)(2,1)S(1)} %get-tuple-element.41.mine), channel_id=1, source_target_pairs={{0,8},{8,0},{16,24},{24,16},{1,9},{9,1},{17,25},{25,17},{2,10},{10... | collective-permute-start | bytes 417800 | tf_op jit(solution)/shard_map/ppermute | solution.py:503
  36.8 5.1 %collective-permute-start.12 = (bf16[32,2176]{1,0:T(8,128)(2,1)S(1)}, bf16[32,2176]{1,0:T(8,128)(2,1)S(1)}, u32[]{:S(2)}, u32[]{:S(2)}) collective-permute-start(bf16[32,2176]{1,0:T(8,128)(2,1)S(1)} %get-tuple-element.51.mine), channel_id=1, source_target_pairs={{0,8},{8,0},{16,24},{24,16},{1,9},{9,1},{17,25},{25,17},{2,10},{10... | collective-permute-start | bytes 417800 | tf_op jit(solution)/shard_map/ppermute | solution.py:503
  39.2 6.5 %collective-permute-start.5 = (bf16[32,2176]{1,0:T(8,128)(2,1)S(1)}, bf16[32,2176]{1,0:T(8,128)(2,1)S(1)}, u32[]{:S(2)}, u32[]{:S(2)}) collective-permute-start(bf16[32,2176]{1,0:T(8,128)(2,1)S(1)} %shard_map.67), channel_id=1, source_target_pairs={{0,16},{8,24},{16,0},{24,8},{1,17},{9,25},{17,1},{25,9},{2,18},{10... | collective-permute-start | bytes 417800 | tf_op jit(solution)/shard_map/ppermute | solution.py:509
  42.8 8.4 %collective-permute-start.13 = (bf16[32,2176]{1,0:T(8,128)(2,1)S(1)}, bf16[32,2176]{1,0:T(8,128)(2,1)S(1)}, u32[]{:S(2)}, u32[]{:S(2)}) collective-permute-start(bf16[32,2176]{1,0:T(8,128)(2,1)S(1)} %shard_map.71), channel_id=1, source_target_pairs={{0,16},{8,24},{16,0},{24,8},{1,17},{9,25},{17,1},{25,9},{2,18},{10... | collective-permute-start | bytes 417800 | tf_op jit(solution)/shard_map/ppermute | solution.py:509
  46.7 8.7 %collective-permute-start.6 = (bf16[32,2048]{1,0:T(8,128)(2,1)S(1)}, bf16[32,2048]{1,0:T(8,128)(2,1)S(1)}, u32[]{:S(2)}, u32[]{:S(2)}) collective-permute-start(bf16[32,2048]{1,0:T(8,128)(2,1)S(1)} %get-tuple-element.44), channel_id=1, source_target_pairs={{0,2},{2,0},{4,6},{6,4},{1,3},{3,1},{5,7},{7,5},{8,10},{10,8},{12,... | collective-permute-start | bytes 393224 | tf_op jit(solution)/shard_map/ppermute | solution.py:473
  48.8 12.8 %collective-permute-start.7 = (bf16[32,2048]{1,0:T(8,128)(2,1)S(1)}, bf16[32,2048]{1,0:T(8,128)(2,1)S(1)}, u32[]{:S(2)}, u32[]{:S(2)}) collective-permute-start(bf16[32,2048]{1,0:T(8,128)(2,1)S(1)} %get-tuple-element.45), channel_id=1, source_target_pairs={{0,4},{2,6},{4,0},{6,2},{1,5},{3,7},{5,1},{7,3},{8,12},{10,14},{12... | collective-permute-start | bytes 393224 | tf_op jit(solution)/shard_map/ppermute | solution.py:473
  49.9 13.3 %collective-permute-start.8 = (bf16[32,2048]{1,0:T(8,128)(2,1)S(1)}, bf16[32,2048]{1,0:T(8,128)(2,1)S(1)}, u32[]{:S(2)}, u32[]{:S(2)}) collective-permute-start(bf16[32,2048]{1,0:T(8,128)(2,1)S(1)} %get-tuple-element.46), channel_id=1, source_target_pairs={{0,6},{2,4},{4,2},{6,0},{1,7},{3,5},{5,3},{7,1},{8,14},{10,12},{12... | collective-permute-start | bytes 393224 | tf_op jit(solution)/shard_map/ppermute | solution.py:473
  52.3 19.0 %copy-start = (bf16[256,1024]{1,0:T(8,128)(2,1)S(1)}, bf16[256,1024]{1,0:T(8,128)(2,1)}, u32[]{:S(2)}) copy-start(bf16[256,1024]{1,0:T(8,128)(2,1)} %c.3) | copy-start | bytes 1572868
  52.3 19.0 %copy-start.1 = (f32[128]{0:T(128)S(1)}, f32[128]{0:T(128)}, u32[]{:S(2)}) copy-start(f32[128]{0:T(128)} %param.11) | copy-start | bytes 1540
  52.3 10.8 %collective-permute-start.14 = (bf16[32,2048]{1,0:T(8,128)(2,1)S(1)}, bf16[32,2048]{1,0:T(8,128)(2,1)S(1)}, u32[]{:S(2)}, u32[]{:S(2)}) collective-permute-start(bf16[32,2048]{1,0:T(8,128)(2,1)S(1)} %get-tuple-element.54), channel_id=1, source_target_pairs={{0,2},{2,0},{4,6},{6,4},{1,3},{3,1},{5,7},{7,5},{8,10},{10,8},{12,... | collective-permute-start | bytes 393224 | tf_op jit(solution)/shard_map/ppermute | solution.py:473
  53.4 17.0 %collective-permute-start.15 = (bf16[32,2048]{1,0:T(8,128)(2,1)S(1)}, bf16[32,2048]{1,0:T(8,128)(2,1)S(1)}, u32[]{:S(2)}, u32[]{:S(2)}) collective-permute-start(bf16[32,2048]{1,0:T(8,128)(2,1)S(1)} %get-tuple-element.55), channel_id=1, source_target_pairs={{0,4},{2,6},{4,0},{6,2},{1,5},{3,7},{5,1},{7,3},{8,12},{10,14},{12... | collective-permute-start | bytes 393224 | tf_op jit(solution)/shard_map/ppermute | solution.py:473
  55.4 15.0 %collective-permute-start.16 = (bf16[32,2048]{1,0:T(8,128)(2,1)S(1)}, bf16[32,2048]{1,0:T(8,128)(2,1)S(1)}, u32[]{:S(2)}, u32[]{:S(2)}) collective-permute-start(bf16[32,2048]{1,0:T(8,128)(2,1)S(1)} %get-tuple-element.56), channel_id=1, source_target_pairs={{0,6},{2,4},{4,2},{6,0},{1,7},{3,5},{5,3},{7,1},{8,14},{10,12},{12... | collective-permute-start | bytes 393224 | tf_op jit(solution)/shard_map/ppermute | solution.py:473
  61.6 19.4 %collective-permute-start.18 = (bf16[136,4096]{1,0:T(8,128)(2,1)S(1)}, bf16[136,4096]{1,0:T(8,128)(2,1)S(1)}, u32[]{:S(2)}, u32[]{:S(2)}) collective-permute-start(bf16[136,4096]{1,0:T(8,128)(2,1)S(1)} %get-tuple-element.35.own), channel_id=1, source_target_pairs={{0,1},{2,3},{4,5},{6,7},{8,9},{10,11},{12,13},{14,15},{16,17},{18,... | collective-permute-start | bytes 3342344 | tf_op jit(solution)/shard_map/ppermute | solution.py:624
  71.1 21.9 %collective-permute-start.17 = (bf16[128,4096]{1,0:T(8,128)(2,1)S(1)}, bf16[128,4096]{1,0:T(8,128)(2,1)S(1)}, u32[]{:S(2)}, u32[]{:S(2)}) collective-permute-start(bf16[128,4096]{1,0:T(8,128)(2,1)S(1)} %shard_map.73.state), channel_id=1, source_target_pairs={{0,1},{1,0},{2,3},{3,2},{4,5},{5,4},{6,7},{7,6},{8,9},{9,8},{10,11... | collective-permute-start | bytes 3145736 | tf_op jit(solution)/shard_map/ppermute | solution.py:666

commit v8 on v7

--- a/solution.py
+++ b/solution.py
@@ -142,6 +142,8 @@
 
 def send_state_kernel(
     half,
+    chip,
+    outer,
     x,
     b,
     step,
@@ -160,6 +162,7 @@
     *,
     dims,
 ):
+    del chip, outer
     first = pltpu.make_async_copy(log, log_here, sems.at[2 * dims[0]])
     second = pltpu.make_async_copy(step, step_here, sems.at[2 * dims[0] + 1])
     first.start()
@@ -234,6 +237,13 @@
     out[:, cols:] = jnp.concatenate([packed_decay] * (states // ROW_TILE), axis=0).astype(BF16)
 
 
+def placed(kernel):
+    def body(core, chip, outer, *refs, **options):
+        return kernel((core[0], chip[0], outer[0]), *refs, **options)
+
+    return body
+
+
 def pieces_kernel(at, own, got, total, *outs, states, chunk):
     base_out = outs[-1]
     first = at[0] == 0
@@ -353,14 +363,21 @@
 
 
 def within_kernel(
-    at, x_ref, b_ref, c_ref, step_ref, run_ref, run_t_ref, skip_ref, before_ref, out, matrix, *, dims
+    half, flag, x_ref, b_ref, c_ref, step_ref, run_ref, run_t_ref, skip_ref, before_ref, out, matrix, *, dims, first_group
 ):
     per_half, per_group, width = dims
     turn = pl.program_id(0)
-    group = at[0] * per_half + at[2] + turn
-    head = group * per_group
+    place = first_group + turn
+    head = (half[0] * per_half + place) * per_group
     rows = x_ref.shape[0]
     pair = LANES // width
+    group_cols = per_group * width
+    states = b_ref.shape[1] // per_half
+    x_ref = x_ref.at[:, pl.ds(pl.multiple_of(place * group_cols, group_cols), group_cols)]
+    b_ref = b_ref.at[:, pl.ds(pl.multiple_of(place * states, states), states)]
+    c_ref = c_ref.at[:, pl.ds(pl.multiple_of((half[0] * per_half + place) * states, states), states)]
+    before_ref = before_ref.at[:states, pl.ds(pl.multiple_of(place * group_cols, group_cols), group_cols)]
+    out = out.at[:, pl.ds(pl.multiple_of(turn * group_cols, group_cols), group_cols)]
 
     @pl.when(turn == 0)
     def _():
@@ -375,7 +392,7 @@
     run_t = run_t_ref[pl.ds(pl.multiple_of(head, per_group), per_group), :]
     x = x_ref[...].astype(F32)
     scaled = (x * spread(step)).astype(BF16)
-    before = dot(c_ref[...], before_ref[...] * at[1].astype(BF16))
+    before = dot(c_ref[...], before_ref[...] * flag[0].astype(BF16))
     outer = spread(skip)[:1, :] * x + spread(jnp.exp2(run)) * before
     lane = lax.broadcasted_iota(jnp.int32, (HALF_ROWS, LANES), 1) // width
     lower = lax.broadcasted_iota(jnp.int32, (HALF_ROWS, HALF_ROWS), 1) <= lax.broadcasted_iota(
@@ -407,25 +424,27 @@
             out[start:stop, cols] = (added[:, cols] + part).astype(BF16)
 
 
-def add_carried(half, within, rows_c, state, run, base, out, result, matrix, sems, dims):
-    per_half, group_cols, _ = dims
-    operand = packed_half(jnp.exp2(run[...] + base[:1, :]), half)
+def final_kernel(half, c, state, run, base, matrix, within, *refs, dims):
+    out, result, sems = refs[-3:]
+    per_half, group_cols, states, first = dims
+    operand = packed_half(jnp.exp2(run[...] + base[:1, :]), half[0])
     copies = []
-    for k in range(per_half):
-        rows = rows_c(k)
-        part = within(k)
+    for k in range(state.shape[1] // group_cols):
+        group = half[0] * per_half + first + k
+        rows = c[:, pl.ds(pl.multiple_of(group * states, states), states)]
         tiles = group_cols // TILE
         products = {}
         for n in range(tiles + AHEAD):
             if n < tiles:
-                cols = slice(k * group_cols + n * TILE, k * group_cols + (n + 1) * TILE)
-                products[n] = dot(rows, state[:, cols]), dot(operand, matrix[:, cols])
+                start = k * group_cols + n * TILE
+                spread = matrix[:, first * group_cols + start : first * group_cols + start + TILE]
+                products[n] = dot(rows, state[:, start : start + TILE]), dot(operand, spread)
             m = n - AHEAD
             if m >= 0:
                 cols = slice(k * group_cols + m * TILE, k * group_cols + (m + 1) * TILE)
                 carried, factor = products.pop(m)
-                result[:, cols] = (part[:, m * TILE : (m + 1) * TILE].astype(F32) + factor * carried).astype(BF16)
-        home = pl.multiple_of((half * per_half + k) * group_cols, group_cols)
+                result[:, cols] = (within[:, cols].astype(F32) + factor * carried).astype(BF16)
+        home = pl.multiple_of(group * group_cols, group_cols)
         copies.append(
             pltpu.make_async_copy(
                 result.at[:, pl.ds(k * group_cols, group_cols)], out.at[:, pl.ds(home, group_cols)], sems.at[k]
@@ -434,21 +453,6 @@
         copies[-1].start()
     for copy in copies:
         copy.wait()
-
-
-def final_kernel(half, c, state, run, base, matrix, *refs, dims, parts):
-    within = refs[:parts]
-    out, result, stores = refs[-3:]
-    per_half, group_cols, states = dims
-    each = per_half // parts
-
-    def part(k):
-        return within[k // each][:, k % each * group_cols : (k % each + 1) * group_cols]
-
-    def rows_c(k):
-        return c[:, pl.ds(pl.multiple_of((half[0] * per_half + k) * states, states), states)]
-
-    add_carried(half[0], part, rows_c, state, run, base, out, result, matrix, stores, dims)
 
 
 def small_call(kernel, in_specs, out_shape, scratch=(), out_specs=None):
@@ -486,38 +490,38 @@
     gathered = []
     for chunk in range(CHUNKS):
         *pieces, base = small_call(
-            functools.partial(pieces_kernel, states=states, chunk=chunk),
-            [smem] + [vmem] * 3,
+            functools.partial(placed(pieces_kernel), states=states, chunk=chunk),
+            [smem] * 3 + [vmem] * 3,
             [shape((rows, cols + heads), BF16)] * count + [shape((ROW_TILE, heads), F32)],
-        )(at, own, got, total)
+        )(*at, own, got, total)
         gathered.append(swapped(pieces, chip_axis))
     entering = []
     for chunk in range(CHUNKS):
         first_head = chunk * cols // width
         pieces = gathered[chunk]
         column, decay = small_call(
-            functools.partial(column_kernel, first_head=first_head, width=width, count=count),
-            [smem] + [vmem] * count,
+            functools.partial(placed(column_kernel), first_head=first_head, width=width, count=count),
+            [smem] * 3 + [vmem] * count,
             [shape((rows, cols + heads), BF16), shape((ROW_TILE, cols), F32)],
-        )(at, *pieces)
+        )(*at, *pieces)
         neighbour = lax.ppermute(column, outer_axis, xor_route(4, 1))
         (pair,) = small_call(
-            functools.partial(pair_kernel, first_head=first_head, width=width, cols=cols),
-            [smem] + [vmem] * 2,
+            functools.partial(placed(pair_kernel), first_head=first_head, width=width, cols=cols),
+            [smem] * 3 + [vmem] * 2,
             [shape((rows, cols + heads), BF16)],
-        )(at, column, neighbour)
+        )(*at, column, neighbour)
         pair = lax.ppermute(pair, outer_axis, xor_route(4, 2))
         states_out = small_call(
-            functools.partial(chips_kernel, first_head=first_head, width=width, count=count),
-            [smem] + [vmem] * (count + 3),
+            functools.partial(placed(chips_kernel), first_head=first_head, width=width, count=count),
+            [smem] * 3 + [vmem] * (count + 3),
             [shape((rows, cols), BF16)] * count,
-        )(at, neighbour, pair, decay, *pieces)
-        entering += swapped(states_out, chip_axis)
-    (entering,) = small_call(
-        functools.partial(assemble_kernel, count=count),
-        [smem] + [vmem] * len(entering),
-        [shape((states, half_cols), BF16)],
-    )(at, *entering)
+        )(*at, neighbour, pair, decay, *pieces)
+        states_out = swapped(states_out, chip_axis)
+        entering += small_call(
+            functools.partial(placed(assemble_kernel), count=count),
+            [smem] * 3 + [vmem] * count,
+            [shape((states, cols), BF16)],
+        )(*at, *states_out)
     return entering, base
 
 
@@ -529,10 +533,10 @@
     smem = pl.BlockSpec(memory_space=pltpu.SMEM)
     vmem = pl.BlockSpec(memory_space=pltpu.VMEM)
     chip_total, base = small_call(
-        chip_total_kernel,
-        [smem] + [vmem] * 3,
+        placed(chip_total_kernel),
+        [smem] * 3 + [vmem] * 3,
         [jax.ShapeDtypeStruct((states, half_cols + heads), BF16), jax.ShapeDtypeStruct((ROW_TILE, heads), F32)],
-    )(at, own, got, total)
+    )(*at, own, got, total)
     sent = lax.all_to_all(
         chip_total.reshape(chips, rows, half_cols + heads),
         (outer_axis, chip_axis),
@@ -549,7 +553,8 @@
         [pl.BlockSpec(memory_space=pltpu.HBM)],
     )(sent)
     entering = lax.all_to_all(entering, (outer_axis, chip_axis), split_axis=0, concat_axis=0, tiled=True)
-    return entering.reshape(states, half_cols), base
+    entering = entering.reshape(states, half_cols)
+    return jnp.split(entering, CHUNKS, axis=1), base
 
 
 def local(inputs, step_size, log_decay, b_matrix, c_matrix, skip_gain, *, outer_axis, chip_axis, core_axis):
@@ -568,89 +573,76 @@
     core = lax.axis_index(core_axis).astype(jnp.int32)
     mine = core.reshape(1)
     other = (1 - core).reshape(1)
-    at = jnp.stack([core, lax.axis_index(chip_axis).astype(jnp.int32), lax.axis_index(outer_axis).astype(jnp.int32)])
+    at = (mine,) + tuple(lax.axis_index(axis).astype(jnp.int32).reshape(1) for axis in (chip_axis, outer_axis))
 
     smem = pl.BlockSpec(memory_space=pltpu.SMEM)
     vmem = pl.BlockSpec(memory_space=pltpu.VMEM)
     hbm = pl.BlockSpec(memory_space=pltpu.HBM)
 
-    def whole(shape):
-        return pl.BlockSpec(shape, lambda i, *_: (0,) * len(shape))
-
-    def by_group(cols):
-        return pl.BlockSpec((tokens, cols), lambda i, at: (0, at[0] * per_half + at[2] + i))
-
     state_dims = (per_half, group_cols, states)
     half_dims = (per_half, per_group, width)
-    half_scratch = [
-        pltpu.VMEM((tokens, half_cols), BF16),
-        pltpu.VMEM((tokens, per_half * states), BF16),
+    half_inputs = [
+        jax.ShapeDtypeStruct((tokens, half_cols), BF16),
+        jax.ShapeDtypeStruct((tokens, per_half * states), BF16),
     ]
 
+    whole_step = step_size
     inputs, step_size, log_decay, b_matrix = (
         pltpu.with_memory_space_constraint(array, pltpu.HBM) for array in (inputs, step_size, log_decay, b_matrix)
     )
-    send, run, run_t, factor, total = pl.pallas_call(
+    send, run, run_t, factor, total, other_x, other_b = pl.pallas_call(
         functools.partial(send_state_kernel, dims=state_dims),
-        in_specs=[smem, hbm, hbm, hbm, hbm],
-        out_specs=[vmem] * 5,
+        in_specs=[smem] * 3 + [hbm] * 4,
+        out_specs=[vmem] * 7,
         out_shape=[
             jax.ShapeDtypeStruct((tall, half_cols), BF16),
             jax.ShapeDtypeStruct((tokens, heads), F32),
             jax.ShapeDtypeStruct((heads, tokens), F32),
             jax.ShapeDtypeStruct((tokens, heads), F32),
             jax.ShapeDtypeStruct((ROW_TILE, heads), F32),
-        ],
-        scratch_shapes=half_scratch
-        + [pltpu.VMEM((heads, half_cols), BF16)]
+        ]
+        + half_inputs,
+        scratch_shapes=[pltpu.VMEM((heads, half_cols), BF16)]
         + [pltpu.VMEM((tokens, heads), F32)] * 2
         + [pltpu.SemaphoreType.DMA((2 * per_half + 2,))],
         compiler_params=plain_params(),
         name="send_state",
-    )(other, inputs, b_matrix, step_size, log_decay)
+    )(other, *at[1:], inputs, b_matrix, step_size, log_decay)
 
     swap = [(0, 1), (1, 0)]
     got = lax.ppermute(send, core_axis, swap)
 
-    own, matrix = small_call(
+    own, matrix, own_x, own_b = small_call(
         functools.partial(own_state_kernel, dims=state_dims),
         [smem, hbm, hbm, vmem, vmem],
-        [jax.ShapeDtypeStruct((tall, half_cols), BF16), jax.ShapeDtypeStruct((heads, half_cols), BF16)],
-        half_scratch + [pltpu.SemaphoreType.DMA((2 * per_half,))],
+        [jax.ShapeDtypeStruct((tall, half_cols), BF16), jax.ShapeDtypeStruct((heads, half_cols), BF16)] + half_inputs,
+        [pltpu.SemaphoreType.DMA((2 * per_half,))],
     )(mine, inputs, b_matrix, factor, total)
 
     find_entering = entering_by_swaps if by_swaps else entering_by_all_to_all
     entering, base = find_entering(at, own, got, total, width, states, outer_axis, chip_axis)
     late = lax.ppermute(own, core_axis, swap[:1])
 
-    def within(half, before, first):
+    def within(half, x, b, before, first):
         return pl.pallas_call(
-            functools.partial(within_kernel, dims=half_dims),
+            functools.partial(within_kernel, dims=half_dims, first_group=first),
             grid_spec=pltpu.PrefetchScalarGridSpec(
-                num_scalar_prefetch=1,
+                num_scalar_prefetch=2,
                 grid=(PER_CALL,),
-                in_specs=[
-                    by_group(group_cols),
-                    by_group(states),
-                    by_group(states),
-                    whole((tokens, heads)),
-                    whole((tokens, heads)),
-                    whole((heads, tokens)),
-                    whole((1, heads)),
-                    pl.BlockSpec((states, group_cols), lambda i, at: (0, at[2] + i)),
-                ],
-                out_specs=pl.BlockSpec((tokens, group_cols), lambda i, at: (0, i)),
+                in_specs=[vmem] * 8,
+                out_specs=vmem,
                 scratch_shapes=[pltpu.VMEM((2 * per_group, group_cols), BF16)],
             ),
             out_shape=jax.ShapeDtypeStruct((tokens, PER_CALL * group_cols), BF16),
             compiler_params=params(),
             name="within",
         )(
-            jnp.concatenate([half, mine, jnp.full((1,), first, jnp.int32)]),
-            inputs,
-            b_matrix,
+            half,
+            mine,
+            x,
+            b,
             c_matrix,
-            step_size,
+            whole_step,
             run,
             run_t,
             skip_gain.reshape(1, heads),
@@ -660,27 +652,30 @@
     own_within = []
     other_within = []
     for first in range(0, per_half, PER_CALL):
-        own_within.append(within(mine, got, first))
-        other_within.append(within(other, late, first))
-
-    got_entering = lax.ppermute(entering, core_axis, swap)
+        own_within.append(within(mine, own_x, own_b, got, first))
+        other_within.append(within(other, other_x, other_b, late, first))
+
     mixed = jax.ShapeDtypeStruct((tokens, channels), BF16)
-    final_scratch = [pltpu.VMEM((tokens, half_cols), BF16), pltpu.SemaphoreType.DMA((per_half,))]
-    parts = len(own_within)
-    final = functools.partial(final_kernel, dims=state_dims, parts=parts)
-    (result,) = small_call(
-        final, [smem] + [vmem] * (5 + parts), [mixed], final_scratch, [hbm]
-    )(mine, c_matrix, entering, run, base, matrix, *own_within)
-    return pl.pallas_call(
-        final,
-        in_specs=[smem] + [vmem] * (5 + parts) + [hbm],
-        out_specs=hbm,
-        out_shape=mixed,
-        scratch_shapes=final_scratch,
-        input_output_aliases={6 + parts: 0},
-        compiler_params=plain_params(),
-        name="finish_other",
-    )(other, c_matrix, got_entering, run, base, matrix, *other_within, result)
+
+    def finish(half, chunk, state, part, *result):
+        cols = PER_CALL * group_cols
+        return pl.pallas_call(
+            functools.partial(final_kernel, dims=state_dims + (chunk * PER_CALL,)),
+            in_specs=[smem] + [vmem] * 6 + [hbm] * len(result),
+            out_specs=hbm,
+            out_shape=mixed,
+            scratch_shapes=[pltpu.VMEM((tokens, cols), BF16), pltpu.SemaphoreType.DMA((PER_CALL,))],
+            input_output_aliases={7: 0} if result else {},
+            compiler_params=plain_params(),
+            name="finish",
+        )(half, c_matrix, state, run, base, matrix, part, *result)
+
+    result = ()
+    for chunk in reversed(range(CHUNKS)):
+        got_entering = lax.ppermute(entering[chunk], core_axis, swap)
+        result = (finish(mine, chunk, entering[chunk], own_within[chunk], *result),)
+        result = (finish(other, chunk, got_entering, other_within[chunk], *result),)
+    return result[0]
 
 
 def solution(mesh):

time: 95.8 us -> 87.8 us (0.916)
  Pallas kernels: 38.4 us -> 28.8 us
  waiting for transfers between devices: 25.7 us -> 29 us
  starting transfers between devices: 30.8 us -> 29.3 us
    pallas_call x15 -> x18, Pallas kernels: 32.6 us -> 23 us  [the longest x4 12.2 us: within(): pl.pallas_call(functools.partial(within_kernel, dims=half_dims, first_gro...]
    ppermute x12, waiting for transfers between devices: 23.2 us -> 25.9 us  [swapped(): done[k] = lax.ppermute(arrays[k], axis, xor_route(size, k))]
    ppermute x12, starting transfers between devices: 22.5 us -> 20.6 us  [swapped(): done[k] = lax.ppermute(arrays[k], axis, xor_route(size, k))]
  transfers between devices with their start and end apart: 19 -> 20, of which waited for: 6 -> 8; matrix products, arithmetic and copies ran while one was open for 0% -> 0% of each run, Pallas kernels for 33% -> 27%
where the time goes in v8:
time: 87.8 us; the launch traced here: 87.6 us
  starting transfers between devices  29.3 us (33%)
  waiting for transfers between devices  29 us (33%)
  Pallas kernels  28.8 us (33%)
    ppermute x12, waiting for transfers between devices, swapped(): done[k] = lax.ppermute(arrays[k], axis, xor_route(size, k))  25.9 us
    ppermute x12, starting transfers between devices, swapped(): done[k] = lax.ppermute(arrays[k], axis, xor_route(size, k))  20.6 us
    pallas_call x4, Pallas kernels, within(): pl.pallas_call(functools.partial(within_kernel, dims=half_dims, first_gro...  12.2 us
    pallas_call x4, Pallas kernels, finish(): pl.pallas_call(functools.partial(final_kernel, dims=state_dims + (chunk *...  6.79 us
    ppermute x2, starting transfers between devices, entering_by_swaps(): pair = lax.ppermute(pair, outer_axis, xor_route(4, 2))  3.16 us
    ppermute x2, starting transfers between devices, entering_by_swaps(): neighbour = lax.ppermute(column, outer_axis, xor_route(4, 1))  2.99 us
    pallas_call x1, Pallas kernels, local(): pl.pallas_call(functools.partial(send_state_kernel, dims=state_dims), in_...  2.95 us
    pallas_call x1, Pallas kernels, local(): small_call(functools.partial(own_state_kernel, dims=state_dims), [smem, h...  2.89 us
  transfers between devices with their start and end apart: 20, of which 8 were waited for; matrix products, arithmetic and copies ran while one was open for 0% of the time, Pallas kernels for 27%

profile of v8, /device:TPU:0, one launch (start us, length us, event | category | flops | bytes accessed | tf_op | source)
XLA Modules:
  0.0 87.6 jit_solution(18099592801512729743)
XLA Ops:
  0.0 2.9 %send_state.1 = (bf16[136,4096]{1,0:T(8,128)(2,1)S(1)}, f32[256,128]{1,0:T(8,128)S(1)}, f32[128,256]{1,0:T(8,128)S(1)}, f32[256,128]{1,0:T(8,128)S(1)}, f32[8,12...) custom-call(s32[1]{0:T(128)} %bitcast.half, s32[1]{0:T(128)} %bitcast.2.chip, ...), custom_call_target="tpu_custom_call" | custom-call | tf_op jit(solution)/shard_map/send_state/pallas_call | solution.py:593
  3.5 2.9 %shard_map.64 = (bf16[136,4096]{1,0:T(8,128)(2,1)S(1)}, bf16[128,4096]{1,0:T(8,128)(2,1)S(1)}, bf16[256,4096]{1,0:T(8,128)(2,1)S(1)}, bf16[256,512]{1,0:T(8,128)(2,1)S(1)}) custom-call(s32[1]{0:T(128)} %bitcast.1.half.core.flag, bf16[256,8192]{1,0:T(8,128)(2,1)} %x.3, bf16[256,1024]{1,0:T(8,128)(2,1)} %b.3, f32[256,128]{1,0:T(8,128)S(1)} %get-tuple-element.37.factor, ...), custom_call_target="tpu_custom_call" | custom-call | tf_op jit(solution)/shard_map/pallas_call | solution.py:615
  6.7 2.6 %collective-permute-start.11 = (bf16[32,2176]{1,0:T(8,128)(2,1)S(1)}, bf16[32,2176]{1,0:T(8,128)(2,1)S(1)}, u32[]{:S(2)}, u32[]{:S(2)}) collective-permute-start(bf16[32,2176]{1,0:T(8,128)(2,1)S(1)} %get-tuple-element.60), channel_id=1, source_target_pairs={{0,2},{2,0},{4,6},{6,4},{1,3},{3,1},{5,7},{7,5},{8,10},{10,8},{12,... | collective-permute-start | bytes 417800 | tf_op jit(solution)/shard_map/ppermute | solution.py:477
  9.4 2.6 %collective-permute-start.12 = (bf16[32,2176]{1,0:T(8,128)(2,1)S(1)}, bf16[32,2176]{1,0:T(8,128)(2,1)S(1)}, u32[]{:S(2)}, u32[]{:S(2)}) collective-permute-start(bf16[32,2176]{1,0:T(8,128)(2,1)S(1)} %get-tuple-element.61), channel_id=1, source_target_pairs={{0,4},{2,6},{4,0},{6,2},{1,5},{3,7},{5,1},{7,3},{8,12},{10,14},{12... | collective-permute-start | bytes 417800 | tf_op jit(solution)/shard_map/ppermute | solution.py:477
  12.0 1.9 %collective-permute-start.10 = (bf16[136,4096]{1,0:T(8,128)(2,1)S(1)}, bf16[136,4096]{1,0:T(8,128)(2,1)S(1)}, u32[]{:S(2)}, u32[]{:S(2)}) collective-permute-start(bf16[136,4096]{1,0:T(8,128)(2,1)S(1)} %get-tuple-element.39.refs_0_), channel_id=1, source_target_pairs={{0,1},{2,3},{4,5},{6,7},{8,9},{10,11},{12,13},{14,15},{16,17},{18,... | collective-permute-start | bytes 3342344 | tf_op jit(solution)/shard_map/ppermute | solution.py:624
  16.1 2.6 %collective-permute-start.2 = (bf16[32,2176]{1,0:T(8,128)(2,1)S(1)}, bf16[32,2176]{1,0:T(8,128)(2,1)S(1)}, u32[]{:S(2)}, u32[]{:S(2)}) collective-permute-start(bf16[32,2176]{1,0:T(8,128)(2,1)S(1)} %get-tuple-element.43), channel_id=1, source_target_pairs={{0,4},{2,6},{4,0},{6,2},{1,5},{3,7},{5,1},{7,3},{8,12},{10,14},{12... | collective-permute-start | bytes 417800 | tf_op jit(solution)/shard_map/ppermute | solution.py:477
  18.7 4.2 %collective-permute-done.12.refs_2_.refs_5_ = bf16[32,2176]{1,0:T(8,128)(2,1)S(1)} collective-permute-done((bf16[32,2176]{1,0:T(8,128)(2,1)S(1)}, bf16[32,2176]{1,0:T(8,128)(2,1)S(1)}, u32[]{:S(2)}, u32[]{:S(2)}) %collective-permute-start.12) | collective-permute-done | bytes 139296 | tf_op jit(solution)/shard_map/ppermute | solution.py:477
  22.9 2.5 %collective-permute-start.3 = (bf16[32,2176]{1,0:T(8,128)(2,1)S(1)}, bf16[32,2176]{1,0:T(8,128)(2,1)S(1)}, u32[]{:S(2)}, u32[]{:S(2)}) collective-permute-start(bf16[32,2176]{1,0:T(8,128)(2,1)S(1)} %get-tuple-element.44), channel_id=1, source_target_pairs={{0,6},{2,4},{4,2},{6,0},{1,7},{3,5},{5,3},{7,1},{8,14},{10,12},{12... | collective-permute-start | bytes 417800 | tf_op jit(solution)/shard_map/ppermute | solution.py:477
  27.4 7.4 %collective-permute-done.2.refs_2_.refs_5_ = bf16[32,2176]{1,0:T(8,128)(2,1)S(1)} collective-permute-done((bf16[32,2176]{1,0:T(8,128)(2,1)S(1)}, bf16[32,2176]{1,0:T(8,128)(2,1)S(1)}, u32[]{:S(2)}, u32[]{:S(2)}) %collective-permute-start.2) | collective-permute-done | bytes 139296 | tf_op jit(solution)/shard_map/ppermute | solution.py:477
  37.3 1.6 %collective-permute-start.15 = (bf16[32,2176]{1,0:T(8,128)(2,1)S(1)}, bf16[32,2176]{1,0:T(8,128)(2,1)S(1)}, u32[]{:S(2)}, u32[]{:S(2)}) collective-permute-start(bf16[32,2176]{1,0:T(8,128)(2,1)S(1)} %shard_map.72), channel_id=1, source_target_pairs={{0,16},{8,24},{16,0},{24,8},{1,17},{9,25},{17,1},{25,9},{2,18},{10... | collective-permute-start | bytes 417800 | tf_op jit(solution)/shard_map/ppermute | solution.py:513
  40.7 1.6 %collective-permute-start.5 = (bf16[32,2176]{1,0:T(8,128)(2,1)S(1)}, bf16[32,2176]{1,0:T(8,128)(2,1)S(1)}, u32[]{:S(2)}, u32[]{:S(2)}) collective-permute-start(bf16[32,2176]{1,0:T(8,128)(2,1)S(1)} %shard_map.67), channel_id=1, source_target_pairs={{0,16},{8,24},{16,0},{24,8},{1,17},{9,25},{17,1},{25,9},{2,18},{10... | collective-permute-start | bytes 417800 | tf_op jit(solution)/shard_map/ppermute | solution.py:513
  44.3 2.2 %collective-permute-start.16 = (bf16[32,2048]{1,0:T(8,128)(2,1)S(1)}, bf16[32,2048]{1,0:T(8,128)(2,1)S(1)}, u32[]{:S(2)}, u32[]{:S(2)}) collective-permute-start(bf16[32,2048]{1,0:T(8,128)(2,1)S(1)} %get-tuple-element.66), channel_id=1, source_target_pairs={{0,2},{2,0},{4,6},{6,4},{1,3},{3,1},{5,7},{7,5},{8,10},{10,8},{12,... | collective-permute-start | bytes 393224 | tf_op jit(solution)/shard_map/ppermute | solution.py:477
  50.7 2.0 %collective-permute-done.16.refs_1_ = bf16[32,2048]{1,0:T(8,128)(2,1)S(1)} collective-permute-done((bf16[32,2048]{1,0:T(8,128)(2,1)S(1)}, bf16[32,2048]{1,0:T(8,128)(2,1)S(1)}, u32[]{:S(2)}, u32[]{:S(2)}) %collective-permute-start.16) | collective-permute-done | bytes 131104 | tf_op jit(solution)/shard_map/ppermute | solution.py:477
  54.1 5.3 %collective-permute-done.17.refs_2_ = bf16[32,2048]{1,0:T(8,128)(2,1)S(1)} collective-permute-done((bf16[32,2048]{1,0:T(8,128)(2,1)S(1)}, bf16[32,2048]{1,0:T(8,128)(2,1)S(1)}, u32[]{:S(2)}, u32[]{:S(2)}) %collective-permute-start.17) | collective-permute-done | bytes 131104 | tf_op jit(solution)/shard_map/ppermute | solution.py:477
  59.4 2.6 %collective-permute-start.8 = (bf16[32,2048]{1,0:T(8,128)(2,1)S(1)}, bf16[32,2048]{1,0:T(8,128)(2,1)S(1)}, u32[]{:S(2)}, u32[]{:S(2)}) collective-permute-start(bf16[32,2048]{1,0:T(8,128)(2,1)S(1)} %get-tuple-element.50), channel_id=1, source_target_pairs={{0,6},{2,4},{4,2},{6,0},{1,7},{3,5},{5,3},{7,1},{8,14},{10,12},{12... | collective-permute-start | bytes 393224 | tf_op jit(solution)/shard_map/ppermute | solution.py:477
  62.1 6.1 %collective-permute-done.7.refs_2_ = bf16[32,2048]{1,0:T(8,128)(2,1)S(1)} collective-permute-done((bf16[32,2048]{1,0:T(8,128)(2,1)S(1)}, bf16[32,2048]{1,0:T(8,128)(2,1)S(1)}, u32[]{:S(2)}, u32[]{:S(2)}) %collective-permute-start.7) | collective-permute-done | bytes 131104 | tf_op jit(solution)/shard_map/ppermute | solution.py:477
  68.3 3.0 %within.7 = bf16[256,2048]{1,0:T(8,128)(2,1)S(1)} custom-call(s32[1]{0:T(128)} %bitcast.1.half.core.flag, s32[1]{0:T(128)} %bitcast.1.half.core.flag, bf16[256,4096]{1,0:T(8,128)(2,1)S(1)} %get-tuple-element.57.x_ref, bf16[256,512]{1,0:T(8,128)(2,1)S(1)} %get-tuple-element.58.b_ref, bf16[256,1024]{1,0:T(8,128)(2,1)S(1)} %copy-done, ...), custom_call_target="tpu_custom_call" | custom-call | tf_op jit(solution)/shard_map/within/pallas_call | solution.py:627
  71.4 3.1 %within.5 = bf16[256,2048]{1,0:T(8,128)(2,1)S(1)} custom-call(s32[1]{0:T(128)} %bitcast.1.half.core.flag, s32[1]{0:T(128)} %bitcast.1.half.core.flag, bf16[256,4096]{1,0:T(8,128)(2,1)S(1)} %get-tuple-element.57.x_ref, bf16[256,512]{1,0:T(8,128)(2,1)S(1)} %get-tuple-element.58.b_ref, bf16[256,1024]{1,0:T(8,128)(2,1)S(1)} %copy-done, ...), custom_call_target="tpu_custom_call" | custom-call | tf_op jit(solution)/shard_map/within/pallas_call | solution.py:627
  74.5 3.0 %within.6 = bf16[256,2048]{1,0:T(8,128)(2,1)S(1)} custom-call(s32[1]{0:T(128)} %bitcast.half, s32[1]{0:T(128)} %bitcast.1.half.core.flag, bf16[256,4096]{1,0:T(8,128)(2,1)S(1)} %get-tuple-element.54.x_ref, bf16[256,512]{1,0:T(8,128)(2,1)S(1)} %get-tuple-element.55.b_ref, bf16[256,1024]{1,0:T(8,128)(2,1)S(1)} %copy-done, f32[256,128]{1,0:T(8,128)S(1)} %copy-done.1, ...), custom_call_target="tpu_custom_call" | custom-call | tf_op jit(solution)/shard_map/within/pallas_call | solution.py:627
  77.5 3.1 %within.4 = bf16[256,2048]{1,0:T(8,128)(2,1)S(1)} custom-call(s32[1]{0:T(128)} %bitcast.half, s32[1]{0:T(128)} %bitcast.1.half.core.flag, bf16[256,4096]{1,0:T(8,128)(2,1)S(1)} %get-tuple-element.54.x_ref, bf16[256,512]{1,0:T(8,128)(2,1)S(1)} %get-tuple-element.55.b_ref, bf16[256,1024]{1,0:T(8,128)(2,1)S(1)} %copy-done, f32[256,128]{1,0:T(8,128)S(1)} %copy-done.1, ...), custom_call_target="tpu_custom_call" | custom-call | tf_op jit(solution)/shard_map/within/pallas_call | solution.py:627
  80.6 1.7 %finish.4.refs_0_ = bf16[256,8192]{1,0:T(8,128)(2,1)} custom-call(s32[1]{0:T(128)} %bitcast.1.half.core.flag, bf16[256,1024]{1,0:T(8,128)(2,1)S(1)} %copy-done, bf16[128,2048]{1,0:T(8,128)(2,1)S(1)} %shard_map.74.state, f32[256,128]{1,0:T(8,128)S(1)} %get-tuple-element.51.run_ref.run, f32[8,128]{1,0:T(8,128)S(1)} %get-tuple-element.52.base, ...), custom_call_target="tpu_custom_call" | custom-call | tf_op jit(solution)/shard_map/finish/pallas_call | solution.py:662
  82.3 1.7 %finish.5.refs_0_ = bf16[256,8192]{1,0:T(8,128)(2,1)} custom-call(s32[1]{0:T(128)} %bitcast.half, bf16[256,1024]{1,0:T(8,128)(2,1)S(1)} %copy-done, bf16[128,2048]{1,0:T(8,128)(2,1)S(1)} %collective-permute-done.19.state, f32[256,128]{1,0:T(8,128)S(1)} %get-tuple-element.51.run_ref.run, ...), custom_call_target="tpu_custom_call", output_to_operand_aliasing={{}: (7, {})} | custom-call | tf_op jit(solution)/shard_map/finish/pallas_call | solution.py:662
  84.0 1.7 %finish.6.refs_0_ = bf16[256,8192]{1,0:T(8,128)(2,1)} custom-call(s32[1]{0:T(128)} %bitcast.1.half.core.flag, bf16[256,1024]{1,0:T(8,128)(2,1)S(1)} %copy-done, bf16[128,2048]{1,0:T(8,128)(2,1)S(1)} %shard_map.69.state, f32[256,128]{1,0:T(8,128)S(1)} %get-tuple-element.51.run_ref.run, ...), custom_call_target="tpu_custom_call", output_to_operand_aliasing={{}: (7, {})} | custom-call | tf_op jit(solution)/shard_map/finish/pallas_call | solution.py:662
  85.7 1.7 %finish.7 = bf16[256,8192]{1,0:T(8,128)(2,1)} custom-call(s32[1]{0:T(128)} %bitcast.half, bf16[256,1024]{1,0:T(8,128)(2,1)S(1)} %copy-done, bf16[128,2048]{1,0:T(8,128)(2,1)S(1)} %collective-permute-done.9.state, f32[256,128]{1,0:T(8,128)S(1)} %get-tuple-element.51.run_ref.run, f32[8,128]{1,0:T(8,128)S(1)} %get-tuple-element.52.base, ...), custom_call_target="tpu_custom_call", output_to_operand_aliasing={{}: (7, {})} | custom-call | tf_op jit(solution)/shard_map/finish/pallas_call | solution.py:662
  (42 shorter events, 17.3 us)
Async XLA Ops:
  3.0 3.5 %collective-permute-start = (bf16[136,4096]{1,0:T(8,128)(2,1)S(1)}, bf16[136,4096]{1,0:T(8,128)(2,1)S(1)}, u32[]{:S(2)}, u32[]{:S(2)}) collective-permute-start(bf16[136,4096]{1,0:T(8,128)(2,1)S(1)} %get-tuple-element.40), channel_id=1, source_target_pairs={{0,1},{1,0},{2,3},{3,2},{4,5},{5,4},{6,7},{7,6},{8,9},{9,8},{10,11... | collective-permute-start | bytes 3342344 | tf_op jit(solution)/shard_map/ppermute | solution.py:613
  6.7 9.4 %collective-permute-start.11 = (bf16[32,2176]{1,0:T(8,128)(2,1)S(1)}, bf16[32,2176]{1,0:T(8,128)(2,1)S(1)}, u32[]{:S(2)}, u32[]{:S(2)}) collective-permute-start(bf16[32,2176]{1,0:T(8,128)(2,1)S(1)} %get-tuple-element.60), channel_id=1, source_target_pairs={{0,2},{2,0},{4,6},{6,4},{1,3},{3,1},{5,7},{7,5},{8,10},{10,8},{12,... | collective-permute-start | bytes 417800 | tf_op jit(solution)/shard_map/ppermute | solution.py:477
  9.4 13.5 %collective-permute-start.12 = (bf16[32,2176]{1,0:T(8,128)(2,1)S(1)}, bf16[32,2176]{1,0:T(8,128)(2,1)S(1)}, u32[]{:S(2)}, u32[]{:S(2)}) collective-permute-start(bf16[32,2176]{1,0:T(8,128)(2,1)S(1)} %get-tuple-element.61), channel_id=1, source_target_pairs={{0,4},{2,6},{4,0},{6,2},{1,5},{3,7},{5,1},{7,3},{8,12},{10,14},{12... | collective-permute-start | bytes 417800 | tf_op jit(solution)/shard_map/ppermute | solution.py:477
  12.0 13.4 %collective-permute-start.13 = (bf16[32,2176]{1,0:T(8,128)(2,1)S(1)}, bf16[32,2176]{1,0:T(8,128)(2,1)S(1)}, u32[]{:S(2)}, u32[]{:S(2)}) collective-permute-start(bf16[32,2176]{1,0:T(8,128)(2,1)S(1)} %get-tuple-element.62), channel_id=1, source_target_pairs={{0,6},{2,4},{4,2},{6,0},{1,7},{3,5},{5,3},{7,1},{8,14},{10,12},{12... | collective-permute-start | bytes 417800 | tf_op jit(solution)/shard_map/ppermute | solution.py:477
  12.0 62.5 %collective-permute-start.10 = (bf16[136,4096]{1,0:T(8,128)(2,1)S(1)}, bf16[136,4096]{1,0:T(8,128)(2,1)S(1)}, u32[]{:S(2)}, u32[]{:S(2)}) collective-permute-start(bf16[136,4096]{1,0:T(8,128)(2,1)S(1)} %get-tuple-element.39.refs_0_), channel_id=1, source_target_pairs={{0,1},{2,3},{4,5},{6,7},{8,9},{10,11},{12,13},{14,15},{16,17},{18,... | collective-permute-start | bytes 3342344 | tf_op jit(solution)/shard_map/ppermute | solution.py:624
  14.6 12.9 %collective-permute-start.1 = (bf16[32,2176]{1,0:T(8,128)(2,1)S(1)}, bf16[32,2176]{1,0:T(8,128)(2,1)S(1)}, u32[]{:S(2)}, u32[]{:S(2)}) collective-permute-start(bf16[32,2176]{1,0:T(8,128)(2,1)S(1)} %get-tuple-element.42), channel_id=1, source_target_pairs={{0,2},{2,0},{4,6},{6,4},{1,3},{3,1},{5,7},{7,5},{8,10},{10,8},{12,... | collective-permute-start | bytes 417800 | tf_op jit(solution)/shard_map/ppermute | solution.py:477
  16.1 18.7 %collective-permute-start.2 = (bf16[32,2176]{1,0:T(8,128)(2,1)S(1)}, bf16[32,2176]{1,0:T(8,128)(2,1)S(1)}, u32[]{:S(2)}, u32[]{:S(2)}) collective-permute-start(bf16[32,2176]{1,0:T(8,128)(2,1)S(1)} %get-tuple-element.43), channel_id=1, source_target_pairs={{0,4},{2,6},{4,0},{6,2},{1,5},{3,7},{5,1},{7,3},{8,12},{10,14},{12... | collective-permute-start | bytes 417800 | tf_op jit(solution)/shard_map/ppermute | solution.py:477
  22.9 11.9 %collective-permute-start.3 = (bf16[32,2176]{1,0:T(8,128)(2,1)S(1)}, bf16[32,2176]{1,0:T(8,128)(2,1)S(1)}, u32[]{:S(2)}, u32[]{:S(2)}) collective-permute-start(bf16[32,2176]{1,0:T(8,128)(2,1)S(1)} %get-tuple-element.44), channel_id=1, source_target_pairs={{0,6},{2,4},{4,2},{6,0},{1,7},{3,5},{5,3},{7,1},{8,14},{10,12},{12... | collective-permute-start | bytes 417800 | tf_op jit(solution)/shard_map/ppermute | solution.py:477
  25.9 10.9 %collective-permute-start.14 = (bf16[32,2176]{1,0:T(8,128)(2,1)S(1)}, bf16[32,2176]{1,0:T(8,128)(2,1)S(1)}, u32[]{:S(2)}, u32[]{:S(2)}) collective-permute-start(bf16[32,2176]{1,0:T(8,128)(2,1)S(1)} %get-tuple-element.63.refs_0_), channel_id=1, source_target_pairs={{0,8},{8,0},{16,24},{24,16},{1,9},{9,1},{17,25},{25,17},{2,10},{10... | collective-permute-start | bytes 417800 | tf_op jit(solution)/shard_map/ppermute | solution.py:507
  35.3 5.1 %collective-permute-start.4 = (bf16[32,2176]{1,0:T(8,128)(2,1)S(1)}, bf16[32,2176]{1,0:T(8,128)(2,1)S(1)}, u32[]{:S(2)}, u32[]{:S(2)}) collective-permute-start(bf16[32,2176]{1,0:T(8,128)(2,1)S(1)} %get-tuple-element.45.refs_0_), channel_id=1, source_target_pairs={{0,8},{8,0},{16,24},{24,16},{1,9},{9,1},{17,25},{25,17},{2,10},{10... | collective-permute-start | bytes 417800 | tf_op jit(solution)/shard_map/ppermute | solution.py:507
  37.2 31.1 %copy-start = (bf16[256,1024]{1,0:T(8,128)(2,1)S(1)}, bf16[256,1024]{1,0:T(8,128)(2,1)}, u32[]{:S(2)}) copy-start(bf16[256,1024]{1,0:T(8,128)(2,1)} %c.7) | copy-start | bytes 1572868
  37.2 31.1 %copy-start.1 = (f32[256,128]{1,0:T(8,128)S(1)}, f32[256,128]{1,0:T(8,128)}, u32[]{:S(2)}) copy-start(f32[256,128]{1,0:T(8,128)} %step_ref.7) | copy-start | bytes 393220
  37.2 31.1 %copy-start.2 = (f32[128]{0:T(128)S(1)}, f32[128]{0:T(128)}, u32[]{:S(2)}) copy-start(f32[128]{0:T(128)} %param.11) | copy-start | bytes 1540
  37.3 6.6 %collective-permute-start.15 = (bf16[32,2176]{1,0:T(8,128)(2,1)S(1)}, bf16[32,2176]{1,0:T(8,128)(2,1)S(1)}, u32[]{:S(2)}, u32[]{:S(2)}) collective-permute-start(bf16[32,2176]{1,0:T(8,128)(2,1)S(1)} %shard_map.72), channel_id=1, source_target_pairs={{0,16},{8,24},{16,0},{24,8},{1,17},{9,25},{17,1},{25,9},{2,18},{10... | collective-permute-start | bytes 417800 | tf_op jit(solution)/shard_map/ppermute | solution.py:513
  40.7 8.3 %collective-permute-start.5 = (bf16[32,2176]{1,0:T(8,128)(2,1)S(1)}, bf16[32,2176]{1,0:T(8,128)(2,1)S(1)}, u32[]{:S(2)}, u32[]{:S(2)}) collective-permute-start(bf16[32,2176]{1,0:T(8,128)(2,1)S(1)} %shard_map.67), channel_id=1, source_target_pairs={{0,16},{8,24},{16,0},{24,8},{1,17},{9,25},{17,1},{25,9},{2,18},{10... | collective-permute-start | bytes 417800 | tf_op jit(solution)/shard_map/ppermute | solution.py:513
  44.3 8.4 %collective-permute-start.16 = (bf16[32,2048]{1,0:T(8,128)(2,1)S(1)}, bf16[32,2048]{1,0:T(8,128)(2,1)S(1)}, u32[]{:S(2)}, u32[]{:S(2)}) collective-permute-start(bf16[32,2048]{1,0:T(8,128)(2,1)S(1)} %get-tuple-element.66), channel_id=1, source_target_pairs={{0,2},{2,0},{4,6},{6,4},{1,3},{3,1},{5,7},{7,5},{8,10},{10,8},{12,... | collective-permute-start | bytes 393224 | tf_op jit(solution)/shard_map/ppermute | solution.py:477
  46.5 12.8 %collective-permute-start.17 = (bf16[32,2048]{1,0:T(8,128)(2,1)S(1)}, bf16[32,2048]{1,0:T(8,128)(2,1)S(1)}, u32[]{:S(2)}, u32[]{:S(2)}) collective-permute-start(bf16[32,2048]{1,0:T(8,128)(2,1)S(1)} %get-tuple-element.67), channel_id=1, source_target_pairs={{0,4},{2,6},{4,0},{6,2},{1,5},{3,7},{5,1},{7,3},{8,12},{10,14},{12... | collective-permute-start | bytes 393224 | tf_op jit(solution)/shard_map/ppermute | solution.py:477
  47.6 14.3 %collective-permute-start.18 = (bf16[32,2048]{1,0:T(8,128)(2,1)S(1)}, bf16[32,2048]{1,0:T(8,128)(2,1)S(1)}, u32[]{:S(2)}, u32[]{:S(2)}) collective-permute-start(bf16[32,2048]{1,0:T(8,128)(2,1)S(1)} %get-tuple-element.68), channel_id=1, source_target_pairs={{0,6},{2,4},{4,2},{6,0},{1,7},{3,5},{5,3},{7,1},{8,14},{10,12},{12... | collective-permute-start | bytes 393224 | tf_op jit(solution)/shard_map/ppermute | solution.py:477
  49.6 12.4 %collective-permute-start.6 = (bf16[32,2048]{1,0:T(8,128)(2,1)S(1)}, bf16[32,2048]{1,0:T(8,128)(2,1)S(1)}, u32[]{:S(2)}, u32[]{:S(2)}) collective-permute-start(bf16[32,2048]{1,0:T(8,128)(2,1)S(1)} %get-tuple-element.48), channel_id=1, source_target_pairs={{0,2},{2,0},{4,6},{6,4},{1,3},{3,1},{5,7},{7,5},{8,10},{10,8},{12,... | collective-permute-start | bytes 393224 | tf_op jit(solution)/shard_map/ppermute | solution.py:477
  52.7 15.5 %collective-permute-start.7 = (bf16[32,2048]{1,0:T(8,128)(2,1)S(1)}, bf16[32,2048]{1,0:T(8,128)(2,1)S(1)}, u32[]{:S(2)}, u32[]{:S(2)}) collective-permute-start(bf16[32,2048]{1,0:T(8,128)(2,1)S(1)} %get-tuple-element.49), channel_id=1, source_target_pairs={{0,4},{2,6},{4,0},{6,2},{1,5},{3,7},{5,1},{7,3},{8,12},{10,14},{12... | collective-permute-start | bytes 393224 | tf_op jit(solution)/shard_map/ppermute | solution.py:477
  59.4 8.8 %collective-permute-start.8 = (bf16[32,2048]{1,0:T(8,128)(2,1)S(1)}, bf16[32,2048]{1,0:T(8,128)(2,1)S(1)}, u32[]{:S(2)}, u32[]{:S(2)}) collective-permute-start(bf16[32,2048]{1,0:T(8,128)(2,1)S(1)} %get-tuple-element.50), channel_id=1, source_target_pairs={{0,6},{2,4},{4,2},{6,0},{1,7},{3,5},{5,3},{7,1},{8,14},{10,12},{12... | collective-permute-start | bytes 393224 | tf_op jit(solution)/shard_map/ppermute | solution.py:477
  62.0 20.3 %collective-permute-start.19 = (bf16[128,2048]{1,0:T(8,128)(2,1)S(1)}, bf16[128,2048]{1,0:T(8,128)(2,1)S(1)}, u32[]{:S(2)}, u32[]{:S(2)}) collective-permute-start(bf16[128,2048]{1,0:T(8,128)(2,1)S(1)} %shard_map.74.state), channel_id=1, source_target_pairs={{0,1},{1,0},{2,3},{3,2},{4,5},{5,4},{6,7},{7,6},{8,9},{9,8},{10,11... | collective-permute-start | bytes 1572872 | tf_op jit(solution)/shard_map/ppermute | solution.py:675
  68.2 17.5 %collective-permute-start.9 = (bf16[128,2048]{1,0:T(8,128)(2,1)S(1)}, bf16[128,2048]{1,0:T(8,128)(2,1)S(1)}, u32[]{:S(2)}, u32[]{:S(2)}) collective-permute-start(bf16[128,2048]{1,0:T(8,128)(2,1)S(1)} %shard_map.69.state), channel_id=1, source_target_pairs={{0,1},{1,0},{2,3},{3,2},{4,5},{5,4},{6,7},{7,6},{8,9},{9,8},{10,11... | collective-permute-start | bytes 1572872 | tf_op jit(solution)/shard_map/ppermute | solution.py:675

commit v9 on v8

--- a/solution.py
+++ b/solution.py
@@ -298,29 +298,26 @@
     out[:, cols:] = jnp.concatenate([product] * (out.shape[0] // ROW_TILE), axis=0).astype(BF16)
 
 
-def pair_kernel(at, mine, theirs, out, *, first_head, width, cols):
-    odd = jnp.bitwise_and(at[2], 1) == 1
-    values, decay = decays_of((mine, theirs), cols, first_head, width)
-    one = jnp.ones_like(decay[:1, :])
-    on_mine = jnp.where(odd, one, decay[1:2, :])
-    on_theirs = jnp.where(odd, decay[:1, :], one)
-    out[:, :cols] = (on_mine * mine[:, :cols].astype(F32) + on_theirs * theirs[:, :cols].astype(F32)).astype(BF16)
-    fill_decay(out, cols, values, 2)
-
-
-def chips_kernel(at, neighbour, lower_pair, decay, *refs, first_head, width, count):
-    pieces, outs = refs[:count], refs[count:]
-    _, cols = outs[0].shape
-    odd = jnp.bitwise_and(at[2], 1) == 1
-    late = at[2] >= 2
-    _, passed = decays_of((neighbour,), cols, first_head, width)
-    on_pair = jnp.where(late, jnp.where(odd, passed[:1, :], jnp.ones_like(passed[:1, :])), 0.0)
-    carry = on_pair * lower_pair[:, :cols].astype(F32) + jnp.where(odd, neighbour[:, :cols].astype(F32), 0.0)
+def chips_kernel(at, *refs, first_head, width, count, blocks):
+    others, decay = refs[: blocks - 1], refs[blocks - 1]
+    pieces, outs, carry = refs[blocks : blocks + count], refs[blocks + count : -1], refs[-1]
+    rows, cols = outs[0].shape
+    _, passed = decays_of(others, cols, first_head, width)
+    for place in range(blocks):
+
+        @pl.when(at[2] == place)
+        def _():
+            state = jnp.zeros((rows, cols), F32)
+            for k in range(place):
+                k = (k ^ place) - 1
+                state = passed[k : k + 1, :] * state + others[k][:, :cols].astype(F32)
+            carry[...] = state
+
     for place in range(count):
 
         @pl.when(at[1] == place)
         def _():
-            state = carry
+            state = carry[...]
             for k in range(count):
                 k = k ^ place
                 outs[k][...] = state.astype(BF16)
@@ -482,6 +479,7 @@
     half_cols = own.shape[1]
     heads = total.shape[1]
     count = lax.axis_size(chip_axis)
+    blocks = lax.axis_size(outer_axis)
     rows = states // count
     cols = half_cols // CHUNKS
     smem = pl.BlockSpec(memory_space=pltpu.SMEM)
@@ -504,18 +502,15 @@
             [smem] * 3 + [vmem] * count,
             [shape((rows, cols + heads), BF16), shape((ROW_TILE, cols), F32)],
         )(*at, *pieces)
-        neighbour = lax.ppermute(column, outer_axis, xor_route(4, 1))
-        (pair,) = small_call(
-            functools.partial(placed(pair_kernel), first_head=first_head, width=width, cols=cols),
-            [smem] * 3 + [vmem] * 2,
-            [shape((rows, cols + heads), BF16)],
-        )(*at, column, neighbour)
-        pair = lax.ppermute(pair, outer_axis, xor_route(4, 2))
+        others = swapped([column] * blocks, outer_axis)[1:]
         states_out = small_call(
-            functools.partial(placed(chips_kernel), first_head=first_head, width=width, count=count),
-            [smem] * 3 + [vmem] * (count + 3),
+            functools.partial(
+                placed(chips_kernel), first_head=first_head, width=width, count=count, blocks=blocks
+            ),
+            [smem] * 3 + [vmem] * (count + blocks),
             [shape((rows, cols), BF16)] * count,
-        )(*at, neighbour, pair, decay, *pieces)
+            [pltpu.VMEM((rows, cols), F32)],
+        )(*at, *others, decay, *pieces)
         states_out = swapped(states_out, chip_axis)
         entering += small_call(
             functools.partial(placed(assemble_kernel), count=count),

time: 87.8 us -> 87 us (level)
  starting transfers between devices: 29.3 us -> 32.5 us
  waiting for transfers between devices: 29 us -> 25.8 us
    ppermute x12 -> x18, starting transfers between devices: 20.6 us -> 29.9 us  [swapped(): done[k] = lax.ppermute(arrays[k], axis, xor_route(size, k))]
    ppermute x4 -> x0, starting transfers between devices: 6.15 us -> none  [the longest x2 3.16 us: entering_by_swaps(): pair = lax.ppermute(pair, outer_axis, xor_route(4, 2))]
    ppermute x4 -> x0, waiting for transfers between devices: 3.06 us -> none  [the longest x2 1.56 us: entering_by_swaps(): neighbour = lax.ppermute(column, outer_axis, xor_route(4, 1))]
    ppermute x12 -> x18, waiting for transfers between devices: 25.9 us -> 25.8 us  [swapped(): done[k] = lax.ppermute(arrays[k], axis, xor_route(size, k))]
  transfers between devices with their start and end apart: 20 -> 22, of which waited for: 8 -> 7; matrix products, arithmetic and copies ran while one was open for 0% -> 0% of each run, Pallas kernels for 27% -> 27%
where the time goes in v9:
time: 87 us; the launch traced here: 86.8 us
  starting transfers between devices  32.5 us (37%)
  Pallas kernels  28.1 us (32%)
  waiting for transfers between devices  25.8 us (30%)
    ppermute x18, starting transfers between devices, swapped(): done[k] = lax.ppermute(arrays[k], axis, xor_route(size, k))  29.9 us
    ppermute x18, waiting for transfers between devices, swapped(): done[k] = lax.ppermute(arrays[k], axis, xor_route(size, k))  25.8 us
    pallas_call x4, Pallas kernels, within(): pl.pallas_call(functools.partial(within_kernel, dims=half_dims, first_gro...  12.2 us
    pallas_call x4, Pallas kernels, finish(): pl.pallas_call(functools.partial(final_kernel, dims=state_dims + (chunk *...  6.79 us
    pallas_call x1, Pallas kernels, local(): pl.pallas_call(functools.partial(send_state_kernel, dims=state_dims), in_...  2.95 us
    pallas_call x1, Pallas kernels, local(): small_call(functools.partial(own_state_kernel, dims=state_dims), [smem, h...  2.9 us
    ppermute x1, starting transfers between devices, local(): late = lax.ppermute(own, core_axis, swap[:1])  1.9 us
  transfers between devices with their start and end apart: 22, of which 7 were waited for; matrix products, arithmetic and copies ran while one was open for 0% of the time, Pallas kernels for 27%

profile of v9, /device:TPU:0, one launch (start us, length us, event | category | flops | bytes accessed | tf_op | source)
XLA Modules:
  0.0 86.8 jit_solution(8626779544425836347)
XLA Ops:
  0.0 2.9 %send_state.1 = (bf16[136,4096]{1,0:T(8,128)(2,1)S(1)}, f32[256,128]{1,0:T(8,128)S(1)}, f32[128,256]{1,0:T(8,128)S(1)}, f32[256,128]{1,0:T(8,128)S(1)}, f32[8,12...) custom-call(s32[1]{0:T(128)} %bitcast.half, s32[1]{0:T(128)} %bitcast.2.chip, ...), custom_call_target="tpu_custom_call" | custom-call | tf_op jit(solution)/shard_map/send_state/pallas_call | solution.py:588
  3.5 2.9 %shard_map.64 = (bf16[136,4096]{1,0:T(8,128)(2,1)S(1)}, bf16[128,4096]{1,0:T(8,128)(2,1)S(1)}, bf16[256,4096]{1,0:T(8,128)(2,1)S(1)}, bf16[256,512]{1,0:T(8,128)(2,1)S(1)}) custom-call(s32[1]{0:T(128)} %bitcast.1.half.core.flag, bf16[256,8192]{1,0:T(8,128)(2,1)} %x.3, bf16[256,1024]{1,0:T(8,128)(2,1)} %b.3, f32[256,128]{1,0:T(8,128)S(1)} %get-tuple-element.37.factor, ...), custom_call_target="tpu_custom_call" | custom-call | tf_op jit(solution)/shard_map/pallas_call | solution.py:610
  6.7 2.6 %collective-permute-start.12 = (bf16[32,2176]{1,0:T(8,128)(2,1)S(1)}, bf16[32,2176]{1,0:T(8,128)(2,1)S(1)}, u32[]{:S(2)}, u32[]{:S(2)}) collective-permute-start(bf16[32,2176]{1,0:T(8,128)(2,1)S(1)} %get-tuple-element.60), channel_id=1, source_target_pairs={{0,2},{2,0},{4,6},{6,4},{1,3},{3,1},{5,7},{7,5},{8,10},{10,8},{12,... | collective-permute-start | bytes 417800 | tf_op jit(solution)/shard_map/ppermute | solution.py:474
  9.4 2.6 %collective-permute-start.13 = (bf16[32,2176]{1,0:T(8,128)(2,1)S(1)}, bf16[32,2176]{1,0:T(8,128)(2,1)S(1)}, u32[]{:S(2)}, u32[]{:S(2)}) collective-permute-start(bf16[32,2176]{1,0:T(8,128)(2,1)S(1)} %get-tuple-element.61), channel_id=1, source_target_pairs={{0,4},{2,6},{4,0},{6,2},{1,5},{3,7},{5,1},{7,3},{8,12},{10,14},{12... | collective-permute-start | bytes 417800 | tf_op jit(solution)/shard_map/ppermute | solution.py:474
  12.0 1.9 %collective-permute-start.11 = (bf16[136,4096]{1,0:T(8,128)(2,1)S(1)}, bf16[136,4096]{1,0:T(8,128)(2,1)S(1)}, u32[]{:S(2)}, u32[]{:S(2)}) collective-permute-start(bf16[136,4096]{1,0:T(8,128)(2,1)S(1)} %get-tuple-element.39.refs_0_), channel_id=1, source_target_pairs={{0,1},{2,3},{4,5},{6,7},{8,9},{10,11},{12,13},{14,15},{16,17},{18,... | collective-permute-start | bytes 3342344 | tf_op jit(solution)/shard_map/ppermute | solution.py:619
  16.3 2.7 %collective-permute-start.2 = (bf16[32,2176]{1,0:T(8,128)(2,1)S(1)}, bf16[32,2176]{1,0:T(8,128)(2,1)S(1)}, u32[]{:S(2)}, u32[]{:S(2)}) collective-permute-start(bf16[32,2176]{1,0:T(8,128)(2,1)S(1)} %get-tuple-element.43), channel_id=1, source_target_pairs={{0,4},{2,6},{4,0},{6,2},{1,5},{3,7},{5,1},{7,3},{8,12},{10,14},{12... | collective-permute-start | bytes 417800 | tf_op jit(solution)/shard_map/ppermute | solution.py:474
  19.0 3.6 %collective-permute-done.13.refs_2_.refs_6_ = bf16[32,2176]{1,0:T(8,128)(2,1)S(1)} collective-permute-done((bf16[32,2176]{1,0:T(8,128)(2,1)S(1)}, bf16[32,2176]{1,0:T(8,128)(2,1)S(1)}, u32[]{:S(2)}, u32[]{:S(2)}) %collective-permute-start.13) | collective-permute-done | bytes 139296 | tf_op jit(solution)/shard_map/ppermute | solution.py:474
  22.7 2.7 %collective-permute-start.3 = (bf16[32,2176]{1,0:T(8,128)(2,1)S(1)}, bf16[32,2176]{1,0:T(8,128)(2,1)S(1)}, u32[]{:S(2)}, u32[]{:S(2)}) collective-permute-start(bf16[32,2176]{1,0:T(8,128)(2,1)S(1)} %get-tuple-element.44), channel_id=1, source_target_pairs={{0,6},{2,4},{4,2},{6,0},{1,7},{3,5},{5,3},{7,1},{8,14},{10,12},{12... | collective-permute-start | bytes 417800 | tf_op jit(solution)/shard_map/ppermute | solution.py:474
  25.9 2.5 %collective-permute-start.17 = (bf16[32,2176]{1,0:T(8,128)(2,1)S(1)}, bf16[32,2176]{1,0:T(8,128)(2,1)S(1)}, u32[]{:S(2)}, u32[]{:S(2)}) collective-permute-start(bf16[32,2176]{1,0:T(8,128)(2,1)S(1)} %get-tuple-element.63), channel_id=1, source_target_pairs={{0,24},{8,16},{16,8},{24,0},{1,25},{9,17},{17,9},{25,1},{2,26},{10... | collective-permute-start | bytes 417800 | tf_op jit(solution)/shard_map/ppermute | solution.py:474
  28.9 5.7 %collective-permute-done.2.refs_2_.refs_6_ = bf16[32,2176]{1,0:T(8,128)(2,1)S(1)} collective-permute-done((bf16[32,2176]{1,0:T(8,128)(2,1)S(1)}, bf16[32,2176]{1,0:T(8,128)(2,1)S(1)}, u32[]{:S(2)}, u32[]{:S(2)}) %collective-permute-start.2) | collective-permute-done | bytes 139296 | tf_op jit(solution)/shard_map/ppermute | solution.py:474
  42.6 2.3 %collective-permute-done.6.refs_2_ = bf16[32,2176]{1,0:T(8,128)(2,1)S(1)} collective-permute-done((bf16[32,2176]{1,0:T(8,128)(2,1)S(1)}, bf16[32,2176]{1,0:T(8,128)(2,1)S(1)}, u32[]{:S(2)}, u32[]{:S(2)}) %collective-permute-start.6) | collective-permute-done | bytes 139296 | tf_op jit(solution)/shard_map/ppermute | solution.py:474
  44.8 2.1 %collective-permute-start.19 = (bf16[32,2048]{1,0:T(8,128)(2,1)S(1)}, bf16[32,2048]{1,0:T(8,128)(2,1)S(1)}, u32[]{:S(2)}, u32[]{:S(2)}) collective-permute-start(bf16[32,2048]{1,0:T(8,128)(2,1)S(1)} %get-tuple-element.67), channel_id=1, source_target_pairs={{0,4},{2,6},{4,0},{6,2},{1,5},{3,7},{5,1},{7,3},{8,12},{10,14},{12... | collective-permute-start | bytes 393224 | tf_op jit(solution)/shard_map/ppermute | solution.py:474
  49.8 2.2 %collective-permute-start.8 = (bf16[32,2048]{1,0:T(8,128)(2,1)S(1)}, bf16[32,2048]{1,0:T(8,128)(2,1)S(1)}, u32[]{:S(2)}, u32[]{:S(2)}) collective-permute-start(bf16[32,2048]{1,0:T(8,128)(2,1)S(1)} %get-tuple-element.49), channel_id=1, source_target_pairs={{0,4},{2,6},{4,0},{6,2},{1,5},{3,7},{5,1},{7,3},{8,12},{10,14},{12... | collective-permute-start | bytes 393224 | tf_op jit(solution)/shard_map/ppermute | solution.py:474
  52.0 5.3 %collective-permute-done.19.refs_2_ = bf16[32,2048]{1,0:T(8,128)(2,1)S(1)} collective-permute-done((bf16[32,2048]{1,0:T(8,128)(2,1)S(1)}, bf16[32,2048]{1,0:T(8,128)(2,1)S(1)}, u32[]{:S(2)}, u32[]{:S(2)}) %collective-permute-start.19) | collective-permute-done | bytes 131104 | tf_op jit(solution)/shard_map/ppermute | solution.py:474
  57.3 2.1 %collective-permute-start.9 = (bf16[32,2048]{1,0:T(8,128)(2,1)S(1)}, bf16[32,2048]{1,0:T(8,128)(2,1)S(1)}, u32[]{:S(2)}, u32[]{:S(2)}) collective-permute-start(bf16[32,2048]{1,0:T(8,128)(2,1)S(1)} %get-tuple-element.50), channel_id=1, source_target_pairs={{0,6},{2,4},{4,2},{6,0},{1,7},{3,5},{5,3},{7,1},{8,14},{10,12},{12... | collective-permute-start | bytes 393224 | tf_op jit(solution)/shard_map/ppermute | solution.py:474
  59.6 7.8 %collective-permute-done.8.refs_2_ = bf16[32,2048]{1,0:T(8,128)(2,1)S(1)} collective-permute-done((bf16[32,2048]{1,0:T(8,128)(2,1)S(1)}, bf16[32,2048]{1,0:T(8,128)(2,1)S(1)}, u32[]{:S(2)}, u32[]{:S(2)}) %collective-permute-start.8) | collective-permute-done | bytes 131104 | tf_op jit(solution)/shard_map/ppermute | solution.py:474
  67.5 3.1 %within.7 = bf16[256,2048]{1,0:T(8,128)(2,1)S(1)} custom-call(s32[1]{0:T(128)} %bitcast.1.half.core.flag, s32[1]{0:T(128)} %bitcast.1.half.core.flag, bf16[256,4096]{1,0:T(8,128)(2,1)S(1)} %get-tuple-element.57.x_ref, bf16[256,512]{1,0:T(8,128)(2,1)S(1)} %get-tuple-element.58.b_ref, bf16[256,1024]{1,0:T(8,128)(2,1)S(1)} %copy-done, ...), custom_call_target="tpu_custom_call" | custom-call | tf_op jit(solution)/shard_map/within/pallas_call | solution.py:622
  70.6 3.1 %within.5 = bf16[256,2048]{1,0:T(8,128)(2,1)S(1)} custom-call(s32[1]{0:T(128)} %bitcast.1.half.core.flag, s32[1]{0:T(128)} %bitcast.1.half.core.flag, bf16[256,4096]{1,0:T(8,128)(2,1)S(1)} %get-tuple-element.57.x_ref, bf16[256,512]{1,0:T(8,128)(2,1)S(1)} %get-tuple-element.58.b_ref, bf16[256,1024]{1,0:T(8,128)(2,1)S(1)} %copy-done, ...), custom_call_target="tpu_custom_call" | custom-call | tf_op jit(solution)/shard_map/within/pallas_call | solution.py:622
  73.7 3.1 %within.6 = bf16[256,2048]{1,0:T(8,128)(2,1)S(1)} custom-call(s32[1]{0:T(128)} %bitcast.half, s32[1]{0:T(128)} %bitcast.1.half.core.flag, bf16[256,4096]{1,0:T(8,128)(2,1)S(1)} %get-tuple-element.54.x_ref, bf16[256,512]{1,0:T(8,128)(2,1)S(1)} %get-tuple-element.55.b_ref, bf16[256,1024]{1,0:T(8,128)(2,1)S(1)} %copy-done, f32[256,128]{1,0:T(8,128)S(1)} %copy-done.1, ...), custom_call_target="tpu_custom_call" | custom-call | tf_op jit(solution)/shard_map/within/pallas_call | solution.py:622
  76.7 3.1 %within.4 = bf16[256,2048]{1,0:T(8,128)(2,1)S(1)} custom-call(s32[1]{0:T(128)} %bitcast.half, s32[1]{0:T(128)} %bitcast.1.half.core.flag, bf16[256,4096]{1,0:T(8,128)(2,1)S(1)} %get-tuple-element.54.x_ref, bf16[256,512]{1,0:T(8,128)(2,1)S(1)} %get-tuple-element.55.b_ref, bf16[256,1024]{1,0:T(8,128)(2,1)S(1)} %copy-done, f32[256,128]{1,0:T(8,128)S(1)} %copy-done.1, ...), custom_call_target="tpu_custom_call" | custom-call | tf_op jit(solution)/shard_map/within/pallas_call | solution.py:622
  79.8 1.7 %finish.4.refs_0_ = bf16[256,8192]{1,0:T(8,128)(2,1)} custom-call(s32[1]{0:T(128)} %bitcast.1.half.core.flag, bf16[256,1024]{1,0:T(8,128)(2,1)S(1)} %copy-done, bf16[128,2048]{1,0:T(8,128)(2,1)S(1)} %shard_map.72.state, f32[256,128]{1,0:T(8,128)S(1)} %get-tuple-element.51.run_ref.run, f32[8,128]{1,0:T(8,128)S(1)} %get-tuple-element.52.base, ...), custom_call_target="tpu_custom_call" | custom-call | tf_op jit(solution)/shard_map/finish/pallas_call | solution.py:657
  81.5 1.7 %finish.5.refs_0_ = bf16[256,8192]{1,0:T(8,128)(2,1)} custom-call(s32[1]{0:T(128)} %bitcast.half, bf16[256,1024]{1,0:T(8,128)(2,1)S(1)} %copy-done, bf16[128,2048]{1,0:T(8,128)(2,1)S(1)} %collective-permute-done.21.state, f32[256,128]{1,0:T(8,128)S(1)} %get-tuple-element.51.run_ref.run, ...), custom_call_target="tpu_custom_call", output_to_operand_aliasing={{}: (7, {})} | custom-call | tf_op jit(solution)/shard_map/finish/pallas_call | solution.py:657
  83.2 1.7 %finish.6.refs_0_ = bf16[256,8192]{1,0:T(8,128)(2,1)} custom-call(s32[1]{0:T(128)} %bitcast.1.half.core.flag, bf16[256,1024]{1,0:T(8,128)(2,1)S(1)} %copy-done, bf16[128,2048]{1,0:T(8,128)(2,1)S(1)} %shard_map.68.state, f32[256,128]{1,0:T(8,128)S(1)} %get-tuple-element.51.run_ref.run, ...), custom_call_target="tpu_custom_call", output_to_operand_aliasing={{}: (7, {})} | custom-call | tf_op jit(solution)/shard_map/finish/pallas_call | solution.py:657
  84.9 1.7 %finish.7 = bf16[256,8192]{1,0:T(8,128)(2,1)} custom-call(s32[1]{0:T(128)} %bitcast.half, bf16[256,1024]{1,0:T(8,128)(2,1)S(1)} %copy-done, bf16[128,2048]{1,0:T(8,128)(2,1)S(1)} %collective-permute-done.10.state, f32[256,128]{1,0:T(8,128)S(1)} %get-tuple-element.51.run_ref.run, ...), custom_call_target="tpu_custom_call", output_to_operand_aliasing={{}: (7, {})} | custom-call | tf_op jit(solution)/shard_map/finish/pallas_call | solution.py:657
  (44 shorter events, 15.4 us)
Async XLA Ops:
  3.0 3.5 %collective-permute-start = (bf16[136,4096]{1,0:T(8,128)(2,1)S(1)}, bf16[136,4096]{1,0:T(8,128)(2,1)S(1)}, u32[]{:S(2)}, u32[]{:S(2)}) collective-permute-start(bf16[136,4096]{1,0:T(8,128)(2,1)S(1)} %get-tuple-element.40), channel_id=1, source_target_pairs={{0,1},{1,0},{2,3},{3,2},{4,5},{5,4},{6,7},{7,6},{8,9},{9,8},{10,11... | collective-permute-start | bytes 3342344 | tf_op jit(solution)/shard_map/ppermute | solution.py:608
  6.7 9.6 %collective-permute-start.12 = (bf16[32,2176]{1,0:T(8,128)(2,1)S(1)}, bf16[32,2176]{1,0:T(8,128)(2,1)S(1)}, u32[]{:S(2)}, u32[]{:S(2)}) collective-permute-start(bf16[32,2176]{1,0:T(8,128)(2,1)S(1)} %get-tuple-element.60), channel_id=1, source_target_pairs={{0,2},{2,0},{4,6},{6,4},{1,3},{3,1},{5,7},{7,5},{8,10},{10,8},{12,... | collective-permute-start | bytes 417800 | tf_op jit(solution)/shard_map/ppermute | solution.py:474
  9.4 13.3 %collective-permute-start.13 = (bf16[32,2176]{1,0:T(8,128)(2,1)S(1)}, bf16[32,2176]{1,0:T(8,128)(2,1)S(1)}, u32[]{:S(2)}, u32[]{:S(2)}) collective-permute-start(bf16[32,2176]{1,0:T(8,128)(2,1)S(1)} %get-tuple-element.61), channel_id=1, source_target_pairs={{0,4},{2,6},{4,0},{6,2},{1,5},{3,7},{5,1},{7,3},{8,12},{10,14},{12... | collective-permute-start | bytes 417800 | tf_op jit(solution)/shard_map/ppermute | solution.py:474
  12.0 61.7 %collective-permute-start.11 = (bf16[136,4096]{1,0:T(8,128)(2,1)S(1)}, bf16[136,4096]{1,0:T(8,128)(2,1)S(1)}, u32[]{:S(2)}, u32[]{:S(2)}) collective-permute-start(bf16[136,4096]{1,0:T(8,128)(2,1)S(1)} %get-tuple-element.39.refs_0_), channel_id=1, source_target_pairs={{0,1},{2,3},{4,5},{6,7},{8,9},{10,11},{12,13},{14,15},{16,17},{18,... | collective-permute-start | bytes 3342344 | tf_op jit(solution)/shard_map/ppermute | solution.py:619
  13.9 11.5 %collective-permute-start.14 = (bf16[32,2176]{1,0:T(8,128)(2,1)S(1)}, bf16[32,2176]{1,0:T(8,128)(2,1)S(1)}, u32[]{:S(2)}, u32[]{:S(2)}) collective-permute-start(bf16[32,2176]{1,0:T(8,128)(2,1)S(1)} %get-tuple-element.62), channel_id=1, source_target_pairs={{0,6},{2,4},{4,2},{6,0},{1,7},{3,5},{5,3},{7,1},{8,14},{10,12},{12... | collective-permute-start | bytes 417800 | tf_op jit(solution)/shard_map/ppermute | solution.py:474
  14.8 13.6 %collective-permute-start.1 = (bf16[32,2176]{1,0:T(8,128)(2,1)S(1)}, bf16[32,2176]{1,0:T(8,128)(2,1)S(1)}, u32[]{:S(2)}, u32[]{:S(2)}) collective-permute-start(bf16[32,2176]{1,0:T(8,128)(2,1)S(1)} %get-tuple-element.42), channel_id=1, source_target_pairs={{0,2},{2,0},{4,6},{6,4},{1,3},{3,1},{5,7},{7,5},{8,10},{10,8},{12,... | collective-permute-start | bytes 417800 | tf_op jit(solution)/shard_map/ppermute | solution.py:474
  16.3 18.3 %collective-permute-start.2 = (bf16[32,2176]{1,0:T(8,128)(2,1)S(1)}, bf16[32,2176]{1,0:T(8,128)(2,1)S(1)}, u32[]{:S(2)}, u32[]{:S(2)}) collective-permute-start(bf16[32,2176]{1,0:T(8,128)(2,1)S(1)} %get-tuple-element.43), channel_id=1, source_target_pairs={{0,4},{2,6},{4,0},{6,2},{1,5},{3,7},{5,1},{7,3},{8,12},{10,14},{12... | collective-permute-start | bytes 417800 | tf_op jit(solution)/shard_map/ppermute | solution.py:474
  22.7 13.4 %collective-permute-start.3 = (bf16[32,2176]{1,0:T(8,128)(2,1)S(1)}, bf16[32,2176]{1,0:T(8,128)(2,1)S(1)}, u32[]{:S(2)}, u32[]{:S(2)}) collective-permute-start(bf16[32,2176]{1,0:T(8,128)(2,1)S(1)} %get-tuple-element.44), channel_id=1, source_target_pairs={{0,6},{2,4},{4,2},{6,0},{1,7},{3,5},{5,3},{7,1},{8,14},{10,12},{12... | collective-permute-start | bytes 417800 | tf_op jit(solution)/shard_map/ppermute | solution.py:474
  25.9 12.2 %collective-permute-start.17 = (bf16[32,2176]{1,0:T(8,128)(2,1)S(1)}, bf16[32,2176]{1,0:T(8,128)(2,1)S(1)}, u32[]{:S(2)}, u32[]{:S(2)}) collective-permute-start(bf16[32,2176]{1,0:T(8,128)(2,1)S(1)} %get-tuple-element.63), channel_id=1, source_target_pairs={{0,24},{8,16},{16,8},{24,0},{1,25},{9,17},{17,9},{25,1},{2,26},{10... | collective-permute-start | bytes 417800 | tf_op jit(solution)/shard_map/ppermute | solution.py:474
  28.4 10.2 %collective-permute-start.16 = (bf16[32,2176]{1,0:T(8,128)(2,1)S(1)}, bf16[32,2176]{1,0:T(8,128)(2,1)S(1)}, u32[]{:S(2)}, u32[]{:S(2)}) collective-permute-start(bf16[32,2176]{1,0:T(8,128)(2,1)S(1)} %get-tuple-element.63), channel_id=1, source_target_pairs={{0,16},{8,24},{16,0},{24,8},{1,17},{9,25},{17,1},{25,9},{2,18},{10... | collective-permute-start | bytes 417800 | tf_op jit(solution)/shard_map/ppermute | solution.py:474
  34.6 5.8 %collective-permute-start.15 = (bf16[32,2176]{1,0:T(8,128)(2,1)S(1)}, bf16[32,2176]{1,0:T(8,128)(2,1)S(1)}, u32[]{:S(2)}, u32[]{:S(2)}) collective-permute-start(bf16[32,2176]{1,0:T(8,128)(2,1)S(1)} %get-tuple-element.63), channel_id=1, source_target_pairs={{0,8},{8,0},{16,24},{24,16},{1,9},{9,1},{17,25},{25,17},{2,10},{10... | collective-permute-start | bytes 417800 | tf_op jit(solution)/shard_map/ppermute | solution.py:474
  36.6 8.2 %collective-permute-start.6 = (bf16[32,2176]{1,0:T(8,128)(2,1)S(1)}, bf16[32,2176]{1,0:T(8,128)(2,1)S(1)}, u32[]{:S(2)}, u32[]{:S(2)}) collective-permute-start(bf16[32,2176]{1,0:T(8,128)(2,1)S(1)} %get-tuple-element.45), channel_id=1, source_target_pairs={{0,24},{8,16},{16,8},{24,0},{1,25},{9,17},{17,9},{25,1},{2,26},{10... | collective-permute-start | bytes 417800 | tf_op jit(solution)/shard_map/ppermute | solution.py:474
  38.1 8.8 %collective-permute-start.5 = (bf16[32,2176]{1,0:T(8,128)(2,1)S(1)}, bf16[32,2176]{1,0:T(8,128)(2,1)S(1)}, u32[]{:S(2)}, u32[]{:S(2)}) collective-permute-start(bf16[32,2176]{1,0:T(8,128)(2,1)S(1)} %get-tuple-element.45), channel_id=1, source_target_pairs={{0,16},{8,24},{16,0},{24,8},{1,17},{9,25},{17,1},{25,9},{2,18},{10... | collective-permute-start | bytes 417800 | tf_op jit(solution)/shard_map/ppermute | solution.py:474
  38.6 9.3 %collective-permute-start.4 = (bf16[32,2176]{1,0:T(8,128)(2,1)S(1)}, bf16[32,2176]{1,0:T(8,128)(2,1)S(1)}, u32[]{:S(2)}, u32[]{:S(2)}) collective-permute-start(bf16[32,2176]{1,0:T(8,128)(2,1)S(1)} %get-tuple-element.45), channel_id=1, source_target_pairs={{0,8},{8,0},{16,24},{24,16},{1,9},{9,1},{17,25},{25,17},{2,10},{10... | collective-permute-start | bytes 417800 | tf_op jit(solution)/shard_map/ppermute | solution.py:474
  40.4 27.1 %copy-start.1 = (f32[256,128]{1,0:T(8,128)S(1)}, f32[256,128]{1,0:T(8,128)}, u32[]{:S(2)}) copy-start(f32[256,128]{1,0:T(8,128)} %step_ref.7) | copy-start | bytes 393220
  40.4 27.1 %copy-start.2 = (f32[128]{0:T(128)S(1)}, f32[128]{0:T(128)}, u32[]{:S(2)}) copy-start(f32[128]{0:T(128)} %param.11) | copy-start | bytes 1540
  40.9 8.9 %collective-permute-start.18 = (bf16[32,2048]{1,0:T(8,128)(2,1)S(1)}, bf16[32,2048]{1,0:T(8,128)(2,1)S(1)}, u32[]{:S(2)}, u32[]{:S(2)}) collective-permute-start(bf16[32,2048]{1,0:T(8,128)(2,1)S(1)} %get-tuple-element.66), channel_id=1, source_target_pairs={{0,2},{2,0},{4,6},{6,4},{1,3},{3,1},{5,7},{7,5},{8,10},{10,8},{12,... | collective-permute-start | bytes 393224 | tf_op jit(solution)/shard_map/ppermute | solution.py:474
  44.8 12.5 %collective-permute-start.19 = (bf16[32,2048]{1,0:T(8,128)(2,1)S(1)}, bf16[32,2048]{1,0:T(8,128)(2,1)S(1)}, u32[]{:S(2)}, u32[]{:S(2)}) collective-permute-start(bf16[32,2048]{1,0:T(8,128)(2,1)S(1)} %get-tuple-element.67), channel_id=1, source_target_pairs={{0,4},{2,6},{4,0},{6,2},{1,5},{3,7},{5,1},{7,3},{8,12},{10,14},{12... | collective-permute-start | bytes 393224 | tf_op jit(solution)/shard_map/ppermute | solution.py:474
  47.0 12.5 %collective-permute-start.20 = (bf16[32,2048]{1,0:T(8,128)(2,1)S(1)}, bf16[32,2048]{1,0:T(8,128)(2,1)S(1)}, u32[]{:S(2)}, u32[]{:S(2)}) collective-permute-start(bf16[32,2048]{1,0:T(8,128)(2,1)S(1)} %get-tuple-element.68), channel_id=1, source_target_pairs={{0,6},{2,4},{4,2},{6,0},{1,7},{3,5},{5,3},{7,1},{8,14},{10,12},{12... | collective-permute-start | bytes 393224 | tf_op jit(solution)/shard_map/ppermute | solution.py:474
  48.5 11.1 %collective-permute-start.7 = (bf16[32,2048]{1,0:T(8,128)(2,1)S(1)}, bf16[32,2048]{1,0:T(8,128)(2,1)S(1)}, u32[]{:S(2)}, u32[]{:S(2)}) collective-permute-start(bf16[32,2048]{1,0:T(8,128)(2,1)S(1)} %get-tuple-element.48), channel_id=1, source_target_pairs={{0,2},{2,0},{4,6},{6,4},{1,3},{3,1},{5,7},{7,5},{8,10},{10,8},{12,... | collective-permute-start | bytes 393224 | tf_op jit(solution)/shard_map/ppermute | solution.py:474
  49.8 17.6 %collective-permute-start.8 = (bf16[32,2048]{1,0:T(8,128)(2,1)S(1)}, bf16[32,2048]{1,0:T(8,128)(2,1)S(1)}, u32[]{:S(2)}, u32[]{:S(2)}) collective-permute-start(bf16[32,2048]{1,0:T(8,128)(2,1)S(1)} %get-tuple-element.49), channel_id=1, source_target_pairs={{0,4},{2,6},{4,0},{6,2},{1,5},{3,7},{5,1},{7,3},{8,12},{10,14},{12... | collective-permute-start | bytes 393224 | tf_op jit(solution)/shard_map/ppermute | solution.py:474
  57.3 10.1 %collective-permute-start.9 = (bf16[32,2048]{1,0:T(8,128)(2,1)S(1)}, bf16[32,2048]{1,0:T(8,128)(2,1)S(1)}, u32[]{:S(2)}, u32[]{:S(2)}) collective-permute-start(bf16[32,2048]{1,0:T(8,128)(2,1)S(1)} %get-tuple-element.50), channel_id=1, source_target_pairs={{0,6},{2,4},{4,2},{6,0},{1,7},{3,5},{5,3},{7,1},{8,14},{10,12},{12... | collective-permute-start | bytes 393224 | tf_op jit(solution)/shard_map/ppermute | solution.py:474
  59.5 22.0 %collective-permute-start.21 = (bf16[128,2048]{1,0:T(8,128)(2,1)S(1)}, bf16[128,2048]{1,0:T(8,128)(2,1)S(1)}, u32[]{:S(2)}, u32[]{:S(2)}) collective-permute-start(bf16[128,2048]{1,0:T(8,128)(2,1)S(1)} %shard_map.72.state), channel_id=1, source_target_pairs={{0,1},{1,0},{2,3},{3,2},{4,5},{5,4},{6,7},{7,6},{8,9},{9,8},{10,11... | collective-permute-start | bytes 1572872 | tf_op jit(solution)/shard_map/ppermute | solution.py:670
  67.4 17.5 %collective-permute-start.10 = (bf16[128,2048]{1,0:T(8,128)(2,1)S(1)}, bf16[128,2048]{1,0:T(8,128)(2,1)S(1)}, u32[]{:S(2)}, u32[]{:S(2)}) collective-permute-start(bf16[128,2048]{1,0:T(8,128)(2,1)S(1)} %shard_map.68.state), channel_id=1, source_target_pairs={{0,1},{1,0},{2,3},{3,2},{4,5},{5,4},{6,7},{7,6},{8,9},{9,8},{10,11... | collective-permute-start | bytes 1572872 | tf_op jit(solution)/shard_map/ppermute | solution.py:670
  (1 other events, 27.1 us)

commit v10 on v9

--- a/solution.py
+++ b/solution.py
@@ -244,11 +244,11 @@
     return body
 
 
-def pieces_kernel(at, own, got, total, *outs, states, chunk):
+def pieces_kernel(at, own, got, total, *outs, states, chunk, with_decay):
     base_out = outs[-1]
     first = at[0] == 0
     rows, cols = outs[0].shape
-    cols = cols - total.shape[1]
+    cols = cols - total.shape[1] if with_decay else cols
     here = slice(chunk * cols, (chunk + 1) * cols)
     on_own, on_got = mixing_rows(first, own, got, states, here)
     packed_decay = chip_decay(first, got, total, states, base_out)
@@ -258,7 +258,8 @@
             take = pl.ds(start + row, ROW_BLOCK)
             mixed = on_own * own[take, here].astype(F32) + on_got * got[take, here].astype(F32)
             out[row : row + ROW_BLOCK, :cols] = mixed.astype(BF16)
-        out[:, cols:] = jnp.concatenate([packed_decay] * (rows // ROW_TILE), axis=0).astype(BF16)
+        if with_decay:
+            out[:, cols:] = jnp.concatenate([packed_decay] * (rows // ROW_TILE), axis=0).astype(BF16)
 
 
 def decays_of(pieces, cols, first_head, width):
@@ -271,11 +272,11 @@
     return values, dot(packed(here, heads), spreader(heads, width))
 
 
-def column_kernel(at, *refs, first_head, width, count):
-    pieces, out, decay_out = refs[:count], refs[count], refs[count + 1]
+def column_kernel(at, *refs, first_head, width, count, with_decay):
+    pieces, tails, out, decay_out = refs[:count], refs[count:-2], refs[-2], refs[-1]
     cols = decay_out.shape[1]
     rows = out.shape[0]
-    values, decay = decays_of(pieces, cols, first_head, width)
+    values, decay = decays_of(tails, cols, first_head, width)
     decay_out[...] = decay
     for place in range(count):
 
@@ -287,7 +288,8 @@
                 state = decay[k : k + 1, :] * state + pieces[k][:, :cols].astype(F32)
             out[:, :cols] = state.astype(BF16)
 
-    fill_decay(out, cols, values, count)
+    if with_decay:
+        fill_decay(out, cols, values, count)
 
 
 def fill_decay(out, cols, values, count):
@@ -299,10 +301,11 @@
 
 
 def chips_kernel(at, *refs, first_head, width, count, blocks):
-    others, decay = refs[: blocks - 1], refs[blocks - 1]
-    pieces, outs, carry = refs[blocks : blocks + count], refs[blocks + count : -1], refs[-1]
+    others, refs = refs[: blocks - 1], refs[blocks - 1 :]
+    tails, decay, refs = refs[: blocks - 1], refs[blocks - 1], refs[blocks:]
+    pieces, outs, carry = refs[:count], refs[count:-1], refs[-1]
     rows, cols = outs[0].shape
-    _, passed = decays_of(others, cols, first_head, width)
+    _, passed = decays_of(tails, cols, first_head, width)
     for place in range(blocks):
 
         @pl.when(at[2] == place)
@@ -421,13 +424,39 @@
             out[start:stop, cols] = (added[:, cols] + part).astype(BF16)
 
 
-def final_kernel(half, c, state, run, base, matrix, within, *refs, dims):
+def own_final_kernel(half, c, state, run, base, matrix, within, result, *, dims):
+    add_carried(half[0], c, state, run, base, matrix, within, result, dims, lambda k: None)
+
+
+def final_kernel(half, c, state, run, base, matrix, within, own_result, *refs, dims):
     out, result, sems = refs[-3:]
+    per_half, group_cols, _, first = dims
+    count = state.shape[1] // group_cols
+    copies = []
+
+    def send(source, side, k, sem):
+        home = pl.multiple_of((side * per_half + first + k) * group_cols, group_cols)
+        copies.append(
+            pltpu.make_async_copy(
+                source.at[:, pl.ds(k * group_cols, group_cols)], out.at[:, pl.ds(home, group_cols)], sems.at[sem]
+            )
+        )
+        copies[-1].start()
+
+    for k in range(count):
+        send(own_result, 1 - half[0], k, count + k)
+    add_carried(
+        half[0], c, state, run, base, matrix, within, result, dims, lambda k: send(result, half[0], k, k)
+    )
+    for copy in copies:
+        copy.wait()
+
+
+def add_carried(half, c, state, run, base, matrix, within, result, dims, when_done):
     per_half, group_cols, states, first = dims
-    operand = packed_half(jnp.exp2(run[...] + base[:1, :]), half[0])
-    copies = []
+    operand = packed_half(jnp.exp2(run[...] + base[:1, :]), half)
     for k in range(state.shape[1] // group_cols):
-        group = half[0] * per_half + first + k
+        group = half * per_half + first + k
         rows = c[:, pl.ds(pl.multiple_of(group * states, states), states)]
         tiles = group_cols // TILE
         products = {}
@@ -441,15 +470,7 @@
                 cols = slice(k * group_cols + m * TILE, k * group_cols + (m + 1) * TILE)
                 carried, factor = products.pop(m)
                 result[:, cols] = (within[:, cols].astype(F32) + factor * carried).astype(BF16)
-        home = pl.multiple_of(group * group_cols, group_cols)
-        copies.append(
-            pltpu.make_async_copy(
-                result.at[:, pl.ds(k * group_cols, group_cols)], out.at[:, pl.ds(home, group_cols)], sems.at[k]
-            )
-        )
-        copies[-1].start()
-    for copy in copies:
-        copy.wait()
+        when_done(k)
 
 
 def small_call(kernel, in_specs, out_shape, scratch=(), out_specs=None):
@@ -485,34 +506,39 @@
     smem = pl.BlockSpec(memory_space=pltpu.SMEM)
     vmem = pl.BlockSpec(memory_space=pltpu.VMEM)
     shape = jax.ShapeDtypeStruct
-    gathered = []
-    for chunk in range(CHUNKS):
+    gathered = {}
+    lead = CHUNKS - 1
+    for chunk in reversed(range(CHUNKS)):
+        extra = heads if chunk == lead else 0
         *pieces, base = small_call(
-            functools.partial(placed(pieces_kernel), states=states, chunk=chunk),
+            functools.partial(placed(pieces_kernel), states=states, chunk=chunk, with_decay=chunk == lead),
             [smem] * 3 + [vmem] * 3,
-            [shape((rows, cols + heads), BF16)] * count + [shape((ROW_TILE, heads), F32)],
+            [shape((rows, cols + extra), BF16)] * count + [shape((ROW_TILE, heads), F32)],
         )(*at, own, got, total)
-        gathered.append(swapped(pieces, chip_axis))
-    entering = []
-    for chunk in range(CHUNKS):
+        gathered[chunk] = swapped(pieces, chip_axis)
+    entering = {}
+    for chunk in reversed(range(CHUNKS)):
+        extra = heads if chunk == lead else 0
         first_head = chunk * cols // width
         pieces = gathered[chunk]
         column, decay = small_call(
-            functools.partial(placed(column_kernel), first_head=first_head, width=width, count=count),
-            [smem] * 3 + [vmem] * count,
-            [shape((rows, cols + heads), BF16), shape((ROW_TILE, cols), F32)],
-        )(*at, *pieces)
+            functools.partial(placed(column_kernel), first_head=first_head, width=width, count=count, with_decay=chunk == lead),
+            [smem] * 3 + [vmem] * (2 * count),
+            [shape((rows, cols + extra), BF16), shape((ROW_TILE, cols), F32)],
+        )(*at, *pieces, *gathered[lead])
         others = swapped([column] * blocks, outer_axis)[1:]
+        if chunk == lead:
+            tails = others
         states_out = small_call(
             functools.partial(
                 placed(chips_kernel), first_head=first_head, width=width, count=count, blocks=blocks
             ),
-            [smem] * 3 + [vmem] * (count + blocks),
+            [smem] * 3 + [vmem] * (count + 2 * blocks - 1),
             [shape((rows, cols), BF16)] * count,
             [pltpu.VMEM((rows, cols), F32)],
-        )(*at, *others, decay, *pieces)
+        )(*at, *others, *tails, decay, *pieces)
         states_out = swapped(states_out, chip_axis)
-        entering += small_call(
+        (entering[chunk],) = small_call(
             functools.partial(placed(assemble_kernel), count=count),
             [smem] * 3 + [vmem] * count,
             [shape((states, cols), BF16)],
@@ -652,24 +678,32 @@
 
     mixed = jax.ShapeDtypeStruct((tokens, channels), BF16)
 
-    def finish(half, chunk, state, part, *result):
-        cols = PER_CALL * group_cols
+    cols = PER_CALL * group_cols
+
+    def finish_own(chunk, state, part):
+        return small_call(
+            functools.partial(own_final_kernel, dims=state_dims + (chunk * PER_CALL,)),
+            [smem] + [vmem] * 6,
+            [jax.ShapeDtypeStruct((tokens, cols), BF16)],
+        )(mine, c_matrix, state, run, base, matrix, part)
+
+    def finish_other(chunk, state, part, own_result, *result):
         return pl.pallas_call(
             functools.partial(final_kernel, dims=state_dims + (chunk * PER_CALL,)),
-            in_specs=[smem] + [vmem] * 6 + [hbm] * len(result),
+            in_specs=[smem] + [vmem] * 7 + [hbm] * len(result),
             out_specs=hbm,
             out_shape=mixed,
-            scratch_shapes=[pltpu.VMEM((tokens, cols), BF16), pltpu.SemaphoreType.DMA((PER_CALL,))],
-            input_output_aliases={7: 0} if result else {},
+            scratch_shapes=[pltpu.VMEM((tokens, cols), BF16), pltpu.SemaphoreType.DMA((2 * PER_CALL,))],
+            input_output_aliases={8: 0} if result else {},
             compiler_params=plain_params(),
-            name="finish",
-        )(half, c_matrix, state, run, base, matrix, part, *result)
+            name="finish_other",
+        )(other, c_matrix, state, run, base, matrix, part, own_result, *result)
 
     result = ()
     for chunk in reversed(range(CHUNKS)):
         got_entering = lax.ppermute(entering[chunk], core_axis, swap)
-        result = (finish(mine, chunk, entering[chunk], own_within[chunk], *result),)
-        result = (finish(other, chunk, got_entering, other_within[chunk], *result),)
+        (own_result,) = finish_own(chunk, entering[chunk], own_within[chunk])
+        result = (finish_other(chunk, got_entering, other_within[chunk], own_result, *result),)
     return result[0]
 
 

time: 87 us -> 85.2 us (0.979)
  waiting for transfers between devices: 25.8 us -> 16.4 us
  starting transfers between devices: 32.5 us -> 41.9 us
  Pallas kernels: 28.1 us -> 26.3 us
    ppermute x18, waiting for transfers between devices: 25.8 us -> 16.4 us  [swapped(): done[k] = lax.ppermute(arrays[k], axis, xor_route(size, k))]
    ppermute x18, starting transfers between devices: 29.9 us -> 39.3 us  [swapped(): done[k] = lax.ppermute(arrays[k], axis, xor_route(size, k))]
    pallas_call x4, Pallas kernels: 6.79 us -> 5.21 us  [the longest x2 3.43 us: finish_other(): pl.pallas_call(functools.partial(final_kernel, dims=state_dims + (chunk *...]
  transfers between devices with their start and end apart: 22 -> 22, of which waited for: 7 -> 6; matrix products, arithmetic and copies ran while one was open for 0% -> 0% of each run, Pallas kernels for 27% -> 25%
where the time goes in v10:
time: 85.2 us; the launch traced here: 85.1 us
  starting transfers between devices  41.9 us (49%)
  Pallas kernels  26.3 us (31%)
  waiting for transfers between devices  16.4 us (19%)
    ppermute x18, starting transfers between devices, swapped(): done[k] = lax.ppermute(arrays[k], axis, xor_route(size, k))  39.3 us
    ppermute x18, waiting for transfers between devices, swapped(): done[k] = lax.ppermute(arrays[k], axis, xor_route(size, k))  16.4 us
    pallas_call x4, Pallas kernels, within(): pl.pallas_call(functools.partial(within_kernel, dims=half_dims, first_gro...  12.2 us
    pallas_call x2, Pallas kernels, finish_other(): pl.pallas_call(functools.partial(final_kernel, dims=state_dims + (chunk *...  3.43 us
    pallas_call x1, Pallas kernels, local(): pl.pallas_call(functools.partial(send_state_kernel, dims=state_dims), in_...  2.94 us
    pallas_call x1, Pallas kernels, local(): small_call(functools.partial(own_state_kernel, dims=state_dims), [smem, h...  2.89 us
    ppermute x1, starting transfers between devices, local(): late = lax.ppermute(own, core_axis, swap[:1])  1.9 us
    pallas_call x2, Pallas kernels, finish_own(): small_call(functools.partial(own_final_kernel, dims=state_dims + (chunk *...  1.77 us
  transfers between devices with their start and end apart: 22, of which 6 were waited for; matrix products, arithmetic and copies ran while one was open for 0% of the time, Pallas kernels for 25%

profile of v10, /device:TPU:0, one launch (start us, length us, event | category | flops | bytes accessed | tf_op | source)
XLA Modules:
  0.0 85.1 jit_solution(13569042496280734883)
XLA Ops:
  0.0 2.9 %send_state.1 = (bf16[136,4096]{1,0:T(8,128)(2,1)S(1)}, f32[256,128]{1,0:T(8,128)S(1)}, f32[128,256]{1,0:T(8,128)S(1)}, f32[256,128]{1,0:T(8,128)S(1)}, f32[8,12...) custom-call(s32[1]{0:T(128)} %bitcast.half, s32[1]{0:T(128)} %bitcast.2.chip, ...), custom_call_target="tpu_custom_call" | custom-call | tf_op jit(solution)/shard_map/send_state/pallas_call | solution.py:614
  3.5 2.9 %shard_map.64 = (bf16[136,4096]{1,0:T(8,128)(2,1)S(1)}, bf16[128,4096]{1,0:T(8,128)(2,1)S(1)}, bf16[256,4096]{1,0:T(8,128)(2,1)S(1)}, bf16[256,512]{1,0:T(8,128)(2,1)S(1)}) custom-call(s32[1]{0:T(128)} %bitcast.1.half.core.flag, bf16[256,8192]{1,0:T(8,128)(2,1)} %x.3, bf16[256,1024]{1,0:T(8,128)(2,1)} %b.3, f32[256,128]{1,0:T(8,128)S(1)} %get-tuple-element.37.factor, ...), custom_call_target="tpu_custom_call" | custom-call | tf_op jit(solution)/shard_map/pallas_call | solution.py:636
  7.1 2.6 %collective-permute-start.4 = (bf16[32,2176]{1,0:T(8,128)(2,1)S(1)}, bf16[32,2176]{1,0:T(8,128)(2,1)S(1)}, u32[]{:S(2)}, u32[]{:S(2)}) collective-permute-start(bf16[32,2176]{1,0:T(8,128)(2,1)S(1)} %get-tuple-element.46), channel_id=1, source_target_pairs={{0,2},{2,0},{4,6},{6,4},{1,3},{3,1},{5,7},{7,5},{8,10},{10,8},{12,... | collective-permute-start | bytes 417800 | tf_op jit(solution)/shard_map/ppermute | solution.py:495
  9.7 2.6 %collective-permute-start.5 = (bf16[32,2176]{1,0:T(8,128)(2,1)S(1)}, bf16[32,2176]{1,0:T(8,128)(2,1)S(1)}, u32[]{:S(2)}, u32[]{:S(2)}) collective-permute-start(bf16[32,2176]{1,0:T(8,128)(2,1)S(1)} %get-tuple-element.47), channel_id=1, source_target_pairs={{0,4},{2,6},{4,0},{6,2},{1,5},{3,7},{5,1},{7,3},{8,12},{10,14},{12... | collective-permute-start | bytes 417800 | tf_op jit(solution)/shard_map/ppermute | solution.py:495
  12.3 1.9 %collective-permute-start.17 = (bf16[136,4096]{1,0:T(8,128)(2,1)S(1)}, bf16[136,4096]{1,0:T(8,128)(2,1)S(1)}, u32[]{:S(2)}, u32[]{:S(2)}) collective-permute-start(bf16[136,4096]{1,0:T(8,128)(2,1)S(1)} %get-tuple-element.39.refs_0_), channel_id=1, source_target_pairs={{0,1},{2,3},{4,5},{6,7},{8,9},{10,11},{12,13},{14,15},{16,17},{18,... | collective-permute-start | bytes 3342344 | tf_op jit(solution)/shard_map/ppermute | solution.py:645
  16.8 2.1 %collective-permute-start.2 = (bf16[32,2048]{1,0:T(8,128)(2,1)S(1)}, bf16[32,2048]{1,0:T(8,128)(2,1)S(1)}, u32[]{:S(2)}, u32[]{:S(2)}) collective-permute-start(bf16[32,2048]{1,0:T(8,128)(2,1)S(1)} %get-tuple-element.43), channel_id=1, source_target_pairs={{0,4},{2,6},{4,0},{6,2},{1,5},{3,7},{5,1},{7,3},{8,12},{10,14},{12... | collective-permute-start | bytes 393224 | tf_op jit(solution)/shard_map/ppermute | solution.py:495
  19.0 4.0 %collective-permute-done.5.refs_6_.refs_2_.refs_9_ = bf16[32,2176]{1,0:T(8,128)(2,1)S(1)} collective-permute-done((bf16[32,2176]{1,0:T(8,128)(2,1)S(1)}, bf16[32,2176]{1,0:T(8,128)(2,1)S(1)}, u32[]{:S(2)}, u32[]{:S(2)}) %collective-permute-start.5) | collective-permute-done | bytes 139296 | tf_op jit(solution)/shard_map/ppermute | solution.py:495
  23.0 2.7 %collective-permute-start.3 = (bf16[32,2048]{1,0:T(8,128)(2,1)S(1)}, bf16[32,2048]{1,0:T(8,128)(2,1)S(1)}, u32[]{:S(2)}, u32[]{:S(2)}) collective-permute-start(bf16[32,2048]{1,0:T(8,128)(2,1)S(1)} %get-tuple-element.44), channel_id=1, source_target_pairs={{0,6},{2,4},{4,2},{6,0},{1,7},{3,5},{5,3},{7,1},{8,14},{10,12},{12... | collective-permute-start | bytes 393224 | tf_op jit(solution)/shard_map/ppermute | solution.py:495
  26.3 2.5 %collective-permute-start.12 = (bf16[32,2176]{1,0:T(8,128)(2,1)S(1)}, bf16[32,2176]{1,0:T(8,128)(2,1)S(1)}, u32[]{:S(2)}, u32[]{:S(2)}) collective-permute-start(bf16[32,2176]{1,0:T(8,128)(2,1)S(1)} %get-tuple-element.50), channel_id=1, source_target_pairs={{0,24},{8,16},{16,8},{24,0},{1,25},{9,17},{17,9},{25,1},{2,26},{10... | collective-permute-start | bytes 417800 | tf_op jit(solution)/shard_map/ppermute | solution.py:495
  29.2 5.2 %collective-permute-done.2.refs_2_.refs_9_ = bf16[32,2048]{1,0:T(8,128)(2,1)S(1)} collective-permute-done((bf16[32,2048]{1,0:T(8,128)(2,1)S(1)}, bf16[32,2048]{1,0:T(8,128)(2,1)S(1)}, u32[]{:S(2)}, u32[]{:S(2)}) %collective-permute-start.2) | collective-permute-done | bytes 131104 | tf_op jit(solution)/shard_map/ppermute | solution.py:495
  36.3 1.5 %collective-permute-start.9 = (bf16[32,2048]{1,0:T(8,128)(2,1)S(1)}, bf16[32,2048]{1,0:T(8,128)(2,1)S(1)}, u32[]{:S(2)}, u32[]{:S(2)}) collective-permute-start(bf16[32,2048]{1,0:T(8,128)(2,1)S(1)} %get-tuple-element.49), channel_id=1, source_target_pairs={{0,24},{8,16},{16,8},{24,0},{1,25},{9,17},{17,9},{25,1},{2,26},{10... | collective-permute-start | bytes 393224 | tf_op jit(solution)/shard_map/ppermute | solution.py:495
  38.4 1.5 %collective-permute-start.7 = (bf16[32,2048]{1,0:T(8,128)(2,1)S(1)}, bf16[32,2048]{1,0:T(8,128)(2,1)S(1)}, u32[]{:S(2)}, u32[]{:S(2)}) collective-permute-start(bf16[32,2048]{1,0:T(8,128)(2,1)S(1)} %get-tuple-element.49), channel_id=1, source_target_pairs={{0,8},{8,0},{16,24},{24,16},{1,9},{9,1},{17,25},{25,17},{2,10},{10... | collective-permute-start | bytes 393224 | tf_op jit(solution)/shard_map/ppermute | solution.py:495
  40.7 1.8 %collective-permute-start.18 = (bf16[32,2048]{1,0:T(8,128)(2,1)S(1)}, bf16[32,2048]{1,0:T(8,128)(2,1)S(1)}, u32[]{:S(2)}, u32[]{:S(2)}) collective-permute-start(bf16[32,2048]{1,0:T(8,128)(2,1)S(1)} %get-tuple-element.66), channel_id=1, source_target_pairs={{0,2},{2,0},{4,6},{6,4},{1,3},{3,1},{5,7},{7,5},{8,10},{10,8},{12,... | collective-permute-start | bytes 393224 | tf_op jit(solution)/shard_map/ppermute | solution.py:495
  42.6 1.8 %collective-permute-done.9.refs_2_ = bf16[32,2048]{1,0:T(8,128)(2,1)S(1)} collective-permute-done((bf16[32,2048]{1,0:T(8,128)(2,1)S(1)}, bf16[32,2048]{1,0:T(8,128)(2,1)S(1)}, u32[]{:S(2)}, u32[]{:S(2)}) %collective-permute-start.9) | collective-permute-done | bytes 131104 | tf_op jit(solution)/shard_map/ppermute | solution.py:495
  44.4 2.6 %collective-permute-start.19 = (bf16[32,2048]{1,0:T(8,128)(2,1)S(1)}, bf16[32,2048]{1,0:T(8,128)(2,1)S(1)}, u32[]{:S(2)}, u32[]{:S(2)}) collective-permute-start(bf16[32,2048]{1,0:T(8,128)(2,1)S(1)} %get-tuple-element.67), channel_id=1, source_target_pairs={{0,4},{2,6},{4,0},{6,2},{1,5},{3,7},{5,1},{7,3},{8,12},{10,14},{12... | collective-permute-start | bytes 393224 | tf_op jit(solution)/shard_map/ppermute | solution.py:495
  48.9 1.8 %collective-permute-start.20 = (bf16[32,2048]{1,0:T(8,128)(2,1)S(1)}, bf16[32,2048]{1,0:T(8,128)(2,1)S(1)}, u32[]{:S(2)}, u32[]{:S(2)}) collective-permute-start(bf16[32,2048]{1,0:T(8,128)(2,1)S(1)} %get-tuple-element.68), channel_id=1, source_target_pairs={{0,6},{2,4},{4,2},{6,0},{1,7},{3,5},{5,3},{7,1},{8,14},{10,12},{12... | collective-permute-start | bytes 393224 | tf_op jit(solution)/shard_map/ppermute | solution.py:495
  52.0 11.4 %collective-permute-start.15 = (bf16[32,2048]{1,0:T(8,128)(2,1)S(1)}, bf16[32,2048]{1,0:T(8,128)(2,1)S(1)}, u32[]{:S(2)}, u32[]{:S(2)}) collective-permute-start(bf16[32,2048]{1,0:T(8,128)(2,1)S(1)} %get-tuple-element.55), channel_id=1, source_target_pairs={{0,6},{2,4},{4,2},{6,0},{1,7},{3,5},{5,3},{7,1},{8,14},{10,12},{12... | collective-permute-start | bytes 393224 | tf_op jit(solution)/shard_map/ppermute | solution.py:495
  63.5 3.7 %collective-permute-done.14.refs_2_ = bf16[32,2048]{1,0:T(8,128)(2,1)S(1)} collective-permute-done((bf16[32,2048]{1,0:T(8,128)(2,1)S(1)}, bf16[32,2048]{1,0:T(8,128)(2,1)S(1)}, u32[]{:S(2)}, u32[]{:S(2)}) %collective-permute-start.14) | collective-permute-done | bytes 131104 | tf_op jit(solution)/shard_map/ppermute | solution.py:495
  67.4 3.0 %within.7 = bf16[256,2048]{1,0:T(8,128)(2,1)S(1)} custom-call(s32[1]{0:T(128)} %bitcast.1.half.core.flag, s32[1]{0:T(128)} %bitcast.1.half.core.flag, bf16[256,4096]{1,0:T(8,128)(2,1)S(1)} %get-tuple-element.62.x_ref, bf16[256,512]{1,0:T(8,128)(2,1)S(1)} %get-tuple-element.63.b_ref, bf16[256,1024]{1,0:T(8,128)(2,1)S(1)} %copy-done, ...), custom_call_target="tpu_custom_call" | custom-call | tf_op jit(solution)/shard_map/within/pallas_call | solution.py:648
  70.4 3.1 %within.5 = bf16[256,2048]{1,0:T(8,128)(2,1)S(1)} custom-call(s32[1]{0:T(128)} %bitcast.1.half.core.flag, s32[1]{0:T(128)} %bitcast.1.half.core.flag, bf16[256,4096]{1,0:T(8,128)(2,1)S(1)} %get-tuple-element.62.x_ref, bf16[256,512]{1,0:T(8,128)(2,1)S(1)} %get-tuple-element.63.b_ref, bf16[256,1024]{1,0:T(8,128)(2,1)S(1)} %copy-done, ...), custom_call_target="tpu_custom_call" | custom-call | tf_op jit(solution)/shard_map/within/pallas_call | solution.py:648
  73.5 3.1 %within.6 = bf16[256,2048]{1,0:T(8,128)(2,1)S(1)} custom-call(s32[1]{0:T(128)} %bitcast.half, s32[1]{0:T(128)} %bitcast.1.half.core.flag, bf16[256,4096]{1,0:T(8,128)(2,1)S(1)} %get-tuple-element.59.x_ref, bf16[256,512]{1,0:T(8,128)(2,1)S(1)} %get-tuple-element.60.b_ref, bf16[256,1024]{1,0:T(8,128)(2,1)S(1)} %copy-done, f32[256,128]{1,0:T(8,128)S(1)} %copy-done.1, ...), custom_call_target="tpu_custom_call" | custom-call | tf_op jit(solution)/shard_map/within/pallas_call | solution.py:648
  76.6 3.1 %within.4 = bf16[256,2048]{1,0:T(8,128)(2,1)S(1)} custom-call(s32[1]{0:T(128)} %bitcast.half, s32[1]{0:T(128)} %bitcast.1.half.core.flag, bf16[256,4096]{1,0:T(8,128)(2,1)S(1)} %get-tuple-element.59.x_ref, bf16[256,512]{1,0:T(8,128)(2,1)S(1)} %get-tuple-element.60.b_ref, bf16[256,1024]{1,0:T(8,128)(2,1)S(1)} %copy-done, f32[256,128]{1,0:T(8,128)S(1)} %copy-done.1, ...), custom_call_target="tpu_custom_call" | custom-call | tf_op jit(solution)/shard_map/within/pallas_call | solution.py:648
  81.4 1.7 %finish_other.2.refs_0_ = bf16[256,8192]{1,0:T(8,128)(2,1)} custom-call(s32[1]{0:T(128)} %bitcast.half, bf16[256,1024]{1,0:T(8,128)(2,1)S(1)} %copy-done, bf16[128,2048]{1,0:T(8,128)(2,1)S(1)} %collective-permute-done.21.state, f32[256,128]{1,0:T(8,128)S(1)} %get-tuple-element.56.run_ref.run, f32[8,128]{1,0:T(8,128)S(1)} %get-tuple-element.57.base, ...), custom_call_target="tpu_custom_call" | custom-call | tf_op jit(solution)/shard_map/finish_other/pallas_call | solution.py:691
  83.2 1.7 %finish_other.3 = bf16[256,8192]{1,0:T(8,128)(2,1)} custom-call(s32[1]{0:T(128)} %bitcast.half, bf16[256,1024]{1,0:T(8,128)(2,1)S(1)} %copy-done, bf16[128,2048]{1,0:T(8,128)(2,1)S(1)} %collective-permute-done.16.state, f32[256,128]{1,0:T(8,128)S(1)} %get-tuple-element.56.run_ref.run, ...), custom_call_target="tpu_custom_call", output_to_operand_aliasing={{}: (8, {})} | custom-call | tf_op jit(solution)/shard_map/finish_other/pallas_call | solution.py:691
  (44 shorter events, 13.4 us)
Async XLA Ops:
  3.0 3.5 %collective-permute-start = (bf16[136,4096]{1,0:T(8,128)(2,1)S(1)}, bf16[136,4096]{1,0:T(8,128)(2,1)S(1)}, u32[]{:S(2)}, u32[]{:S(2)}) collective-permute-start(bf16[136,4096]{1,0:T(8,128)(2,1)S(1)} %get-tuple-element.40), channel_id=1, source_target_pairs={{0,1},{1,0},{2,3},{3,2},{4,5},{5,4},{6,7},{7,6},{8,9},{9,8},{10,11... | collective-permute-start | bytes 3342344 | tf_op jit(solution)/shard_map/ppermute | solution.py:634
  7.1 9.7 %collective-permute-start.4 = (bf16[32,2176]{1,0:T(8,128)(2,1)S(1)}, bf16[32,2176]{1,0:T(8,128)(2,1)S(1)}, u32[]{:S(2)}, u32[]{:S(2)}) collective-permute-start(bf16[32,2176]{1,0:T(8,128)(2,1)S(1)} %get-tuple-element.46), channel_id=1, source_target_pairs={{0,2},{2,0},{4,6},{6,4},{1,3},{3,1},{5,7},{7,5},{8,10},{10,8},{12,... | collective-permute-start | bytes 417800 | tf_op jit(solution)/shard_map/ppermute | solution.py:495
  9.7 13.3 %collective-permute-start.5 = (bf16[32,2176]{1,0:T(8,128)(2,1)S(1)}, bf16[32,2176]{1,0:T(8,128)(2,1)S(1)}, u32[]{:S(2)}, u32[]{:S(2)}) collective-permute-start(bf16[32,2176]{1,0:T(8,128)(2,1)S(1)} %get-tuple-element.47), channel_id=1, source_target_pairs={{0,4},{2,6},{4,0},{6,2},{1,5},{3,7},{5,1},{7,3},{8,12},{10,14},{12... | collective-permute-start | bytes 417800 | tf_op jit(solution)/shard_map/ppermute | solution.py:495
  12.3 61.2 %collective-permute-start.17 = (bf16[136,4096]{1,0:T(8,128)(2,1)S(1)}, bf16[136,4096]{1,0:T(8,128)(2,1)S(1)}, u32[]{:S(2)}, u32[]{:S(2)}) collective-permute-start(bf16[136,4096]{1,0:T(8,128)(2,1)S(1)} %get-tuple-element.39.refs_0_), channel_id=1, source_target_pairs={{0,1},{2,3},{4,5},{6,7},{8,9},{10,11},{12,13},{14,15},{16,17},{18,... | collective-permute-start | bytes 3342344 | tf_op jit(solution)/shard_map/ppermute | solution.py:645
  14.2 11.5 %collective-permute-start.6 = (bf16[32,2176]{1,0:T(8,128)(2,1)S(1)}, bf16[32,2176]{1,0:T(8,128)(2,1)S(1)}, u32[]{:S(2)}, u32[]{:S(2)}) collective-permute-start(bf16[32,2176]{1,0:T(8,128)(2,1)S(1)} %get-tuple-element.48), channel_id=1, source_target_pairs={{0,6},{2,4},{4,2},{6,0},{1,7},{3,5},{5,3},{7,1},{8,14},{10,12},{12... | collective-permute-start | bytes 417800 | tf_op jit(solution)/shard_map/ppermute | solution.py:495
  14.7 14.1 %collective-permute-start.1 = (bf16[32,2048]{1,0:T(8,128)(2,1)S(1)}, bf16[32,2048]{1,0:T(8,128)(2,1)S(1)}, u32[]{:S(2)}, u32[]{:S(2)}) collective-permute-start(bf16[32,2048]{1,0:T(8,128)(2,1)S(1)} %get-tuple-element.42), channel_id=1, source_target_pairs={{0,2},{2,0},{4,6},{6,4},{1,3},{3,1},{5,7},{7,5},{8,10},{10,8},{12,... | collective-permute-start | bytes 393224 | tf_op jit(solution)/shard_map/ppermute | solution.py:495
  16.8 17.6 %collective-permute-start.2 = (bf16[32,2048]{1,0:T(8,128)(2,1)S(1)}, bf16[32,2048]{1,0:T(8,128)(2,1)S(1)}, u32[]{:S(2)}, u32[]{:S(2)}) collective-permute-start(bf16[32,2048]{1,0:T(8,128)(2,1)S(1)} %get-tuple-element.43), channel_id=1, source_target_pairs={{0,4},{2,6},{4,0},{6,2},{1,5},{3,7},{5,1},{7,3},{8,12},{10,14},{12... | collective-permute-start | bytes 393224 | tf_op jit(solution)/shard_map/ppermute | solution.py:495
  23.0 12.9 %collective-permute-start.3 = (bf16[32,2048]{1,0:T(8,128)(2,1)S(1)}, bf16[32,2048]{1,0:T(8,128)(2,1)S(1)}, u32[]{:S(2)}, u32[]{:S(2)}) collective-permute-start(bf16[32,2048]{1,0:T(8,128)(2,1)S(1)} %get-tuple-element.44), channel_id=1, source_target_pairs={{0,6},{2,4},{4,2},{6,0},{1,7},{3,5},{5,3},{7,1},{8,14},{10,12},{12... | collective-permute-start | bytes 393224 | tf_op jit(solution)/shard_map/ppermute | solution.py:495
  26.3 11.6 %collective-permute-start.12 = (bf16[32,2176]{1,0:T(8,128)(2,1)S(1)}, bf16[32,2176]{1,0:T(8,128)(2,1)S(1)}, u32[]{:S(2)}, u32[]{:S(2)}) collective-permute-start(bf16[32,2176]{1,0:T(8,128)(2,1)S(1)} %get-tuple-element.50), channel_id=1, source_target_pairs={{0,24},{8,16},{16,8},{24,0},{1,25},{9,17},{17,9},{25,1},{2,26},{10... | collective-permute-start | bytes 417800 | tf_op jit(solution)/shard_map/ppermute | solution.py:495
  28.7 9.7 %collective-permute-start.11 = (bf16[32,2176]{1,0:T(8,128)(2,1)S(1)}, bf16[32,2176]{1,0:T(8,128)(2,1)S(1)}, u32[]{:S(2)}, u32[]{:S(2)}) collective-permute-start(bf16[32,2176]{1,0:T(8,128)(2,1)S(1)} %get-tuple-element.50), channel_id=1, source_target_pairs={{0,16},{8,24},{16,0},{24,8},{1,17},{9,25},{17,1},{25,9},{2,18},{10... | collective-permute-start | bytes 417800 | tf_op jit(solution)/shard_map/ppermute | solution.py:495
  34.4 5.8 %collective-permute-start.10 = (bf16[32,2176]{1,0:T(8,128)(2,1)S(1)}, bf16[32,2176]{1,0:T(8,128)(2,1)S(1)}, u32[]{:S(2)}, u32[]{:S(2)}) collective-permute-start(bf16[32,2176]{1,0:T(8,128)(2,1)S(1)} %get-tuple-element.50), channel_id=1, source_target_pairs={{0,8},{8,0},{16,24},{24,16},{1,9},{9,1},{17,25},{25,17},{2,10},{10... | collective-permute-start | bytes 417800 | tf_op jit(solution)/shard_map/ppermute | solution.py:495
  36.3 8.0 %collective-permute-start.9 = (bf16[32,2048]{1,0:T(8,128)(2,1)S(1)}, bf16[32,2048]{1,0:T(8,128)(2,1)S(1)}, u32[]{:S(2)}, u32[]{:S(2)}) collective-permute-start(bf16[32,2048]{1,0:T(8,128)(2,1)S(1)} %get-tuple-element.49), channel_id=1, source_target_pairs={{0,24},{8,16},{16,8},{24,0},{1,25},{9,17},{17,9},{25,1},{2,26},{10... | collective-permute-start | bytes 393224 | tf_op jit(solution)/shard_map/ppermute | solution.py:495
  37.9 9.1 %collective-permute-start.8 = (bf16[32,2048]{1,0:T(8,128)(2,1)S(1)}, bf16[32,2048]{1,0:T(8,128)(2,1)S(1)}, u32[]{:S(2)}, u32[]{:S(2)}) collective-permute-start(bf16[32,2048]{1,0:T(8,128)(2,1)S(1)} %get-tuple-element.49), channel_id=1, source_target_pairs={{0,16},{8,24},{16,0},{24,8},{1,17},{9,25},{17,1},{25,9},{2,18},{10... | collective-permute-start | bytes 393224 | tf_op jit(solution)/shard_map/ppermute | solution.py:495
  38.4 8.6 %collective-permute-start.7 = (bf16[32,2048]{1,0:T(8,128)(2,1)S(1)}, bf16[32,2048]{1,0:T(8,128)(2,1)S(1)}, u32[]{:S(2)}, u32[]{:S(2)}) collective-permute-start(bf16[32,2048]{1,0:T(8,128)(2,1)S(1)} %get-tuple-element.49), channel_id=1, source_target_pairs={{0,8},{8,0},{16,24},{24,16},{1,9},{9,1},{17,25},{25,17},{2,10},{10... | collective-permute-start | bytes 393224 | tf_op jit(solution)/shard_map/ppermute | solution.py:495
  40.7 26.7 %copy-start = (bf16[256,1024]{1,0:T(8,128)(2,1)S(1)}, bf16[256,1024]{1,0:T(8,128)(2,1)}, u32[]{:S(2)}) copy-start(bf16[256,1024]{1,0:T(8,128)(2,1)} %c.7) | copy-start | bytes 1572868
  40.7 26.7 %copy-start.1 = (f32[256,128]{1,0:T(8,128)S(1)}, f32[256,128]{1,0:T(8,128)}, u32[]{:S(2)}) copy-start(f32[256,128]{1,0:T(8,128)} %step_ref.7) | copy-start | bytes 393220
  40.7 10.0 %collective-permute-start.18 = (bf16[32,2048]{1,0:T(8,128)(2,1)S(1)}, bf16[32,2048]{1,0:T(8,128)(2,1)S(1)}, u32[]{:S(2)}, u32[]{:S(2)}) collective-permute-start(bf16[32,2048]{1,0:T(8,128)(2,1)S(1)} %get-tuple-element.66), channel_id=1, source_target_pairs={{0,2},{2,0},{4,6},{6,4},{1,3},{3,1},{5,7},{7,5},{8,10},{10,8},{12,... | collective-permute-start | bytes 393224 | tf_op jit(solution)/shard_map/ppermute | solution.py:495
  44.4 7.6 %collective-permute-start.19 = (bf16[32,2048]{1,0:T(8,128)(2,1)S(1)}, bf16[32,2048]{1,0:T(8,128)(2,1)S(1)}, u32[]{:S(2)}, u32[]{:S(2)}) collective-permute-start(bf16[32,2048]{1,0:T(8,128)(2,1)S(1)} %get-tuple-element.67), channel_id=1, source_target_pairs={{0,4},{2,6},{4,0},{6,2},{1,5},{3,7},{5,1},{7,3},{8,12},{10,14},{12... | collective-permute-start | bytes 393224 | tf_op jit(solution)/shard_map/ppermute | solution.py:495
  47.6 15.9 %collective-permute-start.13 = (bf16[32,2048]{1,0:T(8,128)(2,1)S(1)}, bf16[32,2048]{1,0:T(8,128)(2,1)S(1)}, u32[]{:S(2)}, u32[]{:S(2)}) collective-permute-start(bf16[32,2048]{1,0:T(8,128)(2,1)S(1)} %get-tuple-element.53), channel_id=1, source_target_pairs={{0,2},{2,0},{4,6},{6,4},{1,3},{3,1},{5,7},{7,5},{8,10},{10,8},{12,... | collective-permute-start | bytes 393224 | tf_op jit(solution)/shard_map/ppermute | solution.py:495
  48.9 14.5 %collective-permute-start.20 = (bf16[32,2048]{1,0:T(8,128)(2,1)S(1)}, bf16[32,2048]{1,0:T(8,128)(2,1)S(1)}, u32[]{:S(2)}, u32[]{:S(2)}) collective-permute-start(bf16[32,2048]{1,0:T(8,128)(2,1)S(1)} %get-tuple-element.68), channel_id=1, source_target_pairs={{0,6},{2,4},{4,2},{6,0},{1,7},{3,5},{5,3},{7,1},{8,14},{10,12},{12... | collective-permute-start | bytes 393224 | tf_op jit(solution)/shard_map/ppermute | solution.py:495
  50.7 16.6 %collective-permute-start.14 = (bf16[32,2048]{1,0:T(8,128)(2,1)S(1)}, bf16[32,2048]{1,0:T(8,128)(2,1)S(1)}, u32[]{:S(2)}, u32[]{:S(2)}) collective-permute-start(bf16[32,2048]{1,0:T(8,128)(2,1)S(1)} %get-tuple-element.54), channel_id=1, source_target_pairs={{0,4},{2,6},{4,0},{6,2},{1,5},{3,7},{5,1},{7,3},{8,12},{10,14},{12... | collective-permute-start | bytes 393224 | tf_op jit(solution)/shard_map/ppermute | solution.py:495
  52.0 15.3 %collective-permute-start.15 = (bf16[32,2048]{1,0:T(8,128)(2,1)S(1)}, bf16[32,2048]{1,0:T(8,128)(2,1)S(1)}, u32[]{:S(2)}, u32[]{:S(2)}) collective-permute-start(bf16[32,2048]{1,0:T(8,128)(2,1)S(1)} %get-tuple-element.55), channel_id=1, source_target_pairs={{0,6},{2,4},{4,2},{6,0},{1,7},{3,5},{5,3},{7,1},{8,14},{10,12},{12... | collective-permute-start | bytes 393224 | tf_op jit(solution)/shard_map/ppermute | solution.py:495
  63.4 18.0 %collective-permute-start.21 = (bf16[128,2048]{1,0:T(8,128)(2,1)S(1)}, bf16[128,2048]{1,0:T(8,128)(2,1)S(1)}, u32[]{:S(2)}, u32[]{:S(2)}) collective-permute-start(bf16[128,2048]{1,0:T(8,128)(2,1)S(1)} %shard_map.73.state), channel_id=1, source_target_pairs={{0,1},{1,0},{2,3},{3,2},{4,5},{5,4},{6,7},{7,6},{8,9},{9,8},{10,11... | collective-permute-start | bytes 1572872 | tf_op jit(solution)/shard_map/ppermute | solution.py:704
  67.3 15.9 %collective-permute-start.16 = (bf16[128,2048]{1,0:T(8,128)(2,1)S(1)}, bf16[128,2048]{1,0:T(8,128)(2,1)S(1)}, u32[]{:S(2)}, u32[]{:S(2)}) collective-permute-start(bf16[128,2048]{1,0:T(8,128)(2,1)S(1)} %shard_map.70.state), channel_id=1, source_target_pairs={{0,1},{1,0},{2,3},{3,2},{4,5},{5,4},{6,7},{7,6},{8,9},{9,8},{10,11... | collective-permute-start | bytes 1572872 | tf_op jit(solution)/shard_map/ppermute | solution.py:704
  (1 other events, 26.7 us)

commit v11 on v10

--- a/solution.py
+++ b/solution.py
@@ -244,22 +244,24 @@
     return body
 
 
-def pieces_kernel(at, own, got, total, *outs, states, chunk, with_decay):
-    base_out = outs[-1]
+def pieces_kernel(at, own, got, *refs, states, chunk, count):
     first = at[0] == 0
+    outs = refs[-count - 1 : -1] if len(refs) > count else refs
     rows, cols = outs[0].shape
-    cols = cols - total.shape[1] if with_decay else cols
+    if len(refs) > count:
+        total, base_out = refs[0], refs[-1]
+        cols = cols - total.shape[1]
+        packed_decay = chip_decay(first, got, total, states, base_out)
+        for out in outs:
+            out[:, cols:] = jnp.concatenate([packed_decay] * (rows // ROW_TILE), axis=0).astype(BF16)
     here = slice(chunk * cols, (chunk + 1) * cols)
     on_own, on_got = mixing_rows(first, own, got, states, here)
-    packed_decay = chip_decay(first, got, total, states, base_out)
-    for k, out in enumerate(outs[:-1]):
+    for k, out in enumerate(outs):
         start = pl.multiple_of(jnp.bitwise_xor(at[1], k) * rows, rows)
         for row in range(0, rows, ROW_BLOCK):
             take = pl.ds(start + row, ROW_BLOCK)
             mixed = on_own * own[take, here].astype(F32) + on_got * got[take, here].astype(F32)
             out[row : row + ROW_BLOCK, :cols] = mixed.astype(BF16)
-        if with_decay:
-            out[:, cols:] = jnp.concatenate([packed_decay] * (rows // ROW_TILE), axis=0).astype(BF16)
 
 
 def decays_of(pieces, cols, first_head, width):
@@ -510,11 +512,15 @@
     lead = CHUNKS - 1
     for chunk in reversed(range(CHUNKS)):
         extra = heads if chunk == lead else 0
-        *pieces, base = small_call(
-            functools.partial(placed(pieces_kernel), states=states, chunk=chunk, with_decay=chunk == lead),
-            [smem] * 3 + [vmem] * 3,
-            [shape((rows, cols + extra), BF16)] * count + [shape((ROW_TILE, heads), F32)],
-        )(*at, own, got, total)
+        taken = [total] if chunk == lead else []
+        given = [shape((ROW_TILE, heads), F32)] if chunk == lead else []
+        pieces = small_call(
+            functools.partial(placed(pieces_kernel), states=states, chunk=chunk, count=count),
+            [smem] * 3 + [vmem] * (2 + len(taken)),
+            [shape((rows, cols + extra), BF16)] * count + given,
+        )(*at, own, got, *taken)
+        if chunk == lead:
+            *pieces, base = pieces
         gathered[chunk] = swapped(pieces, chip_axis)
     entering = {}
     for chunk in reversed(range(CHUNKS)):

time: 85.2 us -> 84.9 us (level)
  no operation moved by 1% of the time
where the time goes in v11:
time: 84.9 us; the launch traced here: 84.7 us
  starting transfers between devices  41.9 us (49%)
  Pallas kernels  25.9 us (31%)
  waiting for transfers between devices  16.5 us (19%)
    ppermute x18, starting transfers between devices, swapped(): done[k] = lax.ppermute(arrays[k], axis, xor_route(size, k))  39.3 us
    ppermute x18, waiting for transfers between devices, swapped(): done[k] = lax.ppermute(arrays[k], axis, xor_route(size, k))  16.5 us
    pallas_call x4, Pallas kernels, within(): pl.pallas_call(functools.partial(within_kernel, dims=half_dims, first_gro...  12.2 us
    pallas_call x2, Pallas kernels, finish_other(): pl.pallas_call(functools.partial(final_kernel, dims=state_dims + (chunk *...  3.43 us
    pallas_call x1, Pallas kernels, local(): pl.pallas_call(functools.partial(send_state_kernel, dims=state_dims), in_...  2.94 us
    pallas_call x1, Pallas kernels, local(): small_call(functools.partial(own_state_kernel, dims=state_dims), [smem, h...  2.89 us
    ppermute x1, starting transfers between devices, local(): late = lax.ppermute(own, core_axis, swap[:1])  1.9 us
    pallas_call x2, Pallas kernels, finish_own(): small_call(functools.partial(own_final_kernel, dims=state_dims + (chunk *...  1.77 us
  transfers between devices with their start and end apart: 22, of which 6 were waited for; matrix products, arithmetic and copies ran while one was open for 0% of the time, Pallas kernels for 25%

profile of v11, /device:TPU:0, one launch (start us, length us, event | category | flops | bytes accessed | tf_op | source)
XLA Modules:
  0.0 84.7 jit_solution(13530257604915257615)
XLA Ops:
  0.0 2.9 %send_state.1 = (bf16[136,4096]{1,0:T(8,128)(2,1)S(1)}, f32[256,128]{1,0:T(8,128)S(1)}, f32[128,256]{1,0:T(8,128)S(1)}, f32[256,128]{1,0:T(8,128)S(1)}, f32[8,12...) custom-call(s32[1]{0:T(128)} %bitcast.half, s32[1]{0:T(128)} %bitcast.2.chip, ...), custom_call_target="tpu_custom_call" | custom-call | tf_op jit(solution)/shard_map/send_state/pallas_call | solution.py:620
  3.5 2.9 %shard_map.64 = (bf16[136,4096]{1,0:T(8,128)(2,1)S(1)}, bf16[128,4096]{1,0:T(8,128)(2,1)S(1)}, bf16[256,4096]{1,0:T(8,128)(2,1)S(1)}, bf16[256,512]{1,0:T(8,128)(2,1)S(1)}) custom-call(s32[1]{0:T(128)} %bitcast.1.half.core.flag, bf16[256,8192]{1,0:T(8,128)(2,1)} %x.3, bf16[256,1024]{1,0:T(8,128)(2,1)} %b.3, f32[256,128]{1,0:T(8,128)S(1)} %get-tuple-element.37.factor, ...), custom_call_target="tpu_custom_call" | custom-call | tf_op jit(solution)/shard_map/pallas_call | solution.py:642
  6.7 2.6 %collective-permute-start.4 = (bf16[32,2176]{1,0:T(8,128)(2,1)S(1)}, bf16[32,2176]{1,0:T(8,128)(2,1)S(1)}, u32[]{:S(2)}, u32[]{:S(2)}) collective-permute-start(bf16[32,2176]{1,0:T(8,128)(2,1)S(1)} %get-tuple-element.46), channel_id=1, source_target_pairs={{0,2},{2,0},{4,6},{6,4},{1,3},{3,1},{5,7},{7,5},{8,10},{10,8},{12,... | collective-permute-start | bytes 417800 | tf_op jit(solution)/shard_map/ppermute | solution.py:497
  9.4 2.6 %collective-permute-start.5 = (bf16[32,2176]{1,0:T(8,128)(2,1)S(1)}, bf16[32,2176]{1,0:T(8,128)(2,1)S(1)}, u32[]{:S(2)}, u32[]{:S(2)}) collective-permute-start(bf16[32,2176]{1,0:T(8,128)(2,1)S(1)} %get-tuple-element.47), channel_id=1, source_target_pairs={{0,4},{2,6},{4,0},{6,2},{1,5},{3,7},{5,1},{7,3},{8,12},{10,14},{12... | collective-permute-start | bytes 417800 | tf_op jit(solution)/shard_map/ppermute | solution.py:497
  12.0 1.9 %collective-permute-start.17 = (bf16[136,4096]{1,0:T(8,128)(2,1)S(1)}, bf16[136,4096]{1,0:T(8,128)(2,1)S(1)}, u32[]{:S(2)}, u32[]{:S(2)}) collective-permute-start(bf16[136,4096]{1,0:T(8,128)(2,1)S(1)} %get-tuple-element.39.refs_0_), channel_id=1, source_target_pairs={{0,1},{2,3},{4,5},{6,7},{8,9},{10,11},{12,13},{14,15},{16,17},{18,... | collective-permute-start | bytes 3342344 | tf_op jit(solution)/shard_map/ppermute | solution.py:651
  16.5 2.1 %collective-permute-start.2 = (bf16[32,2048]{1,0:T(8,128)(2,1)S(1)}, bf16[32,2048]{1,0:T(8,128)(2,1)S(1)}, u32[]{:S(2)}, u32[]{:S(2)}) collective-permute-start(bf16[32,2048]{1,0:T(8,128)(2,1)S(1)} %get-tuple-element.43), channel_id=1, source_target_pairs={{0,4},{2,6},{4,0},{6,2},{1,5},{3,7},{5,1},{7,3},{8,12},{10,14},{12... | collective-permute-start | bytes 393224 | tf_op jit(solution)/shard_map/ppermute | solution.py:497
  18.6 4.0 %collective-permute-done.5.refs_6_.refs_2_.refs_9_ = bf16[32,2176]{1,0:T(8,128)(2,1)S(1)} collective-permute-done((bf16[32,2176]{1,0:T(8,128)(2,1)S(1)}, bf16[32,2176]{1,0:T(8,128)(2,1)S(1)}, u32[]{:S(2)}, u32[]{:S(2)}) %collective-permute-start.5) | collective-permute-done | bytes 139296 | tf_op jit(solution)/shard_map/ppermute | solution.py:497
  22.6 2.7 %collective-permute-start.3 = (bf16[32,2048]{1,0:T(8,128)(2,1)S(1)}, bf16[32,2048]{1,0:T(8,128)(2,1)S(1)}, u32[]{:S(2)}, u32[]{:S(2)}) collective-permute-start(bf16[32,2048]{1,0:T(8,128)(2,1)S(1)} %get-tuple-element.44), channel_id=1, source_target_pairs={{0,6},{2,4},{4,2},{6,0},{1,7},{3,5},{5,3},{7,1},{8,14},{10,12},{12... | collective-permute-start | bytes 393224 | tf_op jit(solution)/shard_map/ppermute | solution.py:497
  25.9 2.4 %collective-permute-start.12 = (bf16[32,2176]{1,0:T(8,128)(2,1)S(1)}, bf16[32,2176]{1,0:T(8,128)(2,1)S(1)}, u32[]{:S(2)}, u32[]{:S(2)}) collective-permute-start(bf16[32,2176]{1,0:T(8,128)(2,1)S(1)} %get-tuple-element.50), channel_id=1, source_target_pairs={{0,24},{8,16},{16,8},{24,0},{1,25},{9,17},{17,9},{25,1},{2,26},{10... | collective-permute-start | bytes 417800 | tf_op jit(solution)/shard_map/ppermute | solution.py:497
  28.9 5.2 %collective-permute-done.2.refs_2_.refs_9_ = bf16[32,2048]{1,0:T(8,128)(2,1)S(1)} collective-permute-done((bf16[32,2048]{1,0:T(8,128)(2,1)S(1)}, bf16[32,2048]{1,0:T(8,128)(2,1)S(1)}, u32[]{:S(2)}, u32[]{:S(2)}) %collective-permute-start.2) | collective-permute-done | bytes 131104 | tf_op jit(solution)/shard_map/ppermute | solution.py:497
  36.0 1.6 %collective-permute-start.9 = (bf16[32,2048]{1,0:T(8,128)(2,1)S(1)}, bf16[32,2048]{1,0:T(8,128)(2,1)S(1)}, u32[]{:S(2)}, u32[]{:S(2)}) collective-permute-start(bf16[32,2048]{1,0:T(8,128)(2,1)S(1)} %get-tuple-element.49), channel_id=1, source_target_pairs={{0,24},{8,16},{16,8},{24,0},{1,25},{9,17},{17,9},{25,1},{2,26},{10... | collective-permute-start | bytes 393224 | tf_op jit(solution)/shard_map/ppermute | solution.py:497
  38.1 1.5 %collective-permute-start.7 = (bf16[32,2048]{1,0:T(8,128)(2,1)S(1)}, bf16[32,2048]{1,0:T(8,128)(2,1)S(1)}, u32[]{:S(2)}, u32[]{:S(2)}) collective-permute-start(bf16[32,2048]{1,0:T(8,128)(2,1)S(1)} %get-tuple-element.49), channel_id=1, source_target_pairs={{0,8},{8,0},{16,24},{24,16},{1,9},{9,1},{17,25},{25,17},{2,10},{10... | collective-permute-start | bytes 393224 | tf_op jit(solution)/shard_map/ppermute | solution.py:497
  40.4 1.8 %collective-permute-start.18 = (bf16[32,2048]{1,0:T(8,128)(2,1)S(1)}, bf16[32,2048]{1,0:T(8,128)(2,1)S(1)}, u32[]{:S(2)}, u32[]{:S(2)}) collective-permute-start(bf16[32,2048]{1,0:T(8,128)(2,1)S(1)} %get-tuple-element.66), channel_id=1, source_target_pairs={{0,2},{2,0},{4,6},{6,4},{1,3},{3,1},{5,7},{7,5},{8,10},{10,8},{12,... | collective-permute-start | bytes 393224 | tf_op jit(solution)/shard_map/ppermute | solution.py:497
  42.2 1.8 %collective-permute-done.9.refs_2_ = bf16[32,2048]{1,0:T(8,128)(2,1)S(1)} collective-permute-done((bf16[32,2048]{1,0:T(8,128)(2,1)S(1)}, bf16[32,2048]{1,0:T(8,128)(2,1)S(1)}, u32[]{:S(2)}, u32[]{:S(2)}) %collective-permute-start.9) | collective-permute-done | bytes 131104 | tf_op jit(solution)/shard_map/ppermute | solution.py:497
  44.0 2.6 %collective-permute-start.19 = (bf16[32,2048]{1,0:T(8,128)(2,1)S(1)}, bf16[32,2048]{1,0:T(8,128)(2,1)S(1)}, u32[]{:S(2)}, u32[]{:S(2)}) collective-permute-start(bf16[32,2048]{1,0:T(8,128)(2,1)S(1)} %get-tuple-element.67), channel_id=1, source_target_pairs={{0,4},{2,6},{4,0},{6,2},{1,5},{3,7},{5,1},{7,3},{8,12},{10,14},{12... | collective-permute-start | bytes 393224 | tf_op jit(solution)/shard_map/ppermute | solution.py:497
  48.6 1.8 %collective-permute-start.20 = (bf16[32,2048]{1,0:T(8,128)(2,1)S(1)}, bf16[32,2048]{1,0:T(8,128)(2,1)S(1)}, u32[]{:S(2)}, u32[]{:S(2)}) collective-permute-start(bf16[32,2048]{1,0:T(8,128)(2,1)S(1)} %get-tuple-element.68), channel_id=1, source_target_pairs={{0,6},{2,4},{4,2},{6,0},{1,7},{3,5},{5,3},{7,1},{8,14},{10,12},{12... | collective-permute-start | bytes 393224 | tf_op jit(solution)/shard_map/ppermute | solution.py:497
  51.6 11.4 %collective-permute-start.15 = (bf16[32,2048]{1,0:T(8,128)(2,1)S(1)}, bf16[32,2048]{1,0:T(8,128)(2,1)S(1)}, u32[]{:S(2)}, u32[]{:S(2)}) collective-permute-start(bf16[32,2048]{1,0:T(8,128)(2,1)S(1)} %get-tuple-element.55), channel_id=1, source_target_pairs={{0,6},{2,4},{4,2},{6,0},{1,7},{3,5},{5,3},{7,1},{8,14},{10,12},{12... | collective-permute-start | bytes 393224 | tf_op jit(solution)/shard_map/ppermute | solution.py:497
  63.1 3.7 %collective-permute-done.14.refs_2_ = bf16[32,2048]{1,0:T(8,128)(2,1)S(1)} collective-permute-done((bf16[32,2048]{1,0:T(8,128)(2,1)S(1)}, bf16[32,2048]{1,0:T(8,128)(2,1)S(1)}, u32[]{:S(2)}, u32[]{:S(2)}) %collective-permute-start.14) | collective-permute-done | bytes 131104 | tf_op jit(solution)/shard_map/ppermute | solution.py:497
  67.0 3.1 %within.7 = bf16[256,2048]{1,0:T(8,128)(2,1)S(1)} custom-call(s32[1]{0:T(128)} %bitcast.1.half.core.flag, s32[1]{0:T(128)} %bitcast.1.half.core.flag, bf16[256,4096]{1,0:T(8,128)(2,1)S(1)} %get-tuple-element.62.x_ref, bf16[256,512]{1,0:T(8,128)(2,1)S(1)} %get-tuple-element.63.b_ref, bf16[256,1024]{1,0:T(8,128)(2,1)S(1)} %copy-done, ...), custom_call_target="tpu_custom_call" | custom-call | tf_op jit(solution)/shard_map/within/pallas_call | solution.py:654
  70.1 3.1 %within.5 = bf16[256,2048]{1,0:T(8,128)(2,1)S(1)} custom-call(s32[1]{0:T(128)} %bitcast.1.half.core.flag, s32[1]{0:T(128)} %bitcast.1.half.core.flag, bf16[256,4096]{1,0:T(8,128)(2,1)S(1)} %get-tuple-element.62.x_ref, bf16[256,512]{1,0:T(8,128)(2,1)S(1)} %get-tuple-element.63.b_ref, bf16[256,1024]{1,0:T(8,128)(2,1)S(1)} %copy-done, ...), custom_call_target="tpu_custom_call" | custom-call | tf_op jit(solution)/shard_map/within/pallas_call | solution.py:654
  73.2 3.1 %within.6 = bf16[256,2048]{1,0:T(8,128)(2,1)S(1)} custom-call(s32[1]{0:T(128)} %bitcast.half, s32[1]{0:T(128)} %bitcast.1.half.core.flag, bf16[256,4096]{1,0:T(8,128)(2,1)S(1)} %get-tuple-element.59.x_ref, bf16[256,512]{1,0:T(8,128)(2,1)S(1)} %get-tuple-element.60.b_ref, bf16[256,1024]{1,0:T(8,128)(2,1)S(1)} %copy-done, f32[256,128]{1,0:T(8,128)S(1)} %copy-done.1, ...), custom_call_target="tpu_custom_call" | custom-call | tf_op jit(solution)/shard_map/within/pallas_call | solution.py:654
  76.2 3.1 %within.4 = bf16[256,2048]{1,0:T(8,128)(2,1)S(1)} custom-call(s32[1]{0:T(128)} %bitcast.half, s32[1]{0:T(128)} %bitcast.1.half.core.flag, bf16[256,4096]{1,0:T(8,128)(2,1)S(1)} %get-tuple-element.59.x_ref, bf16[256,512]{1,0:T(8,128)(2,1)S(1)} %get-tuple-element.60.b_ref, bf16[256,1024]{1,0:T(8,128)(2,1)S(1)} %copy-done, f32[256,128]{1,0:T(8,128)S(1)} %copy-done.1, ...), custom_call_target="tpu_custom_call" | custom-call | tf_op jit(solution)/shard_map/within/pallas_call | solution.py:654
  81.1 1.7 %finish_other.2.refs_0_ = bf16[256,8192]{1,0:T(8,128)(2,1)} custom-call(s32[1]{0:T(128)} %bitcast.half, bf16[256,1024]{1,0:T(8,128)(2,1)S(1)} %copy-done, bf16[128,2048]{1,0:T(8,128)(2,1)S(1)} %collective-permute-done.21.state, f32[256,128]{1,0:T(8,128)S(1)} %get-tuple-element.56.run_ref.run, f32[8,128]{1,0:T(8,128)S(1)} %get-tuple-element.57.base, ...), custom_call_target="tpu_custom_call" | custom-call | tf_op jit(solution)/shard_map/finish_other/pallas_call | solution.py:697
  82.8 1.7 %finish_other.3 = bf16[256,8192]{1,0:T(8,128)(2,1)} custom-call(s32[1]{0:T(128)} %bitcast.half, bf16[256,1024]{1,0:T(8,128)(2,1)S(1)} %copy-done, bf16[128,2048]{1,0:T(8,128)(2,1)S(1)} %collective-permute-done.16.state, f32[256,128]{1,0:T(8,128)S(1)} %get-tuple-element.56.run_ref.run, ...), custom_call_target="tpu_custom_call", output_to_operand_aliasing={{}: (8, {})} | custom-call | tf_op jit(solution)/shard_map/finish_other/pallas_call | solution.py:697
  (44 shorter events, 13.0 us)
Async XLA Ops:
  3.0 3.5 %collective-permute-start = (bf16[136,4096]{1,0:T(8,128)(2,1)S(1)}, bf16[136,4096]{1,0:T(8,128)(2,1)S(1)}, u32[]{:S(2)}, u32[]{:S(2)}) collective-permute-start(bf16[136,4096]{1,0:T(8,128)(2,1)S(1)} %get-tuple-element.40), channel_id=1, source_target_pairs={{0,1},{1,0},{2,3},{3,2},{4,5},{5,4},{6,7},{7,6},{8,9},{9,8},{10,11... | collective-permute-start | bytes 3342344 | tf_op jit(solution)/shard_map/ppermute | solution.py:640
  6.7 9.7 %collective-permute-start.4 = (bf16[32,2176]{1,0:T(8,128)(2,1)S(1)}, bf16[32,2176]{1,0:T(8,128)(2,1)S(1)}, u32[]{:S(2)}, u32[]{:S(2)}) collective-permute-start(bf16[32,2176]{1,0:T(8,128)(2,1)S(1)} %get-tuple-element.46), channel_id=1, source_target_pairs={{0,2},{2,0},{4,6},{6,4},{1,3},{3,1},{5,7},{7,5},{8,10},{10,8},{12,... | collective-permute-start | bytes 417800 | tf_op jit(solution)/shard_map/ppermute | solution.py:497
  9.4 13.3 %collective-permute-start.5 = (bf16[32,2176]{1,0:T(8,128)(2,1)S(1)}, bf16[32,2176]{1,0:T(8,128)(2,1)S(1)}, u32[]{:S(2)}, u32[]{:S(2)}) collective-permute-start(bf16[32,2176]{1,0:T(8,128)(2,1)S(1)} %get-tuple-element.47), channel_id=1, source_target_pairs={{0,4},{2,6},{4,0},{6,2},{1,5},{3,7},{5,1},{7,3},{8,12},{10,14},{12... | collective-permute-start | bytes 417800 | tf_op jit(solution)/shard_map/ppermute | solution.py:497
  12.0 61.2 %collective-permute-start.17 = (bf16[136,4096]{1,0:T(8,128)(2,1)S(1)}, bf16[136,4096]{1,0:T(8,128)(2,1)S(1)}, u32[]{:S(2)}, u32[]{:S(2)}) collective-permute-start(bf16[136,4096]{1,0:T(8,128)(2,1)S(1)} %get-tuple-element.39.refs_0_), channel_id=1, source_target_pairs={{0,1},{2,3},{4,5},{6,7},{8,9},{10,11},{12,13},{14,15},{16,17},{18,... | collective-permute-start | bytes 3342344 | tf_op jit(solution)/shard_map/ppermute | solution.py:651
  13.9 11.5 %collective-permute-start.6 = (bf16[32,2176]{1,0:T(8,128)(2,1)S(1)}, bf16[32,2176]{1,0:T(8,128)(2,1)S(1)}, u32[]{:S(2)}, u32[]{:S(2)}) collective-permute-start(bf16[32,2176]{1,0:T(8,128)(2,1)S(1)} %get-tuple-element.48), channel_id=1, source_target_pairs={{0,6},{2,4},{4,2},{6,0},{1,7},{3,5},{5,3},{7,1},{8,14},{10,12},{12... | collective-permute-start | bytes 417800 | tf_op jit(solution)/shard_map/ppermute | solution.py:497
  14.3 14.1 %collective-permute-start.1 = (bf16[32,2048]{1,0:T(8,128)(2,1)S(1)}, bf16[32,2048]{1,0:T(8,128)(2,1)S(1)}, u32[]{:S(2)}, u32[]{:S(2)}) collective-permute-start(bf16[32,2048]{1,0:T(8,128)(2,1)S(1)} %get-tuple-element.42), channel_id=1, source_target_pairs={{0,2},{2,0},{4,6},{6,4},{1,3},{3,1},{5,7},{7,5},{8,10},{10,8},{12,... | collective-permute-start | bytes 393224 | tf_op jit(solution)/shard_map/ppermute | solution.py:497
  16.5 17.6 %collective-permute-start.2 = (bf16[32,2048]{1,0:T(8,128)(2,1)S(1)}, bf16[32,2048]{1,0:T(8,128)(2,1)S(1)}, u32[]{:S(2)}, u32[]{:S(2)}) collective-permute-start(bf16[32,2048]{1,0:T(8,128)(2,1)S(1)} %get-tuple-element.43), channel_id=1, source_target_pairs={{0,4},{2,6},{4,0},{6,2},{1,5},{3,7},{5,1},{7,3},{8,12},{10,14},{12... | collective-permute-start | bytes 393224 | tf_op jit(solution)/shard_map/ppermute | solution.py:497
  22.6 12.9 %collective-permute-start.3 = (bf16[32,2048]{1,0:T(8,128)(2,1)S(1)}, bf16[32,2048]{1,0:T(8,128)(2,1)S(1)}, u32[]{:S(2)}, u32[]{:S(2)}) collective-permute-start(bf16[32,2048]{1,0:T(8,128)(2,1)S(1)} %get-tuple-element.44), channel_id=1, source_target_pairs={{0,6},{2,4},{4,2},{6,0},{1,7},{3,5},{5,3},{7,1},{8,14},{10,12},{12... | collective-permute-start | bytes 393224 | tf_op jit(solution)/shard_map/ppermute | solution.py:497
  25.9 11.6 %collective-permute-start.12 = (bf16[32,2176]{1,0:T(8,128)(2,1)S(1)}, bf16[32,2176]{1,0:T(8,128)(2,1)S(1)}, u32[]{:S(2)}, u32[]{:S(2)}) collective-permute-start(bf16[32,2176]{1,0:T(8,128)(2,1)S(1)} %get-tuple-element.50), channel_id=1, source_target_pairs={{0,24},{8,16},{16,8},{24,0},{1,25},{9,17},{17,9},{25,1},{2,26},{10... | collective-permute-start | bytes 417800 | tf_op jit(solution)/shard_map/ppermute | solution.py:497
  28.4 9.7 %collective-permute-start.11 = (bf16[32,2176]{1,0:T(8,128)(2,1)S(1)}, bf16[32,2176]{1,0:T(8,128)(2,1)S(1)}, u32[]{:S(2)}, u32[]{:S(2)}) collective-permute-start(bf16[32,2176]{1,0:T(8,128)(2,1)S(1)} %get-tuple-element.50), channel_id=1, source_target_pairs={{0,16},{8,24},{16,0},{24,8},{1,17},{9,25},{17,1},{25,9},{2,18},{10... | collective-permute-start | bytes 417800 | tf_op jit(solution)/shard_map/ppermute | solution.py:497
  34.1 5.8 %collective-permute-start.10 = (bf16[32,2176]{1,0:T(8,128)(2,1)S(1)}, bf16[32,2176]{1,0:T(8,128)(2,1)S(1)}, u32[]{:S(2)}, u32[]{:S(2)}) collective-permute-start(bf16[32,2176]{1,0:T(8,128)(2,1)S(1)} %get-tuple-element.50), channel_id=1, source_target_pairs={{0,8},{8,0},{16,24},{24,16},{1,9},{9,1},{17,25},{25,17},{2,10},{10... | collective-permute-start | bytes 417800 | tf_op jit(solution)/shard_map/ppermute | solution.py:497
  36.0 8.0 %collective-permute-start.9 = (bf16[32,2048]{1,0:T(8,128)(2,1)S(1)}, bf16[32,2048]{1,0:T(8,128)(2,1)S(1)}, u32[]{:S(2)}, u32[]{:S(2)}) collective-permute-start(bf16[32,2048]{1,0:T(8,128)(2,1)S(1)} %get-tuple-element.49), channel_id=1, source_target_pairs={{0,24},{8,16},{16,8},{24,0},{1,25},{9,17},{17,9},{25,1},{2,26},{10... | collective-permute-start | bytes 393224 | tf_op jit(solution)/shard_map/ppermute | solution.py:497
  37.6 9.1 %collective-permute-start.8 = (bf16[32,2048]{1,0:T(8,128)(2,1)S(1)}, bf16[32,2048]{1,0:T(8,128)(2,1)S(1)}, u32[]{:S(2)}, u32[]{:S(2)}) collective-permute-start(bf16[32,2048]{1,0:T(8,128)(2,1)S(1)} %get-tuple-element.49), channel_id=1, source_target_pairs={{0,16},{8,24},{16,0},{24,8},{1,17},{9,25},{17,1},{25,9},{2,18},{10... | collective-permute-start | bytes 393224 | tf_op jit(solution)/shard_map/ppermute | solution.py:497
  38.1 8.6 %collective-permute-start.7 = (bf16[32,2048]{1,0:T(8,128)(2,1)S(1)}, bf16[32,2048]{1,0:T(8,128)(2,1)S(1)}, u32[]{:S(2)}, u32[]{:S(2)}) collective-permute-start(bf16[32,2048]{1,0:T(8,128)(2,1)S(1)} %get-tuple-element.49), channel_id=1, source_target_pairs={{0,8},{8,0},{16,24},{24,16},{1,9},{9,1},{17,25},{25,17},{2,10},{10... | collective-permute-start | bytes 393224 | tf_op jit(solution)/shard_map/ppermute | solution.py:497
  40.4 26.6 %copy-start = (bf16[256,1024]{1,0:T(8,128)(2,1)S(1)}, bf16[256,1024]{1,0:T(8,128)(2,1)}, u32[]{:S(2)}) copy-start(bf16[256,1024]{1,0:T(8,128)(2,1)} %c.7) | copy-start | bytes 1572868
  40.4 26.6 %copy-start.1 = (f32[256,128]{1,0:T(8,128)S(1)}, f32[256,128]{1,0:T(8,128)}, u32[]{:S(2)}) copy-start(f32[256,128]{1,0:T(8,128)} %step_ref.7) | copy-start | bytes 393220
  40.4 9.9 %collective-permute-start.18 = (bf16[32,2048]{1,0:T(8,128)(2,1)S(1)}, bf16[32,2048]{1,0:T(8,128)(2,1)S(1)}, u32[]{:S(2)}, u32[]{:S(2)}) collective-permute-start(bf16[32,2048]{1,0:T(8,128)(2,1)S(1)} %get-tuple-element.66), channel_id=1, source_target_pairs={{0,2},{2,0},{4,6},{6,4},{1,3},{3,1},{5,7},{7,5},{8,10},{10,8},{12,... | collective-permute-start | bytes 393224 | tf_op jit(solution)/shard_map/ppermute | solution.py:497
  44.0 7.6 %collective-permute-start.19 = (bf16[32,2048]{1,0:T(8,128)(2,1)S(1)}, bf16[32,2048]{1,0:T(8,128)(2,1)S(1)}, u32[]{:S(2)}, u32[]{:S(2)}) collective-permute-start(bf16[32,2048]{1,0:T(8,128)(2,1)S(1)} %get-tuple-element.67), channel_id=1, source_target_pairs={{0,4},{2,6},{4,0},{6,2},{1,5},{3,7},{5,1},{7,3},{8,12},{10,14},{12... | collective-permute-start | bytes 393224 | tf_op jit(solution)/shard_map/ppermute | solution.py:497
  47.2 15.9 %collective-permute-start.13 = (bf16[32,2048]{1,0:T(8,128)(2,1)S(1)}, bf16[32,2048]{1,0:T(8,128)(2,1)S(1)}, u32[]{:S(2)}, u32[]{:S(2)}) collective-permute-start(bf16[32,2048]{1,0:T(8,128)(2,1)S(1)} %get-tuple-element.53), channel_id=1, source_target_pairs={{0,2},{2,0},{4,6},{6,4},{1,3},{3,1},{5,7},{7,5},{8,10},{10,8},{12,... | collective-permute-start | bytes 393224 | tf_op jit(solution)/shard_map/ppermute | solution.py:497
  48.6 14.5 %collective-permute-start.20 = (bf16[32,2048]{1,0:T(8,128)(2,1)S(1)}, bf16[32,2048]{1,0:T(8,128)(2,1)S(1)}, u32[]{:S(2)}, u32[]{:S(2)}) collective-permute-start(bf16[32,2048]{1,0:T(8,128)(2,1)S(1)} %get-tuple-element.68), channel_id=1, source_target_pairs={{0,6},{2,4},{4,2},{6,0},{1,7},{3,5},{5,3},{7,1},{8,14},{10,12},{12... | collective-permute-start | bytes 393224 | tf_op jit(solution)/shard_map/ppermute | solution.py:497
  50.3 16.6 %collective-permute-start.14 = (bf16[32,2048]{1,0:T(8,128)(2,1)S(1)}, bf16[32,2048]{1,0:T(8,128)(2,1)S(1)}, u32[]{:S(2)}, u32[]{:S(2)}) collective-permute-start(bf16[32,2048]{1,0:T(8,128)(2,1)S(1)} %get-tuple-element.54), channel_id=1, source_target_pairs={{0,4},{2,6},{4,0},{6,2},{1,5},{3,7},{5,1},{7,3},{8,12},{10,14},{12... | collective-permute-start | bytes 393224 | tf_op jit(solution)/shard_map/ppermute | solution.py:497
  51.6 15.3 %collective-permute-start.15 = (bf16[32,2048]{1,0:T(8,128)(2,1)S(1)}, bf16[32,2048]{1,0:T(8,128)(2,1)S(1)}, u32[]{:S(2)}, u32[]{:S(2)}) collective-permute-start(bf16[32,2048]{1,0:T(8,128)(2,1)S(1)} %get-tuple-element.55), channel_id=1, source_target_pairs={{0,6},{2,4},{4,2},{6,0},{1,7},{3,5},{5,3},{7,1},{8,14},{10,12},{12... | collective-permute-start | bytes 393224 | tf_op jit(solution)/shard_map/ppermute | solution.py:497
  63.1 18.0 %collective-permute-start.21 = (bf16[128,2048]{1,0:T(8,128)(2,1)S(1)}, bf16[128,2048]{1,0:T(8,128)(2,1)S(1)}, u32[]{:S(2)}, u32[]{:S(2)}) collective-permute-start(bf16[128,2048]{1,0:T(8,128)(2,1)S(1)} %shard_map.73.state), channel_id=1, source_target_pairs={{0,1},{1,0},{2,3},{3,2},{4,5},{5,4},{6,7},{7,6},{8,9},{9,8},{10,11... | collective-permute-start | bytes 1572872 | tf_op jit(solution)/shard_map/ppermute | solution.py:710
  66.9 15.9 %collective-permute-start.16 = (bf16[128,2048]{1,0:T(8,128)(2,1)S(1)}, bf16[128,2048]{1,0:T(8,128)(2,1)S(1)}, u32[]{:S(2)}, u32[]{:S(2)}) collective-permute-start(bf16[128,2048]{1,0:T(8,128)(2,1)S(1)} %shard_map.70.state), channel_id=1, source_target_pairs={{0,1},{1,0},{2,3},{3,2},{4,5},{5,4},{6,7},{7,6},{8,9},{9,8},{10,11... | collective-permute-start | bytes 1572872 | tf_op jit(solution)/shard_map/ppermute | solution.py:710
  (1 other events, 26.6 us)
